TPU v7x, 32 devices: a whole 2x2x4 slice. The times are simulated.
32 devices in a mesh: dp: 8 (over y, x, core), mp: 4 (over z).
Axes of the slice: x: 2, y: 2, z: 4, core: 2. Of those that a mesh axis runs over, the one named last changes fastest.
Arguments:
- tokens_in: bfloat16 [8192, 2048], P('dp'), may hold values from -6 to 6
- cotangent: bfloat16 [8192, 2048], P('dp'), may hold values from -6 to 6
- seq_lengths: int32 [8, 4], P('dp'), may hold values from 0 to 512, as said below
- qkv_weight: bfloat16 [2, 2048, 6144], P(None, 'dp', 'mp'), may hold values from -0.125 to 0.125
- dense_weight: bfloat16 [2, 2048, 2048], P(None, 'mp', 'dp'), may hold values from -0.5 to 0.5
- up_weight: bfloat16 [2, 2048, 8192], P(None, 'dp', 'mp'), may hold values from -0.125 to 0.125
- down_weight: bfloat16 [2, 8192, 2048], P(None, 'mp', 'dp'), may hold values from -0.0625 to 0.0625
- qkv_bias: bfloat16 [2, 48, 128], P(None, 'mp', 'dp'), may hold values from -3 to 3
- up_bias: bfloat16 [2, 64, 128], P(None, 'mp', 'dp'), may hold values from -3 to 3
- vectors: bfloat16 [2, 6, 2048], P(None, None, 'dp')
- qkv_weight_first: float32 [2, 2048, 6144], P(None, 'dp', 'mp'), may hold values from -96 to 96
- dense_weight_first: float32 [2, 2048, 2048], P(None, 'mp', 'dp'), may hold values from -48 to 48
- up_weight_first: float32 [2, 2048, 8192], P(None, 'dp', 'mp'), may hold values from -16 to 16
- down_weight_first: float32 [2, 8192, 2048], P(None, 'mp', 'dp'), may hold values from -40 to 40
- qkv_bias_first: float32 [2, 48, 128], P(None, 'mp', 'dp'), may hold values from -128 to 128
- up_bias_first: float32 [2, 64, 128], P(None, 'mp', 'dp'), may hold values from -16 to 16
- vectors_first: float32 [2, 6, 2048], P(None, None, 'dp'), may hold values from -128 to 128
- qkv_weight_second: float32 [2, 2048, 6144], P(None, 'dp', 'mp'), may hold values from 1720.32 to 6799.36
- dense_weight_second: float32 [2, 2048, 2048], P(None, 'mp', 'dp'), may hold values from 450.56 to 1802.24
- up_weight_second: float32 [2, 2048, 8192], P(None, 'dp', 'mp'), may hold values from 61.44 to 245.76
- down_weight_second: float32 [2, 8192, 2048], P(None, 'mp', 'dp'), may hold values from 327.68 to 1310.72
- qkv_bias_second: float32 [2, 48, 128], P(None, 'mp', 'dp'), may hold values from 4096 to 16384
- up_bias_second: float32 [2, 64, 128], P(None, 'mp', 'dp'), may hold values from 39.3216 to 155.648
- vectors_second: float32 [2, 6, 2048], P(None, None, 'dp'), may hold values from 2293.76 to 9256.96
Outputs:
- block_output: bfloat16 [8192, 2048], P('dp')
- input_grad: float32 [8192, 2048], P('dp')
- qkv_weight_grad: float32 [2, 2048, 6144], P(None, 'dp', 'mp')
- qkv_weight_first_new: float32 [2, 2048, 6144], P(None, 'dp', 'mp')
- qkv_weight_second_new: float32 [2, 2048, 6144], P(None, 'dp', 'mp')
- qkv_weight_step: float32 [2, 2048, 6144], P(None, 'dp', 'mp')
- dense_weight_grad: float32 [2, 2048, 2048], P(None, 'mp', 'dp')
- dense_weight_first_new: float32 [2, 2048, 2048], P(None, 'mp', 'dp')
- dense_weight_second_new: float32 [2, 2048, 2048], P(None, 'mp', 'dp')
- dense_weight_step: float32 [2, 2048, 2048], P(None, 'mp', 'dp')
- up_weight_grad: float32 [2, 2048, 8192], P(None, 'dp', 'mp')
- up_weight_first_new: float32 [2, 2048, 8192], P(None, 'dp', 'mp')
- up_weight_second_new: float32 [2, 2048, 8192], P(None, 'dp', 'mp')
- up_weight_step: float32 [2, 2048, 8192], P(None, 'dp', 'mp')
- down_weight_grad: float32 [2, 8192, 2048], P(None, 'mp', 'dp')
- down_weight_first_new: float32 [2, 8192, 2048], P(None, 'mp', 'dp')
- down_weight_second_new: float32 [2, 8192, 2048], P(None, 'mp', 'dp')
- down_weight_step: float32 [2, 8192, 2048], P(None, 'mp', 'dp')
- qkv_bias_grad: float32 [2, 48, 128], P(None, 'mp', 'dp')
- qkv_bias_first_new: float32 [2, 48, 128], P(None, 'mp', 'dp')
- qkv_bias_second_new: float32 [2, 48, 128], P(None, 'mp', 'dp')
- qkv_bias_step: float32 [2, 48, 128], P(None, 'mp', 'dp')
- up_bias_grad: float32 [2, 64, 128], P(None, 'mp', 'dp')
- up_bias_first_new: float32 [2, 64, 128], P(None, 'mp', 'dp')
- up_bias_second_new: float32 [2, 64, 128], P(None, 'mp', 'dp')
- up_bias_step: float32 [2, 64, 128], P(None, 'mp', 'dp')
- vectors_grad: float32 [2, 6, 2048], P(None, None, 'dp')
- updated_vector_first_moment: float32 [2, 6, 2048], P(None, None, 'dp')
- vectors_second_new: float32 [2, 6, 2048], P(None, None, 'dp')
- vectors_step: float32 [2, 6, 2048], P(None, None, 'dp')
Inputs may be any that keep to these rules, and one draw needn't show every extreme that they name: `seq_lengths`: A zero marks an empty slot; the lengths of one index of dp sum to at most 1024, and in every draw some index of dp sums to exactly 1024 with sequences of 512; any other length lies between 64 and 512.
All inputs are finite; a program needn't handle non-finite values.
Results may differ from a plain program's by a relative error of at most 0.012.
Values may be sent and summed in bfloat16 or wider, within the bound.
A program may use at most 384 MiB of HBM per device.

v0:
```python
import jax
import jax.numpy as jnp
from jax import lax
from jax.sharding import PartitionSpec as P

HD = 256
ROT = 64
LAYERS = 2
MAXLEN = 512
ADAM_STEP = 10


norm_eps = 1e-05
beta_one = 0.9
beta_two = 0.95
adam_eps = 1e-08
rate = 0.02
decay = 0.01
masked_score = -1e30


def layout(lengths_row, rows):
    slots = lengths_row.shape[0]
    ends = jnp.cumsum(lengths_row)
    starts = ends - lengths_row
    index = jnp.arange(rows, dtype=jnp.int32)
    inside = (index[:, None] >= starts[None, :]) & (index[:, None] < ends[None, :])
    valid = jnp.any(inside, axis=1)
    number = jnp.arange(slots, dtype=jnp.int32)
    slot = jnp.sum(jnp.where(inside, number[None, :], 0), axis=1)
    first = jnp.sum(jnp.where(inside, starts[None, :], 0), axis=1)
    segment = jnp.where(valid, slot, slots + index)
    position = index - first
    return (segment, position, valid)


def rotary_tables(position):
    half = ROT // 2
    freq = 10000.0 ** (-(jnp.arange(half, dtype=jnp.float32) * 2.0) / ROT)
    angle = position.astype(jnp.float32)[:, None] * freq[None, :]
    return (jnp.cos(angle), jnp.sin(angle))


def rotate(values, cosine, sine):
    half = cosine.shape[1]
    first = values[..., :half]
    second = values[..., half : 2 * half]
    rest = values[..., 2 * half :]
    cfac = cosine[:, None, :]
    sfac = sine[:, None, :]
    return jnp.concatenate(
        [first * cfac - second * sfac, second * cfac + first * sfac, rest], axis=-1
    )


def apply_layer_norm(residual_stream):
    centre = jnp.mean(residual_stream, axis=1, keepdims=True)
    centred = residual_stream - centre
    spread = jnp.mean(centred * centred, axis=1, keepdims=True)
    return centred * lax.rsqrt(spread + norm_eps)


def norm_pair(residual_stream, model_parameters):
    normalized_input_rows = apply_layer_norm(residual_stream)
    return (
        normalized_input_rows * model_parameters[0] + model_parameters[1],
        normalized_input_rows * model_parameters[2] + model_parameters[3],
    )


def gelu_exact(values):
    return jax.nn.gelu(values, approximate=False)


def padded_inputs(keys, values, segment):
    block = MAXLEN
    rows, heads, width = keys.shape
    zeros = jnp.zeros((block, heads, width), keys.dtype)
    keys_pad = jnp.concatenate([zeros, keys], axis=0)
    values_pad = jnp.concatenate([zeros, values], axis=0)
    seg_pad = jnp.concatenate([jnp.full((block,), -1, jnp.int32), segment])
    padded_index_rows = jnp.arange(-block, rows, dtype=jnp.int32)
    return (keys_pad, values_pad, seg_pad, padded_index_rows)


def window(query, keys_pad, values_pad, seg_pad, padded_index_rows, segment, number):
    block = MAXLEN
    start = number * block
    q_blk = lax.dynamic_slice_in_dim(query, start, block, 0)
    k_win = lax.dynamic_slice_in_dim(keys_pad, start, 2 * block, 0)
    v_win = lax.dynamic_slice_in_dim(values_pad, start, 2 * block, 0)
    seg_q = lax.dynamic_slice_in_dim(segment, start, block, 0)
    seg_k = lax.dynamic_slice_in_dim(seg_pad, start, 2 * block, 0)
    idx_q = start + jnp.arange(block, dtype=jnp.int32)
    idx_k = lax.dynamic_slice_in_dim(padded_index_rows, start, 2 * block, 0)
    allowed = (seg_q[:, None] == seg_k[None, :]) & (idx_k[None, :] <= idx_q[:, None])
    scores = jnp.einsum("qhd,khd->hqk", q_blk, k_win, preferred_element_type=jnp.float32) * HD ** (
        -0.5
    )
    scores = jnp.where(allowed[None], scores, masked_score)
    return (start, q_blk, k_win, v_win, scores)


def attention_forward(query, keys, values, segment):
    rows, heads, width = query.shape
    count = rows // MAXLEN
    keys_pad, values_pad, seg_pad, padded_index_rows = padded_inputs(keys, values, segment)

    def one_block(number):
        start, q_blk, k_win, v_win, scores = window(
            query, keys_pad, values_pad, seg_pad, padded_index_rows, segment, number
        )
        top = jnp.max(scores, axis=2, keepdims=True)
        expo = jnp.exp(scores - top)
        total = jnp.sum(expo, axis=2, keepdims=True)
        prob = (expo / total).astype(jnp.bfloat16)
        context = jnp.einsum("hqk,khd->qhd", prob, v_win, preferred_element_type=jnp.float32)
        return (context.astype(jnp.bfloat16), (top + jnp.log(total))[:, :, 0])

    context, logsum = lax.map(one_block, jnp.arange(count, dtype=jnp.int32))
    return (context.reshape(rows, heads * width), logsum)


def attention_backward(query, keys, values, d_context, logsum, segment):
    rows, heads, width = query.shape
    block = MAXLEN
    count = rows // block
    keys_pad, values_pad, seg_pad, padded_index_rows = padded_inputs(keys, values, segment)

    def one_block(carry, inputs):
        dk_acc, dv_acc = carry
        number, lse_blk = inputs
        start, q_blk, k_win, v_win, scores = window(
            query, keys_pad, values_pad, seg_pad, padded_index_rows, segment, number
        )
        do_blk = lax.dynamic_slice_in_dim(d_context, start, block, 0)
        prob = jnp.exp(scores - lse_blk[:, :, None])
        d_prob = jnp.einsum("qhd,khd->hqk", do_blk, v_win, preferred_element_type=jnp.float32)
        delta = jnp.sum(prob * d_prob, axis=2, keepdims=True)
        d_score = (prob * (d_prob - delta)).astype(jnp.bfloat16)
        d_query = jnp.einsum(
            "hqk,khd->qhd", d_score, k_win, preferred_element_type=jnp.float32
        ) * HD ** (-0.5)
        d_keys = jnp.einsum(
            "hqk,qhd->khd", d_score, q_blk, preferred_element_type=jnp.float32
        ) * HD ** (-0.5)
        d_values = jnp.einsum(
            "hqk,qhd->khd", prob.astype(jnp.bfloat16), do_blk, preferred_element_type=jnp.float32
        )
        dk_acc = lax.dynamic_update_slice_in_dim(
            dk_acc, lax.dynamic_slice_in_dim(dk_acc, start, 2 * block, 0) + d_keys, start, 0
        )
        dv_acc = lax.dynamic_update_slice_in_dim(
            dv_acc, lax.dynamic_slice_in_dim(dv_acc, start, 2 * block, 0) + d_values, start, 0
        )
        return ((dk_acc, dv_acc), d_query)

    empty = jnp.zeros((rows + block, heads, width), jnp.float32)
    (dk_acc, dv_acc), d_query = lax.scan(
        one_block, (empty, empty), (jnp.arange(count, dtype=jnp.int32), logsum)
    )
    return (d_query.reshape(rows, heads, width), dk_acc[block:], dv_acc[block:])


def fetch(shards, layer):
    return (
        lax.all_gather(shards[0][layer], "dp", axis=0, tiled=True),
        lax.all_gather(shards[1][layer], "dp", axis=1, tiled=True),
        lax.all_gather(shards[2][layer], "dp", axis=0, tiled=True),
        lax.all_gather(shards[3][layer], "dp", axis=1, tiled=True),
        lax.all_gather(shards[4][layer], "dp", axis=1, tiled=True),
        lax.all_gather(shards[5][layer], "dp", axis=1, tiled=True),
        lax.all_gather(shards[6][layer], "dp", axis=1, tiled=True),
    )


def reduce_grads(grads):
    return (
        lax.psum_scatter(grads[0], "dp", scatter_dimension=1, tiled=True),
        lax.psum_scatter(grads[1], "dp", scatter_dimension=2, tiled=True),
        lax.psum_scatter(grads[2], "dp", scatter_dimension=1, tiled=True),
        lax.psum_scatter(grads[3], "dp", scatter_dimension=2, tiled=True),
        lax.psum_scatter(grads[4], "dp", scatter_dimension=2, tiled=True),
        lax.psum_scatter(grads[5], "dp", scatter_dimension=2, tiled=True),
        lax.psum_scatter(grads[6], "dp", scatter_dimension=2, tiled=True),
    )


def layer_forward(residual_stream, weights, segment, cosine, sine):
    qkv_w, dense_w, up_w, down_w, qkv_b, up_b, vec = weights
    heads = qkv_w.shape[1] // (3 * HD)
    vec_wide = vec.astype(jnp.float32)
    first_branch_input, second_in = norm_pair(residual_stream, vec_wide[:4])
    first_branch_input = first_branch_input.astype(jnp.bfloat16)
    second_in = second_in.astype(jnp.bfloat16)
    rows = first_branch_input.shape[0]
    mixed = jnp.dot(first_branch_input, qkv_w, preferred_element_type=jnp.float32) + qkv_b.reshape(
        -1
    ).astype(jnp.float32)
    mixed = mixed.reshape(rows, heads, 3, HD)
    query = rotate(mixed[:, :, 0], cosine, sine).astype(jnp.bfloat16)
    keys = rotate(mixed[:, :, 1], cosine, sine).astype(jnp.bfloat16)
    values = mixed[:, :, 2].astype(jnp.bfloat16)
    context, logsum = attention_forward(query, keys, values, segment)
    hidden = jnp.dot(second_in, up_w, preferred_element_type=jnp.float32) + up_b.reshape(-1).astype(
        jnp.float32
    )
    active = gelu_exact(hidden).astype(jnp.bfloat16)
    branch = jnp.dot(context, dense_w, preferred_element_type=jnp.float32) + jnp.dot(
        active, down_w, preferred_element_type=jnp.float32
    )
    branch = lax.psum(branch, "mp")
    result = residual_stream + branch + vec_wide[4] + vec_wide[5]
    return (
        result,
        (first_branch_input, second_in, query, keys, values, context, logsum, hidden, active),
    )


def layer_backward(residual_stream, weights, kept, grad_out, segment, cosine, sine):
    qkv_w, dense_w, up_w, down_w, qkv_b, up_b, vec = weights
    first_branch_input, second_in, query, keys, values, context, logsum, hidden, active = kept
    rows, heads = (query.shape[0], query.shape[1])
    grad_low = grad_out.astype(jnp.bfloat16)
    d_dense = jnp.dot(context.T, grad_low, preferred_element_type=jnp.float32)
    d_down = jnp.dot(active.T, grad_low, preferred_element_type=jnp.float32)
    d_context = (
        jnp.dot(grad_low, dense_w.T, preferred_element_type=jnp.float32)
        .astype(jnp.bfloat16)
        .reshape(rows, heads, HD)
    )
    d_active = jnp.dot(grad_low, down_w.T, preferred_element_type=jnp.float32)
    d_hidden = jax.vjp(gelu_exact, hidden)[1](d_active)[0].astype(jnp.bfloat16)
    d_up = jnp.dot(second_in.T, d_hidden, preferred_element_type=jnp.float32)
    d_up_bias = jnp.sum(d_hidden.astype(jnp.float32), axis=0)
    d_second = jnp.dot(d_hidden, up_w.T, preferred_element_type=jnp.float32)
    d_query, d_keys, d_values = attention_backward(query, keys, values, d_context, logsum, segment)
    d_mixed = jnp.stack(
        [rotate(d_query, cosine, -sine), rotate(d_keys, cosine, -sine), d_values], axis=2
    )
    d_mixed = d_mixed.reshape(rows, heads * 3 * HD).astype(jnp.bfloat16)
    d_qkv = jnp.dot(first_branch_input.T, d_mixed, preferred_element_type=jnp.float32)
    d_qkv_bias = jnp.sum(d_mixed.astype(jnp.float32), axis=0)
    d_first = jnp.dot(d_mixed, qkv_w.T, preferred_element_type=jnp.float32)
    vec_wide = vec.astype(jnp.float32)
    pullback = jax.vjp(norm_pair, residual_stream, vec_wide[:4])[1]
    d_resid, d_norm = pullback((d_first, d_second))
    d_resid, d_norm = lax.psum((d_resid, d_norm), "mp")
    d_out_bias = jnp.sum(grad_out, axis=0)
    d_vec = jnp.concatenate([d_norm, d_out_bias[None], d_out_bias[None]], axis=0)
    grads = (
        d_qkv,
        d_dense,
        d_up,
        d_down,
        d_qkv_bias.reshape(qkv_b.shape[0], -1),
        d_up_bias.reshape(up_b.shape[0], -1),
        d_vec,
    )
    return (grad_out + d_resid, grads)


def adam(weight, grad, first, second):
    first_new = beta_one * first + (1.0 - beta_one) * grad
    second_new = beta_two * second + (1.0 - beta_two) * grad * grad
    mean_hat = first_new / (1.0 - beta_one**ADAM_STEP)
    square_hat = second_new / (1.0 - beta_two**ADAM_STEP)
    old = weight.astype(jnp.float32)
    new_weight = old - rate * (mean_hat / (jnp.sqrt(square_hat) + adam_eps) + decay * old)
    return (grad, first_new, second_new, new_weight - old)


def body(
    tokens_in,
    cotangent,
    seq_lengths,
    qkv_weight,
    dense_weight,
    up_weight,
    down_weight,
    qkv_bias,
    up_bias,
    vectors,
    qkv_weight_first,
    dense_weight_first,
    up_weight_first,
    down_weight_first,
    qkv_bias_first,
    up_bias_first,
    vectors_first,
    qkv_weight_second,
    dense_weight_second,
    up_weight_second,
    down_weight_second,
    qkv_bias_second,
    up_bias_second,
    vectors_second,
):
    rows = tokens_in.shape[0]
    segment, position, valid = layout(seq_lengths[0], rows)
    cosine, sine = rotary_tables(position)
    shards = (qkv_weight, dense_weight, up_weight, down_weight, qkv_bias, up_bias, vectors)
    firsts = (
        qkv_weight_first,
        dense_weight_first,
        up_weight_first,
        down_weight_first,
        qkv_bias_first,
        up_bias_first,
        vectors_first,
    )
    seconds = (
        qkv_weight_second,
        dense_weight_second,
        up_weight_second,
        down_weight_second,
        qkv_bias_second,
        up_bias_second,
        vectors_second,
    )
    live = valid.astype(jnp.float32)[:, None]
    residual_stream = tokens_in.astype(jnp.float32)
    inputs, saved, fetched = ([], [], [])
    for layer in range(LAYERS):
        weights = fetch(shards, layer)
        inputs.append(residual_stream)
        residual_stream, kept = layer_forward(residual_stream, weights, segment, cosine, sine)
        saved.append(kept)
        fetched.append(weights)
    output = (residual_stream * live).astype(jnp.bfloat16)
    grad = cotangent.astype(jnp.float32) * live
    per_layer = [None] * LAYERS
    for layer in reversed(range(LAYERS)):
        weights = fetch(shards, layer)
        grad, grads = layer_backward(
            inputs[layer], weights, saved[layer], grad, segment, cosine, sine
        )
        per_layer[layer] = reduce_grads(tuple((item[None] for item in grads)))
    owned = tuple(
        (
            jnp.concatenate([per_layer[layer][slot] for layer in range(LAYERS)], axis=0)
            for slot in range(7)
        )
    )
    outs = [output, grad]
    for weight, summed, first, second in zip(shards, owned, firsts, seconds):
        outs.extend(adam(weight, summed, first, second))
    return tuple(outs)


def solution(mesh):
    placed = (
        P("dp", None),
        P("dp", None),
        P("dp", None),
        P(None, "dp", "mp"),
        P(None, "mp", "dp"),
        P(None, "dp", "mp"),
        P(None, "mp", "dp"),
        P(None, "mp", "dp"),
        P(None, "mp", "dp"),
        P(None, None, "dp"),
        P(None, "dp", "mp"),
        P(None, "mp", "dp"),
        P(None, "dp", "mp"),
        P(None, "mp", "dp"),
        P(None, "mp", "dp"),
        P(None, "mp", "dp"),
        P(None, None, "dp"),
        P(None, "dp", "mp"),
        P(None, "mp", "dp"),
        P(None, "dp", "mp"),
        P(None, "mp", "dp"),
        P(None, "mp", "dp"),
        P(None, "mp", "dp"),
        P(None, None, "dp"),
    )
    return jax.shard_map(
        body,
        mesh=mesh,
        in_specs=placed,
        out_specs=(
            P("dp", None),
            P("dp", None),
            P(None, "dp", "mp"),
            P(None, "dp", "mp"),
            P(None, "dp", "mp"),
            P(None, "dp", "mp"),
            P(None, "mp", "dp"),
            P(None, "mp", "dp"),
            P(None, "mp", "dp"),
            P(None, "mp", "dp"),
            P(None, "dp", "mp"),
            P(None, "dp", "mp"),
            P(None, "dp", "mp"),
            P(None, "dp", "mp"),
            P(None, "mp", "dp"),
            P(None, "mp", "dp"),
            P(None, "mp", "dp"),
            P(None, "mp", "dp"),
            P(None, "mp", "dp"),
            P(None, "mp", "dp"),
            P(None, "mp", "dp"),
            P(None, "mp", "dp"),
            P(None, "mp", "dp"),
            P(None, "mp", "dp"),
            P(None, "mp", "dp"),
            P(None, "mp", "dp"),
            P(None, None, "dp"),
            P(None, None, "dp"),
            P(None, None, "dp"),
            P(None, None, "dp"),
        ),
        check_vma=False,
    )
```

profile of v0, /device:TPU:0, one launch (start us, length us, event | category | flops | bytes accessed | tf_op | source)
XLA Modules:
  0.0 2900.1 jit_solution(7552632364524277170)
XLA Ops:
  17.3 10.6 all-gather
  44.0 9.3 all-gather.5
  59.1 12.5 fusion.148
  88.0 19.0 while.52
  115.0 31.7 %all-gather.27.cloned.1.call-done = bf16[1,2048,2048]{2,1,0:T(8,128)(2,1)} async-done(((bf16[1,256,2048]{2,1,0:T(8,128)(2,1)}), bf16[1,2048,2048]{2,1,0:T(8,128)(2,1)}) %all-gather.27.cloned.1.call-update) | async-done | bytes 8388624 | tf_op jit(solution)/shard_map/all_gather | solution.py:169
  146.7 33.9 %multiply_convert_fusion.4 = (bf16[1024,2048]{1,0:T(8,128)(2,1)}, f32[1024,2048]{1,0:T(8,128)}, f32[1024,2048]{1,0:T(8,128)}) fusion(f32[2048]{0:T(1024)S(1)} %bitcast_convert_fusion.2, bf16[1,2048,2048]{2,1,0:T(8,128)(2,1)} %all-gather.27.cloned.1.call-done, bf16[1024,2048]{1,0:T(8,128)(2,1)} %param.32, f32[2048]{0:T(1024)S(1)} %bitcast.349, ...), kind=kOutput, calls=%fused_computation.189 | convolution fusion | flops 8740929536 | bytes 33587200 | tf_op jit(solution)/shard_map/dot_general | solution.py:205
  180.5 24.4 all-gather.29.cloned.1.call-done
  205.0 15.7 fusion.142
  241.2 9.3 all-gather.12
  257.5 272.0 %all-reduce.20.cloned.1.call-done = f32[1024,2048]{1,0:T(8,128)} async-done(((f32[1024,2048]{1,0:T(8,128)}), f32[1024,2048]{1,0:T(8,128)}) %all-reduce.20.cloned.1.call-update) | async-done | bytes 8388624 | tf_op jit(solution)/shard_map/psum | solution.py:212
  539.5 37.0 %all-gather.31.cloned.1.call-done = bf16[1,2048,1536]{2,1,0:T(8,128)(2,1)} async-done(((bf16[1,256,1536]{2,1,0:T(8,128)(2,1)}), bf16[1,2048,1536]{2,1,0:T(8,128)(2,1)}) %all-gather.31.cloned.1.call-update) | async-done | bytes 6291472 | tf_op jit(solution)/shard_map/all_gather | solution.py:167
  576.5 13.6 fusion.151
  608.3 17.6 while.53
  630.0 72.7 %while.54 = (s32[]{:T(128)}, f32[1536,2,256]{0,2,1:T(8,128)}, f32[1536,2,256]{0,2,1:T(8,128)}, f32[2,512,2,256]{1,0,3,2:T(2,128)}, s32[2]{0:T(128)S(1)}, /*index...) while((s32[]{:T(128)}, f32[1536,2,256]{0,2,1:T(8,128)}, ...), condition=%wide.region_20.21_spmd, body=%wide.region_18.20_spmd.sunk | while | flops 2703490560 | bytes 109115848 | solution.py:159
  646.8 19.7 dynamic_update_slice.58
  683.1 19.6 dynamic_update_slice.58
  714.0 9.4 fusion.134
  723.4 33.7 %multiply_convert_fusion.3 = (bf16[1024,2048]{1,0:T(8,128)(2,1)}, f32[1024,2048]{1,0:T(8,128)}, f32[1024,2048]{1,0:T(8,128)}) fusion(f32[2048]{0:T(1024)S(1)} %copy-done.109, bf16[1,2048,2048]{2,1,0:T(8,128)(2,1)} %all-gather.35.cloned.1.call-done, f32[1024,2048]{1,0:T(8,128)} %copy-done.1, f32[2048]{0:T(1024)S(1)} %bitcast.353, f32[2048]{0:T(1024)S(1)} %bitcast.337, ...), kind=kOutput, calls=%fused_computation.173 | convolution fusion | flops 8738832384 | bytes 37781504 | tf_op jit(solution)/shard_map/dot_general | solution.py:205
  757.2 23.6 convert_reduce_fusion.1
  780.8 22.2 multiply_reduce_fusion.3
  803.1 10.1 fusion.220
  821.5 14.0 fusion.145
  835.6 272.7 %all-reduce.22.cloned.1.call-done = f32[1024,2048]{1,0:T(8,128)} async-done(((f32[1024,2048]{1,0:T(8,128)}), f32[1024,2048]{1,0:T(8,128)}) %all-reduce.22.cloned.1.call-update) | async-done | bytes 8388624 | tf_op jit(solution)/shard_map/psum | solution.py:248
  1121.3 70.4 %while.55 = (s32[]{:T(128)}, f32[1536,2,256]{0,2,1:T(8,128)}, f32[1536,2,256]{2,0,1:T(8,128)}, f32[2,512,2,256]{3,1,0,2:T(8,128)}, s32[2]{0:T(128)S(1)}, /*index...) while((s32[]{:T(128)}, f32[1536,2,256]{0,2,1:T(8,128)}, ...), condition=%wide.region_26.27_spmd, body=%wide.region_24.26_spmd.sunk | while | flops 2703490560 | bytes 98629992 | solution.py:159
  1217.6 11.9 fusion.138
  1229.6 18.5 convert_reduce_fusion.2
  1248.2 18.7 fusion.93
  1298.7 542.4 %all-reduce.26.cloned.1.call-done = (f32[1024,2048]{1,0:T(8,128)}, f32[1024,2048]{1,0:T(8,128)}) async-done(((f32[1024,2048]{1,0:T(8,128)}, f32[1024,2048]{1,0:T(8,128)}), (f32[1024,2048]{1,0:T(8,128)}, f32[1024,2048]{1,0:T(8,128)})) %all-reduce.26.cloned.1.call-update) | async-done | bytes 16777232 | tf_op jit(solution)/shard_map/psum | solution.py:212
  1841.1 19.8 fusion.117
  1860.9 16.1 all-reduce.24.cloned.1.call-done
  1880.0 14.0 convolution_bitcast_fusion.5
  1895.8 14.8 convolution_bitcast_fusion.4
  1911.4 15.8 convolution_bitcast_fusion.3
  1927.4 15.4 convolution_bitcast_fusion.1
  1943.5 16.4 convolution_bitcast_fusion.2
  1960.2 15.6 convolution_bitcast_fusion
  1977.6 9.9 reduce-scatter.43.cloned.1.call-done
  1990.7 33.4 %reduce-scatter.47.cloned.1.call-done = f32[16,16]{1,0:T(8,128)} async-done(((f32[128,16]{1,0:T(8,128)}), f32[16,16]{1,0:T(8,128)}) %reduce-scatter.47.cloned.1.call-update) | async-done | bytes 1040
  2025.6 54.1 %reduce-scatter.27.cloned.1.call-done = f32[1,512,256]{2,1,0:T(8,128)} async-done(((f32[1,512,2048]{2,1,0:T(8,128)}), f32[1,512,256]{2,1,0:T(8,128)}) %reduce-scatter.27.cloned.1.call-update) | async-done | bytes 524304 | tf_op jit(solution)/shard_map/reduce_scatter | solution.py:180
  2080.8 54.0 %reduce-scatter.29.cloned.1.call-done = f32[1,512,256]{2,1,0:T(8,128)} async-done(((f32[1,512,2048]{2,1,0:T(8,128)}), f32[1,512,256]{2,1,0:T(8,128)}) %reduce-scatter.29.cloned.1.call-update) | async-done | bytes 524304 | tf_op jit(solution)/shard_map/reduce_scatter | solution.py:180
  2139.7 32.2 %reduce-scatter.39.cloned.1.call-done = f32[1,6,256]{2,1,0:T(8,128)} async-done(((f32[1,6,2048]{2,1,0:T(8,128)}), f32[1,6,256]{2,1,0:T(8,128)}) %reduce-scatter.39.cloned.1.call-update) | async-done | bytes 6160 | tf_op jit(solution)/shard_map/reduce_scatter | solution.py:185
  2172.6 36.0 %reduce-scatter.41.cloned.1.call-done = f32[1,6,256]{2,1,0:T(8,128)} async-done(((f32[1,6,2048]{2,1,0:T(8,128)}), f32[1,6,256]{2,1,0:T(8,128)}) %reduce-scatter.41.cloned.1.call-update) | async-done | bytes 6160 | tf_op jit(solution)/shard_map/reduce_scatter | solution.py:185
  2211.8 93.2 %reduce-scatter.23.cloned.1.call-done = f32[1,256,1536]{2,1,0:T(8,128)} async-done(((f32[1,2048,1536]{2,1,0:T(8,128)}), f32[1,256,1536]{2,1,0:T(8,128)}) %reduce-scatter.23.cloned.1.call-update) | async-done | bytes 1572880 | tf_op jit(solution)/shard_map/reduce_scatter | solution.py:179
  2306.5 94.8 %reduce-scatter.25.cloned.1.call-done = f32[1,256,1536]{2,1,0:T(8,128)} async-done(((f32[1,2048,1536]{2,1,0:T(8,128)}), f32[1,256,1536]{2,1,0:T(8,128)}) %reduce-scatter.25.cloned.1.call-update) | async-done | bytes 1572880 | tf_op jit(solution)/shard_map/reduce_scatter | solution.py:179
  2410.8 110.5 %reduce-scatter.31.cloned.1.call-done = f32[1,256,2048]{2,1,0:T(8,128)} async-done(((f32[1,2048,2048]{2,1,0:T(8,128)}), f32[1,256,2048]{2,1,0:T(8,128)}) %reduce-scatter.31.cloned.1.call-update) | async-done | bytes 2097168 | tf_op jit(solution)/shard_map/reduce_scatter | solution.py:181
  2524.4 116.7 %reduce-scatter.35.cloned.1.call-done = f32[1,2048,256]{2,1,0:T(8,128)} async-done(((f32[1,2048,2048]{2,1,0:T(8,128)}), f32[1,2048,256]{2,1,0:T(8,128)}) %reduce-scatter.35.cloned.1.call-update) | async-done | bytes 2097168 | tf_op jit(solution)/shard_map/reduce_scatter | solution.py:182
  2644.1 116.9 %reduce-scatter.33.cloned.1.call-done = f32[1,256,2048]{2,1,0:T(8,128)} async-done(((f32[1,2048,2048]{2,1,0:T(8,128)}), f32[1,256,2048]{2,1,0:T(8,128)}) %reduce-scatter.33.cloned.1.call-update) | async-done | bytes 2097168 | tf_op jit(solution)/shard_map/reduce_scatter | solution.py:181
  2773.1 107.8 %reduce-scatter.37.cloned.1.call-done = f32[1,2048,256]{2,1,0:T(8,128)} async-done(((f32[1,2048,2048]{2,1,0:T(8,128)}), f32[1,2048,256]{2,1,0:T(8,128)}) %reduce-scatter.37.cloned.1.call-update) | async-done | bytes 2097168 | tf_op jit(solution)/shard_map/reduce_scatter | solution.py:182
  (592 shorter events, 403.8 us)
Async XLA Ops:
  7.2 51.9 %all-gather.23.cloned.1.call-start = ((), (), s32[]{:S(2)}) async-start(), calls=%async_computation.26 | async-start | bytes 7077888 | tf_op jit(solution)/shard_map/all_gather | solution.py:167
  10.1 97.2 %all-gather.25.cloned.1.call-start = ((), (), s32[]{:S(2)}) async-start(), calls=%async_computation.27 | async-start | bytes 2359296 | tf_op jit(solution)/shard_map/all_gather | solution.py:168
  11.0 135.7 %all-gather.27.cloned.1.call-start = ((), (), s32[]{:S(2)}) async-start(), calls=%async_computation.28 | async-start | bytes 9437184 | tf_op jit(solution)/shard_map/all_gather | solution.py:169
  12.5 192.4 %all-gather.29.cloned.1.call-start = ((), (), s32[]{:S(2)}) async-start(), calls=%async_computation.29 | async-start | bytes 9437184 | tf_op jit(solution)/shard_map/all_gather | solution.py:170
  15.6 235.6 %all-gather.33.cloned.1.call-start = ((), (), s32[]{:S(2)}) async-start(), calls=%async_computation.31 | async-start | bytes 2359296 | tf_op jit(solution)/shard_map/all_gather | solution.py:168
  16.2 513.3 %all-reduce.20.cloned.1.call-start = ((), (), s32[]{:S(2)}) async-start(), calls=%async_computation.14 | async-start | bytes 16777216 | tf_op jit(solution)/shard_map/psum | solution.py:212
  28.6 118.1 %copy-start.68 = (f32[1,1,2048]{2,0,1:T(1,128)}, f32[1,1,2048]{2,0,1:T(1,128)S(1)}, u32[]{:S(2)}) copy-start(f32[1,1,2048]{2,0,1:T(1,128)S(1)} %get-tuple-element.833) | copy-start | bytes 24580
  28.6 118.1 %copy-start.98 = (f32[1,1,2048]{2,0,1:T(1,128)}, f32[1,1,2048]{2,0,1:T(1,128)S(1)}, u32[]{:S(2)}) copy-start(f32[1,1,2048]{2,0,1:T(1,128)S(1)} %get-tuple-element.835) | copy-start | bytes 24580
  42.0 104.6 %copy-start.62 = (f32[1024]{0:T(1024)}, f32[1024]{0:T(1024)S(1)}, u32[]{:S(2)}) copy-start(f32[1024]{0:T(1024)S(1)} %broadcast_multiply_fusion.1) | copy-start | bytes 12292
  43.3 103.4 %copy-start.84 = (f32[1024]{0:T(1024)}, f32[1024]{0:T(1024)S(1)}, u32[]{:S(2)}) copy-start(f32[1024]{0:T(1024)S(1)} %fusion.195) | copy-start | bytes 12292
  53.3 93.3 %copy-start.107 = (f32[2048]{0:T(1024)}, f32[2048]{0:T(1024)S(1)}, u32[]{:S(2)}) copy-start(f32[2048]{0:T(1024)S(1)} %bitcast_convert_fusion.2) | copy-start | bytes 24580
  220.7 355.8 %all-gather.31.cloned.1.call-start = ((), (), s32[]{:S(2)}) async-start(), calls=%async_computation.30 | async-start | bytes 7077888 | tf_op jit(solution)/shard_map/all_gather | solution.py:167
  221.4 501.9 %all-gather.35.cloned.1.call-start = ((), (), s32[]{:S(2)}) async-start(), calls=%async_computation.32 | async-start | bytes 9437184 | tf_op jit(solution)/shard_map/all_gather | solution.py:169
  222.2 535.0 %all-gather.37.cloned.1.call-start = ((), (), s32[]{:S(2)}) async-start(), calls=%async_computation.33 | async-start | bytes 9437184 | tf_op jit(solution)/shard_map/all_gather | solution.py:170
  222.9 885.3 %all-reduce.22.cloned.1.call-start = ((), (), s32[]{:S(2)}) async-start(), calls=%async_computation.15 | async-start | bytes 16777216 | tf_op jit(solution)/shard_map/psum | solution.py:248
  241.1 335.4 %copy-start.74 = (f32[1,1,2048]{2,0,1:T(1,128)}, f32[1,1,2048]{2,0,1:T(1,128)S(1)}, u32[]{:S(2)}) copy-start(f32[1,1,2048]{2,0,1:T(1,128)S(1)} %get-tuple-element.831) | copy-start | bytes 24580
  241.1 335.4 %copy-start.104 = (f32[1,1,2048]{2,0,1:T(1,128)}, f32[1,1,2048]{2,0,1:T(1,128)S(1)}, u32[]{:S(2)}) copy-start(f32[1,1,2048]{2,0,1:T(1,128)S(1)} %get-tuple-element.832) | copy-start | bytes 24580
  251.2 278.3 %copy-start.66 = (f32[1,1,2048]{2,0,1:T(1,128)S(1)}, f32[1,1,2048]{2,0,1:T(1,128)}, u32[]{:S(2)}) copy-start(f32[1,1,2048]{2,0,1:T(1,128)} %get-tuple-element.834) | copy-start | bytes 24580
  251.2 278.3 %copy-start.67 = (f32[1,1,2048]{2,0,1:T(1,128)S(1)}, f32[1,1,2048]{2,0,1:T(1,128)}, u32[]{:S(2)}) copy-start(f32[1,1,2048]{2,0,1:T(1,128)} %get-tuple-element.838) | copy-start | bytes 24580
  539.5 50.7 %copy-start.86 = (f32[1024]{0:T(1024)}, f32[1024]{0:T(1024)S(1)}, u32[]{:S(2)}) copy-start(f32[1024]{0:T(1024)S(1)} %fusion.196) | copy-start | bytes 12292
  817.2 1023.8 %all-reduce.26.cloned.1.call-start = ((), (), s32[]{:S(2)}) async-start(), calls=%async_computation.39 | async-start | bytes 33554432 | tf_op jit(solution)/shard_map/psum | solution.py:212
  835.6 278.4 %copy-start.114 = (bf16[1,512,2048]{2,1,0:T(8,128)(2,1)S(1)}, bf16[1,512,2048]{2,1,0:T(8,128)(2,1)}, u32[]{:S(2)}) copy-start(bf16[1,512,2048]{2,1,0:T(8,128)(2,1)} %all-gather.25.cloned.1.call-done) | copy-start | bytes 6291460
  1278.6 598.3 %all-reduce.24.cloned.1.call-start = ((), (), s32[]{:S(2)}) async-start(), calls=%async_computation.38 | async-start | bytes 131072 | tf_op jit(solution)/shard_map/psum | solution.py:248
  1280.6 695.3 %reduce-scatter.45.cloned.1.call-start = ((), (), s32[]{:S(2)}) async-start(), calls=%async_computation.35 | async-start | bytes 73728
  1281.5 695.4 %reduce-scatter.49.cloned.1.call-start = ((), (), s32[]{:S(2)}) async-start(), calls=%async_computation.37 | async-start | bytes 73728
  1282.3 705.2 %reduce-scatter.43.cloned.1.call-start = ((), (), s32[]{:S(2)}) async-start(), calls=%async_computation.34 | async-start | bytes 73728
  1283.1 741.0 %reduce-scatter.47.cloned.1.call-start = ((), (), s32[]{:S(2)}) async-start(), calls=%async_computation.36 | async-start | bytes 73728
  1283.9 795.7 %reduce-scatter.27.cloned.1.call-start = ((), (), s32[]{:S(2)}) async-start(), calls=%async_computation.18 | async-start | bytes 4718592 | tf_op jit(solution)/shard_map/reduce_scatter | solution.py:180
  1290.7 844.1 %reduce-scatter.29.cloned.1.call-start = ((), (), s32[]{:S(2)}) async-start(), calls=%async_computation.19 | async-start | bytes 4718592 | tf_op jit(solution)/shard_map/reduce_scatter | solution.py:180
  1298.6 542.4 %copy-start.79 = (f32[1,1,2048]{2,0,1:T(1,128)S(1)}, f32[1,1,2048]{2,0,1:T(1,128)}, u32[]{:S(2)}) copy-start(f32[1,1,2048]{2,0,1:T(1,128)} %get-tuple-element.827) | copy-start | bytes 24580
  1298.6 542.4 %copy-start.80 = (f32[1,1,2048]{2,0,1:T(1,128)S(1)}, f32[1,1,2048]{2,0,1:T(1,128)}, u32[]{:S(2)}) copy-start(f32[1,1,2048]{2,0,1:T(1,128)} %get-tuple-element.828) | copy-start | bytes 24580
  1298.7 873.3 %reduce-scatter.39.cloned.1.call-start = ((), (), s32[]{:S(2)}) async-start(), calls=%async_computation.24 | async-start | bytes 73728 | tf_op jit(solution)/shard_map/reduce_scatter | solution.py:185
  1878.4 330.2 %reduce-scatter.41.cloned.1.call-start = ((), (), s32[]{:S(2)}) async-start(), calls=%async_computation.25 | async-start | bytes 73728 | tf_op jit(solution)/shard_map/reduce_scatter | solution.py:185
  1879.9 425.1 %reduce-scatter.23.cloned.1.call-start = ((), (), s32[]{:S(2)}) async-start(), calls=%async_computation.16 | async-start | bytes 14155776 | tf_op jit(solution)/shard_map/reduce_scatter | solution.py:179
  1894.0 507.3 %reduce-scatter.25.cloned.1.call-start = ((), (), s32[]{:S(2)}) async-start(), calls=%async_computation.17 | async-start | bytes 14155776 | tf_op jit(solution)/shard_map/reduce_scatter | solution.py:179
  1910.7 610.6 %reduce-scatter.31.cloned.1.call-start = ((), (), s32[]{:S(2)}) async-start(), calls=%async_computation.20 | async-start | bytes 18874368 | tf_op jit(solution)/shard_map/reduce_scatter | solution.py:181
  1927.2 713.9 %reduce-scatter.35.cloned.1.call-start = ((), (), s32[]{:S(2)}) async-start(), calls=%async_computation.22 | async-start | bytes 18874368 | tf_op jit(solution)/shard_map/reduce_scatter | solution.py:182
  1942.8 818.2 %reduce-scatter.33.cloned.1.call-start = ((), (), s32[]{:S(2)}) async-start(), calls=%async_computation.21 | async-start | bytes 18874368 | tf_op jit(solution)/shard_map/reduce_scatter | solution.py:181
  1959.9 921.0 %reduce-scatter.37.cloned.1.call-start = ((), (), s32[]{:S(2)}) async-start(), calls=%async_computation.23 | async-start | bytes 18874368 | tf_op jit(solution)/shard_map/reduce_scatter | solution.py:182
  1975.8 49.1 %copy-start.78 = (bf16[2,16,16]{2,1,0:T(8,128)(2,1)S(1)}, bf16[2,16,16]{2,1,0:T(8,128)(2,1)}, u32[]{:S(2)}) copy-start(bf16[2,16,16]{2,1,0:T(8,128)(2,1)} %param.40) | copy-start | bytes 3076
  1975.9 160.0 %copy-start.32 = (bf16[2,512,256]{2,1,0:T(8,128)(2,1)S(1)}, bf16[2,512,256]{2,1,0:T(8,128)(2,1)}, u32[]{:S(2)}) copy-start(bf16[2,512,256]{2,1,0:T(8,128)(2,1)} %param.36) | copy-start | bytes 1572868
  1975.9 160.0 %copy-start.39 = (f32[2,512,256]{2,1,0:T(8,128)S(1)}, f32[2,512,256]{2,1,0:T(8,128)}, u32[]{:S(2)}) copy-start(f32[2,512,256]{2,1,0:T(8,128)} %param.50) | copy-start | bytes 3145732
  2080.8 129.1 %copy-start.53 = (bf16[2,6,256]{2,0,1:T(2,128)(2,1)S(1)}, bf16[2,6,256]{2,0,1:T(2,128)(2,1)}, u32[]{:S(2)}) copy-start(bf16[2,6,256]{2,0,1:T(2,128)(2,1)} %param.41) | copy-start | bytes 18436
  2080.8 129.1 %copy-start.94 = (f32[2,6,256]{2,0,1:T(2,128)S(1)}, f32[2,6,256]{2,0,1:T(2,128)}, u32[]{:S(2)}) copy-start(f32[2,6,256]{2,0,1:T(2,128)} %param.55) | copy-start | bytes 36868
  2080.8 129.1 %copy-start.95 = (f32[2,6,256]{2,0,1:T(2,128)S(1)}, f32[2,6,256]{2,0,1:T(2,128)}, u32[]{:S(2)}) copy-start(f32[2,6,256]{2,0,1:T(2,128)} %param.48) | copy-start | bytes 36868
  2135.9 75.8 %copy-start.30 = (f32[2,512,256]{2,1,0:T(8,128)}, f32[2,512,256]{2,1,0:T(8,128)S(1)}, u32[]{:S(2)}) copy-start(f32[2,512,256]{2,1,0:T(8,128)S(1)} %constant_dynamic-update-slice_fusion.6) | copy-start | bytes 3145732
  2524.4 240.0 %copy-start.12 = (bf16[2,256,2048]{2,1,0:T(8,128)(2,1)S(1)}, bf16[2,256,2048]{2,1,0:T(8,128)(2,1)}, u32[]{:S(2)}) copy-start(bf16[2,256,2048]{2,1,0:T(8,128)(2,1)} %param.37) | copy-start | bytes 6291460
  2773.1 110.8 %copy-start.13 = (bf16[2,2048,256]{2,1,0:T(8,128)(2,1)S(1)}, bf16[2,2048,256]{2,1,0:T(8,128)(2,1)}, u32[]{:S(2)}) copy-start(bf16[2,2048,256]{2,1,0:T(8,128)(2,1)} %param.38) | copy-start | bytes 6291460
  (106 other events, 1015.4 us)
Sparse Core Ops, SparseCore 0:
  10.5 48.5 all-gather.22
  61.5 28.1 all-gather.24
  92.2 54.3 all-gather.26
  149.0 55.9 all-gather.28
  207.3 28.4 all-gather.32
  238.6 290.8 all-reduce.19
  531.9 44.5 all-gather.30
  579.0 54.3 all-gather.34
  635.9 55.9 all-gather.36
  817.4 290.8 all-reduce.21
  1278.8 562.2 all-reduce.25
  1843.9 33.0 all-reduce.23
  1880.8 32.8 reduce-scatter.44
  1917.2 33.2 reduce-scatter.48
  1954.2 33.2 reduce-scatter.42
  1990.9 33.2 reduce-scatter.46
  2028.3 51.3 reduce-scatter.26
  2083.5 51.3 reduce-scatter.28
  2138.7 33.2 reduce-scatter.38
  2175.3 33.2 reduce-scatter.40
  2212.5 92.4 reduce-scatter.22
  2308.9 92.3 reduce-scatter.24
  2405.3 115.9 reduce-scatter.30
  2525.1 115.9 reduce-scatter.34
  2645.1 115.9 reduce-scatter.32
  2764.9 115.9 reduce-scatter.36
where the time goes:
time: 2910 us; the launch traced here: 2900 us
  waiting for transfers between devices  2060 us (71%)
  matrix products  430 us (15%)
  local copies, waits for them, and re-layouts  204 us (7%)
  other arithmetic  123 us (4%)
  blocking collectives  55.7 us (2%)
    psum x2, waiting for transfers between devices, layer_forward(): branch = lax.psum(branch, 'mp')  814 us
    psum x2, waiting for transfers between devices, layer_backward(): d_resid, d_norm = lax.psum((d_resid, d_norm), 'mp')  289 us
    reduce_scatter x2, waiting for transfers between devices, reduce_grads(): lax.psum_scatter(grads[2], 'dp', scatter_dimension=1, tiled=True)  227 us
    reduce_scatter x2, waiting for transfers between devices, reduce_grads(): lax.psum_scatter(grads[3], 'dp', scatter_dimension=2, tiled=True)  224 us
    reduce_scatter x2, waiting for transfers between devices, reduce_grads(): lax.psum_scatter(grads[0], 'dp', scatter_dimension=1, tiled=True)  188 us
    reduce_scatter x2, waiting for transfers between devices, reduce_grads(): lax.psum_scatter(grads[1], 'dp', scatter_dimension=2, tiled=True)  108 us
    reduce_scatter x2, waiting for transfers between devices, reduce_grads(): lax.psum_scatter(grads[6], 'dp', scatter_dimension=2, tiled=True)  68.2 us
    dot_general x2, matrix products, layer_forward(): jnp.dot(second_in, up_w, preferred_element_type=jnp.float32)  67.6 us
  transfers between devices with their start and end apart: 26, of which 20 were waited for; matrix products, arithmetic and copies ran while one was open for 17% of the time, Pallas kernels for 0%

commit v1 on v0

v1 whole, which is shorter than its diff:
```python
import functools
import jax
import jax.numpy as jnp
from jax import lax
from jax.experimental import pallas as pl
from jax.experimental.pallas import tpu as pltpu
from jax.sharding import PartitionSpec as P

HD = 256
ROT = 64
MAXLEN = 512
norm_eps = 1e-05
masked_score = -1e30
LAYERS = 2
ADAM_STEP = 10
beta_one = 0.9
beta_two = 0.95
adam_eps = 1e-08
rate = 0.02
decay = 0.01
VM = 60 * 1024 * 1024
BF = jnp.bfloat16
F32 = jnp.float32


def call(kernel, grid, in_specs, out_specs, out_shape, scratch=(), flops=0, nbytes=0, name=None):
    return pl.pallas_call(
        kernel,
        grid_spec=pltpu.PrefetchScalarGridSpec(num_scalar_prefetch=0, grid=grid, in_specs=in_specs, out_specs=out_specs, scratch_shapes=list(scratch)),
        out_shape=out_shape,
        compiler_params=pltpu.CompilerParams(vmem_limit_bytes=VM),
        cost_estimate=pl.CostEstimate(flops=flops, bytes_accessed=nbytes, transcendentals=0),
        name=name,
    )


def spec(shape, index, single=False):
    if single:
        return pl.BlockSpec(shape, index, pipeline_mode=pl.Buffered(1))
    return pl.BlockSpec(shape, index)


def rope_tables(position):
    half = ROT // 2
    freq = 10000.0 ** (-(jnp.arange(half, dtype=F32) * 2.0) / ROT)
    angle = position.astype(F32)[:, None] * freq[None, :]
    c, s = jnp.cos(angle), jnp.sin(angle)
    rows = position.shape[0]
    one = jnp.ones((rows, 128 - ROT), F32)
    zero = jnp.zeros((rows, 128 - ROT), F32)
    return jnp.concatenate([c, c, one], axis=1), jnp.concatenate([-s, s, zero], axis=1)


def turn(u, c, s):
    lane = lax.broadcasted_iota(jnp.int32, u.shape, 1)
    other = jnp.where(lane < ROT // 2, pltpu.roll(u, 128 - ROT // 2, 1), pltpu.roll(u, ROT // 2, 1))
    return u * c + other * s


def normed(x):
    mean = jnp.mean(x, axis=1, keepdims=True)
    centred = x - mean
    var = jnp.mean(centred * centred, axis=1, keepdims=True)
    rstd = lax.rsqrt(var + norm_eps)
    return centred * rstd, mean, rstd


def project(base, extra, vec, wq, bq, cos, sin, wu, bu):
    n, D = base.shape
    C, U = wq.shape[1], wu.shape[1]
    NB = 256
    nq, nu = C // NB, U // NB
    RB = min(n, 128)

    def kernel(*refs):
        if extra is None:
            base_r, vec_r, wq_r, bq_r, cos_r, sin_r, wu_r, bu_r, h1_r, h2_r, mix_r, a_r, gp_r, st_r = refs
        else:
            base_r, extra_r, vec_r, wq_r, bq_r, cos_r, sin_r, wu_r, bu_r, h1_r, h2_r, mix_r, a_r, gp_r, st_r = refs
        j = pl.program_id(0)

        @pl.when(j == 0)
        def _():
            @pl.loop(0, n // RB)
            def _(i):
                rows = pl.ds(pl.multiple_of(i * RB, RB), RB)
                x = base_r[rows, :].astype(F32)
                if extra is not None:
                    x = x + extra_r[rows, :].astype(F32) + vec_r[4:5, :] + vec_r[5:6, :]
                xhat, mean, rstd = normed(x)
                st_r[rows, 0:1] = mean
                st_r[rows, 1:2] = rstd
                h1_r[rows, :] = (xhat * vec_r[0:1, :] + vec_r[1:2, :]).astype(BF)
                h2_r[rows, :] = (xhat * vec_r[2:3, :] + vec_r[3:4, :]).astype(BF)

        @pl.when(j < nq)
        def _():
            m = jnp.dot(h1_r[...], wq_r[...], preferred_element_type=F32) + bq_r[...]
            kind = lax.rem(j, 3)

            @pl.when(kind == 2)
            def _():
                mix_r[...] = m.astype(BF)

            @pl.when(kind != 2)
            def _():
                mix_r[:, :128] = turn(m[:, :128], cos_r[...], sin_r[...]).astype(BF)
                mix_r[:, 128:] = m[:, 128:].astype(BF)

        @pl.when(j >= nq)
        def _():
            f = jnp.dot(h2_r[...], wu_r[...], preferred_element_type=F32) + bu_r[...]
            phi = 0.5 * (1.0 + lax.erf(f * 0.7071067811865476))
            a_r[...] = (f * phi).astype(BF)
            gp_r[...] = (phi + f * (jnp.exp(-0.5 * f * f) * 0.3989422804014327)).astype(BF)

    whole = lambda j: (0, 0)
    qcol = lambda j: (0, jnp.minimum(j, nq - 1))
    ucol = lambda j: (0, jnp.maximum(j - nq, 0))
    ins = [spec((n, D), whole, True)] + ([] if extra is None else [spec((n, D), whole, True)]) + [
        spec((6, D), whole), spec((D, NB), qcol), spec((1, NB), qcol), spec((n, 128), whole, True), spec((n, 128), whole, True),
        spec((D, NB), ucol), spec((1, NB), ucol)]
    outs = [spec((n, D), whole, True), spec((n, D), whole, True), spec((n, NB), qcol), spec((n, NB), ucol), spec((n, NB), ucol), spec((n, 128), whole)]
    shapes = [jax.ShapeDtypeStruct(s, BF) for s in ((n, D), (n, D), (n, C), (n, U), (n, U))] + [jax.ShapeDtypeStruct((n, 128), F32)]
    args = [base] + ([] if extra is None else [extra]) + [vec, wq, bq, cos, sin, wu, bu]
    return call(kernel, (nq + nu,), ins, outs, shapes, flops=2 * n * D * (C + U), nbytes=2 * (n * D * 3 + D * (C + U) + n * (C + 2 * U)), name="project")(*args)


def softmax_block(q, k, segq, segk, q0, k0):
    s = lax.dot_general(q, k, (((1,), (1,)), ((), ())), preferred_element_type=F32) * HD ** (-0.5)
    qi = q0 + lax.broadcasted_iota(jnp.int32, s.shape, 0)
    ki = k0 + lax.broadcasted_iota(jnp.int32, s.shape, 1)
    allowed = (segq == segk) & (ki <= qi)
    s = jnp.where(allowed, s, masked_score)
    top = jnp.max(s, axis=1, keepdims=True)
    e = jnp.exp(s - top)
    return e / jnp.sum(e, axis=1, keepdims=True)


def windows(n, qb):
    for i in range(n // qb):
        q0 = i * qb
        yield q0, max(0, q0 - MAXLEN)


def attend_forward(mixed, seg_col, seg_row):
    n, C = mixed.shape
    H = C // (3 * HD)
    qb = 256

    def kernel(q_r, k_r, v_r, sc_r, sr_r, o_r):
        for q0, k0 in windows(n, qb):
            qs, ks = slice(q0, q0 + qb), slice(k0, q0 + qb)
            p = softmax_block(q_r[qs, :], k_r[ks, :], sc_r[qs, :], sr_r[:, ks], q0, k0)
            o_r[qs, :] = jnp.dot(p.astype(BF), v_r[ks, :], preferred_element_type=F32).astype(BF)

    part = lambda t: spec((n, HD), lambda h: (0, 3 * h + t))
    return call(kernel, (H,), [part(0), part(1), part(2), spec((n, 1), lambda h: (0, 0)), spec((1, n), lambda h: (0, 0))],
                spec((n, HD), lambda h: (0, h)), jax.ShapeDtypeStruct((n, H * HD), BF),
                flops=H * n * 640 * HD * 4, nbytes=2 * n * C, name="attend")(mixed, mixed, mixed, seg_col, seg_row)


def attend_backward(mixed, dctx, seg_col, seg_row, cos, sin):
    n, C = mixed.shape
    H = C // (3 * HD)
    qb = 256
    scale = HD ** (-0.5)

    def kernel(q_r, k_r, v_r, do_r, sc_r, sr_r, cos_r, sin_r, o_r, dk_s, dv_s):
        def back(u, rows):
            c, s = cos_r[rows, :], -sin_r[rows, :]
            return jnp.concatenate([turn(u[:, :128], c, s), u[:, 128:]], axis=1).astype(BF)

        dk_s[...] = jnp.zeros_like(dk_s)
        dv_s[...] = jnp.zeros_like(dv_s)
        for q0, k0 in reversed(list(windows(n, qb))):
            qs, ks = slice(q0, q0 + qb), slice(k0, q0 + qb)
            q, k, do = q_r[qs, :], k_r[ks, :], do_r[qs, :]
            p = softmax_block(q, k, sc_r[qs, :], sr_r[:, ks], q0, k0)
            dp = lax.dot_general(do, v_r[ks, :], (((1,), (1,)), ((), ())), preferred_element_type=F32)
            delta = jnp.sum(p * dp, axis=1, keepdims=True)
            ds = (p * (dp - delta)).astype(BF)
            dq = jnp.dot(ds, k, preferred_element_type=F32) * scale
            dk_s[ks, :] += lax.dot_general(ds, q, (((0,), (0,)), ((), ())), preferred_element_type=F32)
            dv_s[ks, :] += lax.dot_general(p.astype(BF), do, (((0,), (0,)), ((), ())), preferred_element_type=F32)
            o_r[qs, :HD] = back(dq, qs)
            o_r[qs, HD:2 * HD] = back(dk_s[qs, :] * scale, qs)
            o_r[qs, 2 * HD:] = dv_s[qs, :].astype(BF)

    part = lambda t: spec((n, HD), lambda h: (0, 3 * h + t))
    whole = lambda h: (0, 0)
    return call(kernel, (H,), [part(0), part(1), part(2), spec((n, HD), lambda h: (0, h)), spec((n, 1), whole), spec((1, n), whole),
                spec((n, 128), whole), spec((n, 128), whole)],
                spec((n, 3 * HD), lambda h: (0, h)), jax.ShapeDtypeStruct((n, C), BF),
                scratch=[pltpu.VMEM((n, HD), F32), pltpu.VMEM((n, HD), F32)],
                flops=H * n * 640 * HD * 10, nbytes=4 * n * C, name="attend_back")(mixed, mixed, mixed, dctx, seg_col, seg_row, cos, sin)


def branch_out(ctx, act, wd, wn):
    n, R = ctx.shape
    U = act.shape[1]
    dp, _, w = wd.shape

    def kernel(c_r, a_r, wd_r, wn_r, o_r):
        o_r[...] = (jnp.dot(c_r[...], wd_r[...], preferred_element_type=F32) + jnp.dot(a_r[...], wn_r[...], preferred_element_type=F32)).astype(BF)

    whole = lambda s: (0, 0)
    pick = lambda s: (s, 0, 0)
    return call(kernel, (dp,), [spec((n, R), whole, True), spec((n, U), whole, True), spec((None, R, w), pick), spec((None, U, w), pick)],
                spec((n, w), lambda s: (0, s)), jax.ShapeDtypeStruct((n, dp * w), BF),
                flops=2 * n * dp * w * (R + U), nbytes=2 * (n * (R + U) + dp * w * (R + U + n)), name="branch")(ctx, act, wd, wn)


def back_in(gr, gp, wd, wn):
    n, D = gr.shape
    dp, R, w = wd.shape
    U = wn.shape[1]
    NB = 256
    nr, nu = R // NB, U // NB

    def kernel(g_r, gp_r, wd_r, wn_r, dc_r, df_r):
        j = pl.program_id(0)

        def times(w_r):
            acc = None
            for s in range(dp):
                t = lax.dot_general(g_r[:, s * w:(s + 1) * w], w_r[s], (((1,), (1,)), ((), ())), preferred_element_type=F32)
                acc = t if acc is None else acc + t
            return acc

        @pl.when(j < nr)
        def _():
            dc_r[...] = times(wd_r).astype(BF)

        @pl.when(j >= nr)
        def _():
            df_r[...] = (times(wn_r) * gp_r[...].astype(F32)).astype(BF)

    rc = lambda j: jnp.minimum(j, nr - 1)
    uc = lambda j: jnp.maximum(j - nr, 0)
    return call(kernel, (nr + nu,), [spec((n, D), lambda j: (0, 0), True), spec((n, NB), lambda j: (0, uc(j))),
                spec((dp, NB, w), lambda j: (0, rc(j), 0)), spec((dp, NB, w), lambda j: (0, uc(j), 0))],
                [spec((n, NB), lambda j: (0, rc(j))), spec((n, NB), lambda j: (0, uc(j)))],
                [jax.ShapeDtypeStruct((n, R), BF), jax.ShapeDtypeStruct((n, U), BF)],
                flops=2 * n * D * (R + U), nbytes=2 * (n * D + D * (R + U) + n * (R + 2 * U)), name="back_in")(gr, gp, wd, wn)


def back_out(dmix, df, wq, wu, base, extra, vec, stats):
    n, C = dmix.shape
    U = df.shape[1]
    D = wq.shape[0]
    NB = 256

    def kernel(*refs):
        if extra is None:
            dm_r, df_r, wq_r, wu_r, base_r, vec_r, st_r, e_r, g_r = refs
        else:
            dm_r, df_r, wq_r, wu_r, base_r, extra_r, vec_r, st_r, e_r, g_r = refs
        nt = (((1,), (1,)), ((), ()))
        d1 = lax.dot_general(dm_r[...], wq_r[...], nt, preferred_element_type=F32)
        d2 = lax.dot_general(df_r[...], wu_r[...], nt, preferred_element_type=F32)
        e_r[...] = (d1 * vec_r[0:1, :] + d2 * vec_r[2:3, :]).astype(BF)
        x = base_r[...].astype(F32)
        if extra is not None:
            x = x + extra_r[...].astype(F32) + vec_r[4:5, :] + vec_r[5:6, :]
        xhat = (x - st_r[:, 0:1]) * st_r[:, 1:2]
        g_r[0:1, :] = jnp.sum(d1 * xhat, axis=0, keepdims=True)
        g_r[1:2, :] = jnp.sum(d1, axis=0, keepdims=True)
        g_r[2:3, :] = jnp.sum(d2 * xhat, axis=0, keepdims=True)
        g_r[3:4, :] = jnp.sum(d2, axis=0, keepdims=True)

    whole = lambda j: (0, 0)
    col = lambda j: (0, j)
    row = lambda j: (j, 0)
    xs = [spec((n, NB), col)] + ([] if extra is None else [spec((n, NB), col)])
    args = [base] + ([] if extra is None else [extra])
    return call(kernel, (D // NB,), [spec((n, C), whole, True), spec((n, U), whole, True), spec((NB, C), row), spec((NB, U), row)] + xs +
                [spec((6, NB), col), spec((n, 128), whole)],
                [spec((n, NB), col), spec((4, NB), col)],
                [jax.ShapeDtypeStruct((n, D), BF), jax.ShapeDtypeStruct((4, D), F32)],
                flops=2 * n * D * (C + U), nbytes=2 * (n * (C + U) + D * (C + U) + n * D * 3), name="back_out")(dmix, df, wq, wu, *args, vec, stats)


def weight_grad(left, right, w=None):
    n, M = left.shape
    N = right.shape[1]
    MB = 256

    def kernel(l_r, r_r, o_r, s_r):
        g = lax.dot_general(l_r[...], r_r[...], (((0,), (0,)), ((), ())), preferred_element_type=F32)
        if w is None:
            o_r[...] = g.astype(BF)
        else:
            for s in range(N // w):
                o_r[s] = g[:, s * w:(s + 1) * w].astype(BF)

        @pl.when(pl.program_id(0) == 0)
        def _():
            s_r[...] = jnp.sum(r_r[...].astype(F32), axis=0, keepdims=True)

    whole = lambda j: (0, 0)
    if w is None:
        out, shape = spec((MB, N), lambda j: (j, 0)), (M, N)
    else:
        out, shape = spec((N // w, MB, w), lambda j: (0, j, 0)), (N // w, M, w)
    return call(kernel, (M // MB,), [spec((n, MB), lambda j: (0, j)), spec((n, N), whole, True)], [out, spec((1, N), whole)],
                [jax.ShapeDtypeStruct(shape, BF), jax.ShapeDtypeStruct((1, N), F32)],
                flops=2 * n * M * N, nbytes=2 * (n * M + n * N + M * N), name="wgrad")(left, right)


def norm_back(gout, e, base, extra, vec, stats, last):
    n, D = base.shape
    RB = 128

    def kernel(*refs):
        g_r, e_r, base_r = refs[:3]
        refs = refs[3:]
        if extra is not None:
            extra_r, refs = refs[0], refs[1:]
        vec_r, st_r, dx_r = refs[:3]
        x = base_r[...].astype(F32)
        if extra is not None:
            x = x + extra_r[...].astype(F32) + vec_r[4:5, :] + vec_r[5:6, :]
        xhat = (x - st_r[:, 0:1]) * st_r[:, 1:2]
        ev = e_r[...].astype(F32)
        me = jnp.mean(ev, axis=1, keepdims=True)
        mx = jnp.mean(ev * xhat, axis=1, keepdims=True)
        dx = g_r[...].astype(F32) + (ev - me - xhat * mx) * st_r[:, 1:2]
        dx_r[...] = dx
        if not last:
            low_r, sum_r = refs[3:]
            low_r[...] = dx.astype(BF)

            @pl.when(pl.program_id(0) == 0)
            def _():
                sum_r[...] = jnp.zeros_like(sum_r)

            sum_r[...] += jnp.sum(dx, axis=0, keepdims=True)

    row = lambda i: (i, 0)
    whole = lambda i: (0, 0)
    rows = spec((RB, D), row)
    ins = [rows, rows, rows] + ([] if extra is None else [rows]) + [spec((6, D), whole), spec((RB, 128), row)]
    args = [gout, e, base] + ([] if extra is None else [extra]) + [vec, stats]
    outs, shapes = [rows], [jax.ShapeDtypeStruct((n, D), F32)]
    if not last:
        outs += [rows, spec((1, D), whole)]
        shapes += [jax.ShapeDtypeStruct((n, D), BF), jax.ShapeDtypeStruct((1, D), F32)]
    return call(kernel, (n // RB,), ins, outs, shapes, flops=10 * n * D, nbytes=16 * n * D, name="norm_back")(*args)


def adam_update(weight, grad, first, second):
    first_new = beta_one * first + (1.0 - beta_one) * grad
    second_new = beta_two * second + (1.0 - beta_two) * grad * grad
    mean_hat = first_new / (1.0 - beta_one**ADAM_STEP)
    square_hat = second_new / (1.0 - beta_two**ADAM_STEP)
    new_weight = weight - rate * (mean_hat / (jnp.sqrt(square_hat) + adam_eps) + decay * weight)
    return grad, first_new, second_new, new_weight - weight


def adam_layer(layer, weights, grads, firsts, seconds, before):
    steps = 8
    blocks = [(w.shape[1] // steps, w.shape[2]) for w in weights]

    def kernel(*refs):
        ins, outs = refs[:16], refs[-16:]
        for i in range(4):
            g = ins[4 + i][...].astype(F32)
            made = adam_update(ins[i][...].astype(F32), g, ins[8 + i][...], ins[12 + i][...])
            for k in range(4):
                outs[4 * i + k][...] = made[k]

    at = lambda b: spec((None,) + b, lambda j: (layer, j, 0))
    ins = [at(b) for b in blocks] + [spec(b, lambda j: (j, 0)) for b in blocks] + [at(b) for b in blocks] * 2
    args = [*weights, *grads, *firsts, *seconds]
    alias = {}
    if before is not None:
        ins += [pl.BlockSpec(memory_space=pl.ANY)] * 16
        args += list(before)
        alias = {16 + i: i for i in range(16)}
    shapes = [jax.ShapeDtypeStruct(w.shape, F32) for w in weights for _ in range(4)]
    count = sum(w.shape[1] * w.shape[2] for w in weights)
    return pl.pallas_call(
        kernel, grid=(steps,), in_specs=ins, out_specs=[at(b) for b in blocks for _ in range(4)], out_shape=shapes,
        input_output_aliases=alias, compiler_params=pltpu.CompilerParams(vmem_limit_bytes=VM),
        cost_estimate=pl.CostEstimate(flops=20 * count, bytes_accessed=30 * count, transcendentals=0), name="adam")(*args)


def layout(lengths_row, rows):
    slots = lengths_row.shape[0]
    number = jnp.arange(slots, dtype=jnp.int32)
    ends = jnp.sum(jnp.where(number[None, :] <= number[:, None], lengths_row[None, :], 0), axis=1)
    starts = ends - lengths_row
    index = jnp.arange(rows, dtype=jnp.int32)
    inside = (index[:, None] >= starts[None, :]) & (index[:, None] < ends[None, :])
    valid = jnp.any(inside, axis=1)
    slot = jnp.sum(jnp.where(inside, number[None, :], 0), axis=1)
    first = jnp.sum(jnp.where(inside, starts[None, :], 0), axis=1)
    segment = jnp.where(valid, slot, slots + index)
    return segment, index - first, valid


def gather_small(parts):
    flat = jnp.concatenate([p.reshape(-1) for p in parts])
    got = lax.all_gather(flat, "dp", axis=0, tiled=False)
    out, at = [], 0
    for p in parts:
        piece = got[:, at:at + p.size].reshape((-1,) + p.shape)
        out.append(jnp.moveaxis(piece, 0, 2).reshape(p.shape[0], p.shape[1], -1))
        at += p.size
    return out


class PlainLinks:
    def gather(self, shards):
        wq, wd, wu, wn = shards
        rows = lambda v: lax.all_gather(v, "dp", axis=0, tiled=True)
        stack = lambda v: lax.all_gather(v, "dp", axis=0, tiled=False)
        return rows(wq), stack(wd), rows(wu), stack(wn)

    def share(self, v):
        return lax.psum(v, "mp")

    def scatter(self, grads):
        cut = lambda g: lax.psum_scatter(g, "dp", scatter_dimension=0, tiled=True)
        gq, gd, gu, gn = grads
        return cut(gq), cut(gd)[0], cut(gu), cut(gn)[0]


def body(links, tokens_in, cotangent, seq_lengths, *params):
    weights, small = params[:4], params[4:7]
    firsts, small_firsts = params[7:11], params[11:14]
    seconds, small_seconds = params[14:18], params[18:21]
    rows, D = tokens_in.shape
    segment, position, valid = layout(seq_lengths[0], rows)
    cos, sin = rope_tables(position)
    seg_col, seg_row = segment[:, None], segment[None, :]
    live = valid[:, None]
    qb, ub, vecs = gather_small(small)
    qb = qb.reshape(LAYERS, 1, -1).astype(F32)
    ub = ub.reshape(LAYERS, 1, -1).astype(F32)
    vecs = vecs.astype(F32)

    held = [jnp.concatenate([vecs[layer, :4], vecs[layer - 1, 4:]]) for layer in range(LAYERS)]

    full, kept, extra = [], [], None
    for layer in range(LAYERS):
        wq, wd, wu, wn = links.gather([w[layer] for w in weights])
        h1, h2, mixed, act, gp, stats = project(tokens_in, extra, held[layer], wq, qb[layer], cos, sin, wu, ub[layer])
        ctx = attend_forward(mixed, seg_col, seg_row)
        branch = links.share(branch_out(ctx, act, wd, wn))
        full.append((wq, wd, wu, wn))
        kept.append((h1, h2, mixed, act, gp, stats, ctx, extra))
        if layer + 1 < LAYERS:
            extra = branch
    x_last = tokens_in.astype(F32) + extra.astype(F32) + vecs[0, 4] + vecs[0, 5] + branch.astype(F32) + vecs[1, 4] + vecs[1, 5]
    output = jnp.where(live, x_last, 0.0).astype(BF)

    gout = gr = jnp.where(live, cotangent, 0).astype(BF)
    sums = jnp.sum(gout.astype(F32), axis=0, keepdims=True)
    big, little = [None] * LAYERS, [None] * LAYERS
    for layer in reversed(range(LAYERS)):
        wq, wd, wu, wn = full[layer]
        h1, h2, mixed, act, gp, stats, ctx, extra = kept[layer]
        dctx, df = back_in(gr, gp, wd, wn)
        dmix = attend_backward(mixed, dctx, seg_col, seg_row, cos, sin)
        e, norm_sums = back_out(dmix, df, wq, wu, tokens_in, extra, held[layer], stats)
        e = links.share(e)
        gd, _ = weight_grad(ctx, gr, w=wd.shape[2])
        gn, _ = weight_grad(act, gr, w=wn.shape[2])
        gq, qsum = weight_grad(h1, dmix)
        gu, usum = weight_grad(h2, df)
        big[layer] = links.scatter((gq, gd, gu, gn))
        little[layer] = (qsum, usum, norm_sums, sums)
        made = norm_back(gout, e, tokens_in, extra, held[layer], stats, layer == 0)
        if layer:
            gout, gr, sums = made
        else:
            input_grad = made[0]

    done = None
    for layer in reversed(range(LAYERS)):
        done = adam_layer(layer, weights, big[layer], firsts, seconds, done)

    norm_sums = lax.psum(jnp.stack([t[2] for t in little]), "mp")
    qsum = jnp.stack([t[0] for t in little]).reshape(-1)
    usum = jnp.stack([t[1] for t in little]).reshape(-1)
    out_sums = jnp.stack([t[3] for t in little])
    vec_sum = jnp.concatenate([norm_sums, out_sums, out_sums], axis=1).reshape(-1)
    total = lax.psum(jnp.concatenate([qsum, usum, vec_sum]), "dp")
    me = lax.axis_index("dp")
    small_out, at = [], 0
    for p, first, second in zip(small, small_firsts, small_seconds):
        width = p.shape[2]
        wide = p.shape[:2] + (lax.axis_size("dp") * width,)
        size = wide[0] * wide[1] * wide[2]
        g = lax.dynamic_slice_in_dim(total[at:at + size].reshape(wide), me * width, width, 2)
        at += size
        small_out += adam_update(p.astype(F32), g, first, second)
    return (output, input_grad, *done, *small_out)


def solution(mesh):
    rows_dp = P("dp", None)
    wide, tall, vec = P(None, "dp", "mp"), P(None, "mp", "dp"), P(None, None, "dp")
    group = (wide, tall, wide, tall, tall, tall, vec)
    return jax.shard_map(
        functools.partial(body, PlainLinks()),
        mesh=mesh,
        in_specs=(rows_dp,) * 3 + group * 3,
        out_specs=(rows_dp,) * 2 + tuple(s for s in group for _ in range(4)),
        check_vma=False,
    )
```

time: 2910 us -> 1790 us (0.62)
  waiting for transfers between devices: 2060 us -> 1330 us
  matrix products: 430 us -> 0 us
  Pallas kernels: 0 us -> 384 us
  local copies, waits for them, and re-layouts: 204 us -> 20.2 us
  other arithmetic: 123 us -> 22.7 us
  blocking collectives: 55.7 us -> 10.9 us
    psum x4 -> x5, waiting for transfers between devices: 1100 us -> 589 us  [the longest x3 556 us: share(): return lax.psum(v, 'mp')]
    dot_general x52 -> x0, matrix products: 430 us -> none  [the longest x2 67.6 us: layer_forward(): jnp.dot(second_in, up_w, preferred_element_type=jnp.float32)]
    pallas_call x0 -> x24, Pallas kernels: none -> 384 us  [the longest x8 99.5 us: weight_grad(): call(kernel, (M // MB,), [spec((n, MB), lambda j: (0, j)), spec((n, N), w...]
    reduce_scatter x10 -> x8, waiting for transfers between devices: 816 us -> 480 us  [scatter(): cut = lambda g: lax.psum_scatter(g, 'dp', scatter_dimension=0, tiled=True)]
    all_gather x8, waiting for transfers between devices: 97.7 us -> 256 us  [the longest x4 160 us: gather(): rows = lambda v: lax.all_gather(v, 'dp', axis=0, tiled=True)]
    dynamic_update_slice x20 -> x0, local copies, waits for them, and re-layouts: 63.4 us -> none  [the longest x8 46.6 us: attention_backward(): lax.scan(one_block, (empty, empty), (jnp.arange(count, dtype=jnp.int32),...]
    reduce_sum x14 -> x3, other arithmetic: 56.5 us -> 4.47 us  [the longest x1 4.26 us: body(): sums = jnp.sum(gout.astype(F32), axis=0, keepdims=True)]
    all_gather x6 -> x1, blocking collectives: 55.7 us -> 10.9 us  [gather_small(): got = lax.all_gather(flat, 'dp', axis=0, tiled=False)]
  transfers between devices with their start and end apart: 26 -> 21, of which waited for: 20 -> 18; matrix products, arithmetic and copies ran while one was open for 17% -> 2% of each run, Pallas kernels for 0% -> 12%
where the time goes in v1:
time: 1790 us; the launch traced here: 1780 us
  waiting for transfers between devices  1330 us (74%)
  Pallas kernels  384 us (21%)
  other arithmetic  22.7 us (1%)
  local copies, waits for them, and re-layouts  20.2 us (1%)
    psum x3, waiting for transfers between devices, share(): return lax.psum(v, 'mp')  556 us
    reduce_scatter x8, waiting for transfers between devices, scatter(): cut = lambda g: lax.psum_scatter(g, 'dp', scatter_dimension=0, tiled=True)  480 us
    all_gather x4, waiting for transfers between devices, gather(): rows = lambda v: lax.all_gather(v, 'dp', axis=0, tiled=True)  160 us
    pallas_call x8, Pallas kernels, weight_grad(): call(kernel, (M // MB,), [spec((n, MB), lambda j: (0, j)), spec((n, N), w...  99.5 us
    all_gather x4, waiting for transfers between devices, gather(): stack = lambda v: lax.all_gather(v, 'dp', axis=0, tiled=False)  95.8 us
    pallas_call x2, Pallas kernels, project(): call(kernel, (nq + nu,), ins, outs, shapes, flops=2 * n * D * (C + U), nb...  71.4 us
    pallas_call x2, Pallas kernels, back_out(): call(kernel, (D // NB,), [spec((n, C), whole, True), spec((n, U), whole,...  45 us
    pallas_call x2, Pallas kernels, adam_layer(): pl.pallas_call(kernel, grid=(steps,), in_specs=ins, out_specs=[at(b) for...  36.7 us
  transfers between devices with their start and end apart: 21, of which 18 were waited for; matrix products, arithmetic and copies ran while one was open for 2% of the time, Pallas kernels for 12%

profile of v1, /device:TPU:0, one launch (start us, length us, event | category | flops | bytes accessed | tf_op | source)
XLA Modules:
  0.0 1783.8 jit_solution(3326500185650361892)
XLA Ops:
  7.3 2.8 fusion.22
  12.6 3.0 fusion.20
  17.1 10.9 all-gather.5
  33.0 1.9 fusion
  36.2 23.0 %all-gather.23.cloned.1.call-done = bf16[1,2048,1536]{2,1,0:T(8,128)(2,1)} async-done(((bf16[1,256,1536]{2,1,0:T(8,128)(2,1)}), bf16[1,2048,1536]{2,1,0:T(8,128)(2,1)}) %all-gather.23.cloned.1.call-update) | async-done | bytes 6291472 | tf_op jit(solution)/shard_map/all_gather | solution.py:417
  59.2 56.9 %all-gather.25.cloned.1.call-done = bf16[1,2048,2048]{2,1,0:T(8,128)(2,1)} async-done(((bf16[1,256,2048]{2,1,0:T(8,128)(2,1)}), bf16[1,2048,2048]{2,1,0:T(8,128)(2,1)}) %all-gather.25.cloned.1.call-update) | async-done | bytes 8388624 | tf_op jit(solution)/shard_map/all_gather | solution.py:417
  116.1 34.1 %project.2 = (bf16[1024,2048]{1,0:T(8,128)(2,1)}, bf16[1024,2048]{1,0:T(8,128)(2,1)}, bf16[1024,1536]{1,0:T(8,128)(2,1)}, bf16[1024,2048]{1,0:T(8,128)(2,1)}, bf...) custom-call(bf16[1024,2048]{1,0:T(8,128)(2,1)} %refs_2_.5, f32[6,2048]{1,0:T(8,128)} %pad_maximum_fusion.1.refs_1_.refs_5_.refs_3_, ...), custom_call_target="tpu_custom_call" | custom-call | flops 15032385536 | bytes 38797312 | tf_op jit(solution)/shard_map/project/pallas_call | solution.py:126
  150.2 6.5 attend.2.c_r.l_r
  156.7 46.5 %all-gather.17.cloned.1.call-done.wn_r = bf16[8,2048,256]{2,1,0:T(8,128)(2,1)} async-done(((bf16[1,2048,256]{2,1,0:T(8,128)(2,1)}), bf16[8,2048,256]{2,1,0:T(8,128)(2,1)}) %all-gather.17.cloned.1.call-update) | async-done | bytes 8388624 | tf_op jit(solution)/shard_map/all_gather | solution.py:418
  203.2 16.1 branch.2
  223.5 4.3 convert_reduce_fusion
  227.8 23.3 %all-gather.27.cloned.1.call-done = bf16[1,2048,1536]{2,1,0:T(8,128)(2,1)} async-done(((bf16[1,256,1536]{2,1,0:T(8,128)(2,1)}), bf16[1,2048,1536]{2,1,0:T(8,128)(2,1)}) %all-gather.27.cloned.1.call-update) | async-done | bytes 6291472 | tf_op jit(solution)/shard_map/all_gather | solution.py:417
  251.1 56.7 %all-gather.29.cloned.1.call-done = bf16[1,2048,2048]{2,1,0:T(8,128)(2,1)} async-done(((bf16[1,256,2048]{2,1,0:T(8,128)(2,1)}), bf16[1,2048,2048]{2,1,0:T(8,128)(2,1)}) %all-gather.29.cloned.1.call-update) | async-done | bytes 8388624 | tf_op jit(solution)/shard_map/all_gather | solution.py:417
  307.8 157.9 %all-reduce.7.cloned.1.call-done.refs_1_.refs_5_.refs_3_ = bf16[1024,2048]{1,0:T(8,128)(2,1)} async-done(((bf16[1024,2048]{1,0:T(8,128)(2,1)}), bf16[1024,2048]{1,0:T(8,128)(2,1)}) %all-reduce.7.cloned.1.call-update) | async-done | bytes 4194320 | tf_op jit(solution)/shard_map/psum | solution.py:422
  465.8 37.3 %project.3 = (bf16[1024,2048]{1,0:T(8,128)(2,1)}, bf16[1024,2048]{1,0:T(8,128)(2,1)}, bf16[1024,1536]{1,0:T(8,128)(2,1)}, bf16[1024,2048]{1,0:T(8,128)(2,1)}, bf...) custom-call(bf16[1024,2048]{1,0:T(8,128)(2,1)} %refs_2_.5, ...), custom_call_target="tpu_custom_call" | custom-call | flops 15032385536 | bytes 38797312 | tf_op jit(solution)/shard_map/project/pallas_call | solution.py:126
  503.1 49.3 %all-gather.21.cloned.1.call-done.wn_r = bf16[8,2048,256]{2,1,0:T(8,128)(2,1)} async-done(((bf16[1,2048,256]{2,1,0:T(8,128)(2,1)}), bf16[8,2048,256]{2,1,0:T(8,128)(2,1)}) %all-gather.21.cloned.1.call-update) | async-done | bytes 8388624 | tf_op jit(solution)/shard_map/all_gather | solution.py:418
  552.4 18.1 %back_in.2 = (bf16[1024,512]{1,0:T(8,128)(2,1)}, bf16[1024,2048]{1,0:T(8,128)(2,1)}) custom-call(bf16[1024,2048]{1,0:T(8,128)(2,1)} %get-tuple-element.301.g_r.refs_0_.r_r, bf16[1024,2048]{1,0:T(8,128)(2,1)} %get-tuple-element.101.gp_r, bf16[8,512,256]{2,1,0:T(8,128)(2,1)} %all-gather.19.cloned.1.call-done.wd_r, ...), custom_call_target="tpu_custom_call" | custom-call | flops 10737418240 | bytes 24117248 | tf_op jit(solution)/shard_map/back_in/pallas_call | solution.py:241
  570.5 11.4 attend_back.2.refs_0_.r_r
  581.9 22.8 %back_out.2 = (bf16[1024,2048]{1,0:T(8,128)(2,1)}, f32[4,2048]{1,0:T(4,128)}) custom-call(bf16[1024,1536]{1,0:T(8,128)(2,1)} %attend_back.2.refs_0_.r_r, bf16[1024,2048]{1,0:T(8,128)(2,1)} %get-tuple-element.103.refs_1_.r_r, bf16[2048,1536]{1,0:T(8,128)(2,1)} %bitcast.103, bf16[2048,2048]{1,0:T(8,128)(2,1)} %bitcast.99, bf16[1024,2048]{1,0:T(8,128)(2,1)} %refs_2_.5, ...), custom_call_target="tpu_custom_call" | custom-call | flops 15032385536 | bytes 34603008 | tf_op jit(solution)/shard_map/back_out/pallas_call | solution.py:277
  605.0 6.5 attend.3.c_r.l_r
  611.6 12.7 wgrad.12
  624.2 15.0 wgrad.14
  639.2 120.7 %all-reduce.9.cloned.1.call-done.refs_1_ = bf16[1024,2048]{1,0:T(8,128)(2,1)} async-done(((bf16[1024,2048]{1,0:T(8,128)(2,1)}), bf16[1024,2048]{1,0:T(8,128)(2,1)}) %all-reduce.9.cloned.1.call-update) | async-done | bytes 4194320 | tf_op jit(solution)/shard_map/psum | solution.py:422
  759.9 14.8 norm_back.2
  774.7 18.2 %back_in.3 = (bf16[1024,512]{1,0:T(8,128)(2,1)}, bf16[1024,2048]{1,0:T(8,128)(2,1)}) custom-call(bf16[1024,2048]{1,0:T(8,128)(2,1)} %get-tuple-element.107.g_r.r_r, bf16[1024,2048]{1,0:T(8,128)(2,1)} %get-tuple-element.108.gp_r, bf16[8,512,256]{2,1,0:T(8,128)(2,1)} %all-gather.15.cloned.1.call-done.wd_r, bf16[8,2048,256]{2,1,0:T(8,128)(2,1)} %all-gather.17.cloned.1.call-done.wn_r), custom_call_target="tpu_custom_call" | custom-call | flops 10737418240 | bytes 24117248 | tf_op jit(solution)/shard_map/back_in/pallas_call | solution.py:241
  792.9 11.4 attend_back.3.refs_0_.r_r
  804.3 13.0 wgrad.8
  817.3 22.2 %back_out.3 = (bf16[1024,2048]{1,0:T(8,128)(2,1)}, f32[4,2048]{1,0:T(4,128)}) custom-call(bf16[1024,1536]{1,0:T(8,128)(2,1)} %attend_back.3.refs_0_.r_r, bf16[1024,2048]{1,0:T(8,128)(2,1)} %get-tuple-element.110.refs_1_.r_r, bf16[2048,1536]{1,0:T(8,128)(2,1)} %bitcast.101, bf16[2048,2048]{1,0:T(8,128)(2,1)} %bitcast.97, bf16[1024,2048]{1,0:T(8,128)(2,1)} %refs_2_.5, ...), custom_call_target="tpu_custom_call" | custom-call | flops 15032385536 | bytes 34603008 | tf_op jit(solution)/shard_map/back_out/pallas_call | solution.py:277
  839.5 15.1 wgrad.10
  856.1 32.3 %all-reduce.11.cloned.1.call-done = f32[2,4,2048]{2,1,0:T(4,128)} async-done(((f32[2,4,2048]{2,1,0:T(4,128)}), f32[2,4,2048]{2,1,0:T(4,128)}) %all-reduce.11.cloned.1.call-update) | async-done | bytes 65552 | tf_op jit(solution)/shard_map/psum | solution.py:485
  890.1 16.1 branch.3
  906.2 6.8 wgrad.13
  914.2 15.0 wgrad.15
  929.3 6.8 wgrad.9
  937.5 15.3 wgrad.11
  962.0 277.5 %all-reduce.15.cloned.1.call-done = (bf16[1024,2048]{1,0:T(8,128)(2,1)}, bf16[1024,2048]{1,0:T(8,128)(2,1)}) async-done(((bf16[1024,2048]{1,0:T(8,128)(2,1)}, bf16[1024,2048]{1,0:T(8,128)(2,1)}), (bf16[1024,2048]{1,0:T(8,128)(2,1)}, bf16[1024,2048]{1,0:T(8,128)(2,1)})) %all-reduce.15.cloned.1.call-update) | async-done | bytes 8388624 | tf_op jit(solution)/shard_map/psum | solution.py:422
  1239.6 12.4 norm_back.3
  1252.0 31.6 %reduce-scatter.19.cloned.1.call-done = bf16[1,512,256]{2,1,0:T(8,128)(2,1)} async-done(((bf16[8,512,256]{2,1,0:T(8,128)(2,1)}), bf16[1,512,256]{2,1,0:T(8,128)(2,1)}) %reduce-scatter.19.cloned.1.call-update) | async-done | bytes 262160 | tf_op jit(solution)/shard_map/reduce_scatter | solution.py:425
  1283.5 65.4 %reduce-scatter.17.cloned.1.call-done.refs_4_ = bf16[256,1536]{1,0:T(8,128)(2,1)} async-done(((bf16[2048,1536]{1,0:T(8,128)(2,1)}), bf16[256,1536]{1,0:T(8,128)(2,1)}) %reduce-scatter.17.cloned.1.call-update) | async-done | bytes 786448 | tf_op jit(solution)/shard_map/reduce_scatter | solution.py:425
  1348.9 74.6 %reduce-scatter.21.cloned.1.call-done.refs_6_ = bf16[256,2048]{1,0:T(8,128)(2,1)} async-done(((bf16[2048,2048]{1,0:T(8,128)(2,1)}), bf16[256,2048]{1,0:T(8,128)(2,1)}) %reduce-scatter.21.cloned.1.call-update) | async-done | bytes 1048592 | tf_op jit(solution)/shard_map/reduce_scatter | solution.py:425
  1423.5 75.0 %reduce-scatter.23.cloned.1.call-done = bf16[1,2048,256]{2,1,0:T(8,128)(2,1)} async-done(((bf16[8,2048,256]{2,1,0:T(8,128)(2,1)}), bf16[1,2048,256]{2,1,0:T(8,128)(2,1)}) %reduce-scatter.23.cloned.1.call-update) | async-done | bytes 1048592 | tf_op jit(solution)/shard_map/reduce_scatter | solution.py:425
  1498.5 18.5 %adam.2 = (f32[2,256,1536]{2,1,0:T(8,128)}, f32[2,256,1536]{2,1,0:T(8,128)}, f32[2,256,1536]{2,1,0:T(8,128)}, f32[2,256,1536]{2,1,0:T(8,128)}, f32[2,512,256]{2,...) custom-call(bf16[2,256,1536]{2,1,0:T(8,128)(2,1)} %refs_0_.7, ...), custom_call_target="tpu_custom_call" | custom-call | flops 31457280 | bytes 47185920 | tf_op jit(solution)/shard_map/adam/pallas_call | solution.py:383
  1517.0 8.2 select_convert_fusion
  1525.3 17.7 reduce-scatter.11.cloned.1.call-done
  1542.9 65.5 %reduce-scatter.9.cloned.1.call-done.refs_4_ = bf16[256,1536]{1,0:T(8,128)(2,1)} async-done(((bf16[2048,1536]{1,0:T(8,128)(2,1)}), bf16[256,1536]{1,0:T(8,128)(2,1)}) %reduce-scatter.9.cloned.1.call-update) | async-done | bytes 786448 | tf_op jit(solution)/shard_map/reduce_scatter | solution.py:425
  1608.5 74.6 %reduce-scatter.13.cloned.1.call-done.refs_6_ = bf16[256,2048]{1,0:T(8,128)(2,1)} async-done(((bf16[2048,2048]{1,0:T(8,128)(2,1)}), bf16[256,2048]{1,0:T(8,128)(2,1)}) %reduce-scatter.13.cloned.1.call-update) | async-done | bytes 1048592 | tf_op jit(solution)/shard_map/reduce_scatter | solution.py:425
  1683.1 75.2 %reduce-scatter.15.cloned.1.call-done = bf16[1,2048,256]{2,1,0:T(8,128)(2,1)} async-done(((bf16[8,2048,256]{2,1,0:T(8,128)(2,1)}), bf16[1,2048,256]{2,1,0:T(8,128)(2,1)}) %reduce-scatter.15.cloned.1.call-update) | async-done | bytes 1048592 | tf_op jit(solution)/shard_map/reduce_scatter | solution.py:425
  1758.2 18.2 %adam.3 = (f32[2,256,1536]{2,1,0:T(8,128)}, f32[2,256,1536]{2,1,0:T(8,128)}, f32[2,256,1536]{2,1,0:T(8,128)}, f32[2,256,1536]{2,1,0:T(8,128)}, f32[2,512,256]{2,...) custom-call(bf16[2,256,1536]{2,1,0:T(8,128)(2,1)} %refs_0_.7, ...), custom_call_target="tpu_custom_call", output_to_operand_aliasing={{0}: (16, {}), {1}: (17, {}), {2}: (18, {}), {3}: (19, {}),... | custom-call | flops 31457280 | bytes 47185920 | tf_op jit(solution)/shard_map/adam/pallas_call | solution.py:383
  (165 shorter events, 29.3 us)
Async XLA Ops:
  7.2 2.9 copy-start
  7.2 4.5 copy-start.1
  7.2 52.0 %all-gather.23.cloned.1.call-start = ((), (), s32[]{:S(2)}) async-start(), calls=%async_computation.24 | async-start | bytes 7077888 | tf_op jit(solution)/shard_map/all_gather | solution.py:417
  10.1 106.0 %all-gather.25.cloned.1.call-start = ((), (), s32[]{:S(2)}) async-start(), calls=%async_computation.25 | async-start | bytes 9437184 | tf_op jit(solution)/shard_map/all_gather | solution.py:417
  11.6 5.2 copy-start.11
  11.6 5.3 copy-start.5
  11.6 5.4 copy-start.9
  11.6 145.1 %all-gather.15.cloned.1.call-start = ((), (), s32[]{:S(2)}) async-start(), calls=%async_computation.8 | async-start | bytes 2359296 | tf_op jit(solution)/shard_map/all_gather | solution.py:418
  12.5 17.6 copy-start.23
  12.6 190.7 %all-gather.17.cloned.1.call-start = ((), (), s32[]{:S(2)}) async-start(), calls=%async_computation.9 | async-start | bytes 9437184 | tf_op jit(solution)/shard_map/all_gather | solution.py:418
  15.6 235.5 %all-gather.27.cloned.1.call-start = ((), (), s32[]{:S(2)}) async-start(), calls=%async_computation.26 | async-start | bytes 7077888 | tf_op jit(solution)/shard_map/all_gather | solution.py:417
  16.2 291.6 %all-gather.29.cloned.1.call-start = ((), (), s32[]{:S(2)}) async-start(), calls=%async_computation.27 | async-start | bytes 9437184 | tf_op jit(solution)/shard_map/all_gather | solution.py:417
  16.8 449.0 %all-reduce.7.cloned.1.call-start = ((), (), s32[]{:S(2)}) async-start(), calls=%async_computation.10 | async-start | bytes 8388608 | tf_op jit(solution)/shard_map/psum | solution.py:422
  28.1 2.2 copy-start.2
  30.7 192.8 %copy-start.7 = (pred[1024]{0:T(1024)(128)(4,1)}, pred[1024]{0:T(1024)(128)(4,1)S(1)}, u32[]{:S(2)}) copy-start(pred[1024]{0:T(1024)(128)(4,1)S(1)} %fusion.14) | copy-start | bytes 3076
  219.4 283.7 %all-gather.19.cloned.1.call-start = ((), (), s32[]{:S(2)}) async-start(), calls=%async_computation.11 | async-start | bytes 2359296 | tf_op jit(solution)/shard_map/all_gather | solution.py:418
  220.1 332.2 %all-gather.21.cloned.1.call-start = ((), (), s32[]{:S(2)}) async-start(), calls=%async_computation.12 | async-start | bytes 9437184 | tf_op jit(solution)/shard_map/all_gather | solution.py:418
  220.9 539.1 %all-reduce.9.cloned.1.call-start = ((), (), s32[]{:S(2)}) async-start(), calls=%async_computation.13 | async-start | bytes 8388608 | tf_op jit(solution)/shard_map/psum | solution.py:422
  604.8 283.6 %all-reduce.11.cloned.1.call-start = ((), (), s32[]{:S(2)}) async-start(), calls=%async_computation.22 | async-start | bytes 131072 | tf_op jit(solution)/shard_map/psum | solution.py:485
  839.5 15.1 copy-start.3
  839.5 15.1 copy-start.4
  839.5 15.8 copy-start.19
  839.5 16.6 copy-start.21
  839.5 16.5 copy-start.22
  839.5 48.9 %copy-start.20 = (f32[1,2048]{1,0:T(1,128)S(1)}, f32[1,2048]{1,0:T(1,128)}, u32[]{:S(2)}) copy-start(f32[1,2048]{1,0:T(1,128)} %get-tuple-element.163) | copy-start | bytes 24580
  855.3 98.6 %all-reduce.13.cloned.1.call-start = ((), (), s32[]{:S(2)}) async-start(), calls=%async_computation.23 | async-start | bytes 253952 | tf_op jit(solution)/shard_map/psum | solution.py:490
  890.0 349.5 %all-reduce.15.cloned.1.call-start = ((), (), s32[]{:S(2)}) async-start(), calls=%async_computation.28 | async-start | bytes 16777216 | tf_op jit(solution)/shard_map/psum | solution.py:422
  906.2 377.3 %reduce-scatter.19.cloned.1.call-start = ((), (), s32[]{:S(2)}) async-start(), calls=%async_computation.19 | async-start | bytes 2359296 | tf_op jit(solution)/shard_map/reduce_scatter | solution.py:425
  913.0 435.9 %reduce-scatter.17.cloned.1.call-start = ((), (), s32[]{:S(2)}) async-start(), calls=%async_computation.18 | async-start | bytes 7077888 | tf_op jit(solution)/shard_map/reduce_scatter | solution.py:425
  913.6 509.9 %reduce-scatter.21.cloned.1.call-start = ((), (), s32[]{:S(2)}) async-start(), calls=%async_computation.20 | async-start | bytes 9437184 | tf_op jit(solution)/shard_map/reduce_scatter | solution.py:425
  914.2 584.4 %reduce-scatter.23.cloned.1.call-start = ((), (), s32[]{:S(2)}) async-start(), calls=%async_computation.21 | async-start | bytes 9437184 | tf_op jit(solution)/shard_map/reduce_scatter | solution.py:425
  929.2 613.7 %reduce-scatter.11.cloned.1.call-start = ((), (), s32[]{:S(2)}) async-start(), calls=%async_computation.15 | async-start | bytes 2359296 | tf_op jit(solution)/shard_map/reduce_scatter | solution.py:425
  936.1 672.4 %reduce-scatter.9.cloned.1.call-start = ((), (), s32[]{:S(2)}) async-start(), calls=%async_computation.14 | async-start | bytes 7077888 | tf_op jit(solution)/shard_map/reduce_scatter | solution.py:425
  936.8 746.2 %reduce-scatter.13.cloned.1.call-start = ((), (), s32[]{:S(2)}) async-start(), calls=%async_computation.16 | async-start | bytes 9437184 | tf_op jit(solution)/shard_map/reduce_scatter | solution.py:425
  937.4 820.8 %reduce-scatter.15.cloned.1.call-start = ((), (), s32[]{:S(2)}) async-start(), calls=%async_computation.17 | async-start | bytes 9437184 | tf_op jit(solution)/shard_map/reduce_scatter | solution.py:425
  952.7 1.9 copy-start.10
  952.8 1.9 copy-start.15
  952.8 1.9 copy-start.16
  952.8 5.3 copy-start.12
  952.8 5.3 copy-start.17
  952.8 5.3 copy-start.18
  952.8 8.5 copy-start.6
  952.8 8.5 copy-start.13
  952.8 8.5 copy-start.14
  1498.5 18.5 %copy-start.8 = (pred[1024]{0:T(1024)(128)(4,1)S(1)}, pred[1024]{0:T(1024)(128)(4,1)}, u32[]{:S(2)}) copy-start(pred[1024]{0:T(1024)(128)(4,1)} %copy-done.7) | copy-start | bytes 3076
Sparse Core Ops, SparseCore 0:
  10.5 48.6 all-gather.22
  61.6 54.3 all-gather.24
  118.5 27.8 all-gather.14
  148.8 54.3 all-gather.16
  205.5 45.5 all-gather.26
  253.4 54.3 all-gather.28
  310.8 154.9 all-reduce.6
  468.4 26.8 all-gather.18
  498.0 54.3 all-gather.20
  604.9 154.9 all-reduce.8
  855.4 32.9 all-reduce.10
  892.2 52.5 all-reduce.12
  948.6 290.9 all-reduce.14
  1243.3 40.2 reduce-scatter.18
  1287.1 61.7 reduce-scatter.16
  1352.2 71.2 reduce-scatter.20
  1427.2 71.2 reduce-scatter.22
  1501.7 41.2 reduce-scatter.10
  1546.7 61.7 reduce-scatter.8
  1611.8 71.2 reduce-scatter.12
  1686.9 71.2 reduce-scatter.14

commit v2 on v1

--- a/solution.py
+++ b/solution.py
@@ -349,6 +349,388 @@
     return call(kernel, (n // RB,), ins, outs, shapes, flops=10 * n * D, nbytes=16 * n * D, name="norm_back")(*args)
 
 
+MESH = pl.DeviceIdType.MESH
+
+
+class Spot:
+    def __init__(self):
+        i = lax.axis_index("dp")
+        c, x, y = lax.rem(i, 2), lax.rem(lax.div(i, 2), 2), lax.div(i, 4)
+        self.me = i
+        self.dx, self.dy, self.dc = 2 - 4 * x, 4 - 8 * y, 1 - 2 * c
+        self.nx, self.ny, self.nc = i + self.dx, i + self.dy, i + self.dc
+        self.diag = i + self.dx + self.dy
+        z = lax.axis_index("mp")
+        self.z = z
+        self.outer = (z == 0) | (z == 3)
+        self.inner = (z == 1) | (z == 2)
+        self.pair = z + 1 - 2 * lax.rem(z, 2)
+        self.across = 3 - z
+
+    def meet(self, line):
+        barrier = pltpu.get_barrier_semaphore()
+        for peer in (self.nx, self.ny, self.nc):
+            pl.semaphore_signal(barrier, inc=1, device_id={"dp": peer}, device_id_type=MESH)
+        if line:
+            pl.semaphore_signal(barrier, inc=1, device_id={"mp": self.pair}, device_id_type=MESH)
+
+            @pl.when(self.inner)
+            def _():
+                pl.semaphore_signal(barrier, inc=1, device_id={"mp": self.across}, device_id_type=MESH)
+
+            @pl.when(self.inner)
+            def _():
+                pl.semaphore_wait(barrier, 5)
+
+            @pl.when(self.outer)
+            def _():
+                pl.semaphore_wait(barrier, 4)
+        else:
+            pl.semaphore_wait(barrier, 3)
+
+
+def send_to(axis, peer, src, dst, send, recv):
+    return pltpu.make_async_remote_copy(src_ref=src, dst_ref=dst, send_sem=send, recv_sem=recv, device_id={axis: peer}, device_id_type=MESH)
+
+
+class Gather:
+    copies = 9
+
+    def __init__(self, spot, items, send, recv, local):
+        self.spot, self.items, self.send, self.recv, self.local = spot, items, send, recv, local
+        self.sent = []
+        self.own = []
+
+    def go(self, k, n, peer, src, dst):
+        copy = send_to("dp", peer, src, dst, self.send.at[k, n], self.recv.at[k, n])
+        copy.start()
+        self.sent.append(copy)
+
+    def arrived(self, k, n, dst):
+        send_to("dp", self.spot.nc, dst, dst, self.send.at[k, n], self.recv.at[k, n]).wait_recv()
+
+    def first(self, k):
+        s, (src, out) = self.spot, self.items[k]
+        for n, peer in enumerate((s.nx, s.ny, s.nc)):
+            self.go(k, n, peer, src, out.at[s.me])
+        copy = pltpu.make_async_copy(src, out.at[s.me], self.local.at[k])
+        copy.start()
+        self.own.append(copy)
+
+    def halves(self, k):
+        h = self.items[k][1].shape[1] // 2
+        return pl.ds(0, h), pl.ds(h, h)
+
+    def second(self, k):
+        s, (_, out) = self.spot, self.items[k]
+        low, high = self.halves(k)
+        self.arrived(k, 0, out.at[s.nx])
+        self.go(k, 3, s.ny, out.at[s.nx, high], out.at[s.nx, high])
+        self.go(k, 4, s.nc, out.at[s.nx], out.at[s.nx])
+        self.arrived(k, 1, out.at[s.ny])
+        self.go(k, 5, s.nx, out.at[s.ny, low], out.at[s.ny, low])
+        self.go(k, 6, s.nc, out.at[s.ny], out.at[s.ny])
+
+    def third(self, k):
+        s, (_, out) = self.spot, self.items[k]
+        low, high = self.halves(k)
+        self.arrived(k, 3, out.at[s.diag, high])
+        self.go(k, 7, s.nc, out.at[s.diag, high], out.at[s.diag, high])
+        self.arrived(k, 5, out.at[s.diag, low])
+        self.go(k, 8, s.nc, out.at[s.diag, low], out.at[s.diag, low])
+
+    def last(self, k):
+        s, (_, out) = self.spot, self.items[k]
+        low, high = self.halves(k)
+        self.arrived(k, 2, out.at[s.nc])
+        self.arrived(k, 4, out.at[s.nx + s.dc])
+        self.arrived(k, 6, out.at[s.ny + s.dc])
+        self.arrived(k, 7, out.at[s.diag + s.dc, high])
+        self.arrived(k, 8, out.at[s.diag + s.dc, low])
+
+    def close(self):
+        for copy in self.own:
+            copy.wait()
+        for copy in self.sent:
+            copy.wait_send()
+
+
+class LineSum:
+    copies = 3
+
+    def __init__(self, spot, part, stage, land, swap, out, send, recv, local, chunks):
+        self.spot, self.part, self.stage, self.land, self.swap, self.out = spot, part, stage, land, swap, out
+        self.send, self.recv, self.local, self.chunks = send, recv, local, chunks
+        self.rows = part.shape[0] // chunks
+
+    def cut(self, k):
+        return pl.ds(k * self.rows, self.rows)
+
+    def copy(self, k, n):
+        s, rows = self.spot, self.cut(k)
+        if n == 0:
+            peer, src, dst = s.pair, self.part, self.land
+        elif n == 1:
+            peer, src, dst = s.across, self.land, self.swap
+        else:
+            peer, src, dst = s.pair, self.swap, self.swap
+        return send_to("mp", peer, src.at[rows], dst.at[rows], self.send.at[k, n], self.recv.at[k, n])
+
+    def keep(self, k):
+        rows = self.cut(k)
+        return pltpu.make_async_copy(self.swap.at[rows], self.out.at[rows], self.local.at[k])
+
+    def load(self, k):
+        return pltpu.make_async_copy(self.part.at[self.cut(k)], self.stage.at[k % 2], self.local.at[self.chunks + k % 2])
+
+    def add(self, k, dst, one, two, base):
+        step = 32
+
+        @pl.loop(0, self.rows // step)
+        def _(i):
+            rows = pl.ds(pl.multiple_of(k * self.rows + i * step, step), step)
+            there = pl.ds(pl.multiple_of(base + i * step, step), step)
+            dst[rows, :] = (one[there, :].astype(F32) + two[rows, :].astype(F32)).astype(BF)
+
+    def tick(self, t):
+        n = self.chunks
+
+        @pl.when(self.spot.outer)
+        def _():
+            if t < n:
+                if t >= 2:
+                    self.copy(t - 2, 0).wait_send()
+                self.copy(t, 0).start()
+            elif t < n + 2:
+                self.copy(t - 2, 0).wait_send()
+            if 0 <= t - 3 < n:
+                self.copy(t - 3, 2).wait_recv()
+                self.keep(t - 3).start()
+
+        @pl.when(self.spot.inner)
+        def _():
+            if t < n:
+                if t == 0:
+                    self.load(0).start()
+                if t + 1 < n:
+                    self.load(t + 1).start()
+                self.load(t).wait()
+                self.copy(t, 0).wait_recv()
+                self.add(t, self.land, self.stage.at[t % 2], self.land, 0)
+                self.copy(t, 1).start()
+            if 0 <= t - 1 < n:
+                self.copy(t - 1, 1).wait_recv()
+                self.copy(t - 1, 1).wait_send()
+                self.add(t - 1, self.swap, self.land, self.swap, (t - 1) * self.rows)
+                self.copy(t - 1, 2).start()
+                self.keep(t - 1).start()
+
+    def close(self):
+        for k in range(self.chunks):
+            self.keep(k).wait()
+
+        @pl.when(self.spot.inner)
+        def _():
+            for k in range(self.chunks):
+                self.copy(k, 2).wait_send()
+
+
+class Scatter:
+    copies = 10
+
+    def __init__(self, spot, items, own, sib, fx, fy, gx, gy, send, recv, local):
+        self.spot, self.items = spot, items
+        self.own, self.sib, self.fx, self.fy, self.gx, self.gy = own, sib, fx, fy, gx, gy
+        self.send, self.recv, self.local = send, recv, local
+        self.sent, self.loads = [], {}
+
+    def go(self, k, n, peer, src, dst):
+        copy = send_to("dp", peer, src, dst, self.send.at[k, n], self.recv.at[k, n])
+        copy.start()
+        self.sent.append(copy)
+
+    def arrived(self, k, n, dst):
+        send_to("dp", self.spot.nc, dst, dst, self.send.at[k, n], self.recv.at[k, n]).wait_recv()
+
+    def first(self, k):
+        s, grad = self.spot, self.items[k][0]
+        for m, slot in enumerate((s.me, s.nx, s.ny, s.diag)):
+            self.go(k, m, s.nc, grad.at[slot + s.dc], self.sib[k].at[m])
+        self.loads[k] = []
+        for m, slot in enumerate((s.me, s.nx, s.ny, s.diag)):
+            copy = pltpu.make_async_copy(grad.at[slot], self.own[k].at[m], self.local.at[k, m])
+            copy.start()
+            self.loads[k].append(copy)
+
+    def over(self, r, c, body, start=0):
+        step = 16
+        while step * 2 * c <= 32768 and r % (step * 2) == 0:
+            step *= 2
+
+        @pl.loop(0, r // step)
+        def _(i):
+            body(pl.ds(pl.multiple_of(i * step, step), step), pl.ds(pl.multiple_of(start + i * step, step), step))
+
+    def second(self, k):
+        s = self.spot
+        own, sib = self.own[k], self.sib[k]
+        _, r, c = own.shape
+        h = r // 2
+        low, high = pl.ds(0, h), pl.ds(h, h)
+        for m in (3, 1, 2, 0):
+            self.loads[k][m].wait()
+            self.arrived(k, m, sib.at[m])
+
+            def add(rows, _, m=m):
+                own[m, rows, :] = (own[m, rows, :].astype(F32) + sib[m, rows, :].astype(F32)).astype(BF)
+
+            self.over(r, c, add)
+            if m == 3:
+                self.go(k, 5, s.nx, own.at[3, low], self.fx[k].at[1])
+                self.go(k, 7, s.ny, own.at[3, high], self.fy[k].at[1])
+            if m == 1:
+                self.go(k, 4, s.nx, own.at[1, low], self.fx[k].at[0])
+            if m == 2:
+                self.go(k, 6, s.ny, own.at[2, high], self.fy[k].at[0])
+
+    def third(self, k):
+        s = self.spot
+        own, fx, fy = self.own[k], self.fx[k], self.fy[k]
+        _, r, c = own.shape
+        h = r // 2
+        self.arrived(k, 5, fx.at[1])
+
+        def add_low(rows, _):
+            fx[1, rows, :] = (own[2, rows, :].astype(F32) + fx[1, rows, :].astype(F32)).astype(BF)
+
+        self.over(h, c, add_low)
+        self.go(k, 8, s.ny, fx.at[1], self.gy[k])
+        self.arrived(k, 7, fy.at[1])
+
+        def add_high(rows, there):
+            fy[1, rows, :] = (own[1, there, :].astype(F32) + fy[1, rows, :].astype(F32)).astype(BF)
+
+        self.over(h, c, add_high, h)
+        self.go(k, 9, s.nx, fy.at[1], self.gx[k])
+
+    def last(self, k):
+        own, out = self.own[k], self.items[k][1]
+        fx, fy, gx, gy = self.fx[k], self.fy[k], self.gx[k], self.gy[k]
+        _, r, c = own.shape
+        h = r // 2
+        self.arrived(k, 4, fx.at[0])
+        self.arrived(k, 8, gy)
+
+        def low(rows, _):
+            out[rows, :] = own[0, rows, :].astype(F32) + fx[0, rows, :].astype(F32) + gy[rows, :].astype(F32)
+
+        self.over(h, c, low)
+        self.arrived(k, 6, fy.at[0])
+        self.arrived(k, 9, gx)
+
+        def high(rows, there):
+            out[there, :] = own[0, there, :].astype(F32) + fy[0, rows, :].astype(F32) + gx[rows, :].astype(F32)
+
+        self.over(h, c, high, h)
+
+    def close(self):
+        for copy in self.sent:
+            copy.wait_send()
+
+
+def link_kernel(name, ident, gather=None, sums=(), scatter=None, chunks=8, plan=None):
+    shards = [] if gather is None else list(gather[0])
+    layers = [] if gather is None else list(gather[1])
+    sums, grads = list(sums), [] if scatter is None else list(scatter)
+    ng, ns, nr = len(shards), len(sums), len(grads)
+    HBM = pl.BlockSpec(memory_space=pl.ANY)
+    VM_ = pl.BlockSpec(memory_space=pltpu.VMEM)
+    shard_shape = lambda v, l: v.shape if l is None else v.shape[1:]
+    ins = [HBM] * (ng + ns + nr)
+    outs = [HBM] * ng + [HBM] * ns + [VM_] * nr
+    shapes = [jax.ShapeDtypeStruct((8,) + shard_shape(v, l), v.dtype) for v, l in zip(shards, layers)]
+    shapes += [jax.ShapeDtypeStruct(v.shape, BF) for v in sums]
+    shapes += [jax.ShapeDtypeStruct(v.shape[1:], F32) for v in grads]
+    scratch = []
+    DMA = pltpu.SemaphoreType.DMA
+    if ng:
+        scratch += [DMA((ng, 9)), DMA((ng, 9)), DMA((ng,))]
+    for v in sums:
+        scratch += [pltpu.VMEM((2, v.shape[0] // chunks, v.shape[1]), BF), pltpu.VMEM(v.shape, BF), pltpu.VMEM(v.shape, BF), DMA((chunks, 3)), DMA((chunks, 3)), DMA((chunks + 2,))]
+    if nr:
+        scratch += [DMA((nr, 10)), DMA((nr, 10)), DMA((nr, 4))]
+        for v in grads:
+            _, r, c = v.shape
+            scratch += [pltpu.VMEM((4, r, c), BF), pltpu.VMEM((4, r, c), BF), pltpu.VMEM((2, r // 2, c), BF), pltpu.VMEM((2, r // 2, c), BF),
+                        pltpu.VMEM((r // 2, c), BF), pltpu.VMEM((r // 2, c), BF)]
+
+    def kernel(*refs):
+        refs = list(refs)
+        take = lambda n: [refs.pop(0) for _ in range(n)]
+        src, part, grad = take(ng), take(ns), take(nr)
+        full, total, owned = take(ng), take(ns), take(nr)
+        spot = Spot()
+        spot.meet(bool(ns))
+        G = S = None
+        if ng:
+            pick = lambda ref, l: ref if l is None else ref.at[l]
+            G = Gather(spot, [(pick(a, l), b) for a, l, b in zip(src, layers, full)], *take(3))
+        lines = []
+        for k in range(ns):
+            stage, land, swap, send, recv, local = take(6)
+            lines.append(LineSum(spot, part[k], stage, land, swap, total[k], send, recv, local, chunks))
+        if nr:
+            send, recv, local = take(3)
+            bufs = [take(6) for _ in range(nr)]
+            S = Scatter(spot, list(zip(grad, owned)), *[[b[i] for b in bufs] for i in range(6)], send, recv, local)
+        plan(G, lines, S)
+        for part_ in [G, *lines, S]:
+            if part_ is not None:
+                part_.close()
+
+    nbytes = sum(v.size * 2 for v in sums + grads) + sum(8 * v.size for v in shards)
+    return pl.pallas_call(
+        kernel, in_specs=ins, out_specs=outs, out_shape=shapes, scratch_shapes=scratch,
+        compiler_params=pltpu.CompilerParams(vmem_limit_bytes=VM, collective_id=ident, has_side_effects=True),
+        cost_estimate=pl.CostEstimate(flops=0, bytes_accessed=nbytes, transcendentals=0), name=name)(*shards, *sums, *grads)
+
+
+def plan_gather(G, lines, S):
+    n = len(G.items)
+    for k in range(n):
+        G.first(k)
+    for k in range(n):
+        G.second(k)
+    for k in range(n):
+        G.third(k)
+    for k in range(n):
+        G.last(k)
+
+
+def woven(stages):
+    def plan(G, lines, S):
+        side = G if G is not None else S
+        for k in range(len(side.items)):
+            side.first(k)
+        ticks = [(line, t) for line in lines for t in range(line.chunks + 3)]
+        for at, (line, t) in enumerate(ticks):
+            line.tick(t)
+            for name, k in stages.get(at, ()):
+                getattr(side, name)(k)
+        for at in sorted(stages):
+            if at >= len(ticks):
+                for name, k in stages[at]:
+                    getattr(side, name)(k)
+
+    return plan
+
+
+weave_gather = woven({2: [("second", 0), ("second", 1)], 4: [("second", 2)], 6: [("second", 3)], 7: [("third", 0), ("third", 1)], 8: [("third", 2)], 9: [("third", 3)],
+                      99: [("last", 0), ("last", 1), ("last", 2), ("last", 3)]})
+weave_scatter = woven({1: [("second", 0), ("second", 1)], 2: [("second", 2)], 3: [("second", 3)], 4: [("third", 0), ("third", 1)], 6: [("third", 2)], 8: [("third", 3)],
+                       9: [("last", 0), ("last", 1)], 99: [("last", 2), ("last", 3)]})
+
+
 def adam_update(weight, grad, first, second):
     first_new = beta_one * first + (1.0 - beta_one) * grad
     second_new = beta_two * second + (1.0 - beta_two) * grad * grad
@@ -400,31 +782,73 @@
     return segment, index - first, valid
 
 
-def gather_small(parts):
+class PlainLinks:
+    def weights(self, shards, layer):
+        wq, wd, wu, wn = [w[layer] for w in shards]
+        rows = lambda v: lax.all_gather(v, "dp", axis=0, tiled=True)
+        stack = lambda v: lax.all_gather(v, "dp", axis=0, tiled=False)
+        return rows(wq), stack(wd), rows(wu), stack(wn)
+
+    def share(self, v):
+        return lax.psum(v, "mp")
+
+    def owned(self, grads):
+        cut = lambda g: lax.psum_scatter(g, "dp", scatter_dimension=0, tiled=True)
+        gq, gd, gu, gn = grads
+        return cut(gq), cut(gd)[0], cut(gu), cut(gn)[0]
+
+    def begin(self, shards, flat):
+        return self.weights(shards, 0), lax.all_gather(flat, "dp", axis=0, tiled=False)
+
+    def middle(self, branch, shards):
+        return self.share(branch), self.weights(shards, 1)
+
+    def turn(self, e, grads):
+        return self.share(e), self.owned(grads)
+
+    def end(self, e, branch, grads):
+        return self.share(e), self.share(branch), self.owned(grads)
+
+
+class ChipLinks:
+    def full(self, got):
+        wq, wd, wu, wn = got
+        return wq.reshape(-1, wq.shape[2]), wd, wu.reshape(-1, wu.shape[2]), wn
+
+    def slots(self, grads):
+        gq, gd, gu, gn = grads
+        return gq.reshape(8, -1, gq.shape[1]), gd, gu.reshape(8, -1, gu.shape[1]), gn
+
+    def begin(self, shards, flat):
+        got = link_kernel("gather", 1, gather=([flat, *shards], [None, 0, 0, 0, 0]), plan=plan_gather)
+        return self.full(got[1:]), got[0]
+
+    def middle(self, branch, shards):
+        got = link_kernel("sum_gather", 2, gather=(shards, [1] * 4), sums=(branch,), plan=weave_gather)
+        return got[4], self.full(got[:4])
+
+    def turn(self, e, grads):
+        got = link_kernel("sum_scatter", 3, sums=(e,), scatter=self.slots(grads), plan=weave_scatter)
+        return got[0], got[1:]
+
+    def end(self, e, branch, grads):
+        got = link_kernel("sums_scatter", 4, sums=(e, branch), scatter=self.slots(grads), plan=weave_scatter)
+        return got[0], got[1], got[2:]
+
+
+def flatten_small(parts):
     flat = jnp.concatenate([p.reshape(-1) for p in parts])
-    got = lax.all_gather(flat, "dp", axis=0, tiled=False)
+    return jnp.pad(flat, (0, -flat.size % 4096)).reshape(-1, 128)
+
+
+def unpack_small(got, parts):
+    got = got.reshape(got.shape[0], -1)
     out, at = [], 0
     for p in parts:
         piece = got[:, at:at + p.size].reshape((-1,) + p.shape)
         out.append(jnp.moveaxis(piece, 0, 2).reshape(p.shape[0], p.shape[1], -1))
         at += p.size
     return out
-
-
-class PlainLinks:
-    def gather(self, shards):
-        wq, wd, wu, wn = shards
-        rows = lambda v: lax.all_gather(v, "dp", axis=0, tiled=True)
-        stack = lambda v: lax.all_gather(v, "dp", axis=0, tiled=False)
-        return rows(wq), stack(wd), rows(wu), stack(wn)
-
-    def share(self, v):
-        return lax.psum(v, "mp")
-
-    def scatter(self, grads):
-        cut = lambda g: lax.psum_scatter(g, "dp", scatter_dimension=0, tiled=True)
-        gq, gd, gu, gn = grads
-        return cut(gq), cut(gd)[0], cut(gu), cut(gn)[0]
 
 
 def body(links, tokens_in, cotangent, seq_lengths, *params):
@@ -436,25 +860,24 @@
     cos, sin = rope_tables(position)
     seg_col, seg_row = segment[:, None], segment[None, :]
     live = valid[:, None]
-    qb, ub, vecs = gather_small(small)
+    first_full, got = links.begin(weights, flatten_small(small))
+    qb, ub, vecs = unpack_small(got, small)
     qb = qb.reshape(LAYERS, 1, -1).astype(F32)
     ub = ub.reshape(LAYERS, 1, -1).astype(F32)
     vecs = vecs.astype(F32)
 
     held = [jnp.concatenate([vecs[layer, :4], vecs[layer - 1, 4:]]) for layer in range(LAYERS)]
 
-    full, kept, extra = [], [], None
+    full, kept, extra = [first_full], [], None
     for layer in range(LAYERS):
-        wq, wd, wu, wn = links.gather([w[layer] for w in weights])
+        wq, wd, wu, wn = full[layer]
         h1, h2, mixed, act, gp, stats = project(tokens_in, extra, held[layer], wq, qb[layer], cos, sin, wu, ub[layer])
         ctx = attend_forward(mixed, seg_col, seg_row)
-        branch = links.share(branch_out(ctx, act, wd, wn))
-        full.append((wq, wd, wu, wn))
+        branch = branch_out(ctx, act, wd, wn)
         kept.append((h1, h2, mixed, act, gp, stats, ctx, extra))
-        if layer + 1 < LAYERS:
-            extra = branch
-    x_last = tokens_in.astype(F32) + extra.astype(F32) + vecs[0, 4] + vecs[0, 5] + branch.astype(F32) + vecs[1, 4] + vecs[1, 5]
-    output = jnp.where(live, x_last, 0.0).astype(BF)
+        if layer == 0:
+            extra, made = links.middle(branch, weights)
+            full.append(made)
 
     gout = gr = jnp.where(live, cotangent, 0).astype(BF)
     sums = jnp.sum(gout.astype(F32), axis=0, keepdims=True)
@@ -465,29 +888,36 @@
         dctx, df = back_in(gr, gp, wd, wn)
         dmix = attend_backward(mixed, dctx, seg_col, seg_row, cos, sin)
         e, norm_sums = back_out(dmix, df, wq, wu, tokens_in, extra, held[layer], stats)
-        e = links.share(e)
         gd, _ = weight_grad(ctx, gr, w=wd.shape[2])
         gn, _ = weight_grad(act, gr, w=wn.shape[2])
         gq, qsum = weight_grad(h1, dmix)
         gu, usum = weight_grad(h2, df)
-        big[layer] = links.scatter((gq, gd, gu, gn))
+        if layer:
+            e, big[layer] = links.turn(e, (gq, gd, gu, gn))
+        else:
+            e, branch, big[layer] = links.end(e, branch, (gq, gd, gu, gn))
         little[layer] = (qsum, usum, norm_sums, sums)
         made = norm_back(gout, e, tokens_in, extra, held[layer], stats, layer == 0)
         if layer:
             gout, gr, sums = made
         else:
             input_grad = made[0]
+    x_last = tokens_in.astype(F32) + kept[1][-1].astype(F32) + vecs[0, 4] + vecs[0, 5] + branch.astype(F32) + vecs[1, 4] + vecs[1, 5]
+    output = jnp.where(live, x_last, 0.0).astype(BF)
 
     done = None
     for layer in reversed(range(LAYERS)):
         done = adam_layer(layer, weights, big[layer], firsts, seconds, done)
 
-    norm_sums = lax.psum(jnp.stack([t[2] for t in little]), "mp")
-    qsum = jnp.stack([t[0] for t in little]).reshape(-1)
-    usum = jnp.stack([t[1] for t in little]).reshape(-1)
-    out_sums = jnp.stack([t[3] for t in little])
+    z, line = lax.axis_index("mp"), lax.axis_size("mp")
+    bias = jnp.concatenate([jnp.stack([t[i] for t in little]).reshape(-1) for i in (0, 1)])
+    bias = jnp.where(jnp.arange(line)[:, None] == z, bias[None, :], 0.0)
+    norm_sums = jnp.stack([t[2] for t in little])
+    out_sums = jnp.where(z == 0, jnp.stack([t[3] for t in little]), 0.0)
     vec_sum = jnp.concatenate([norm_sums, out_sums, out_sums], axis=1).reshape(-1)
-    total = lax.psum(jnp.concatenate([qsum, usum, vec_sum]), "dp")
+    total = lax.psum(jnp.concatenate([bias.reshape(-1), vec_sum]), ("dp", "mp"))
+    bias = lax.dynamic_slice_in_dim(total[:bias.size].reshape(bias.shape), z, 1, 0)[0]
+    total = jnp.concatenate([bias, total[-vec_sum.size:]])
     me = lax.axis_index("dp")
     small_out, at = [], 0
     for p, first, second in zip(small, small_firsts, small_seconds):
@@ -505,7 +935,7 @@
     wide, tall, vec = P(None, "dp", "mp"), P(None, "mp", "dp"), P(None, None, "dp")
     group = (wide, tall, wide, tall, tall, tall, vec)
     return jax.shard_map(
-        functools.partial(body, PlainLinks()),
+        functools.partial(body, ChipLinks() if dict(mesh.shape) == {"dp": 8, "mp": 4} else PlainLinks()),
         mesh=mesh,
         in_specs=(rows_dp,) * 3 + group * 3,
         out_specs=(rows_dp,) * 2 + tuple(s for s in group for _ in range(4)),

time: 1790 us -> 1050 us (0.59)
  waiting for transfers between devices: 1330 us -> 0.04 us
  Pallas kernels: 384 us -> 984 us
    pallas_call x0 -> x4, Pallas kernels: none -> 599 us  [link_kernel(): pl.pallas_call(kernel, in_specs=ins, out_specs=outs, out_shape=shapes, sc...]
    psum x5 -> x1, waiting for transfers between devices: 589 us -> 0.02 us  [body(): total = lax.psum(jnp.concatenate([bias.reshape(-1), vec_sum]), ('dp', 'mp'))]
    reduce_scatter x8 -> x0, waiting for transfers between devices: 480 us -> none  [scatter(): cut = lambda g: lax.psum_scatter(g, 'dp', scatter_dimension=0, tiled=True)]
    all_gather x8 -> x0, waiting for transfers between devices: 256 us -> none  [the longest x4 160 us: gather(): rows = lambda v: lax.all_gather(v, 'dp', axis=0, tiled=True)]
  transfers between devices with their start and end apart: 21 -> 1, of which waited for: 18 -> 0; matrix products, arithmetic and copies ran while one was open for 2% -> 1% of each run, Pallas kernels for 12% -> 32%
where the time goes in v2:
time: 1050 us; the launch traced here: 1040 us
  Pallas kernels  984 us (94%)
  other arithmetic  22.6 us (2%)
  between operations  15.1 us (1%)
  local copies, waits for them, and re-layouts  14.6 us (1%)
    pallas_call x4, Pallas kernels, link_kernel(): pl.pallas_call(kernel, in_specs=ins, out_specs=outs, out_shape=shapes, sc...  599 us
    pallas_call x8, Pallas kernels, weight_grad(): call(kernel, (M // MB,), [spec((n, MB), lambda j: (0, j)), spec((n, N), w...  99.4 us
    pallas_call x2, Pallas kernels, project(): call(kernel, (nq + nu,), ins, outs, shapes, flops=2 * n * D * (C + U), nb...  71.5 us
    pallas_call x2, Pallas kernels, back_out(): call(kernel, (D // NB,), [spec((n, C), whole, True), spec((n, U), whole,...  45 us
    pallas_call x2, Pallas kernels, adam_layer(): pl.pallas_call(kernel, grid=(steps,), in_specs=ins, out_specs=[at(b) for...  38.3 us
    pallas_call x2, Pallas kernels, back_in(): call(kernel, (nr + nu,), [spec((n, D), lambda j: (0, 0), True), spec((n,...  36.3 us
    pallas_call x2, Pallas kernels, branch_out(): call(kernel, (dp,), [spec((n, R), whole, True), spec((n, U), whole, True)...  32.2 us
    pallas_call x2, Pallas kernels, norm_back(): call(kernel, (n // RB,), ins, outs, shapes, flops=10 * n * D, nbytes=16 *...  27 us
  transfers between devices with their start and end apart: 1, of which 0 were waited for; matrix products, arithmetic and copies ran while one was open for 1% of the time, Pallas kernels for 32%

profile of v2, /device:TPU:0, one launch (start us, length us, event | category | flops | bytes accessed | tf_op | source)
XLA Modules:
  0.0 1036.8 jit_solution(3758826762008573457)
XLA Ops:
  7.3 0.7 copy.125
  8.0 0.8 reshape.275
  8.8 0.7 copy.124
  10.2 110.1 %gather.1 = (bf16[8,32,128]{2,1,0:T(8,128)(2,1)}, bf16[8,256,1536]{2,1,0:T(8,128)(2,1)}, bf16[8,512,256]{2,1,0:T(8,128)(2,1)}, bf16[8,256,2048]{2,1,0:T(8,128)(2,1)}, bf16[8,2048,256]{2,1,0:T(8,128)(2,1)}) custom-call(bf16[32,128]{1,0:T(8,128)(2,1)} %fusion.18.refs_0_, bf16[2,256,1536]{2,1,0:T(8,128)(2,1)} %refs_0_.9, bf16[2,512,256]{2,1,0:T(8,128)(2,1)} %refs_1_.7, ...), custom_call_target="tpu_custom_call" | custom-call | bytes 25198592 | tf_op jit(solution)/shard_map/gather/pallas_call | solution.py:692
  120.2 0.9 copy.182
  121.8 0.7 squeeze.28.refs_3_
  122.8 0.7 squeeze.29.refs_7_
  123.8 4.9 convert_reduce_fusion
  128.6 1.0 add_select_fusion.sc_r
  130.3 0.6 pad_maximum_fusion.2.refs_1_.refs_5_.refs_3_
  130.9 1.9 fusion
  132.8 1.3 maximum_maximum_fusion
  134.1 34.1 %project.2 = (bf16[1024,2048]{1,0:T(8,128)(2,1)}, bf16[1024,2048]{1,0:T(8,128)(2,1)}, bf16[1024,1536]{1,0:T(8,128)(2,1)}, bf16[1024,2048]{1,0:T(8,128)(2,1)}, bf...) custom-call(bf16[1024,2048]{1,0:T(8,128)(2,1)} %refs_2_.9, f32[6,2048]{1,0:T(8,128)} %pad_maximum_fusion.2.refs_1_.refs_5_.refs_3_, ...), custom_call_target="tpu_custom_call" | custom-call | flops 15032385536 | bytes 38797312 | tf_op jit(solution)/shard_map/project/pallas_call | solution.py:126
  168.3 6.5 attend.2.c_r.l_r
  174.8 16.1 %branch.2.refs_4_ = bf16[1024,2048]{1,0:T(8,128)(2,1)} custom-call(bf16[1024,512]{1,0:T(8,128)(2,1)} %attend.2.c_r.l_r, bf16[1024,2048]{1,0:T(8,128)(2,1)} %get-tuple-element.122.a_r.l_r, bf16[8,512,256]{2,1,0:T(8,128)(2,1)} %get-tuple-element.123.wd_r, bf16[8,2048,256]{2,1,0:T(8,128)(2,1)} %get-tuple-element.124.wn_r), custom_call_target="tpu_custom_call" | custom-call | flops 10737418240 | bytes 19922944 | tf_op jit(solution)/shard_map/branch/pallas_call | solution.py:209
  190.9 122.2 %sum_gather.1 = (bf16[8,256,1536]{2,1,0:T(8,128)(2,1)}, bf16[8,512,256]{2,1,0:T(8,128)(2,1)}, bf16[8,256,2048]{2,1,0:T(8,128)(2,1)}, bf16[8,2048,256]{2,1,0:T(8,128)(2,1)}, bf16[1024,2048]{1,0:T(8,128)(2,1)}) custom-call(bf16[2,256,1536]{2,1,0:T(8,128)(2,1)} %refs_0_.9, bf16[2,512,256]{2,1,0:T(8,128)(2,1)} %refs_1_.7, bf16[2,256,2048]{2,1,0:T(8,128)(2,1)} %refs_2_.11, ...), custom_call_target="tpu_custom_call" | custom-call | bytes 29360128 | tf_op jit(solution)/shard_map/sum_gather/pallas_call | solution.py:692
  313.2 0.7 squeeze.32.refs_4_
  313.9 0.7 squeeze.33.refs_8_
  315.2 37.4 %project.3 = (bf16[1024,2048]{1,0:T(8,128)(2,1)}, bf16[1024,2048]{1,0:T(8,128)(2,1)}, bf16[1024,1536]{1,0:T(8,128)(2,1)}, bf16[1024,2048]{1,0:T(8,128)(2,1)}, bf...) custom-call(bf16[1024,2048]{1,0:T(8,128)(2,1)} %refs_2_.9, bf16[1024,2048]{1,0:T(8,128)(2,1)} %get-tuple-element.125.refs_1_.refs_5_.refs_3_, ...), custom_call_target="tpu_custom_call" | custom-call | flops 15032385536 | bytes 38797312 | tf_op jit(solution)/shard_map/project/pallas_call | solution.py:126
  352.6 6.5 attend.3.l_r.c_r
  359.1 18.2 %back_in.2 = (bf16[1024,512]{1,0:T(8,128)(2,1)}, bf16[1024,2048]{1,0:T(8,128)(2,1)}) custom-call(bf16[1024,2048]{1,0:T(8,128)(2,1)} %get-tuple-element.311.g_r.r_r.refs_0_, bf16[1024,2048]{1,0:T(8,128)(2,1)} %get-tuple-element.129.gp_r, bf16[8,512,256]{2,1,0:T(8,128)(2,1)} %get-tuple-element.130.wd_r, bf16[8,2048,256]{2,1,0:T(8,128)(2,1)} %get-tuple-element.131.wn_r), custom_call_target="tpu_custom_call" | custom-call | flops 10737418240 | bytes 24117248 | tf_op jit(solution)/shard_map/back_in/pallas_call | solution.py:241
  377.3 11.4 %attend_back.2.refs_0_.r_r = bf16[1024,1536]{1,0:T(8,128)(2,1)} custom-call(bf16[1024,1536]{1,0:T(8,128)(2,1)} %get-tuple-element.128.q_r.k_r.v_r, bf16[1024,1536]{1,0:T(8,128)(2,1)} %get-tuple-element.128.q_r.k_r.v_r, bf16[1024,1536]{1,0:T(8,128)(2,1)} %get-tuple-element.128.q_r.k_r.v_r, bf16[1024,512]{1,0:T(8,128)(2,1)} %get-tuple-element.132.do_r, ...), custom_call_target="tpu_custom_call" | custom-call | flops 3355443200 | bytes 6291456 | tf_op jit(solution)/shard_map/attend_back/pallas_call | solution.py:192
  388.7 7.1 wgrad.9
  395.9 12.7 %wgrad.8 = (bf16[2048,1536]{1,0:T(8,128)(2,1)}, f32[1,1536]{1,0:T(1,128)}) custom-call(bf16[1024,2048]{1,0:T(8,128)(2,1)} %get-tuple-element.136.l_r, bf16[1024,1536]{1,0:T(8,128)(2,1)} %attend_back.2.refs_0_.r_r), custom_call_target="tpu_custom_call" | custom-call | flops 6442450944 | bytes 13631488 | tf_op jit(solution)/shard_map/wgrad/pallas_call | solution.py:306
  408.6 22.8 %back_out.2 = (bf16[1024,2048]{1,0:T(8,128)(2,1)}, f32[4,2048]{1,0:T(4,128)}) custom-call(bf16[1024,1536]{1,0:T(8,128)(2,1)} %attend_back.2.refs_0_.r_r, bf16[1024,2048]{1,0:T(8,128)(2,1)} %get-tuple-element.133.refs_1_.r_r, bf16[2048,1536]{1,0:T(8,128)(2,1)} %bitcast.103, bf16[2048,2048]{1,0:T(8,128)(2,1)} %bitcast.99, bf16[1024,2048]{1,0:T(8,128)(2,1)} %refs_2_.9, ...), custom_call_target="tpu_custom_call" | custom-call | flops 15032385536 | bytes 34603008 | tf_op jit(solution)/shard_map/back_out/pallas_call | solution.py:277
  431.5 15.0 %wgrad.10 = (bf16[2048,2048]{1,0:T(8,128)(2,1)}, f32[1,2048]{1,0:T(1,128)}) custom-call(bf16[1024,2048]{1,0:T(8,128)(2,1)} %get-tuple-element.139.l_r, bf16[1024,2048]{1,0:T(8,128)(2,1)} %get-tuple-element.133.refs_1_.r_r), custom_call_target="tpu_custom_call" | custom-call | flops 8589934592 | bytes 16777216 | tf_op jit(solution)/shard_map/wgrad/pallas_call | solution.py:306
  446.4 15.0 %wgrad.11 = (bf16[8,2048,256]{2,1,0:T(8,128)(2,1)}, f32[1,2048]{1,0:T(1,128)}) custom-call(bf16[1024,2048]{1,0:T(8,128)(2,1)} %get-tuple-element.141.l_r.a_r, bf16[1024,2048]{1,0:T(8,128)(2,1)} %get-tuple-element.311.g_r.r_r.refs_0_), custom_call_target="tpu_custom_call" | custom-call | flops 8589934592 | bytes 16777216 | tf_op jit(solution)/shard_map/wgrad/pallas_call | solution.py:306
  461.4 120.9 %sum_scatter.1 = (bf16[1024,2048]{1,0:T(8,128)(2,1)}, f32[256,1536]{1,0:T(8,128)}, f32[512,256]{1,0:T(8,128)}, f32[256,2048]{1,0:T(8,128)}, f32[2048,256]{1,0:T(8,128)}) custom-call(bf16[1024,2048]{1,0:T(8,128)(2,1)} %get-tuple-element.135.refs_0_, bf16[8,256,1536]{2,1,0:T(8,128)(2,1)} %bitcast.70, bf16[8,512,256]{2,1,0:T(8,128)(2,1)} %get-tuple-element.138.refs_2_, ...), custom_call_target="tpu_custom_call" | custom-call | bytes 29360128 | tf_op jit(solution)/shard_map/sum_scatter/pallas_call | solution.py:692
  582.3 14.8 %norm_back.2 = (f32[1024,2048]{1,0:T(8,128)}, bf16[1024,2048]{1,0:T(8,128)(2,1)}, f32[1,2048]{1,0:T(1,128)}) custom-call(bf16[1024,2048]{1,0:T(8,128)(2,1)} %get-tuple-element.311.g_r.r_r.refs_0_, bf16[1024,2048]{1,0:T(8,128)(2,1)} %get-tuple-element.143.refs_1_, bf16[1024,2048]{1,0:T(8,128)(2,1)} %refs_2_.9, ...), custom_call_target="tpu_custom_call" | custom-call | flops 20971520 | bytes 33554432 | tf_op jit(solution)/shard_map/norm_back/pallas_call | solution.py:349
  597.0 18.1 %back_in.3 = (bf16[1024,512]{1,0:T(8,128)(2,1)}, bf16[1024,2048]{1,0:T(8,128)(2,1)}) custom-call(bf16[1024,2048]{1,0:T(8,128)(2,1)} %get-tuple-element.144.g_r.r_r, bf16[1024,2048]{1,0:T(8,128)(2,1)} %get-tuple-element.145.gp_r, bf16[8,512,256]{2,1,0:T(8,128)(2,1)} %get-tuple-element.123.wd_r, bf16[8,2048,256]{2,1,0:T(8,128)(2,1)} %get-tuple-element.124.wn_r), custom_call_target="tpu_custom_call" | custom-call | flops 10737418240 | bytes 24117248 | tf_op jit(solution)/shard_map/back_in/pallas_call | solution.py:241
  615.2 11.4 %attend_back.3.refs_0_.r_r = bf16[1024,1536]{1,0:T(8,128)(2,1)} custom-call(bf16[1024,1536]{1,0:T(8,128)(2,1)} %get-tuple-element.121.q_r.k_r.v_r, bf16[1024,1536]{1,0:T(8,128)(2,1)} %get-tuple-element.121.q_r.k_r.v_r, bf16[1024,1536]{1,0:T(8,128)(2,1)} %get-tuple-element.121.q_r.k_r.v_r, bf16[1024,512]{1,0:T(8,128)(2,1)} %get-tuple-element.146.do_r, ...), custom_call_target="tpu_custom_call" | custom-call | flops 3355443200 | bytes 6291456 | tf_op jit(solution)/shard_map/attend_back/pallas_call | solution.py:192
  626.6 12.7 %wgrad.12 = (bf16[2048,1536]{1,0:T(8,128)(2,1)}, f32[1,1536]{1,0:T(1,128)}) custom-call(bf16[1024,2048]{1,0:T(8,128)(2,1)} %get-tuple-element.150.l_r, bf16[1024,1536]{1,0:T(8,128)(2,1)} %attend_back.3.refs_0_.r_r), custom_call_target="tpu_custom_call" | custom-call | flops 6442450944 | bytes 13631488 | tf_op jit(solution)/shard_map/wgrad/pallas_call | solution.py:306
  639.4 22.2 %back_out.3 = (bf16[1024,2048]{1,0:T(8,128)(2,1)}, f32[4,2048]{1,0:T(4,128)}) custom-call(bf16[1024,1536]{1,0:T(8,128)(2,1)} %attend_back.3.refs_0_.r_r, bf16[1024,2048]{1,0:T(8,128)(2,1)} %get-tuple-element.147.refs_1_.r_r, bf16[2048,1536]{1,0:T(8,128)(2,1)} %bitcast.101, bf16[2048,2048]{1,0:T(8,128)(2,1)} %bitcast.97, bf16[1024,2048]{1,0:T(8,128)(2,1)} %refs_2_.9, ...), custom_call_target="tpu_custom_call" | custom-call | flops 15032385536 | bytes 34603008 | tf_op jit(solution)/shard_map/back_out/pallas_call | solution.py:277
  661.6 15.2 %wgrad.14 = (bf16[2048,2048]{1,0:T(8,128)(2,1)}, f32[1,2048]{1,0:T(1,128)}) custom-call(bf16[1024,2048]{1,0:T(8,128)(2,1)} %get-tuple-element.153.l_r, bf16[1024,2048]{1,0:T(8,128)(2,1)} %get-tuple-element.147.refs_1_.r_r), custom_call_target="tpu_custom_call" | custom-call | flops 8589934592 | bytes 16777216 | tf_op jit(solution)/shard_map/wgrad/pallas_call | solution.py:306
  677.0 0.7 pad_maximum_fusion.5
  677.9 0.7 pad_maximum_fusion
  678.6 16.1 %branch.3.refs_1_ = bf16[1024,2048]{1,0:T(8,128)(2,1)} custom-call(bf16[1024,512]{1,0:T(8,128)(2,1)} %attend.3.l_r.c_r, bf16[1024,2048]{1,0:T(8,128)(2,1)} %get-tuple-element.141.l_r.a_r, bf16[8,512,256]{2,1,0:T(8,128)(2,1)} %get-tuple-element.130.wd_r, bf16[8,2048,256]{2,1,0:T(8,128)(2,1)} %get-tuple-element.131.wn_r), custom_call_target="tpu_custom_call" | custom-call | flops 10737418240 | bytes 19922944 | tf_op jit(solution)/shard_map/branch/pallas_call | solution.py:209
  694.7 6.7 wgrad.13
  701.4 15.0 %wgrad.15 = (bf16[8,2048,256]{2,1,0:T(8,128)(2,1)}, f32[1,2048]{1,0:T(1,128)}) custom-call(bf16[1024,2048]{1,0:T(8,128)(2,1)} %get-tuple-element.122.a_r.l_r, bf16[1024,2048]{1,0:T(8,128)(2,1)} %get-tuple-element.144.g_r.r_r), custom_call_target="tpu_custom_call" | custom-call | flops 8589934592 | bytes 16777216 | tf_op jit(solution)/shard_map/wgrad/pallas_call | solution.py:306
  716.4 0.8 fusion.28
  717.3 245.5 %sums_scatter.1 = (bf16[1024,2048]{1,0:T(8,128)(2,1)}, bf16[1024,2048]{1,0:T(8,128)(2,1)}, f32[256,1536]{1,0:T(8,128)}, f32[512,256]{1,0:T(8,128)}, f32[256,2048]{1,0:T(8,128)}, /*index=5*/f32[2048,256]{1,0:T(8,128)}) custom-call(bf16[1024,2048]{1,0:T(8,128)(2,1)} %get-tuple-element.149.refs_0_, bf16[1024,2048]{1,0:T(8,128)(2,1)} %branch.3.refs_1_, ...), custom_call_target="tpu_custom_call" | custom-call | bytes 33554432 | tf_op jit(solution)/shard_map/sums_scatter/pallas_call | solution.py:692
  962.8 8.2 select_convert_fusion
  971.0 12.2 %norm_back.3 = f32[1024,2048]{1,0:T(8,128)} custom-call(f32[1024,2048]{1,0:T(8,128)} %get-tuple-element.157.refs_0_, bf16[1024,2048]{1,0:T(8,128)(2,1)} %get-tuple-element.158.refs_1_, bf16[1024,2048]{1,0:T(8,128)(2,1)} %refs_2_.9, f32[6,2048]{1,0:T(8,128)} %pad_maximum_fusion.2.refs_1_.refs_5_.refs_3_, f32[1024,128]{1,0:T(8,128)} %get-tuple-element.148.refs_6_.refs_4_), custom_call_target="tpu_custom_call" | custom-call | flops 20971520 | bytes 33554432 | tf_op jit(solution)/shard_map/norm_back/pallas_call | solution.py:349
  983.2 19.3 %adam.2 = (f32[2,256,1536]{2,1,0:T(8,128)}, f32[2,256,1536]{2,1,0:T(8,128)}, f32[2,256,1536]{2,1,0:T(8,128)}, f32[2,256,1536]{2,1,0:T(8,128)}, f32[2,512,256]{2,...) custom-call(bf16[2,256,1536]{2,1,0:T(8,128)(2,1)} %refs_0_.9, ...), custom_call_target="tpu_custom_call" | custom-call | flops 31457280 | bytes 47185920 | tf_op jit(solution)/shard_map/adam/pallas_call | solution.py:765
  1002.6 19.1 %adam.3 = (f32[2,256,1536]{2,1,0:T(8,128)}, f32[2,256,1536]{2,1,0:T(8,128)}, f32[2,256,1536]{2,1,0:T(8,128)}, f32[2,256,1536]{2,1,0:T(8,128)}, f32[2,512,256]{2,...) custom-call(bf16[2,256,1536]{2,1,0:T(8,128)(2,1)} %refs_0_.9, ...), custom_call_target="tpu_custom_call", output_to_operand_aliasing={{0}: (16, {}), {1}: (17, {}), {2}: (18, {}), {3}: (19, {}),... | custom-call | flops 31457280 | bytes 47185920 | tf_op jit(solution)/shard_map/adam/pallas_call | solution.py:765
  1021.7 0.9 slice.97
  1025.4 0.9 slice.98
  1028.8 0.7 subtract_subtract_fusion.1
  (99 shorter events, 8.7 us)
Async XLA Ops:
  7.2 114.2 %copy-start.19 = (s32[1,4]{1,0:T(1,128)S(1)}, s32[1,4]{1,0:T(1,128)}, u32[]{:S(2)}) copy-start(s32[1,4]{1,0:T(1,128)} %param.26) | copy-start | bytes 52
  7.2 1014.5 %all-reduce.3.cloned.1.call-start = ((), (), s32[]{:S(2)}) async-start(), calls=%async_computation | async-start | bytes 425984 | tf_op jit(solution)/shard_map/psum | solution.py:918
  121.2 2.3 copy-start
  121.7 8.0 copy-start.5
  661.6 15.3 %copy-start.1 = (f32[2048]{0:T(1024)S(1)}, f32[2048]{0:T(1024)}, u32[]{:S(2)}) copy-start(f32[2048]{0:T(1024)} %get-tuple-element.310) | copy-start | bytes 24580
  661.6 15.3 %copy-start.16 = (f32[1,2048]{1,0:T(1,128)S(1)}, f32[1,2048]{1,0:T(1,128)}, u32[]{:S(2)}) copy-start(f32[1,2048]{1,0:T(1,128)} %get-tuple-element.205) | copy-start | bytes 24580
  661.6 15.3 %copy-start.2 = (f32[4,2048]{1,0:T(4,128)S(1)}, f32[4,2048]{1,0:T(4,128)}, u32[]{:S(2)}) copy-start(f32[4,2048]{1,0:T(4,128)} %get-tuple-element.204) | copy-start | bytes 98308
  661.6 15.3 %copy-start.3 = (f32[4,2048]{1,0:T(4,128)S(1)}, f32[4,2048]{1,0:T(4,128)}, u32[]{:S(2)}) copy-start(f32[4,2048]{1,0:T(4,128)} %get-tuple-element.203) | copy-start | bytes 98308
  661.6 15.4 %copy-start.15 = (f32[1,2048]{1,0:T(1,128)S(1)}, f32[1,2048]{1,0:T(1,128)}, u32[]{:S(2)}) copy-start(f32[1,2048]{1,0:T(1,128)} %get-tuple-element.202) | copy-start | bytes 24580
  661.6 16.1 %copy-start.17 = (f32[1,1536]{1,0:T(1,128)S(1)}, f32[1,1536]{1,0:T(1,128)}, u32[]{:S(2)}) copy-start(f32[1,1536]{1,0:T(1,128)} %get-tuple-element.200) | copy-start | bytes 18436
  661.6 16.1 %copy-start.18 = (f32[1,1536]{1,0:T(1,128)S(1)}, f32[1,1536]{1,0:T(1,128)}, u32[]{:S(2)}) copy-start(f32[1,1536]{1,0:T(1,128)} %get-tuple-element.199) | copy-start | bytes 18436
  717.3 245.5 %copy-start.6 = (pred[1024]{0:T(1024)(128)(4,1)S(1)}, pred[1024]{0:T(1024)(128)(4,1)}, u32[]{:S(2)}) copy-start(pred[1024]{0:T(1024)(128)(4,1)} %copy-done.5) | copy-start | bytes 3076
  1002.5 20.2 %copy-start.7 = (bf16[2,12,16]{2,0,1:T(2,128)(2,1)S(1)}, bf16[2,12,16]{2,0,1:T(2,128)(2,1)}, u32[]{:S(2)}) copy-start(bf16[2,12,16]{2,0,1:T(2,128)(2,1)} %param.31) | copy-start | bytes 2308
  1002.5 20.2 %copy-start.11 = (f32[2,12,16]{2,0,1:T(2,128)S(1)}, f32[2,12,16]{2,0,1:T(2,128)}, u32[]{:S(2)}) copy-start(f32[2,12,16]{2,0,1:T(2,128)} %param.45) | copy-start | bytes 4612
  1002.5 20.2 %copy-start.12 = (f32[2,12,16]{2,0,1:T(2,128)S(1)}, f32[2,12,16]{2,0,1:T(2,128)}, u32[]{:S(2)}) copy-start(f32[2,12,16]{2,0,1:T(2,128)} %param.38) | copy-start | bytes 4612
  1002.5 23.8 %copy-start.8 = (bf16[2,6,256]{2,0,1:T(2,128)(2,1)S(1)}, bf16[2,6,256]{2,0,1:T(2,128)(2,1)}, u32[]{:S(2)}) copy-start(bf16[2,6,256]{2,0,1:T(2,128)(2,1)} %param.33) | copy-start | bytes 18436
  1002.5 23.8 %copy-start.13 = (f32[2,6,256]{2,0,1:T(2,128)S(1)}, f32[2,6,256]{2,0,1:T(2,128)}, u32[]{:S(2)}) copy-start(f32[2,6,256]{2,0,1:T(2,128)} %param.47) | copy-start | bytes 36868
  1002.5 23.8 %copy-start.14 = (f32[2,6,256]{2,0,1:T(2,128)S(1)}, f32[2,6,256]{2,0,1:T(2,128)}, u32[]{:S(2)}) copy-start(f32[2,6,256]{2,0,1:T(2,128)} %param.40) | copy-start | bytes 36868
  1002.6 26.3 %copy-start.4 = (bf16[2,16,16]{2,1,0:T(8,128)(2,1)S(1)}, bf16[2,16,16]{2,1,0:T(8,128)(2,1)}, u32[]{:S(2)}) copy-start(bf16[2,16,16]{2,1,0:T(8,128)(2,1)} %param.32) | copy-start | bytes 3076
  1002.6 26.3 %copy-start.9 = (f32[2,16,16]{2,1,0:T(8,128)S(1)}, f32[2,16,16]{2,1,0:T(8,128)}, u32[]{:S(2)}) copy-start(f32[2,16,16]{2,1,0:T(8,128)} %param.46) | copy-start | bytes 6148
  1002.6 26.2 %copy-start.10 = (f32[2,16,16]{2,1,0:T(8,128)S(1)}, f32[2,16,16]{2,1,0:T(8,128)}, u32[]{:S(2)}) copy-start(f32[2,16,16]{2,1,0:T(8,128)} %param.39) | copy-start | bytes 6148
Sparse Core Ops, SparseCore 0:
  678.7 133.9 all-reduce.2

commit v3 on v2

--- a/solution.py
+++ b/solution.py
@@ -20,15 +20,17 @@
 decay = 0.01
 VM = 60 * 1024 * 1024
 BF = jnp.bfloat16
+ROWS = 256
+UPB = 512
 F32 = jnp.float32
 
 
-def call(kernel, grid, in_specs, out_specs, out_shape, scratch=(), flops=0, nbytes=0, name=None):
+def call(kernel, grid, in_specs, out_specs, out_shape, scratch=(), flops=0, nbytes=0, name=None, ident=None):
     return pl.pallas_call(
         kernel,
         grid_spec=pltpu.PrefetchScalarGridSpec(num_scalar_prefetch=0, grid=grid, in_specs=in_specs, out_specs=out_specs, scratch_shapes=list(scratch)),
         out_shape=out_shape,
-        compiler_params=pltpu.CompilerParams(vmem_limit_bytes=VM),
+        compiler_params=pltpu.CompilerParams(vmem_limit_bytes=VM, collective_id=ident, has_side_effects=ident is not None),
         cost_estimate=pl.CostEstimate(flops=flops, bytes_accessed=nbytes, transcendentals=0),
         name=name,
     )
@@ -65,65 +67,121 @@
     return centred * rstd, mean, rstd
 
 
-def project(base, extra, vec, wq, bq, cos, sin, wu, bu):
+def row_blocks(n):
+    step = min(n, ROWS)
+    return [slice(i, i + step) for i in range(0, n, step)]
+
+
+def project(base, extra, vec, wq, bq, cos, sin, wu, bu, shards=None):
     n, D = base.shape
     C, U = wq.shape[1], wu.shape[1]
-    NB = 256
-    nq, nu = C // NB, U // NB
-    RB = min(n, 128)
+    QB, UB = 3 * HD, min(UPB, U)
+    nq, nu = C // QB, U // UB
+    RB = 128
+    nr = n // RB
+    ng = 0 if shards is None else len(shards)
+    xs = [base] if extra is None else [base, extra]
 
     def kernel(*refs):
-        if extra is None:
-            base_r, vec_r, wq_r, bq_r, cos_r, sin_r, wu_r, bu_r, h1_r, h2_r, mix_r, a_r, gp_r, st_r = refs
-        else:
-            base_r, extra_r, vec_r, wq_r, bq_r, cos_r, sin_r, wu_r, bu_r, h1_r, h2_r, mix_r, a_r, gp_r, st_r = refs
+        refs = list(refs)
+        take = lambda k: [refs.pop(0) for _ in range(k)]
+        x_rs = take(len(xs))
+        vec_r, wq_r, bq_r, cos_r, sin_r, wu_r, bu_r = take(7)
+        shard_rs = take(ng)
+        h1_o, h2_o, mix_r, a_r, gp_r, st_r = take(6)
+        full_rs = take(ng)
+        h1_r, h2_r = take(2)
+        bufs = take(len(xs))
+        in_sem, out_sem = take(2)
         j = pl.program_id(0)
+        side = None
+        if ng:
+            spot = Spot()
+            side = Gather(spot, [(a.at[0], b) for a, b in zip(shard_rs, full_rs)], *take(3))
+
+            @pl.when(j == 0)
+            def _():
+                spot.meet(False)
+                side.first(0)
+                side.first(1)
+
+        def host(step, *stages):
+            if side is not None:
+                @pl.when(j == min(step, nq + nu - 1))
+                def _():
+                    for name, *args in stages:
+                        getattr(side, name)(*args)
+        block = lambda i: pl.ds(i * RB, RB)
+        loads = [[pltpu.make_async_copy(x.at[block(i)], buf.at[block(i)], in_sem.at[k, i]) for k, (x, buf) in enumerate(zip(x_rs, bufs))] for i in range(nr)]
+        stores = [[pltpu.make_async_copy(h.at[block(i)], o.at[block(i)], out_sem.at[k, i]) for k, (h, o) in enumerate(((h1_r, h1_o), (h2_r, h2_o)))] for i in range(nr)]
 
         @pl.when(j == 0)
         def _():
-            @pl.loop(0, n // RB)
-            def _(i):
-                rows = pl.ds(pl.multiple_of(i * RB, RB), RB)
-                x = base_r[rows, :].astype(F32)
+            for group in loads:
+                for copy in group:
+                    copy.start()
+            for i in range(nr):
+                for copy in loads[i]:
+                    copy.wait()
+                rows = block(i)
+                x = bufs[0][rows, :].astype(F32)
                 if extra is not None:
-                    x = x + extra_r[rows, :].astype(F32) + vec_r[4:5, :] + vec_r[5:6, :]
+                    x = x + bufs[1][rows, :].astype(F32) + vec_r[4:5, :] + vec_r[5:6, :]
                 xhat, mean, rstd = normed(x)
                 st_r[rows, 0:1] = mean
                 st_r[rows, 1:2] = rstd
                 h1_r[rows, :] = (xhat * vec_r[0:1, :] + vec_r[1:2, :]).astype(BF)
                 h2_r[rows, :] = (xhat * vec_r[2:3, :] + vec_r[3:4, :]).astype(BF)
+                for copy in stores[i]:
+                    copy.start()
 
         @pl.when(j < nq)
         def _():
-            m = jnp.dot(h1_r[...], wq_r[...], preferred_element_type=F32) + bq_r[...]
-            kind = lax.rem(j, 3)
-
-            @pl.when(kind == 2)
-            def _():
-                mix_r[...] = m.astype(BF)
-
-            @pl.when(kind != 2)
-            def _():
-                mix_r[:, :128] = turn(m[:, :128], cos_r[...], sin_r[...]).astype(BF)
-                mix_r[:, 128:] = m[:, 128:].astype(BF)
+            for rows in row_blocks(n):
+                for part in range(3):
+                    at = part * HD
+                    m = jnp.dot(h1_r[rows, :], wq_r[:, at:at + HD], preferred_element_type=F32) + bq_r[:, at:at + HD]
+                    if part == 2:
+                        mix_r[rows, at:at + HD] = m.astype(BF)
+                    else:
+                        mix_r[rows, at:at + 128] = turn(m[:, :128], cos_r[rows, :], sin_r[rows, :]).astype(BF)
+                        mix_r[rows, at + 128:at + HD] = m[:, 128:].astype(BF)
 
         @pl.when(j >= nq)
         def _():
-            f = jnp.dot(h2_r[...], wu_r[...], preferred_element_type=F32) + bu_r[...]
-            phi = 0.5 * (1.0 + lax.erf(f * 0.7071067811865476))
-            a_r[...] = (f * phi).astype(BF)
-            gp_r[...] = (phi + f * (jnp.exp(-0.5 * f * f) * 0.3989422804014327)).astype(BF)
+            for rows in row_blocks(n):
+                for at in range(0, UB, 256):
+                    cols = slice(at, at + 256)
+                    f = jnp.dot(h2_r[rows, :], wu_r[:, cols], preferred_element_type=F32) + bu_r[:, cols]
+                    phi = 0.5 * (1.0 + lax.erf(f * 0.7071067811865476))
+                    a_r[rows, cols] = (f * phi).astype(BF)
+                    gp_r[rows, cols] = (phi + f * (jnp.exp(-0.5 * f * f) * 0.3989422804014327)).astype(BF)
+
+        host(1, ("second", 0))
+        host(3, ("second", 1), ("third", 0))
+        host(5, ("third", 1), ("last", 0), ("last", 1), ("close",))
+
+        @pl.when(j == nq + nu - 1)
+        def _():
+            for group in stores:
+                for copy in group:
+                    copy.wait()
 
     whole = lambda j: (0, 0)
     qcol = lambda j: (0, jnp.minimum(j, nq - 1))
     ucol = lambda j: (0, jnp.maximum(j - nq, 0))
-    ins = [spec((n, D), whole, True)] + ([] if extra is None else [spec((n, D), whole, True)]) + [
-        spec((6, D), whole), spec((D, NB), qcol), spec((1, NB), qcol), spec((n, 128), whole, True), spec((n, 128), whole, True),
-        spec((D, NB), ucol), spec((1, NB), ucol)]
-    outs = [spec((n, D), whole, True), spec((n, D), whole, True), spec((n, NB), qcol), spec((n, NB), ucol), spec((n, NB), ucol), spec((n, 128), whole)]
+    far = pl.BlockSpec(memory_space=pl.ANY)
+    ins = [far] * len(xs) + [
+        spec((6, D), whole), spec((D, QB), qcol), spec((1, QB), qcol), spec((n, 128), whole, True), spec((n, 128), whole, True),
+        spec((D, UB), ucol), spec((1, UB), ucol)] + [far] * ng
+    outs = [far, far, spec((n, QB), qcol), spec((n, UB), ucol), spec((n, UB), ucol), spec((n, 128), whole)] + [far] * ng
     shapes = [jax.ShapeDtypeStruct(s, BF) for s in ((n, D), (n, D), (n, C), (n, U), (n, U))] + [jax.ShapeDtypeStruct((n, 128), F32)]
-    args = [base] + ([] if extra is None else [extra]) + [vec, wq, bq, cos, sin, wu, bu]
-    return call(kernel, (nq + nu,), ins, outs, shapes, flops=2 * n * D * (C + U), nbytes=2 * (n * D * 3 + D * (C + U) + n * (C + 2 * U)), name="project")(*args)
+    DMA = pltpu.SemaphoreType.DMA
+    scratch = [pltpu.VMEM((n, D), BF)] * (2 + len(xs)) + [DMA((len(xs), nr)), DMA((2, nr))]
+    if ng:
+        scratch += [DMA((ng, 9)), DMA((ng, 9)), DMA((ng,))]
+        shapes += [jax.ShapeDtypeStruct((8,) + v.shape[1:], v.dtype) for v in shards]
+    return call(kernel, (nq + nu,), ins, outs, shapes, scratch, ident=5 if ng else None, flops=2 * n * D * (C + U), nbytes=2 * (n * D * 3 + D * (C + U) + n * (C + 2 * U)), name="project")(*xs, vec, wq, bq, cos, sin, wu, bu, *(shards or ()))
 
 
 def softmax_block(q, k, segq, segk, q0, k0):
@@ -402,9 +460,8 @@
         self.own = []
 
     def go(self, k, n, peer, src, dst):
-        copy = send_to("dp", peer, src, dst, self.send.at[k, n], self.recv.at[k, n])
-        copy.start()
-        self.sent.append(copy)
+        send_to("dp", peer, src, dst, self.send.at[k, n], self.recv.at[k, n]).start()
+        self.sent.append((k, n, peer, src, dst))
 
     def arrived(self, k, n, dst):
         send_to("dp", self.spot.nc, dst, dst, self.send.at[k, n], self.recv.at[k, n]).wait_recv()
@@ -413,9 +470,8 @@
         s, (src, out) = self.spot, self.items[k]
         for n, peer in enumerate((s.nx, s.ny, s.nc)):
             self.go(k, n, peer, src, out.at[s.me])
-        copy = pltpu.make_async_copy(src, out.at[s.me], self.local.at[k])
-        copy.start()
-        self.own.append(copy)
+        pltpu.make_async_copy(src, out.at[s.me], self.local.at[k]).start()
+        self.own.append(k)
 
     def halves(self, k):
         h = self.items[k][1].shape[1] // 2
@@ -449,10 +505,11 @@
         self.arrived(k, 8, out.at[s.diag + s.dc, low])
 
     def close(self):
-        for copy in self.own:
-            copy.wait()
-        for copy in self.sent:
-            copy.wait_send()
+        for k in self.own:
+            src, out = self.items[k]
+            pltpu.make_async_copy(src, out.at[self.spot.me], self.local.at[k]).wait()
+        for k, n, peer, src, dst in self.sent:
+            send_to("dp", peer, src, dst, self.send.at[k, n], self.recv.at[k, n]).wait_send()
 
 
 class LineSum:
@@ -798,16 +855,13 @@
         return cut(gq), cut(gd)[0], cut(gu), cut(gn)[0]
 
     def begin(self, shards, flat):
-        return self.weights(shards, 0), lax.all_gather(flat, "dp", axis=0, tiled=False)
+        return self.weights(shards, 0), lax.all_gather(flat, "dp", axis=0, tiled=False), None
 
     def middle(self, branch, shards):
         return self.share(branch), self.weights(shards, 1)
 
-    def turn(self, e, grads):
+    def turn(self, e, grads, ident):
         return self.share(e), self.owned(grads)
-
-    def end(self, e, branch, grads):
-        return self.share(e), self.share(branch), self.owned(grads)
 
 
 class ChipLinks:
@@ -820,20 +874,17 @@
         return gq.reshape(8, -1, gq.shape[1]), gd, gu.reshape(8, -1, gu.shape[1]), gn
 
     def begin(self, shards, flat):
-        got = link_kernel("gather", 1, gather=([flat, *shards], [None, 0, 0, 0, 0]), plan=plan_gather)
-        return self.full(got[1:]), got[0]
+        wq, wd, wu, wn = shards
+        flat, wq, wu = link_kernel("gather", 1, gather=([flat, wq, wu], [None, 0, 0]), plan=plan_gather)
+        return (wq.reshape(-1, wq.shape[2]), None, wu.reshape(-1, wu.shape[2]), None), flat, (wd, wn)
 
     def middle(self, branch, shards):
         got = link_kernel("sum_gather", 2, gather=(shards, [1] * 4), sums=(branch,), plan=weave_gather)
         return got[4], self.full(got[:4])
 
-    def turn(self, e, grads):
-        got = link_kernel("sum_scatter", 3, sums=(e,), scatter=self.slots(grads), plan=weave_scatter)
+    def turn(self, e, grads, ident):
+        got = link_kernel("sum_scatter", ident, sums=(e,), scatter=self.slots(grads), plan=weave_scatter)
         return got[0], got[1:]
-
-    def end(self, e, branch, grads):
-        got = link_kernel("sums_scatter", 4, sums=(e, branch), scatter=self.slots(grads), plan=weave_scatter)
-        return got[0], got[1], got[2:]
 
 
 def flatten_small(parts):
@@ -860,7 +911,7 @@
     cos, sin = rope_tables(position)
     seg_col, seg_row = segment[:, None], segment[None, :]
     live = valid[:, None]
-    first_full, got = links.begin(weights, flatten_small(small))
+    first_full, got, later = links.begin(weights, flatten_small(small))
     qb, ub, vecs = unpack_small(got, small)
     qb = qb.reshape(LAYERS, 1, -1).astype(F32)
     ub = ub.reshape(LAYERS, 1, -1).astype(F32)
@@ -871,16 +922,22 @@
     full, kept, extra = [first_full], [], None
     for layer in range(LAYERS):
         wq, wd, wu, wn = full[layer]
-        h1, h2, mixed, act, gp, stats = project(tokens_in, extra, held[layer], wq, qb[layer], cos, sin, wu, ub[layer])
+        h1, h2, mixed, act, gp, stats, *more = project(tokens_in, extra, held[layer], wq, qb[layer], cos, sin, wu, ub[layer], later if layer == 0 else None)
+        if more:
+            wd, wn = more
+            full[0] = wq, wd, wu, wn
         ctx = attend_forward(mixed, seg_col, seg_row)
         branch = branch_out(ctx, act, wd, wn)
         kept.append((h1, h2, mixed, act, gp, stats, ctx, extra))
         if layer == 0:
             extra, made = links.middle(branch, weights)
             full.append(made)
-
-    gout = gr = jnp.where(live, cotangent, 0).astype(BF)
-    sums = jnp.sum(gout.astype(F32), axis=0, keepdims=True)
+        else:
+            gout = gr = jnp.where(live, cotangent, 0).astype(BF)
+            sums = jnp.sum(gout.astype(F32), axis=0, keepdims=True)
+            branch, gr = lax.optimization_barrier((branch, gr))
+            branch = lax.psum(branch, "mp")
+
     big, little = [None] * LAYERS, [None] * LAYERS
     for layer in reversed(range(LAYERS)):
         wq, wd, wu, wn = full[layer]
@@ -893,9 +950,10 @@
         gq, qsum = weight_grad(h1, dmix)
         gu, usum = weight_grad(h2, df)
         if layer:
-            e, big[layer] = links.turn(e, (gq, gd, gu, gn))
+            e, big[layer] = links.turn(e, (gq, gd, gu, gn), 3)
+            branch, e = lax.optimization_barrier((branch, e))
         else:
-            e, branch, big[layer] = links.end(e, branch, (gq, gd, gu, gn))
+            e, big[layer] = links.turn(e, (gq, gd, gu, gn), 4)
         little[layer] = (qsum, usum, norm_sums, sums)
         made = norm_back(gout, e, tokens_in, extra, held[layer], stats, layer == 0)
         if layer:

time: 1050 us -> 951 us (0.906)
  Pallas kernels: 984 us -> 885 us
    pallas_call x4, Pallas kernels: 599 us -> 483 us  [link_kernel(): pl.pallas_call(kernel, in_specs=ins, out_specs=outs, out_shape=shapes, sc...]
    pallas_call x2, Pallas kernels: 71.5 us -> 86.5 us  [project(): call(kernel, (nq + nu,), ins, outs, shapes, scratch, ident=5 if ng else N...]
  transfers between devices with their start and end apart: 1 -> 2, of which waited for: 0 -> 0; matrix products, arithmetic and copies ran while one was open for 1% -> 1% of each run, Pallas kernels for 32% -> 48%
where the time goes in v3:
time: 951 us; the launch traced here: 936 us
  Pallas kernels  885 us (93%)
  other arithmetic  22 us (2%)
  between operations  14.8 us (2%)
  local copies, waits for them, and re-layouts  13.8 us (1%)
    pallas_call x4, Pallas kernels, link_kernel(): pl.pallas_call(kernel, in_specs=ins, out_specs=outs, out_shape=shapes, sc...  483 us
    pallas_call x8, Pallas kernels, weight_grad(): call(kernel, (M // MB,), [spec((n, MB), lambda j: (0, j)), spec((n, N), w...  99 us
    pallas_call x2, Pallas kernels, project(): call(kernel, (nq + nu,), ins, outs, shapes, scratch, ident=5 if ng else N...  86.5 us
    pallas_call x2, Pallas kernels, back_out(): call(kernel, (D // NB,), [spec((n, C), whole, True), spec((n, U), whole,...  46.6 us
    pallas_call x2, Pallas kernels, adam_layer(): pl.pallas_call(kernel, grid=(steps,), in_specs=ins, out_specs=[at(b) for...  38.4 us
    pallas_call x2, Pallas kernels, back_in(): call(kernel, (nr + nu,), [spec((n, D), lambda j: (0, 0), True), spec((n,...  36.3 us
    pallas_call x2, Pallas kernels, branch_out(): call(kernel, (dp,), [spec((n, R), whole, True), spec((n, U), whole, True)...  32.2 us
    pallas_call x2, Pallas kernels, norm_back(): call(kernel, (n // RB,), ins, outs, shapes, flops=10 * n * D, nbytes=16 *...  27.1 us
  transfers between devices with their start and end apart: 2, of which 0 were waited for; matrix products, arithmetic and copies ran while one was open for 1% of the time, Pallas kernels for 48%

profile of v3, /device:TPU:0, one launch (start us, length us, event | category | flops | bytes accessed | tf_op | source)
XLA Modules:
  0.0 935.7 jit_solution(3228560397987914340)
XLA Ops:
  7.3 0.7 copy.125
  8.0 0.8 reshape.275
  8.8 0.7 copy.124
  10.2 67.6 %gather.1 = (bf16[8,32,128]{2,1,0:T(8,128)(2,1)}, bf16[8,256,1536]{2,1,0:T(8,128)(2,1)}, bf16[8,256,2048]{2,1,0:T(8,128)(2,1)}) custom-call(bf16[32,128]{1,0:T(8,128)(2,1)} %fusion.18.refs_0_, bf16[2,256,1536]{2,1,0:T(8,128)(2,1)} %refs_0_.9, bf16[2,256,2048]{2,1,0:T(8,128)(2,1)} %refs_2_.11), custom_call_target="tpu_custom_call" | custom-call | bytes 14712832 | tf_op jit(solution)/shard_map/gather/pallas_call | solution.py:749
  77.8 0.9 copy.182
  79.4 0.7 squeeze.28.refs_3_
  80.3 0.7 squeeze.29.refs_7_
  81.3 1.0 add_select_fusion.sc_r
  82.9 0.6 pad_maximum_fusion.2.refs_1_.refs_5_.refs_3_
  83.6 1.9 fusion
  85.5 1.3 maximum_maximum_fusion
  86.8 53.9 %project.2 = (bf16[1024,2048]{1,0:T(8,128)(2,1)}, bf16[1024,2048]{1,0:T(8,128)(2,1)}, bf16[1024,1536]{1,0:T(8,128)(2,1)}, bf16[1024,2048]{1,0:T(8,128)(2,1)}, bf...) custom-call(bf16[1024,2048]{1,0:T(8,128)(2,1)} %refs_2_.9, ...), custom_call_target="tpu_custom_call" | custom-call | flops 15032385536 | bytes 38797312 | tf_op jit(solution)/shard_map/project/pallas_call | solution.py:184
  140.7 6.6 attend.2.c_r.l_r
  147.3 16.1 %branch.2.refs_4_ = bf16[1024,2048]{1,0:T(8,128)(2,1)} custom-call(bf16[1024,512]{1,0:T(8,128)(2,1)} %attend.2.c_r.l_r, bf16[1024,2048]{1,0:T(8,128)(2,1)} %get-tuple-element.125.a_r.l_r, bf16[8,512,256]{2,1,0:T(8,128)(2,1)} %get-tuple-element.126.wd_r, bf16[8,2048,256]{2,1,0:T(8,128)(2,1)} %get-tuple-element.127.wn_r), custom_call_target="tpu_custom_call" | custom-call | flops 10737418240 | bytes 19922944 | tf_op jit(solution)/shard_map/branch/pallas_call | solution.py:267
  163.3 122.6 %sum_gather.1 = (bf16[8,256,1536]{2,1,0:T(8,128)(2,1)}, bf16[8,512,256]{2,1,0:T(8,128)(2,1)}, bf16[8,256,2048]{2,1,0:T(8,128)(2,1)}, bf16[8,2048,256]{2,1,0:T(8,128)(2,1)}, bf16[1024,2048]{1,0:T(8,128)(2,1)}) custom-call(bf16[2,256,1536]{2,1,0:T(8,128)(2,1)} %refs_0_.9, bf16[2,512,256]{2,1,0:T(8,128)(2,1)} %refs_1_.7, bf16[2,256,2048]{2,1,0:T(8,128)(2,1)} %refs_2_.11, ...), custom_call_target="tpu_custom_call" | custom-call | bytes 29360128 | tf_op jit(solution)/shard_map/sum_gather/pallas_call | solution.py:749
  286.0 0.7 squeeze.32.refs_4_
  286.7 0.7 squeeze.33.refs_8_
  287.4 0.6 pad_maximum_fusion.3.refs_2_.refs_6_.refs_4_
  288.0 32.6 %project.3 = (bf16[1024,2048]{1,0:T(8,128)(2,1)}, bf16[1024,2048]{1,0:T(8,128)(2,1)}, bf16[1024,1536]{1,0:T(8,128)(2,1)}, bf16[1024,2048]{1,0:T(8,128)(2,1)}, bf...) custom-call(bf16[1024,2048]{1,0:T(8,128)(2,1)} %refs_2_.9, bf16[1024,2048]{1,0:T(8,128)(2,1)} %get-tuple-element.128.refs_1_.refs_5_.refs_3_, ...), custom_call_target="tpu_custom_call" | custom-call | flops 15032385536 | bytes 38797312 | tf_op jit(solution)/shard_map/project/pallas_call | solution.py:184
  320.6 6.7 attend.3.c_r.l_r
  327.4 4.3 convert_reduce_fusion
  331.7 16.1 %branch.3 = bf16[1024,2048]{1,0:T(8,128)(2,1)} custom-call(bf16[1024,512]{1,0:T(8,128)(2,1)} %attend.3.c_r.l_r, bf16[1024,2048]{1,0:T(8,128)(2,1)} %get-tuple-element.132.a_r.l_r, bf16[8,512,256]{2,1,0:T(8,128)(2,1)} %get-tuple-element.133.wd_r, bf16[8,2048,256]{2,1,0:T(8,128)(2,1)} %get-tuple-element.134.wn_r), custom_call_target="tpu_custom_call" | custom-call | flops 10737418240 | bytes 19922944 | tf_op jit(solution)/shard_map/branch/pallas_call | solution.py:267
  347.8 18.2 %back_in.2 = (bf16[1024,512]{1,0:T(8,128)(2,1)}, bf16[1024,2048]{1,0:T(8,128)(2,1)}) custom-call(bf16[1024,2048]{1,0:T(8,128)(2,1)} %get-tuple-element.136.g_r.r_r.refs_0_, bf16[1024,2048]{1,0:T(8,128)(2,1)} %get-tuple-element.137.gp_r, bf16[8,512,256]{2,1,0:T(8,128)(2,1)} %get-tuple-element.133.wd_r, bf16[8,2048,256]{2,1,0:T(8,128)(2,1)} %get-tuple-element.134.wn_r), custom_call_target="tpu_custom_call" | custom-call | flops 10737418240 | bytes 24117248 | tf_op jit(solution)/shard_map/back_in/pallas_call | solution.py:299
  366.0 11.5 %attend_back.2.refs_0_.r_r = bf16[1024,1536]{1,0:T(8,128)(2,1)} custom-call(bf16[1024,1536]{1,0:T(8,128)(2,1)} %get-tuple-element.131.q_r.k_r.v_r, bf16[1024,1536]{1,0:T(8,128)(2,1)} %get-tuple-element.131.q_r.k_r.v_r, bf16[1024,1536]{1,0:T(8,128)(2,1)} %get-tuple-element.131.q_r.k_r.v_r, bf16[1024,512]{1,0:T(8,128)(2,1)} %get-tuple-element.138.do_r, ...), custom_call_target="tpu_custom_call" | custom-call | flops 3355443200 | bytes 6291456 | tf_op jit(solution)/shard_map/attend_back/pallas_call | solution.py:250
  377.5 6.7 wgrad.9
  384.3 12.8 %wgrad.8 = (bf16[2048,1536]{1,0:T(8,128)(2,1)}, f32[1,1536]{1,0:T(1,128)}) custom-call(bf16[1024,2048]{1,0:T(8,128)(2,1)} %get-tuple-element.142.l_r, bf16[1024,1536]{1,0:T(8,128)(2,1)} %attend_back.2.refs_0_.r_r), custom_call_target="tpu_custom_call" | custom-call | flops 6442450944 | bytes 13631488 | tf_op jit(solution)/shard_map/wgrad/pallas_call | solution.py:364
  397.1 15.0 %wgrad.11 = (bf16[8,2048,256]{2,1,0:T(8,128)(2,1)}, f32[1,2048]{1,0:T(1,128)}) custom-call(bf16[1024,2048]{1,0:T(8,128)(2,1)} %get-tuple-element.132.a_r.l_r, bf16[1024,2048]{1,0:T(8,128)(2,1)} %get-tuple-element.136.g_r.r_r.refs_0_), custom_call_target="tpu_custom_call" | custom-call | flops 8589934592 | bytes 16777216 | tf_op jit(solution)/shard_map/wgrad/pallas_call | solution.py:364
  412.1 15.0 %wgrad.10 = (bf16[2048,2048]{1,0:T(8,128)(2,1)}, f32[1,2048]{1,0:T(1,128)}) custom-call(bf16[1024,2048]{1,0:T(8,128)(2,1)} %get-tuple-element.145.l_r, bf16[1024,2048]{1,0:T(8,128)(2,1)} %get-tuple-element.139.refs_1_.r_r), custom_call_target="tpu_custom_call" | custom-call | flops 8589934592 | bytes 16777216 | tf_op jit(solution)/shard_map/wgrad/pallas_call | solution.py:364
  427.0 24.2 %back_out.2 = (bf16[1024,2048]{1,0:T(8,128)(2,1)}, f32[4,2048]{1,0:T(4,128)}) custom-call(bf16[1024,1536]{1,0:T(8,128)(2,1)} %attend_back.2.refs_0_.r_r, bf16[1024,2048]{1,0:T(8,128)(2,1)} %get-tuple-element.139.refs_1_.r_r, bf16[2048,1536]{1,0:T(8,128)(2,1)} %bitcast.103, bf16[2048,2048]{1,0:T(8,128)(2,1)} %bitcast.99, bf16[1024,2048]{1,0:T(8,128)(2,1)} %refs_2_.9, ...), custom_call_target="tpu_custom_call" | custom-call | flops 15032385536 | bytes 34603008 | tf_op jit(solution)/shard_map/back_out/pallas_call | solution.py:335
  451.2 168.6 %sum_scatter.2 = (bf16[1024,2048]{1,0:T(8,128)(2,1)}, f32[256,1536]{1,0:T(8,128)}, f32[512,256]{1,0:T(8,128)}, f32[256,2048]{1,0:T(8,128)}, f32[2048,256]{1,0:T(8,128)}) custom-call(bf16[1024,2048]{1,0:T(8,128)(2,1)} %get-tuple-element.141.refs_0_, bf16[8,256,1536]{2,1,0:T(8,128)(2,1)} %bitcast.70, bf16[8,512,256]{2,1,0:T(8,128)(2,1)} %get-tuple-element.144.refs_2_, ...), custom_call_target="tpu_custom_call" | custom-call | bytes 29360128 | tf_op jit(solution)/shard_map/sum_scatter/pallas_call | solution.py:749
  619.8 19.4 %adam.2 = (f32[2,256,1536]{2,1,0:T(8,128)}, f32[2,256,1536]{2,1,0:T(8,128)}, f32[2,256,1536]{2,1,0:T(8,128)}, f32[2,256,1536]{2,1,0:T(8,128)}, f32[2,512,256]{2,...) custom-call(bf16[2,256,1536]{2,1,0:T(8,128)(2,1)} %refs_0_.9, ...), custom_call_target="tpu_custom_call" | custom-call | flops 31457280 | bytes 47185920 | tf_op jit(solution)/shard_map/adam/pallas_call | solution.py:822
  639.3 14.9 %norm_back.2 = (f32[1024,2048]{1,0:T(8,128)}, bf16[1024,2048]{1,0:T(8,128)(2,1)}, f32[1,2048]{1,0:T(1,128)}) custom-call(bf16[1024,2048]{1,0:T(8,128)(2,1)} %get-tuple-element.136.g_r.r_r.refs_0_, bf16[1024,2048]{1,0:T(8,128)(2,1)} %get-tuple-element.150.refs_1_, bf16[1024,2048]{1,0:T(8,128)(2,1)} %refs_2_.9, ...), custom_call_target="tpu_custom_call" | custom-call | flops 20971520 | bytes 33554432 | tf_op jit(solution)/shard_map/norm_back/pallas_call | solution.py:407
  654.1 15.0 %wgrad.15 = (bf16[8,2048,256]{2,1,0:T(8,128)(2,1)}, f32[1,2048]{1,0:T(1,128)}) custom-call(bf16[1024,2048]{1,0:T(8,128)(2,1)} %get-tuple-element.125.a_r.l_r, bf16[1024,2048]{1,0:T(8,128)(2,1)} %get-tuple-element.152.g_r.r_r), custom_call_target="tpu_custom_call" | custom-call | flops 8589934592 | bytes 16777216 | tf_op jit(solution)/shard_map/wgrad/pallas_call | solution.py:364
  669.1 18.1 %back_in.3 = (bf16[1024,512]{1,0:T(8,128)(2,1)}, bf16[1024,2048]{1,0:T(8,128)(2,1)}) custom-call(bf16[1024,2048]{1,0:T(8,128)(2,1)} %get-tuple-element.152.g_r.r_r, bf16[1024,2048]{1,0:T(8,128)(2,1)} %get-tuple-element.153.gp_r, bf16[8,512,256]{2,1,0:T(8,128)(2,1)} %get-tuple-element.126.wd_r, bf16[8,2048,256]{2,1,0:T(8,128)(2,1)} %get-tuple-element.127.wn_r), custom_call_target="tpu_custom_call" | custom-call | flops 10737418240 | bytes 24117248 | tf_op jit(solution)/shard_map/back_in/pallas_call | solution.py:299
  687.3 11.4 %attend_back.3.refs_0_.r_r = bf16[1024,1536]{1,0:T(8,128)(2,1)} custom-call(bf16[1024,1536]{1,0:T(8,128)(2,1)} %get-tuple-element.124.q_r.k_r.v_r, bf16[1024,1536]{1,0:T(8,128)(2,1)} %get-tuple-element.124.q_r.k_r.v_r, bf16[1024,1536]{1,0:T(8,128)(2,1)} %get-tuple-element.124.q_r.k_r.v_r, bf16[1024,512]{1,0:T(8,128)(2,1)} %get-tuple-element.154.do_r, ...), custom_call_target="tpu_custom_call" | custom-call | flops 3355443200 | bytes 6291456 | tf_op jit(solution)/shard_map/attend_back/pallas_call | solution.py:250
  698.7 12.7 %wgrad.12 = (bf16[2048,1536]{1,0:T(8,128)(2,1)}, f32[1,1536]{1,0:T(1,128)}) custom-call(bf16[1024,2048]{1,0:T(8,128)(2,1)} %get-tuple-element.158.l_r, bf16[1024,1536]{1,0:T(8,128)(2,1)} %attend_back.3.refs_0_.r_r), custom_call_target="tpu_custom_call" | custom-call | flops 6442450944 | bytes 13631488 | tf_op jit(solution)/shard_map/wgrad/pallas_call | solution.py:364
  711.4 22.4 %back_out.3 = (bf16[1024,2048]{1,0:T(8,128)(2,1)}, f32[4,2048]{1,0:T(4,128)}) custom-call(bf16[1024,1536]{1,0:T(8,128)(2,1)} %attend_back.3.refs_0_.r_r, bf16[1024,2048]{1,0:T(8,128)(2,1)} %get-tuple-element.155.refs_1_.r_r, bf16[2048,1536]{1,0:T(8,128)(2,1)} %bitcast.101, bf16[2048,2048]{1,0:T(8,128)(2,1)} %bitcast.97, bf16[1024,2048]{1,0:T(8,128)(2,1)} %refs_2_.9, ...), custom_call_target="tpu_custom_call" | custom-call | flops 15032385536 | bytes 34603008 | tf_op jit(solution)/shard_map/back_out/pallas_call | solution.py:335
  733.9 15.0 %wgrad.14 = (bf16[2048,2048]{1,0:T(8,128)(2,1)}, f32[1,2048]{1,0:T(1,128)}) custom-call(bf16[1024,2048]{1,0:T(8,128)(2,1)} %get-tuple-element.161.l_r, bf16[1024,2048]{1,0:T(8,128)(2,1)} %get-tuple-element.155.refs_1_.r_r), custom_call_target="tpu_custom_call" | custom-call | flops 8589934592 | bytes 16777216 | tf_op jit(solution)/shard_map/wgrad/pallas_call | solution.py:364
  749.0 0.7 pad_maximum_fusion.5
  749.9 0.7 pad_maximum_fusion
  750.6 8.2 select_convert_fusion
  758.9 6.8 wgrad.13
  765.7 123.7 %sum_scatter.3 = (bf16[1024,2048]{1,0:T(8,128)(2,1)}, f32[256,1536]{1,0:T(8,128)}, f32[512,256]{1,0:T(8,128)}, f32[256,2048]{1,0:T(8,128)}, f32[2048,256]{1,0:T(8,128)}) custom-call(bf16[1024,2048]{1,0:T(8,128)(2,1)} %get-tuple-element.157.refs_0_, bf16[8,256,1536]{2,1,0:T(8,128)(2,1)} %bitcast.69, bf16[8,512,256]{2,1,0:T(8,128)(2,1)} %get-tuple-element.160.refs_2_, ...), custom_call_target="tpu_custom_call" | custom-call | bytes 29360128 | tf_op jit(solution)/shard_map/sum_scatter/pallas_call | solution.py:749
  889.4 12.3 %norm_back.3 = f32[1024,2048]{1,0:T(8,128)} custom-call(f32[1024,2048]{1,0:T(8,128)} %get-tuple-element.151.refs_0_, bf16[1024,2048]{1,0:T(8,128)(2,1)} %get-tuple-element.164.refs_1_, bf16[1024,2048]{1,0:T(8,128)(2,1)} %refs_2_.9, f32[6,2048]{1,0:T(8,128)} %pad_maximum_fusion.2.refs_1_.refs_5_.refs_3_, f32[1024,128]{1,0:T(8,128)} %get-tuple-element.156.refs_6_.refs_4_), custom_call_target="tpu_custom_call" | custom-call | flops 20971520 | bytes 33554432 | tf_op jit(solution)/shard_map/norm_back/pallas_call | solution.py:407
  901.7 19.1 %adam.3 = (f32[2,256,1536]{2,1,0:T(8,128)}, f32[2,256,1536]{2,1,0:T(8,128)}, f32[2,256,1536]{2,1,0:T(8,128)}, f32[2,256,1536]{2,1,0:T(8,128)}, f32[2,512,256]{2,...) custom-call(bf16[2,256,1536]{2,1,0:T(8,128)(2,1)} %refs_0_.9, ...), custom_call_target="tpu_custom_call", output_to_operand_aliasing={{0}: (16, {}), {1}: (17, {}), {2}: (18, {}), {3}: (19, {}),... | custom-call | flops 31457280 | bytes 47185920 | tf_op jit(solution)/shard_map/adam/pallas_call | solution.py:822
  920.9 0.9 slice.97
  924.6 0.9 slice.98
  928.0 0.7 subtract_subtract_fusion.1
  (94 shorter events, 8.2 us)
Async XLA Ops:
  7.2 71.7 %copy-start.15 = (s32[1,4]{1,0:T(1,128)S(1)}, s32[1,4]{1,0:T(1,128)}, u32[]{:S(2)}) copy-start(s32[1,4]{1,0:T(1,128)} %param.26) | copy-start | bytes 52
  7.2 632.1 %all-reduce.4.cloned.1.call-start = ((), (), s32[]{:S(2)}) async-start(), calls=%async_computation | async-start | bytes 8388608 | tf_op jit(solution)/shard_map/psum | solution.py:939
  347.8 573.1 %all-reduce.6.cloned.1.call-start = ((), (), s32[]{:S(2)}) async-start(), calls=%async_computation.1 | async-start | bytes 425984 | tf_op jit(solution)/shard_map/psum | solution.py:976
  733.9 15.1 %copy-start.12 = (f32[1,2048]{1,0:T(1,128)S(1)}, f32[1,2048]{1,0:T(1,128)}, u32[]{:S(2)}) copy-start(f32[1,2048]{1,0:T(1,128)} %get-tuple-element.211) | copy-start | bytes 24580
  733.9 15.1 %copy-start = (f32[4,2048]{1,0:T(4,128)S(1)}, f32[4,2048]{1,0:T(4,128)}, u32[]{:S(2)}) copy-start(f32[4,2048]{1,0:T(4,128)} %get-tuple-element.210) | copy-start | bytes 98308
  733.9 15.1 %copy-start.1 = (f32[4,2048]{1,0:T(4,128)S(1)}, f32[4,2048]{1,0:T(4,128)}, u32[]{:S(2)}) copy-start(f32[4,2048]{1,0:T(4,128)} %get-tuple-element.209) | copy-start | bytes 98308
  733.9 15.2 %copy-start.11 = (f32[1,2048]{1,0:T(1,128)S(1)}, f32[1,2048]{1,0:T(1,128)}, u32[]{:S(2)}) copy-start(f32[1,2048]{1,0:T(1,128)} %get-tuple-element.208) | copy-start | bytes 24580
  733.9 15.9 %copy-start.13 = (f32[1,1536]{1,0:T(1,128)S(1)}, f32[1,1536]{1,0:T(1,128)}, u32[]{:S(2)}) copy-start(f32[1,1536]{1,0:T(1,128)} %get-tuple-element.206) | copy-start | bytes 18436
  733.9 15.9 %copy-start.14 = (f32[1,1536]{1,0:T(1,128)S(1)}, f32[1,1536]{1,0:T(1,128)}, u32[]{:S(2)}) copy-start(f32[1,1536]{1,0:T(1,128)} %get-tuple-element.205) | copy-start | bytes 18436
  901.7 20.2 %copy-start.3 = (bf16[2,12,16]{2,0,1:T(2,128)(2,1)S(1)}, bf16[2,12,16]{2,0,1:T(2,128)(2,1)}, u32[]{:S(2)}) copy-start(bf16[2,12,16]{2,0,1:T(2,128)(2,1)} %param.31) | copy-start | bytes 2308
  901.7 20.2 %copy-start.7 = (f32[2,12,16]{2,0,1:T(2,128)S(1)}, f32[2,12,16]{2,0,1:T(2,128)}, u32[]{:S(2)}) copy-start(f32[2,12,16]{2,0,1:T(2,128)} %param.45) | copy-start | bytes 4612
  901.7 20.2 %copy-start.8 = (f32[2,12,16]{2,0,1:T(2,128)S(1)}, f32[2,12,16]{2,0,1:T(2,128)}, u32[]{:S(2)}) copy-start(f32[2,12,16]{2,0,1:T(2,128)} %param.38) | copy-start | bytes 4612
  901.7 23.8 %copy-start.4 = (bf16[2,6,256]{2,0,1:T(2,128)(2,1)S(1)}, bf16[2,6,256]{2,0,1:T(2,128)(2,1)}, u32[]{:S(2)}) copy-start(bf16[2,6,256]{2,0,1:T(2,128)(2,1)} %param.33) | copy-start | bytes 18436
  901.7 23.8 %copy-start.9 = (f32[2,6,256]{2,0,1:T(2,128)S(1)}, f32[2,6,256]{2,0,1:T(2,128)}, u32[]{:S(2)}) copy-start(f32[2,6,256]{2,0,1:T(2,128)} %param.47) | copy-start | bytes 36868
  901.7 23.8 %copy-start.10 = (f32[2,6,256]{2,0,1:T(2,128)S(1)}, f32[2,6,256]{2,0,1:T(2,128)}, u32[]{:S(2)}) copy-start(f32[2,6,256]{2,0,1:T(2,128)} %param.40) | copy-start | bytes 36868
  901.7 26.3 %copy-start.2 = (bf16[2,16,16]{2,1,0:T(8,128)(2,1)S(1)}, bf16[2,16,16]{2,1,0:T(8,128)(2,1)}, u32[]{:S(2)}) copy-start(bf16[2,16,16]{2,1,0:T(8,128)(2,1)} %param.32) | copy-start | bytes 3076
  901.7 26.3 %copy-start.5 = (f32[2,16,16]{2,1,0:T(8,128)S(1)}, f32[2,16,16]{2,1,0:T(8,128)}, u32[]{:S(2)}) copy-start(f32[2,16,16]{2,1,0:T(8,128)} %param.46) | copy-start | bytes 6148
  901.7 26.2 %copy-start.6 = (f32[2,16,16]{2,1,0:T(8,128)S(1)}, f32[2,16,16]{2,1,0:T(8,128)}, u32[]{:S(2)}) copy-start(f32[2,16,16]{2,1,0:T(8,128)} %param.39) | copy-start | bytes 6148
Sparse Core Ops, SparseCore 0:
  347.9 192.7 all-reduce.3
  750.8 123.8 all-reduce.5

commit v4 on v3

--- a/solution.py
+++ b/solution.py
@@ -19,6 +19,7 @@
 rate = 0.02
 decay = 0.01
 VM = 60 * 1024 * 1024
+VM2 = 62 * 1024 * 1024
 BF = jnp.bfloat16
 ROWS = 256
 UPB = 512
@@ -549,20 +550,21 @@
             there = pl.ds(pl.multiple_of(base + i * step, step), step)
             dst[rows, :] = (one[there, :].astype(F32) + two[rows, :].astype(F32)).astype(BF)
 
-    def tick(self, t):
+    def send_step(self, t):
         n = self.chunks
 
         @pl.when(self.spot.outer)
         def _():
+            if 0 <= t - 2 < n:
+                self.copy(t - 2, 0).wait_send()
             if t < n:
-                if t >= 2:
-                    self.copy(t - 2, 0).wait_send()
                 self.copy(t, 0).start()
-            elif t < n + 2:
-                self.copy(t - 2, 0).wait_send()
-            if 0 <= t - 3 < n:
-                self.copy(t - 3, 2).wait_recv()
-                self.keep(t - 3).start()
+            if 0 <= t - 4 < n:
+                self.copy(t - 4, 2).wait_recv()
+                self.keep(t - 4).start()
+
+    def add_step(self, t):
+        n = self.chunks
 
         @pl.when(self.spot.inner)
         def _():
@@ -695,97 +697,220 @@
             copy.wait_send()
 
 
-def link_kernel(name, ident, gather=None, sums=(), scatter=None, chunks=8, plan=None):
-    shards = [] if gather is None else list(gather[0])
-    layers = [] if gather is None else list(gather[1])
-    sums, grads = list(sums), [] if scatter is None else list(scatter)
-    ng, ns, nr = len(shards), len(sums), len(grads)
+def link_kernel(name, ident, shards, layers, part=None, chunks=8):
+    ng = len(shards)
     HBM = pl.BlockSpec(memory_space=pl.ANY)
-    VM_ = pl.BlockSpec(memory_space=pltpu.VMEM)
-    shard_shape = lambda v, l: v.shape if l is None else v.shape[1:]
-    ins = [HBM] * (ng + ns + nr)
-    outs = [HBM] * ng + [HBM] * ns + [VM_] * nr
-    shapes = [jax.ShapeDtypeStruct((8,) + shard_shape(v, l), v.dtype) for v, l in zip(shards, layers)]
-    shapes += [jax.ShapeDtypeStruct(v.shape, BF) for v in sums]
-    shapes += [jax.ShapeDtypeStruct(v.shape[1:], F32) for v in grads]
-    scratch = []
     DMA = pltpu.SemaphoreType.DMA
-    if ng:
-        scratch += [DMA((ng, 9)), DMA((ng, 9)), DMA((ng,))]
-    for v in sums:
+    parts = [] if part is None else [part]
+    shapes = [jax.ShapeDtypeStruct((8,) + (v.shape if l is None else v.shape[1:]), v.dtype) for v, l in zip(shards, layers)]
+    shapes += [jax.ShapeDtypeStruct(v.shape, BF) for v in parts]
+    scratch = [DMA((ng, 9)), DMA((ng, 9)), DMA((ng,))]
+    for v in parts:
         scratch += [pltpu.VMEM((2, v.shape[0] // chunks, v.shape[1]), BF), pltpu.VMEM(v.shape, BF), pltpu.VMEM(v.shape, BF), DMA((chunks, 3)), DMA((chunks, 3)), DMA((chunks + 2,))]
-    if nr:
-        scratch += [DMA((nr, 10)), DMA((nr, 10)), DMA((nr, 4))]
-        for v in grads:
-            _, r, c = v.shape
-            scratch += [pltpu.VMEM((4, r, c), BF), pltpu.VMEM((4, r, c), BF), pltpu.VMEM((2, r // 2, c), BF), pltpu.VMEM((2, r // 2, c), BF),
-                        pltpu.VMEM((r // 2, c), BF), pltpu.VMEM((r // 2, c), BF)]
 
     def kernel(*refs):
         refs = list(refs)
         take = lambda n: [refs.pop(0) for _ in range(n)]
-        src, part, grad = take(ng), take(ns), take(nr)
-        full, total, owned = take(ng), take(ns), take(nr)
+        src, ins, full, totals = take(ng), take(len(parts)), take(ng), take(len(parts))
         spot = Spot()
-        spot.meet(bool(ns))
-        G = S = None
-        if ng:
-            pick = lambda ref, l: ref if l is None else ref.at[l]
-            G = Gather(spot, [(pick(a, l), b) for a, l, b in zip(src, layers, full)], *take(3))
-        lines = []
-        for k in range(ns):
+        spot.meet(bool(parts))
+        G = Gather(spot, [(a if l is None else a.at[l], b) for a, l, b in zip(src, layers, full)], *take(3))
+        if parts:
             stage, land, swap, send, recv, local = take(6)
-            lines.append(LineSum(spot, part[k], stage, land, swap, total[k], send, recv, local, chunks))
-        if nr:
-            send, recv, local = take(3)
-            bufs = [take(6) for _ in range(nr)]
-            S = Scatter(spot, list(zip(grad, owned)), *[[b[i] for b in bufs] for i in range(6)], send, recv, local)
-        plan(G, lines, S)
-        for part_ in [G, *lines, S]:
-            if part_ is not None:
-                part_.close()
-
-    nbytes = sum(v.size * 2 for v in sums + grads) + sum(8 * v.size for v in shards)
+            line = LineSum(spot, ins[0], stage, land, swap, totals[0], send, recv, local, chunks)
+            plan_sum_gather(G, line)
+            line.close()
+        else:
+            plan_gather(G)
+        G.close()
+
+    nbytes = sum(v.size * 2 for v in parts) + sum(8 * v.size for v in shards)
     return pl.pallas_call(
-        kernel, in_specs=ins, out_specs=outs, out_shape=shapes, scratch_shapes=scratch,
+        kernel, in_specs=[HBM] * (ng + len(parts)), out_specs=[HBM] * (ng + len(parts)), out_shape=shapes, scratch_shapes=scratch,
         compiler_params=pltpu.CompilerParams(vmem_limit_bytes=VM, collective_id=ident, has_side_effects=True),
-        cost_estimate=pl.CostEstimate(flops=0, bytes_accessed=nbytes, transcendentals=0), name=name)(*shards, *sums, *grads)
-
-
-def plan_gather(G, lines, S):
+        cost_estimate=pl.CostEstimate(flops=0, bytes_accessed=nbytes, transcendentals=0), name=name)(*shards, *parts)
+
+
+def plan_gather(G):
     n = len(G.items)
-    for k in range(n):
+    for stage in (G.first, G.second, G.third, G.last):
+        for k in range(n):
+            stage(k)
+
+
+class Products:
+    def __init__(self, lefts, rights, grads, rhs, lbuf, obuf, rsem, lsem, osem):
+        self.lefts, self.rights, self.grads = lefts, rights, grads
+        self.rhs, self.lbuf, self.obuf, self.rsem, self.lsem, self.osem = rhs, lbuf, obuf, rsem, lsem, osem
+
+    def right(self, i, slot):
+        return pltpu.make_async_copy(self.rights[i], self.rhs[slot], self.rsem.at[i])
+
+    def left(self, k, m):
+        cols = pl.ds(pl.multiple_of(m * 256, 256), 256)
+        return pltpu.make_async_copy(self.lefts[k].at[:, cols], self.lbuf.at[lax.rem(m, 2)], self.lsem.at[lax.rem(m, 2)])
+
+    def stores(self, k, m):
+        grad, o = self.grads[k], self.obuf.at[lax.rem(m, 2)]
+        sem = self.osem.at[lax.rem(m, 2)]
+        slots, r, c = grad.shape
+        if r == 256 and self.lefts[k].shape[1] == slots * r:
+            return [pltpu.make_async_copy(o.at[:, pl.ds(0, c)], grad.at[m], sem.at[0])]
+        rows = pl.ds(pl.multiple_of(m * 256, 256), 256)
+        return [pltpu.make_async_copy(o.at[:, pl.ds(s * c, c)], grad.at[s, rows], sem.at[s]) for s in range(slots)]
+
+    def run(self, k, slot, start, stop):
+        count = self.lefts[k].shape[1] // 256
+        right = self.rhs[slot]
+        width = right.shape[1]
+        if start == 0:
+            self.left(k, 0).start()
+
+        @pl.loop(start, stop)
+        def _(m):
+            self.left(k, m).wait()
+
+            @pl.when(m + 1 < count)
+            def _():
+                self.left(k, m + 1).start()
+
+            @pl.when(m >= 2)
+            def _():
+                for copy in self.stores(k, m - 2):
+                    copy.wait()
+
+            g = lax.dot_general(self.lbuf[lax.rem(m, 2)], right[...], (((0,), (0,)), ((), ())), preferred_element_type=F32)
+            self.obuf[lax.rem(m, 2), :, :width] = g.astype(BF)
+            for copy in self.stores(k, m):
+                copy.start()
+
+        if stop == count:
+            for m in (count - 2, count - 1):
+                for copy in self.stores(k, jnp.int32(m)):
+                    copy.wait()
+
+    def sums(self, slot, out):
+        right = self.rhs[slot]
+        out[...] = jnp.zeros_like(out)
+
+        @pl.loop(0, right.shape[0] // 64)
+        def _(i):
+            out[...] += jnp.sum(right[pl.ds(pl.multiple_of(i * 64, 64), 64), :].astype(F32), axis=0, keepdims=True)
+
+
+def plan_sum_gather(G, line):
+    for k in range(4):
         G.first(k)
-    for k in range(n):
-        G.second(k)
-    for k in range(n):
-        G.third(k)
-    for k in range(n):
+    stages = {3: [("second", 0), ("second", 1)], 5: [("second", 2)], 7: [("second", 3)], 8: [("third", 0), ("third", 1)], 9: [("third", 2)],
+              10: [("third", 3)]}
+    line.send_step(0)
+    for at in range(1, 12):
+        line.send_step(at)
+        if at - 1 <= line.chunks:
+            line.add_step(at - 1)
+        for name, k in stages.get(at, ()):
+            getattr(G, name)(k)
+    for k in range(4):
         G.last(k)
 
 
-def woven(stages):
-    def plan(G, lines, S):
-        side = G if G is not None else S
-        for k in range(len(side.items)):
-            side.first(k)
-        ticks = [(line, t) for line in lines for t in range(line.chunks + 3)]
-        for at, (line, t) in enumerate(ticks):
-            line.tick(t)
-            for name, k in stages.get(at, ()):
-                getattr(side, name)(k)
-        for at in sorted(stages):
-            if at >= len(ticks):
-                for name, k in stages[at]:
-                    getattr(side, name)(k)
-
-    return plan
-
-
-weave_gather = woven({2: [("second", 0), ("second", 1)], 4: [("second", 2)], 6: [("second", 3)], 7: [("third", 0), ("third", 1)], 8: [("third", 2)], 9: [("third", 3)],
-                      99: [("last", 0), ("last", 1), ("last", 2), ("last", 3)]})
-weave_scatter = woven({1: [("second", 0), ("second", 1)], 2: [("second", 2)], 3: [("second", 3)], 4: [("third", 0), ("third", 1)], 6: [("third", 2)], 8: [("third", 3)],
-                       9: [("last", 0), ("last", 1)], 99: [("last", 2), ("last", 3)]})
+def sum_scatter(ident, e, lefts, rights, chunks=8):
+    n, D = e.shape
+    HBM = pl.BlockSpec(memory_space=pl.ANY)
+    VM_ = pl.BlockSpec(memory_space=pltpu.VMEM)
+    C, U = rights[1].shape[1], rights[2].shape[1]
+    w = D // 8
+    dims = [(lefts[0].shape[1], w), (lefts[1].shape[1], w), (w, C), (w, U)]
+    DMA = pltpu.SemaphoreType.DMA
+    outs = [HBM] + [HBM] * 4 + [VM_] * 4 + [VM_] * 2
+    shapes = [jax.ShapeDtypeStruct(e.shape, BF)] + [jax.ShapeDtypeStruct((8,) + d, BF) for d in dims] + [jax.ShapeDtypeStruct(d, F32) for d in dims]
+    shapes += [jax.ShapeDtypeStruct((1, C), F32), jax.ShapeDtypeStruct((1, U), F32)]
+    scratch = [pltpu.VMEM((2, n // chunks, D), BF), pltpu.VMEM((n, D), BF), pltpu.VMEM((n, D), BF), DMA((chunks, 3)), DMA((chunks, 3)), DMA((chunks + 2,))]
+    scratch += [DMA((4, 10)), DMA((4, 10)), DMA((4, 4))]
+    for r, c in dims:
+        scratch += [pltpu.VMEM((4, r, c), BF), pltpu.VMEM((4, r, c), BF), pltpu.VMEM((2, r // 2, c), BF), pltpu.VMEM((2, r // 2, c), BF),
+                    pltpu.VMEM((r // 2, c), BF), pltpu.VMEM((r // 2, c), BF)]
+    wide = max(D, U)
+    scratch += [pltpu.VMEM((n, wide), BF), pltpu.VMEM((n, C), BF), pltpu.VMEM((2, n, 256), BF), pltpu.VMEM((2, 256, wide), BF), DMA((3,)), DMA((2,)), DMA((2, 8))]
+    assert D == U
+
+    def kernel(*refs):
+        refs = list(refs)
+        take = lambda k: [refs.pop(0) for _ in range(k)]
+        e_r, left_rs, right_rs = refs.pop(0), take(4), take(3)
+        total, grads, owned, sum_rs = refs.pop(0), take(4), take(4), take(2)
+        stage, land, swap, send, recv, local = take(6)
+        spot = Spot()
+        spot.meet(True)
+        line = LineSum(spot, e_r, stage, land, swap, total, send, recv, local, chunks)
+        send, recv, local = take(3)
+        bufs = [take(6) for _ in range(4)]
+        S = Scatter(spot, list(zip(grads, owned)), *[[b[i] for b in bufs] for i in range(6)], send, recv, local)
+        wide_r, narrow_r, lbuf, obuf, rsem, lsem, osem = take(7)
+        W = Products(left_rs, right_rs, grads, (wide_r, narrow_r), lbuf, obuf, rsem, lsem, osem)
+        W.right(0, 0).start()
+        W.right(1, 1).start()
+        line.send_step(0)
+        line.send_step(1)
+        W.right(0, 0).wait()
+        W.run(0, 0, 0, left_rs[0].shape[1] // 256)
+        S.first(0)
+        half = left_rs[1].shape[1] // 512
+        W.run(1, 0, 0, half)
+        line.add_step(0)
+        line.send_step(2)
+        S.second(0)
+        W.run(1, 0, half, 2 * half)
+        S.first(1)
+        W.right(2, 0).start()
+        W.right(1, 1).wait()
+        W.run(2, 1, 0, 2)
+        line.add_step(1)
+        line.send_step(3)
+        W.run(2, 1, 2, 8)
+        S.first(2)
+        W.sums(1, sum_rs[0])
+        line.add_step(2)
+        line.send_step(4)
+        S.second(1)
+        S.third(0)
+        W.right(2, 0).wait()
+        W.run(3, 0, 0, 4)
+        line.add_step(3)
+        line.send_step(5)
+        S.second(2)
+        W.run(3, 0, 4, 8)
+        S.first(3)
+        line.add_step(4)
+        line.send_step(6)
+        W.sums(0, sum_rs[1])
+        S.third(1)
+        line.add_step(5)
+        line.send_step(7)
+        S.second(3)
+        line.add_step(6)
+        line.send_step(8)
+        S.third(2)
+        line.add_step(7)
+        line.send_step(9)
+        line.add_step(8)
+        line.send_step(10)
+        S.third(3)
+        S.last(0)
+        S.last(1)
+        line.send_step(11)
+        S.last(2)
+        S.last(3)
+        line.close()
+        S.close()
+
+    flops = 2 * n * D * (lefts[0].shape[1] + lefts[1].shape[1] + C + U)
+    got = pl.pallas_call(
+        kernel, in_specs=[HBM] * 8, out_specs=outs, out_shape=shapes, scratch_shapes=scratch,
+        compiler_params=pltpu.CompilerParams(vmem_limit_bytes=VM2, collective_id=ident, has_side_effects=True),
+        cost_estimate=pl.CostEstimate(flops=flops, bytes_accessed=2 * n * D * 12, transcendentals=0), name="sum_scatter")(e, *lefts, *rights)
+    gd, gn, gq, gu = got[5:9]
+    return got[0], (gq, gd, gu, gn), got[9], got[10]
 
 
 def adam_update(weight, grad, first, second):
@@ -860,8 +985,15 @@
     def middle(self, branch, shards):
         return self.share(branch), self.weights(shards, 1)
 
-    def turn(self, e, grads, ident):
-        return self.share(e), self.owned(grads)
+    def turn(self, e, lefts, rights, ident):
+        ctx, act, h1, h2 = lefts
+        gr, dmix, df = rights
+        w = gr.shape[1] // lax.axis_size("dp")
+        gd, _ = weight_grad(ctx, gr, w=w)
+        gn, _ = weight_grad(act, gr, w=w)
+        gq, qsum = weight_grad(h1, dmix)
+        gu, usum = weight_grad(h2, df)
+        return self.share(e), self.owned((gq, gd, gu, gn)), qsum, usum
 
 
 class ChipLinks:
@@ -869,22 +1001,17 @@
         wq, wd, wu, wn = got
         return wq.reshape(-1, wq.shape[2]), wd, wu.reshape(-1, wu.shape[2]), wn
 
-    def slots(self, grads):
-        gq, gd, gu, gn = grads
-        return gq.reshape(8, -1, gq.shape[1]), gd, gu.reshape(8, -1, gu.shape[1]), gn
-
     def begin(self, shards, flat):
         wq, wd, wu, wn = shards
-        flat, wq, wu = link_kernel("gather", 1, gather=([flat, wq, wu], [None, 0, 0]), plan=plan_gather)
+        flat, wq, wu = link_kernel("gather", 1, [flat, wq, wu], [None, 0, 0])
         return (wq.reshape(-1, wq.shape[2]), None, wu.reshape(-1, wu.shape[2]), None), flat, (wd, wn)
 
     def middle(self, branch, shards):
-        got = link_kernel("sum_gather", 2, gather=(shards, [1] * 4), sums=(branch,), plan=weave_gather)
+        got = link_kernel("sum_gather", 2, shards, [1] * 4, branch)
         return got[4], self.full(got[:4])
 
-    def turn(self, e, grads, ident):
-        got = link_kernel("sum_scatter", ident, sums=(e,), scatter=self.slots(grads), plan=weave_scatter)
-        return got[0], got[1:]
+    def turn(self, e, lefts, rights, ident):
+        return sum_scatter(ident, e, lefts, rights)
 
 
 def flatten_small(parts):
@@ -936,7 +1063,8 @@
             gout = gr = jnp.where(live, cotangent, 0).astype(BF)
             sums = jnp.sum(gout.astype(F32), axis=0, keepdims=True)
             branch, gr = lax.optimization_barrier((branch, gr))
-            branch = lax.psum(branch, "mp")
+            half = rows // 2
+            tops, bottom = lax.psum(branch[:half], "mp"), branch[half:]
 
     big, little = [None] * LAYERS, [None] * LAYERS
     for layer in reversed(range(LAYERS)):
@@ -945,21 +1073,19 @@
         dctx, df = back_in(gr, gp, wd, wn)
         dmix = attend_backward(mixed, dctx, seg_col, seg_row, cos, sin)
         e, norm_sums = back_out(dmix, df, wq, wu, tokens_in, extra, held[layer], stats)
-        gd, _ = weight_grad(ctx, gr, w=wd.shape[2])
-        gn, _ = weight_grad(act, gr, w=wn.shape[2])
-        gq, qsum = weight_grad(h1, dmix)
-        gu, usum = weight_grad(h2, df)
+        if layer == 0:
+            bottom, e = lax.optimization_barrier((bottom, e))
+        e, big[layer], qsum, usum = links.turn(e, (ctx, act, h1, h2), (gr, dmix, df), 3 + layer)
+        little[layer] = (qsum, usum, norm_sums, sums)
         if layer:
-            e, big[layer] = links.turn(e, (gq, gd, gu, gn), 3)
-            branch, e = lax.optimization_barrier((branch, e))
-        else:
-            e, big[layer] = links.turn(e, (gq, gd, gu, gn), 4)
-        little[layer] = (qsum, usum, norm_sums, sums)
+            tops, e, bottom = lax.optimization_barrier((tops, e, bottom))
+            bottom = lax.psum(bottom, "mp")
         made = norm_back(gout, e, tokens_in, extra, held[layer], stats, layer == 0)
         if layer:
             gout, gr, sums = made
         else:
             input_grad = made[0]
+    branch = jnp.concatenate([tops, bottom])
     x_last = tokens_in.astype(F32) + kept[1][-1].astype(F32) + vecs[0, 4] + vecs[0, 5] + branch.astype(F32) + vecs[1, 4] + vecs[1, 5]
     output = jnp.where(live, x_last, 0.0).astype(BF)
 

time: 951 us -> 968 us (1.018)
  waiting for transfers between devices: 0.07 us -> 103 us
  Pallas kernels: 885 us -> 800 us
    pallas_call x12 -> x4, Pallas kernels: 582 us -> 497 us  [the longest x2 307 us: sum_scatter(): pl.pallas_call(kernel, in_specs=[HBM] * 8, out_specs=outs, out_shape=shap...]
    psum x1, waiting for transfers between devices: 0.02 us -> 83.4 us  [body(): total = lax.psum(jnp.concatenate([bias.reshape(-1), vec_sum]), ('dp', 'mp'))]
    psum x1 -> x2, waiting for transfers between devices: 0.02 us -> 19.9 us  [the longest x1 19.9 us: body(): bottom = lax.psum(bottom, 'mp')]
  transfers between devices with their start and end apart: 2 -> 3, of which waited for: 0 -> 2; matrix products, arithmetic and copies ran while one was open for 1% -> 1% of each run, Pallas kernels for 48% -> 35%
where the time goes in v4:
time: 968 us; the launch traced here: 961 us
  Pallas kernels  800 us (83%)
  waiting for transfers between devices  103 us (11%)
  other arithmetic  24.7 us (3%)
  local copies, waits for them, and re-layouts  18.6 us (2%)
  between operations  14.5 us (1%)
    pallas_call x2, Pallas kernels, sum_scatter(): pl.pallas_call(kernel, in_specs=[HBM] * 8, out_specs=outs, out_shape=shap...  307 us
    pallas_call x2, Pallas kernels, link_kernel(): pl.pallas_call(kernel, in_specs=[HBM] * (ng + len(parts)), out_specs=[HBM...  190 us
    pallas_call x2, Pallas kernels, project(): call(kernel, (nq + nu,), ins, outs, shapes, scratch, ident=5 if ng else N...  86.4 us
    psum x1, waiting for transfers between devices, body(): total = lax.psum(jnp.concatenate([bias.reshape(-1), vec_sum]), ('dp', 'mp'))  83.4 us
    pallas_call x2, Pallas kernels, back_out(): call(kernel, (D // NB,), [spec((n, C), whole, True), spec((n, U), whole,...  45.1 us
    pallas_call x2, Pallas kernels, adam_layer(): pl.pallas_call(kernel, grid=(steps,), in_specs=ins, out_specs=[at(b) for...  38.5 us
    pallas_call x2, Pallas kernels, back_in(): call(kernel, (nr + nu,), [spec((n, D), lambda j: (0, 0), True), spec((n,...  36.4 us
    pallas_call x2, Pallas kernels, branch_out(): call(kernel, (dp,), [spec((n, R), whole, True), spec((n, U), whole, True)...  32.2 us
  transfers between devices with their start and end apart: 3, of which 2 were waited for; matrix products, arithmetic and copies ran while one was open for 1% of the time, Pallas kernels for 35%

profile of v4, /device:TPU:0, one launch (start us, length us, event | category | flops | bytes accessed | tf_op | source)
XLA Modules:
  0.0 961.1 jit_solution(16133981378644523550)
XLA Ops:
  7.3 0.8 select_reduce_fusion.2
  8.0 0.7 fusion.19
  8.9 0.8 reshape.263
  9.7 0.7 copy.124
  10.5 0.7 copy.125
  11.8 67.6 %gather.1 = (bf16[8,32,128]{2,1,0:T(8,128)(2,1)}, bf16[8,256,1536]{2,1,0:T(8,128)(2,1)}, bf16[8,256,2048]{2,1,0:T(8,128)(2,1)}) custom-call(bf16[32,128]{1,0:T(8,128)(2,1)} %fusion.18.refs_0_, bf16[2,256,1536]{2,1,0:T(8,128)(2,1)} %refs_0_.9, bf16[2,256,2048]{2,1,0:T(8,128)(2,1)} %refs_2_.11), custom_call_target="tpu_custom_call" | custom-call | bytes 14712832 | tf_op jit(solution)/shard_map/gather/pallas_call | solution.py:728
  79.4 0.9 copy.182
  81.5 1.0 add_select_fusion.sc_r
  82.5 4.9 convert_reduce_fusion
  87.5 0.7 squeeze.33.refs_8_
  88.2 0.7 squeeze.29.refs_7_
  89.1 0.7 squeeze.32.refs_4_
  89.8 0.7 squeeze.28.refs_3_
  90.5 1.9 fusion
  92.4 0.7 pad_maximum_fusion.2.refs_1_.refs_5_.refs_3_
  93.1 1.3 maximum_maximum_fusion
  94.4 53.8 %project.2 = (bf16[1024,2048]{1,0:T(8,128)(2,1)}, bf16[1024,2048]{1,0:T(8,128)(2,1)}, bf16[1024,1536]{1,0:T(8,128)(2,1)}, bf16[1024,2048]{1,0:T(8,128)(2,1)}, bf...) custom-call(bf16[1024,2048]{1,0:T(8,128)(2,1)} %refs_2_.9, ...), custom_call_target="tpu_custom_call" | custom-call | flops 15032385536 | bytes 38797312 | tf_op jit(solution)/shard_map/project/pallas_call | solution.py:185
  148.2 6.6 attend.2.c_r.refs_1_
  154.8 16.1 %branch.2.refs_4_ = bf16[1024,2048]{1,0:T(8,128)(2,1)} custom-call(bf16[1024,512]{1,0:T(8,128)(2,1)} %attend.2.c_r.refs_1_, bf16[1024,2048]{1,0:T(8,128)(2,1)} %get-tuple-element.120.a_r.refs_2_, bf16[8,512,256]{2,1,0:T(8,128)(2,1)} %get-tuple-element.121.wd_r, bf16[8,2048,256]{2,1,0:T(8,128)(2,1)} %get-tuple-element.122.wn_r), custom_call_target="tpu_custom_call" | custom-call | flops 10737418240 | bytes 19922944 | tf_op jit(solution)/shard_map/branch/pallas_call | solution.py:268
  170.9 122.5 %sum_gather.1 = (bf16[8,256,1536]{2,1,0:T(8,128)(2,1)}, bf16[8,512,256]{2,1,0:T(8,128)(2,1)}, bf16[8,256,2048]{2,1,0:T(8,128)(2,1)}, bf16[8,2048,256]{2,1,0:T(8,128)(2,1)}, bf16[1024,2048]{1,0:T(8,128)(2,1)}) custom-call(bf16[2,256,1536]{2,1,0:T(8,128)(2,1)} %refs_0_.9, bf16[2,512,256]{2,1,0:T(8,128)(2,1)} %refs_1_.7, bf16[2,256,2048]{2,1,0:T(8,128)(2,1)} %refs_2_.11, ...), custom_call_target="tpu_custom_call" | custom-call | bytes 29360128 | tf_op jit(solution)/shard_map/sum_gather/pallas_call | solution.py:728
  293.4 0.6 pad_maximum_fusion.3.refs_2_.refs_6_.refs_4_
  294.1 32.6 %project.3 = (bf16[1024,2048]{1,0:T(8,128)(2,1)}, bf16[1024,2048]{1,0:T(8,128)(2,1)}, bf16[1024,1536]{1,0:T(8,128)(2,1)}, bf16[1024,2048]{1,0:T(8,128)(2,1)}, bf...) custom-call(bf16[1024,2048]{1,0:T(8,128)(2,1)} %refs_2_.9, bf16[1024,2048]{1,0:T(8,128)(2,1)} %get-tuple-element.123.refs_1_.refs_5_.refs_3_, ...), custom_call_target="tpu_custom_call" | custom-call | flops 15032385536 | bytes 38797312 | tf_op jit(solution)/shard_map/project/pallas_call | solution.py:185
  326.7 6.9 attend.3.c_r.refs_1_
  333.6 16.1 %branch.3 = bf16[1024,2048]{1,0:T(8,128)(2,1)} custom-call(bf16[1024,512]{1,0:T(8,128)(2,1)} %attend.3.c_r.refs_1_, bf16[1024,2048]{1,0:T(8,128)(2,1)} %get-tuple-element.127.a_r.refs_2_, bf16[8,512,256]{2,1,0:T(8,128)(2,1)} %get-tuple-element.128.wd_r, bf16[8,2048,256]{2,1,0:T(8,128)(2,1)} %get-tuple-element.129.wn_r), custom_call_target="tpu_custom_call" | custom-call | flops 10737418240 | bytes 19922944 | tf_op jit(solution)/shard_map/branch/pallas_call | solution.py:268
  349.7 4.8 fusion.26
  354.6 18.2 %back_in.2 = (bf16[1024,512]{1,0:T(8,128)(2,1)}, bf16[1024,2048]{1,0:T(8,128)(2,1)}) custom-call(bf16[1024,2048]{1,0:T(8,128)(2,1)} %get-tuple-element.131.g_r.refs_5_.refs_0_, bf16[1024,2048]{1,0:T(8,128)(2,1)} %get-tuple-element.132.gp_r, bf16[8,512,256]{2,1,0:T(8,128)(2,1)} %get-tuple-element.128.wd_r, bf16[8,2048,256]{2,1,0:T(8,128)(2,1)} %get-tuple-element.129.wn_r), custom_call_target="tpu_custom_call" | custom-call | flops 10737418240 | bytes 24117248 | tf_op jit(solution)/shard_map/back_in/pallas_call | solution.py:300
  372.8 11.5 %attend_back.2.refs_0_.refs_6_ = bf16[1024,1536]{1,0:T(8,128)(2,1)} custom-call(bf16[1024,1536]{1,0:T(8,128)(2,1)} %get-tuple-element.126.q_r.k_r.v_r, bf16[1024,1536]{1,0:T(8,128)(2,1)} %get-tuple-element.126.q_r.k_r.v_r, bf16[1024,1536]{1,0:T(8,128)(2,1)} %get-tuple-element.126.q_r.k_r.v_r, bf16[1024,512]{1,0:T(8,128)(2,1)} %get-tuple-element.133.do_r, ...), custom_call_target="tpu_custom_call" | custom-call | flops 3355443200 | bytes 6291456 | tf_op jit(solution)/shard_map/attend_back/pallas_call | solution.py:251
  384.3 22.9 %back_out.2 = (bf16[1024,2048]{1,0:T(8,128)(2,1)}, f32[4,2048]{1,0:T(4,128)}) custom-call(bf16[1024,1536]{1,0:T(8,128)(2,1)} %attend_back.2.refs_0_.refs_6_, bf16[1024,2048]{1,0:T(8,128)(2,1)} %get-tuple-element.134.refs_1_.refs_7_, bf16[2048,1536]{1,0:T(8,128)(2,1)} %bitcast.95, bf16[2048,2048]{1,0:T(8,128)(2,1)} %bitcast.91, bf16[1024,2048]{1,0:T(8,128)(2,1)} %refs_2_.9, ...), custom_call_target="tpu_custom_call" | custom-call | flops 15032385536 | bytes 34603008 | tf_op jit(solution)/shard_map/back_out/pallas_call | solution.py:336
  407.2 164.5 %sum_scatter.2 = (bf16[1024,2048]{1,0:T(8,128)(2,1)}, bf16[8,512,256]{2,1,0:T(8,128)(2,1)}, bf16[8,2048,256]{2,1,0:T(8,128)(2,1)}, bf16[8,256,1536]{2,1,0:T(8,12...) custom-call(bf16[1024,2048]{1,0:T(8,128)(2,1)} %get-tuple-element.13, ...), custom_call_target="tpu_custom_call" | custom-call | flops 25769803776 | bytes 50331648 | tf_op jit(solution)/shard_map/sum_scatter/pallas_call | solution.py:908
  571.7 19.4 %adam.2 = (f32[2,256,1536]{2,1,0:T(8,128)}, f32[2,256,1536]{2,1,0:T(8,128)}, f32[2,256,1536]{2,1,0:T(8,128)}, f32[2,256,1536]{2,1,0:T(8,128)}, f32[2,512,256]{2,...) custom-call(bf16[2,256,1536]{2,1,0:T(8,128)(2,1)} %refs_0_.9, ...), custom_call_target="tpu_custom_call" | custom-call | flops 31457280 | bytes 47185920 | tf_op jit(solution)/shard_map/adam/pallas_call | solution.py:947
  591.2 15.1 %norm_back.2 = (f32[1024,2048]{1,0:T(8,128)}, bf16[1024,2048]{1,0:T(8,128)(2,1)}, f32[1,2048]{1,0:T(1,128)}) custom-call(bf16[1024,2048]{1,0:T(8,128)(2,1)} %get-tuple-element.131.g_r.refs_5_.refs_0_, bf16[1024,2048]{1,0:T(8,128)(2,1)} %get-tuple-element.142.refs_1_, bf16[1024,2048]{1,0:T(8,128)(2,1)} %refs_2_.9, ...), custom_call_target="tpu_custom_call" | custom-call | flops 20971520 | bytes 33554432 | tf_op jit(solution)/shard_map/norm_back/pallas_call | solution.py:408
  606.2 18.2 %back_in.3 = (bf16[1024,512]{1,0:T(8,128)(2,1)}, bf16[1024,2048]{1,0:T(8,128)(2,1)}) custom-call(bf16[1024,2048]{1,0:T(8,128)(2,1)} %get-tuple-element.143.g_r.refs_5_, bf16[1024,2048]{1,0:T(8,128)(2,1)} %get-tuple-element.144.gp_r, bf16[8,512,256]{2,1,0:T(8,128)(2,1)} %get-tuple-element.121.wd_r, bf16[8,2048,256]{2,1,0:T(8,128)(2,1)} %get-tuple-element.122.wn_r), custom_call_target="tpu_custom_call" | custom-call | flops 10737418240 | bytes 24117248 | tf_op jit(solution)/shard_map/back_in/pallas_call | solution.py:300
  624.5 11.6 %attend_back.3.refs_0_.refs_6_ = bf16[1024,1536]{1,0:T(8,128)(2,1)} custom-call(bf16[1024,1536]{1,0:T(8,128)(2,1)} %get-tuple-element.119.q_r.k_r.v_r, bf16[1024,1536]{1,0:T(8,128)(2,1)} %get-tuple-element.119.q_r.k_r.v_r, bf16[1024,1536]{1,0:T(8,128)(2,1)} %get-tuple-element.119.q_r.k_r.v_r, bf16[1024,512]{1,0:T(8,128)(2,1)} %get-tuple-element.145.do_r, ...), custom_call_target="tpu_custom_call" | custom-call | flops 3355443200 | bytes 6291456 | tf_op jit(solution)/shard_map/attend_back/pallas_call | solution.py:251
  636.1 22.2 %back_out.3 = (bf16[1024,2048]{1,0:T(8,128)(2,1)}, f32[4,2048]{1,0:T(4,128)}) custom-call(bf16[1024,1536]{1,0:T(8,128)(2,1)} %attend_back.3.refs_0_.refs_6_, bf16[1024,2048]{1,0:T(8,128)(2,1)} %get-tuple-element.146.refs_1_.refs_7_, bf16[2048,1536]{1,0:T(8,128)(2,1)} %bitcast.93, bf16[2048,2048]{1,0:T(8,128)(2,1)} %bitcast.89, bf16[1024,2048]{1,0:T(8,128)(2,1)} %refs_2_.9, ...), custom_call_target="tpu_custom_call" | custom-call | flops 15032385536 | bytes 34603008 | tf_op jit(solution)/shard_map/back_out/pallas_call | solution.py:336
  658.3 0.8 pad_maximum_fusion.1
  659.2 19.9 %all-reduce.7.cloned.1.call-done = bf16[512,2048]{1,0:T(8,128)(2,1)} async-done(((bf16[512,2048]{1,0:T(8,128)(2,1)}), bf16[512,2048]{1,0:T(8,128)(2,1)}) %all-reduce.7.cloned.1.call-update) | async-done | bytes 2097168 | tf_op jit(solution)/shard_map/psum | solution.py:1082
  679.1 142.7 %sum_scatter.3 = (bf16[1024,2048]{1,0:T(8,128)(2,1)}, bf16[8,512,256]{2,1,0:T(8,128)(2,1)}, bf16[8,2048,256]{2,1,0:T(8,128)(2,1)}, bf16[8,256,1536]{2,1,0:T(8,12...) custom-call(bf16[1024,2048]{1,0:T(8,128)(2,1)} %get-tuple-element.15, ...), custom_call_target="tpu_custom_call" | custom-call | flops 25769803776 | bytes 50331648 | tf_op jit(solution)/shard_map/sum_scatter/pallas_call | solution.py:908
  821.8 0.7 pad_maximum_fusion.6
  822.5 0.7 pad_maximum_fusion.5
  823.3 0.7 pad_maximum_fusion
  824.1 7.6 select_convert_fusion
  831.6 12.2 %norm_back.3 = f32[1024,2048]{1,0:T(8,128)} custom-call(f32[1024,2048]{1,0:T(8,128)} %get-tuple-element.150.refs_0_, bf16[1024,2048]{1,0:T(8,128)(2,1)} %get-tuple-element.154.refs_1_, bf16[1024,2048]{1,0:T(8,128)(2,1)} %refs_2_.9, f32[6,2048]{1,0:T(8,128)} %pad_maximum_fusion.2.refs_1_.refs_5_.refs_3_, f32[1024,128]{1,0:T(8,128)} %get-tuple-element.147.refs_6_.refs_4_), custom_call_target="tpu_custom_call" | custom-call | flops 20971520 | bytes 33554432 | tf_op jit(solution)/shard_map/norm_back/pallas_call | solution.py:408
  844.0 19.1 %adam.3 = (f32[2,256,1536]{2,1,0:T(8,128)}, f32[2,256,1536]{2,1,0:T(8,128)}, f32[2,256,1536]{2,1,0:T(8,128)}, f32[2,256,1536]{2,1,0:T(8,128)}, f32[2,512,256]{2,...) custom-call(bf16[2,256,1536]{2,1,0:T(8,128)(2,1)} %refs_0_.9, ...), custom_call_target="tpu_custom_call", output_to_operand_aliasing={{0}: (16, {}), {1}: (17, {}), {2}: (18, {}), {3}: (19, {}),... | custom-call | flops 31457280 | bytes 47185920 | tf_op jit(solution)/shard_map/adam/pallas_call | solution.py:947
  863.1 83.4 %all-reduce.9.cloned.1.call-done = f32[53248]{0:T(1024)} async-done(((f32[53248]{0:T(1024)}), f32[53248]{0:T(1024)}) %all-reduce.9.cloned.1.call-update) | async-done | bytes 213008 | tf_op jit(solution)/shard_map/psum | solution.py:1102
  946.5 0.9 slice.105
  947.6 0.9 slice.106
  951.1 0.6 copy.147
  953.6 0.7 subtract_subtract_fusion.1
  (90 shorter events, 7.4 us)
Async XLA Ops:
  7.2 583.9 %all-reduce.5.cloned.1.call-start = ((), (), s32[]{:S(2)}) async-start(), calls=%async_computation | async-start | bytes 4194304 | tf_op jit(solution)/shard_map/psum | solution.py:1067
  8.8 78.6 %copy-start.3 = (pred[1024]{0:T(1024)(128)(4,1)}, pred[1024]{0:T(1024)(128)(4,1)S(1)}, u32[]{:S(2)}) copy-start(pred[1024]{0:T(1024)(128)(4,1)S(1)} %fusion.20) | copy-start | bytes 3076
  354.5 324.6 %all-reduce.7.cloned.1.call-start = ((), (), s32[]{:S(2)}) async-start(), calls=%async_computation.1 | async-start | bytes 4194304 | tf_op jit(solution)/shard_map/psum | solution.py:1082
  591.1 355.3 %all-reduce.9.cloned.1.call-start = ((), (), s32[]{:S(2)}) async-start(), calls=%async_computation.2 | async-start | bytes 425984 | tf_op jit(solution)/shard_map/psum | solution.py:1102
  606.2 18.2 %copy-start = (f32[2048]{0:T(1024)S(1)}, f32[2048]{0:T(1024)}, u32[]{:S(2)}) copy-start(f32[2048]{0:T(1024)} %get-tuple-element.306) | copy-start | bytes 24580
  606.2 18.2 %copy-start.14 = (f32[1,2048]{1,0:T(1,128)S(1)}, f32[1,2048]{1,0:T(1,128)}, u32[]{:S(2)}) copy-start(f32[1,2048]{1,0:T(1,128)} %get-tuple-element.201) | copy-start | bytes 24580
  636.1 22.2 %copy-start.1 = (f32[4,2048]{1,0:T(4,128)S(1)}, f32[4,2048]{1,0:T(4,128)}, u32[]{:S(2)}) copy-start(f32[4,2048]{1,0:T(4,128)} %get-tuple-element.200) | copy-start | bytes 98308
  679.1 142.7 %copy-start.15 = (f32[1,1536]{1,0:T(1,128)S(1)}, f32[1,1536]{1,0:T(1,128)}, u32[]{:S(2)}) copy-start(f32[1,1536]{1,0:T(1,128)} %get-tuple-element.196) | copy-start | bytes 18436
  679.1 143.4 %copy-start.13 = (f32[1,2048]{1,0:T(1,128)S(1)}, f32[1,2048]{1,0:T(1,128)}, u32[]{:S(2)}) copy-start(f32[1,2048]{1,0:T(1,128)} %get-tuple-element.198) | copy-start | bytes 24580
  679.1 145.0 %copy-start.4 = (pred[1024]{0:T(1024)(128)(4,1)S(1)}, pred[1024]{0:T(1024)(128)(4,1)}, u32[]{:S(2)}) copy-start(pred[1024]{0:T(1024)(128)(4,1)} %copy-done.3) | copy-start | bytes 3076
  843.9 104.6 %copy-start.5 = (bf16[2,6,256]{2,0,1:T(2,128)(2,1)S(1)}, bf16[2,6,256]{2,0,1:T(2,128)(2,1)}, u32[]{:S(2)}) copy-start(bf16[2,6,256]{2,0,1:T(2,128)(2,1)} %param.33) | copy-start | bytes 18436
  843.9 104.7 %copy-start.9 = (f32[2,6,256]{2,0,1:T(2,128)S(1)}, f32[2,6,256]{2,0,1:T(2,128)}, u32[]{:S(2)}) copy-start(f32[2,6,256]{2,0,1:T(2,128)} %param.47) | copy-start | bytes 36868
  843.9 104.7 %copy-start.10 = (f32[2,6,256]{2,0,1:T(2,128)S(1)}, f32[2,6,256]{2,0,1:T(2,128)}, u32[]{:S(2)}) copy-start(f32[2,6,256]{2,0,1:T(2,128)} %param.40) | copy-start | bytes 36868
  843.9 107.1 %copy-start.6 = (bf16[2,12,16]{2,0,1:T(2,128)(2,1)S(1)}, bf16[2,12,16]{2,0,1:T(2,128)(2,1)}, u32[]{:S(2)}) copy-start(bf16[2,12,16]{2,0,1:T(2,128)(2,1)} %param.31) | copy-start | bytes 2308
  843.9 107.1 %copy-start.11 = (f32[2,12,16]{2,0,1:T(2,128)S(1)}, f32[2,12,16]{2,0,1:T(2,128)}, u32[]{:S(2)}) copy-start(f32[2,12,16]{2,0,1:T(2,128)} %param.45) | copy-start | bytes 4612
  843.9 107.1 %copy-start.12 = (f32[2,12,16]{2,0,1:T(2,128)S(1)}, f32[2,12,16]{2,0,1:T(2,128)}, u32[]{:S(2)}) copy-start(f32[2,12,16]{2,0,1:T(2,128)} %param.38) | copy-start | bytes 4612
  843.9 109.6 %copy-start.2 = (bf16[2,16,16]{2,1,0:T(8,128)(2,1)S(1)}, bf16[2,16,16]{2,1,0:T(8,128)(2,1)}, u32[]{:S(2)}) copy-start(bf16[2,16,16]{2,1,0:T(8,128)(2,1)} %param.32) | copy-start | bytes 3076
  843.9 109.6 %copy-start.7 = (f32[2,16,16]{2,1,0:T(8,128)S(1)}, f32[2,16,16]{2,1,0:T(8,128)}, u32[]{:S(2)}) copy-start(f32[2,16,16]{2,1,0:T(8,128)} %param.46) | copy-start | bytes 6148
  844.0 109.6 %copy-start.8 = (f32[2,16,16]{2,1,0:T(8,128)S(1)}, f32[2,16,16]{2,1,0:T(8,128)}, u32[]{:S(2)}) copy-start(f32[2,16,16]{2,1,0:T(8,128)} %param.39) | copy-start | bytes 6148
Sparse Core Ops, SparseCore 0:
  354.6 106.8 all-reduce.4
  591.2 87.7 all-reduce.6
  824.2 122.2 all-reduce.8

commit v5 on v4

--- a/solution.py
+++ b/solution.py
@@ -12,6 +12,7 @@
 norm_eps = 1e-05
 masked_score = -1e30
 LAYERS = 2
+BROW = 128
 ADAM_STEP = 10
 beta_one = 0.9
 beta_two = 0.95
@@ -516,10 +517,16 @@
 class LineSum:
     copies = 3
 
-    def __init__(self, spot, part, stage, land, swap, out, send, recv, local, chunks):
-        self.spot, self.part, self.stage, self.land, self.swap, self.out = spot, part, stage, land, swap, out
-        self.send, self.recv, self.local, self.chunks = send, recv, local, chunks
-        self.rows = part.shape[0] // chunks
+    def __init__(self, spot, pairs, stage, land, swap, send, recv, local):
+        self.spot, self.stage, self.land, self.swap = spot, stage, land, swap
+        self.send, self.recv, self.local = send, recv, local
+        self.rows = stage.shape[1]
+        self.parts, self.outs = [], []
+        for part, start, out, rows in pairs:
+            for at in range(0, rows, self.rows):
+                self.parts.append(part.at[pl.ds(start + at, self.rows)])
+                self.outs.append(out.at[pl.ds(at, self.rows)])
+        self.chunks = len(self.parts)
 
     def cut(self, k):
         return pl.ds(k * self.rows, self.rows)
@@ -527,19 +534,19 @@
     def copy(self, k, n):
         s, rows = self.spot, self.cut(k)
         if n == 0:
-            peer, src, dst = s.pair, self.part, self.land
+            peer, src, dst = s.pair, self.parts[k], self.land
         elif n == 1:
-            peer, src, dst = s.across, self.land, self.swap
+            peer, src, dst = s.across, self.land.at[rows], self.swap
         else:
-            peer, src, dst = s.pair, self.swap, self.swap
-        return send_to("mp", peer, src.at[rows], dst.at[rows], self.send.at[k, n], self.recv.at[k, n])
+            peer, src, dst = s.pair, self.swap.at[rows], self.swap
+        return send_to("mp", peer, src, dst.at[rows], self.send.at[k, n], self.recv.at[k, n])
 
     def keep(self, k):
         rows = self.cut(k)
-        return pltpu.make_async_copy(self.swap.at[rows], self.out.at[rows], self.local.at[k])
+        return pltpu.make_async_copy(self.swap.at[rows], self.outs[k], self.local.at[k])
 
     def load(self, k):
-        return pltpu.make_async_copy(self.part.at[self.cut(k)], self.stage.at[k % 2], self.local.at[self.chunks + k % 2])
+        return pltpu.make_async_copy(self.parts[k], self.stage.at[k % 2], self.local.at[self.chunks + k % 2])
 
     def add(self, k, dst, one, two, base):
         step = 32
@@ -717,7 +724,7 @@
         G = Gather(spot, [(a if l is None else a.at[l], b) for a, l, b in zip(src, layers, full)], *take(3))
         if parts:
             stage, land, swap, send, recv, local = take(6)
-            line = LineSum(spot, ins[0], stage, land, swap, totals[0], send, recv, local, chunks)
+            line = LineSum(spot, [(ins[0], 0, totals[0], ins[0].shape[0])], stage, land, swap, send, recv, local)
             plan_sum_gather(G, line)
             line.close()
         else:
@@ -814,7 +821,7 @@
         G.last(k)
 
 
-def sum_scatter(ident, e, lefts, rights, chunks=8):
+def sum_scatter(ident, e, more, first_row, more_rows, lefts, rights, step=128):
     n, D = e.shape
     HBM = pl.BlockSpec(memory_space=pl.ANY)
     VM_ = pl.BlockSpec(memory_space=pltpu.VMEM)
@@ -822,10 +829,11 @@
     w = D // 8
     dims = [(lefts[0].shape[1], w), (lefts[1].shape[1], w), (w, C), (w, U)]
     DMA = pltpu.SemaphoreType.DMA
-    outs = [HBM] + [HBM] * 4 + [VM_] * 4 + [VM_] * 2
-    shapes = [jax.ShapeDtypeStruct(e.shape, BF)] + [jax.ShapeDtypeStruct((8,) + d, BF) for d in dims] + [jax.ShapeDtypeStruct(d, F32) for d in dims]
+    chunks = (n + more_rows) // step
+    outs = [HBM] * 2 + [HBM] * 4 + [VM_] * 4 + [VM_] * 2
+    shapes = [jax.ShapeDtypeStruct(e.shape, BF), jax.ShapeDtypeStruct((more_rows, D), BF)] + [jax.ShapeDtypeStruct((8,) + d, BF) for d in dims] + [jax.ShapeDtypeStruct(d, F32) for d in dims]
     shapes += [jax.ShapeDtypeStruct((1, C), F32), jax.ShapeDtypeStruct((1, U), F32)]
-    scratch = [pltpu.VMEM((2, n // chunks, D), BF), pltpu.VMEM((n, D), BF), pltpu.VMEM((n, D), BF), DMA((chunks, 3)), DMA((chunks, 3)), DMA((chunks + 2,))]
+    scratch = [pltpu.VMEM((2, step, D), BF)] + [pltpu.VMEM((n + more_rows, D), BF)] * 2 + [DMA((chunks, 3)), DMA((chunks, 3)), DMA((chunks + 2,))]
     scratch += [DMA((4, 10)), DMA((4, 10)), DMA((4, 4))]
     for r, c in dims:
         scratch += [pltpu.VMEM((4, r, c), BF), pltpu.VMEM((4, r, c), BF), pltpu.VMEM((2, r // 2, c), BF), pltpu.VMEM((2, r // 2, c), BF),
@@ -837,12 +845,12 @@
     def kernel(*refs):
         refs = list(refs)
         take = lambda k: [refs.pop(0) for _ in range(k)]
-        e_r, left_rs, right_rs = refs.pop(0), take(4), take(3)
-        total, grads, owned, sum_rs = refs.pop(0), take(4), take(4), take(2)
+        (e_r, more_r), left_rs, right_rs = take(2), take(4), take(3)
+        (total, more_total), grads, owned, sum_rs = take(2), take(4), take(4), take(2)
         stage, land, swap, send, recv, local = take(6)
         spot = Spot()
         spot.meet(True)
-        line = LineSum(spot, e_r, stage, land, swap, total, send, recv, local, chunks)
+        line = LineSum(spot, [(e_r, 0, total, n), (more_r, first_row, more_total, more_rows)], stage, land, swap, send, recv, local)
         send, recv, local = take(3)
         bufs = [take(6) for _ in range(4)]
         S = Scatter(spot, list(zip(grads, owned)), *[[b[i] for b in bufs] for i in range(6)], send, recv, local)
@@ -850,67 +858,114 @@
         W = Products(left_rs, right_rs, grads, (wide_r, narrow_r), lbuf, obuf, rsem, lsem, osem)
         W.right(0, 0).start()
         W.right(1, 1).start()
+        half = left_rs[1].shape[1] // 512
+        state = [2, 0]
+
+        def slot():
+            send_at, add_at = state
+            if add_at <= chunks:
+                line.add_step(add_at)
+            if send_at < chunks + 4:
+                line.send_step(send_at)
+            state[:] = send_at + 1, add_at + 1
+
         line.send_step(0)
         line.send_step(1)
         W.right(0, 0).wait()
         W.run(0, 0, 0, left_rs[0].shape[1] // 256)
         S.first(0)
-        half = left_rs[1].shape[1] // 512
         W.run(1, 0, 0, half)
-        line.add_step(0)
-        line.send_step(2)
+        slot()
         S.second(0)
         W.run(1, 0, half, 2 * half)
         S.first(1)
         W.right(2, 0).start()
         W.right(1, 1).wait()
         W.run(2, 1, 0, 2)
-        line.add_step(1)
-        line.send_step(3)
+        slot()
         W.run(2, 1, 2, 8)
         S.first(2)
-        W.sums(1, sum_rs[0])
-        line.add_step(2)
-        line.send_step(4)
         S.second(1)
-        S.third(0)
+        slot()
         W.right(2, 0).wait()
         W.run(3, 0, 0, 4)
-        line.add_step(3)
-        line.send_step(5)
+        S.third(0)
+        slot()
         S.second(2)
         W.run(3, 0, 4, 8)
         S.first(3)
-        line.add_step(4)
-        line.send_step(6)
+        W.sums(1, sum_rs[0])
+        slot()
+        S.third(1)
+        S.second(3)
+        slot()
         W.sums(0, sum_rs[1])
-        S.third(1)
-        line.add_step(5)
-        line.send_step(7)
-        S.second(3)
-        line.add_step(6)
-        line.send_step(8)
+        S.last(0)
+        slot()
         S.third(2)
-        line.add_step(7)
-        line.send_step(9)
-        line.add_step(8)
-        line.send_step(10)
+        S.last(1)
+        slot()
+        slot()
         S.third(3)
-        S.last(0)
-        S.last(1)
-        line.send_step(11)
         S.last(2)
+        while state[0] < chunks + 4:
+            slot()
         S.last(3)
         line.close()
         S.close()
 
     flops = 2 * n * D * (lefts[0].shape[1] + lefts[1].shape[1] + C + U)
     got = pl.pallas_call(
-        kernel, in_specs=[HBM] * 8, out_specs=outs, out_shape=shapes, scratch_shapes=scratch,
+        kernel, in_specs=[HBM] * 9, out_specs=outs, out_shape=shapes, scratch_shapes=scratch,
         compiler_params=pltpu.CompilerParams(vmem_limit_bytes=VM2, collective_id=ident, has_side_effects=True),
-        cost_estimate=pl.CostEstimate(flops=flops, bytes_accessed=2 * n * D * 12, transcendentals=0), name="sum_scatter")(e, *lefts, *rights)
-    gd, gn, gq, gu = got[5:9]
-    return got[0], (gq, gd, gu, gn), got[9], got[10]
+        cost_estimate=pl.CostEstimate(flops=flops, bytes_accessed=2 * n * D * 12, transcendentals=0), name="sum_scatter")(e, more, *lefts, *rights)
+    gd, gn, gq, gu = got[6:10]
+    return got[0], got[1], (gq, gd, gu, gn), got[10], got[11]
+
+
+def small_sum(pieces, shared):
+    ndp, r, _ = pieces.shape
+    nmp = lax.axis_size("mp")
+
+    def kernel(x_r, o_r, land, line, send, recv, send2, recv2):
+        i, z = lax.axis_index("dp"), lax.axis_index("mp")
+        barrier = pltpu.get_barrier_semaphore()
+        for s in range(1, ndp):
+            pl.semaphore_signal(barrier, inc=1, device_id={"dp": lax.rem(i + s, ndp)}, device_id_type=MESH)
+        for s in range(1, nmp):
+            pl.semaphore_signal(barrier, inc=1, device_id={"mp": lax.rem(z + s, nmp)}, device_id_type=MESH)
+        pl.semaphore_wait(barrier, ndp + nmp - 2)
+        first = [send_to("dp", lax.rem(i + s, ndp), x_r.at[lax.rem(i + s, ndp)], land.at[i], send.at[s], recv.at[s]) for s in range(1, ndp)]
+        for copy in first:
+            copy.start()
+        land[pl.ds(i, 1)] = x_r[pl.ds(i, 1)]
+        for s in range(1, ndp):
+            there = land.at[lax.rem(i - s + ndp, ndp)]
+            send_to("dp", i, there, there, send.at[s], recv.at[s]).wait_recv()
+        acc = land[0]
+        for j in range(1, ndp):
+            acc = acc + land[j]
+        o_r[...] = acc
+        line[pl.ds(z, 1)] = acc[None, :shared]
+        second = [send_to("mp", lax.rem(z + s, nmp), line.at[z], line.at[z], send2.at[s], recv2.at[s]) for s in range(1, nmp)]
+        for copy in second:
+            copy.start()
+        for s in range(1, nmp):
+            there = line.at[lax.rem(z - s + nmp, nmp)]
+            send_to("mp", z, there, there, send2.at[s], recv2.at[s]).wait_recv()
+        acc = line[0]
+        for j in range(1, nmp):
+            acc = acc + line[j]
+        o_r[:shared] = acc
+        for copy in first + second:
+            copy.wait_send()
+
+    VM_ = pl.BlockSpec(memory_space=pltpu.VMEM)
+    DMA = pltpu.SemaphoreType.DMA
+    return pl.pallas_call(
+        kernel, in_specs=[VM_], out_specs=VM_, out_shape=jax.ShapeDtypeStruct((r, 128), F32),
+        scratch_shapes=[pltpu.VMEM(pieces.shape, F32), pltpu.VMEM((nmp, shared, 128), F32), DMA((ndp,)), DMA((ndp,)), DMA((nmp,)), DMA((nmp,))],
+        compiler_params=pltpu.CompilerParams(vmem_limit_bytes=VM // 4, collective_id=6, has_side_effects=True), name="small_sum")(pieces)
 
 
 def adam_update(weight, grad, first, second):
@@ -979,13 +1034,17 @@
         gq, gd, gu, gn = grads
         return cut(gq), cut(gd)[0], cut(gu), cut(gn)[0]
 
+    def small(self, pieces, shared):
+        total = lax.psum(pieces, "dp")[lax.axis_index("dp")]
+        return jnp.concatenate([lax.psum(total[:shared], "mp"), total[shared:]])
+
     def begin(self, shards, flat):
         return self.weights(shards, 0), lax.all_gather(flat, "dp", axis=0, tiled=False), None
 
     def middle(self, branch, shards):
         return self.share(branch), self.weights(shards, 1)
 
-    def turn(self, e, lefts, rights, ident):
+    def turn(self, e, more, first_row, more_rows, lefts, rights, ident):
         ctx, act, h1, h2 = lefts
         gr, dmix, df = rights
         w = gr.shape[1] // lax.axis_size("dp")
@@ -993,7 +1052,8 @@
         gn, _ = weight_grad(act, gr, w=w)
         gq, qsum = weight_grad(h1, dmix)
         gu, usum = weight_grad(h2, df)
-        return self.share(e), self.owned((gq, gd, gu, gn)), qsum, usum
+        more = self.share(more[first_row:first_row + more_rows])
+        return self.share(e), more, self.owned((gq, gd, gu, gn)), qsum, usum
 
 
 class ChipLinks:
@@ -1010,8 +1070,11 @@
         got = link_kernel("sum_gather", 2, shards, [1] * 4, branch)
         return got[4], self.full(got[:4])
 
-    def turn(self, e, lefts, rights, ident):
-        return sum_scatter(ident, e, lefts, rights)
+    def turn(self, e, more, first_row, more_rows, lefts, rights, ident):
+        return sum_scatter(ident, e, more, first_row, more_rows, lefts, rights)
+
+    def small(self, pieces, shared):
+        return small_sum(pieces, shared)
 
 
 def flatten_small(parts):
@@ -1063,9 +1126,9 @@
             gout = gr = jnp.where(live, cotangent, 0).astype(BF)
             sums = jnp.sum(gout.astype(F32), axis=0, keepdims=True)
             branch, gr = lax.optimization_barrier((branch, gr))
-            half = rows // 2
-            tops, bottom = lax.psum(branch[:half], "mp"), branch[half:]
-
+            branch_sum = [None] * 4
+            quarter = rows // 4
+            branch_sum[0] = lax.psum(branch[:quarter], "mp")
     big, little = [None] * LAYERS, [None] * LAYERS
     for layer in reversed(range(LAYERS)):
         wq, wd, wu, wn = full[layer]
@@ -1074,18 +1137,19 @@
         dmix = attend_backward(mixed, dctx, seg_col, seg_row, cos, sin)
         e, norm_sums = back_out(dmix, df, wq, wu, tokens_in, extra, held[layer], stats)
         if layer == 0:
-            bottom, e = lax.optimization_barrier((bottom, e))
-        e, big[layer], qsum, usum = links.turn(e, (ctx, act, h1, h2), (gr, dmix, df), 3 + layer)
+            branch_sum[2], e = lax.optimization_barrier((branch_sum[2], e))
+        at = 1 if layer else 3
+        e, branch_sum[at], big[layer], qsum, usum = links.turn(e, branch, at * quarter, quarter, (ctx, act, h1, h2), (gr, dmix, df), 3 + layer)
         little[layer] = (qsum, usum, norm_sums, sums)
         if layer:
-            tops, e, bottom = lax.optimization_barrier((tops, e, bottom))
-            bottom = lax.psum(bottom, "mp")
+            branch_sum[0], e, third = lax.optimization_barrier((branch_sum[0], e, branch[2 * quarter:3 * quarter]))
+            branch_sum[2] = lax.psum(third, "mp")
         made = norm_back(gout, e, tokens_in, extra, held[layer], stats, layer == 0)
         if layer:
             gout, gr, sums = made
         else:
             input_grad = made[0]
-    branch = jnp.concatenate([tops, bottom])
+    branch = jnp.concatenate(branch_sum)
     x_last = tokens_in.astype(F32) + kept[1][-1].astype(F32) + vecs[0, 4] + vecs[0, 5] + branch.astype(F32) + vecs[1, 4] + vecs[1, 5]
     output = jnp.where(live, x_last, 0.0).astype(BF)
 
@@ -1093,23 +1157,27 @@
     for layer in reversed(range(LAYERS)):
         done = adam_layer(layer, weights, big[layer], firsts, seconds, done)
 
-    z, line = lax.axis_index("mp"), lax.axis_size("mp")
-    bias = jnp.concatenate([jnp.stack([t[i] for t in little]).reshape(-1) for i in (0, 1)])
-    bias = jnp.where(jnp.arange(line)[:, None] == z, bias[None, :], 0.0)
-    norm_sums = jnp.stack([t[2] for t in little])
-    out_sums = jnp.where(z == 0, jnp.stack([t[3] for t in little]), 0.0)
-    vec_sum = jnp.concatenate([norm_sums, out_sums, out_sums], axis=1).reshape(-1)
-    total = lax.psum(jnp.concatenate([bias.reshape(-1), vec_sum]), ("dp", "mp"))
-    bias = lax.dynamic_slice_in_dim(total[:bias.size].reshape(bias.shape), z, 1, 0)[0]
-    total = jnp.concatenate([bias, total[-vec_sum.size:]])
-    me = lax.axis_index("dp")
-    small_out, at = [], 0
-    for p, first, second in zip(small, small_firsts, small_seconds):
-        width = p.shape[2]
-        wide = p.shape[:2] + (lax.axis_size("dp") * width,)
-        size = wide[0] * wide[1] * wide[2]
-        g = lax.dynamic_slice_in_dim(total[at:at + size].reshape(wide), me * width, width, 2)
-        at += size
+    ndp = lax.axis_size("dp")
+
+    def pieces(v, width):
+        v = v.reshape(-1, ndp, width // ndp)
+        return jnp.moveaxis(v, 1, 0).reshape(ndp, -1)
+
+    norms = jnp.concatenate([pieces(t[2], D) for t in little], axis=1)
+    rest = [pieces(t[i], BROW) for i in (0, 1) for t in little] + [pieces(t[3], D) for t in little]
+    rest = jnp.concatenate(rest, axis=1)
+    shared, count = norms.shape[1] // 128, rest.shape[1]
+    rest = jnp.pad(rest, ((0, 0), (0, -count % 1024)))
+    total = links.small(jnp.concatenate([norms, rest], axis=1).reshape(ndp, -1, 128), shared)
+    norms, rest = total[:shared].reshape(LAYERS, 4, -1), total[shared:].reshape(-1)
+    small_grads, at = [], 0
+    for p in small[:2]:
+        small_grads.append(rest[at:at + p.size].reshape(p.shape))
+        at += p.size
+    tops_sum = rest[at:count].reshape(LAYERS, 1, -1)
+    small_grads.append(jnp.concatenate([norms, tops_sum, tops_sum], axis=1))
+    small_out = []
+    for p, g, first, second in zip(small, small_grads, small_firsts, small_seconds):
         small_out += adam_update(p.astype(F32), g, first, second)
     return (output, input_grad, *done, *small_out)
 

time: 968 us -> 872 us (0.901)
  waiting for transfers between devices: 103 us -> 0.08 us
    psum x3 -> x2, waiting for transfers between devices: 103 us -> 0.04 us  [the longest x1 0.02 us: body(): branch_sum[0] = lax.psum(branch[:quarter], 'mp')]
    pallas_call x2 -> x3, Pallas kernels: 307 us -> 307 us  [the longest x2 298 us: sum_scatter(): pl.pallas_call(kernel, in_specs=[HBM] * 9, out_specs=outs, out_shape=shap...]
  transfers between devices with their start and end apart: 3 -> 2, of which waited for: 2 -> 0; matrix products, arithmetic and copies ran while one was open for 1% -> 1% of each run, Pallas kernels for 35% -> 34%
where the time goes in v5:
time: 872 us; the launch traced here: 860 us
  Pallas kernels  799 us (92%)
  other arithmetic  31 us (4%)
  between operations  14.9 us (2%)
  local copies, waits for them, and re-layouts  14.8 us (2%)
    pallas_call x2, Pallas kernels, sum_scatter(): pl.pallas_call(kernel, in_specs=[HBM] * 9, out_specs=outs, out_shape=shap...  298 us
    pallas_call x2, Pallas kernels, link_kernel(): pl.pallas_call(kernel, in_specs=[HBM] * (ng + len(parts)), out_specs=[HBM...  190 us
    pallas_call x2, Pallas kernels, project(): call(kernel, (nq + nu,), ins, outs, shapes, scratch, ident=5 if ng else N...  86.5 us
    pallas_call x2, Pallas kernels, back_out(): call(kernel, (D // NB,), [spec((n, C), whole, True), spec((n, U), whole,...  45.2 us
    pallas_call x2, Pallas kernels, adam_layer(): pl.pallas_call(kernel, grid=(steps,), in_specs=ins, out_specs=[at(b) for...  38.3 us
    pallas_call x2, Pallas kernels, back_in(): call(kernel, (nr + nu,), [spec((n, D), lambda j: (0, 0), True), spec((n,...  36.5 us
    pallas_call x2, Pallas kernels, branch_out(): call(kernel, (dp,), [spec((n, R), whole, True), spec((n, U), whole, True)...  32.2 us
    pallas_call x2, Pallas kernels, norm_back(): call(kernel, (n // RB,), ins, outs, shapes, flops=10 * n * D, nbytes=16 *...  27.3 us
  transfers between devices with their start and end apart: 2, of which 0 were waited for; matrix products, arithmetic and copies ran while one was open for 1% of the time, Pallas kernels for 34%

profile of v5, /device:TPU:0, one launch (start us, length us, event | category | flops | bytes accessed | tf_op | source)
XLA Modules:
  0.0 860.2 jit_solution(5419824327776838677)
XLA Ops:
  7.3 0.8 select_reduce_fusion.2
  8.0 0.7 fusion.19
  8.9 0.8 reshape.249
  9.7 0.7 copy.129
  10.5 0.7 copy.130
  11.8 67.6 %gather.1 = (bf16[8,32,128]{2,1,0:T(8,128)(2,1)}, bf16[8,256,1536]{2,1,0:T(8,128)(2,1)}, bf16[8,256,2048]{2,1,0:T(8,128)(2,1)}) custom-call(bf16[32,128]{1,0:T(8,128)(2,1)} %fusion.18.refs_0_, bf16[2,256,1536]{2,1,0:T(8,128)(2,1)} %refs_0_.9, bf16[2,256,2048]{2,1,0:T(8,128)(2,1)} %refs_2_.11), custom_call_target="tpu_custom_call" | custom-call | bytes 14712832 | tf_op jit(solution)/shard_map/gather/pallas_call | solution.py:735
  79.4 0.9 copy.185
  81.5 1.0 add_select_fusion.sc_r
  82.5 4.3 convert_reduce_fusion
  86.9 0.7 squeeze.32.refs_8_
  87.6 0.7 squeeze.28.refs_7_
  88.5 0.7 squeeze.31.refs_4_
  89.2 0.7 squeeze.27.refs_3_
  89.9 1.9 fusion
  91.8 0.6 pad_maximum_fusion.refs_1_.refs_5_.refs_3_
  92.5 1.3 maximum_maximum_fusion
  93.8 53.9 %project.2 = (bf16[1024,2048]{1,0:T(8,128)(2,1)}, bf16[1024,2048]{1,0:T(8,128)(2,1)}, bf16[1024,1536]{1,0:T(8,128)(2,1)}, bf16[1024,2048]{1,0:T(8,128)(2,1)}, bf...) custom-call(bf16[1024,2048]{1,0:T(8,128)(2,1)} %refs_2_.9, ...), custom_call_target="tpu_custom_call" | custom-call | flops 15032385536 | bytes 38797312 | tf_op jit(solution)/shard_map/project/pallas_call | solution.py:186
  147.6 6.6 attend.2.c_r.refs_2_
  154.2 16.1 %branch.2.refs_4_ = bf16[1024,2048]{1,0:T(8,128)(2,1)} custom-call(bf16[1024,512]{1,0:T(8,128)(2,1)} %attend.2.c_r.refs_2_, bf16[1024,2048]{1,0:T(8,128)(2,1)} %get-tuple-element.122.a_r.refs_3_, bf16[8,512,256]{2,1,0:T(8,128)(2,1)} %get-tuple-element.123.wd_r, bf16[8,2048,256]{2,1,0:T(8,128)(2,1)} %get-tuple-element.124.wn_r), custom_call_target="tpu_custom_call" | custom-call | flops 10737418240 | bytes 19922944 | tf_op jit(solution)/shard_map/branch/pallas_call | solution.py:269
  170.3 122.8 %sum_gather.1 = (bf16[8,256,1536]{2,1,0:T(8,128)(2,1)}, bf16[8,512,256]{2,1,0:T(8,128)(2,1)}, bf16[8,256,2048]{2,1,0:T(8,128)(2,1)}, bf16[8,2048,256]{2,1,0:T(8,128)(2,1)}, bf16[1024,2048]{1,0:T(8,128)(2,1)}) custom-call(bf16[2,256,1536]{2,1,0:T(8,128)(2,1)} %refs_0_.9, bf16[2,512,256]{2,1,0:T(8,128)(2,1)} %refs_1_.7, bf16[2,256,2048]{2,1,0:T(8,128)(2,1)} %refs_2_.11, ...), custom_call_target="tpu_custom_call" | custom-call | bytes 29360128 | tf_op jit(solution)/shard_map/sum_gather/pallas_call | solution.py:735
  293.1 0.6 pad_maximum_fusion.1.refs_2_.refs_6_.refs_4_
  293.7 32.6 %project.3 = (bf16[1024,2048]{1,0:T(8,128)(2,1)}, bf16[1024,2048]{1,0:T(8,128)(2,1)}, bf16[1024,1536]{1,0:T(8,128)(2,1)}, bf16[1024,2048]{1,0:T(8,128)(2,1)}, bf...) custom-call(bf16[1024,2048]{1,0:T(8,128)(2,1)} %refs_2_.9, bf16[1024,2048]{1,0:T(8,128)(2,1)} %get-tuple-element.125.refs_1_.refs_5_.refs_3_, ...), custom_call_target="tpu_custom_call" | custom-call | flops 15032385536 | bytes 38797312 | tf_op jit(solution)/shard_map/project/pallas_call | solution.py:186
  326.3 6.7 attend.3.c_r.refs_2_
  333.0 16.1 %branch.3.refs_1_ = bf16[1024,2048]{1,0:T(8,128)(2,1)} custom-call(bf16[1024,512]{1,0:T(8,128)(2,1)} %attend.3.c_r.refs_2_, bf16[1024,2048]{1,0:T(8,128)(2,1)} %get-tuple-element.129.a_r.refs_3_, bf16[8,512,256]{2,1,0:T(8,128)(2,1)} %get-tuple-element.130.wd_r, bf16[8,2048,256]{2,1,0:T(8,128)(2,1)} %get-tuple-element.131.wn_r), custom_call_target="tpu_custom_call" | custom-call | flops 10737418240 | bytes 19922944 | tf_op jit(solution)/shard_map/branch/pallas_call | solution.py:269
  349.1 3.2 fusion.25
  352.3 18.2 %back_in.2 = (bf16[1024,512]{1,0:T(8,128)(2,1)}, bf16[1024,2048]{1,0:T(8,128)(2,1)}) custom-call(bf16[1024,2048]{1,0:T(8,128)(2,1)} %get-tuple-element.133.g_r.refs_6_.refs_0_, bf16[1024,2048]{1,0:T(8,128)(2,1)} %get-tuple-element.134.gp_r, bf16[8,512,256]{2,1,0:T(8,128)(2,1)} %get-tuple-element.130.wd_r, bf16[8,2048,256]{2,1,0:T(8,128)(2,1)} %get-tuple-element.131.wn_r), custom_call_target="tpu_custom_call" | custom-call | flops 10737418240 | bytes 24117248 | tf_op jit(solution)/shard_map/back_in/pallas_call | solution.py:301
  370.6 11.5 %attend_back.2.refs_0_.refs_7_ = bf16[1024,1536]{1,0:T(8,128)(2,1)} custom-call(bf16[1024,1536]{1,0:T(8,128)(2,1)} %get-tuple-element.128.q_r.k_r.v_r, bf16[1024,1536]{1,0:T(8,128)(2,1)} %get-tuple-element.128.q_r.k_r.v_r, bf16[1024,1536]{1,0:T(8,128)(2,1)} %get-tuple-element.128.q_r.k_r.v_r, bf16[1024,512]{1,0:T(8,128)(2,1)} %get-tuple-element.135.do_r, ...), custom_call_target="tpu_custom_call" | custom-call | flops 3355443200 | bytes 6291456 | tf_op jit(solution)/shard_map/attend_back/pallas_call | solution.py:252
  382.0 23.0 %back_out.2 = (bf16[1024,2048]{1,0:T(8,128)(2,1)}, f32[4,2048]{1,0:T(4,128)}) custom-call(bf16[1024,1536]{1,0:T(8,128)(2,1)} %attend_back.2.refs_0_.refs_7_, bf16[1024,2048]{1,0:T(8,128)(2,1)} %get-tuple-element.136.refs_1_.refs_8_, bf16[2048,1536]{1,0:T(8,128)(2,1)} %bitcast.105, bf16[2048,2048]{1,0:T(8,128)(2,1)} %bitcast.101, bf16[1024,2048]{1,0:T(8,128)(2,1)} %refs_2_.9, ...), custom_call_target="tpu_custom_call" | custom-call | flops 15032385536 | bytes 34603008 | tf_op jit(solution)/shard_map/back_out/pallas_call | solution.py:337
  405.0 149.6 %sum_scatter.2 = (bf16[1024,2048]{1,0:T(8,128)(2,1)}, bf16[256,2048]{1,0:T(8,128)(2,1)}, bf16[8,512,256]{2,1,0:T(8,128)(2,1)}, bf16[8,2048,256]{2,1,0:T(8,128)(2...) custom-call(bf16[1024,2048]{1,0:T(8,128)(2,1)} %get-tuple-element.13, ...), custom_call_target="tpu_custom_call" | custom-call | flops 25769803776 | bytes 50331648 | tf_op jit(solution)/shard_map/sum_scatter/pallas_call | solution.py:918
  554.7 0.7 reduce.1
  556.1 1.4 reduce.12
  557.7 19.4 %adam.2 = (f32[2,256,1536]{2,1,0:T(8,128)}, f32[2,256,1536]{2,1,0:T(8,128)}, f32[2,256,1536]{2,1,0:T(8,128)}, f32[2,256,1536]{2,1,0:T(8,128)}, f32[2,512,256]{2,...) custom-call(bf16[2,256,1536]{2,1,0:T(8,128)(2,1)} %refs_0_.9, ...), custom_call_target="tpu_custom_call" | custom-call | flops 31457280 | bytes 47185920 | tf_op jit(solution)/shard_map/adam/pallas_call | solution.py:1002
  577.1 14.9 %norm_back.2 = (f32[1024,2048]{1,0:T(8,128)}, bf16[1024,2048]{1,0:T(8,128)(2,1)}, f32[1,2048]{1,0:T(1,128)}) custom-call(bf16[1024,2048]{1,0:T(8,128)(2,1)} %get-tuple-element.133.g_r.refs_6_.refs_0_, bf16[1024,2048]{1,0:T(8,128)(2,1)} %get-tuple-element.145.refs_1_, bf16[1024,2048]{1,0:T(8,128)(2,1)} %refs_2_.9, ...), custom_call_target="tpu_custom_call" | custom-call | flops 20971520 | bytes 33554432 | tf_op jit(solution)/shard_map/norm_back/pallas_call | solution.py:409
  592.0 18.3 %back_in.3 = (bf16[1024,512]{1,0:T(8,128)(2,1)}, bf16[1024,2048]{1,0:T(8,128)(2,1)}) custom-call(bf16[1024,2048]{1,0:T(8,128)(2,1)} %get-tuple-element.146.g_r.refs_6_, bf16[1024,2048]{1,0:T(8,128)(2,1)} %get-tuple-element.147.gp_r, bf16[8,512,256]{2,1,0:T(8,128)(2,1)} %get-tuple-element.123.wd_r, bf16[8,2048,256]{2,1,0:T(8,128)(2,1)} %get-tuple-element.124.wn_r), custom_call_target="tpu_custom_call" | custom-call | flops 10737418240 | bytes 24117248 | tf_op jit(solution)/shard_map/back_in/pallas_call | solution.py:301
  610.3 11.5 %attend_back.3.refs_0_.refs_7_ = bf16[1024,1536]{1,0:T(8,128)(2,1)} custom-call(bf16[1024,1536]{1,0:T(8,128)(2,1)} %get-tuple-element.121.q_r.k_r.v_r, bf16[1024,1536]{1,0:T(8,128)(2,1)} %get-tuple-element.121.q_r.k_r.v_r, bf16[1024,1536]{1,0:T(8,128)(2,1)} %get-tuple-element.121.q_r.k_r.v_r, bf16[1024,512]{1,0:T(8,128)(2,1)} %get-tuple-element.148.do_r, ...), custom_call_target="tpu_custom_call" | custom-call | flops 3355443200 | bytes 6291456 | tf_op jit(solution)/shard_map/attend_back/pallas_call | solution.py:252
  621.8 22.2 %back_out.3 = (bf16[1024,2048]{1,0:T(8,128)(2,1)}, f32[4,2048]{1,0:T(4,128)}) custom-call(bf16[1024,1536]{1,0:T(8,128)(2,1)} %attend_back.3.refs_0_.refs_7_, bf16[1024,2048]{1,0:T(8,128)(2,1)} %get-tuple-element.149.refs_1_.refs_8_, bf16[2048,1536]{1,0:T(8,128)(2,1)} %bitcast.103, bf16[2048,2048]{1,0:T(8,128)(2,1)} %bitcast.99, bf16[1024,2048]{1,0:T(8,128)(2,1)} %refs_2_.9, ...), custom_call_target="tpu_custom_call" | custom-call | flops 15032385536 | bytes 34603008 | tf_op jit(solution)/shard_map/back_out/pallas_call | solution.py:337
  644.0 0.8 copy.189
  644.8 0.7 reduce.13
  645.5 148.1 %sum_scatter.3 = (bf16[1024,2048]{1,0:T(8,128)(2,1)}, bf16[256,2048]{1,0:T(8,128)(2,1)}, bf16[8,512,256]{2,1,0:T(8,128)(2,1)}, bf16[8,2048,256]{2,1,0:T(8,128)(2...) custom-call(bf16[1024,2048]{1,0:T(8,128)(2,1)} %get-tuple-element.15, ...), custom_call_target="tpu_custom_call" | custom-call | flops 25769803776 | bytes 50331648 | tf_op jit(solution)/shard_map/sum_scatter/pallas_call | solution.py:918
  793.7 1.4 reduce.11
  795.0 0.7 reduce
  796.3 9.1 %small_sum.1 = f32[32,128]{1,0:T(8,128)S(1)} custom-call(f32[8,32,128]{2,1,0:T(8,128)S(1)} %bitcast.76), custom_call_target="tpu_custom_call" | custom-call | tf_op jit(solution)/shard_map/small_sum/pallas_call | solution.py:965
  805.5 0.6 copy.151
  808.2 12.4 %norm_back.3 = f32[1024,2048]{1,0:T(8,128)} custom-call(f32[1024,2048]{1,0:T(8,128)} %get-tuple-element.157.refs_0_, bf16[1024,2048]{1,0:T(8,128)(2,1)} %get-tuple-element.158.refs_1_, bf16[1024,2048]{1,0:T(8,128)(2,1)} %refs_2_.9, f32[6,2048]{1,0:T(8,128)} %pad_maximum_fusion.refs_1_.refs_5_.refs_3_, f32[1024,128]{1,0:T(8,128)} %get-tuple-element.150.refs_6_.refs_4_), custom_call_target="tpu_custom_call" | custom-call | flops 20971520 | bytes 33554432 | tf_op jit(solution)/shard_map/norm_back/pallas_call | solution.py:409
  820.6 0.7 subtract_subtract_fusion.2
  821.3 0.6 subtract_subtract_fusion
  821.9 12.3 %select_convert_fusion = bf16[1024,2048]{1,0:T(8,128)(2,1)} fusion(bf16[1024,2048]{1,0:T(8,128)(2,1)} %get-tuple-element.125.refs_1_.refs_5_.refs_3_, bf16[1024,2048]{1,0:T(8,128)(2,1)} %refs_2_.9, bf16[256,2048]{1,0:T(8,128)(2,1)} %get-tuple-element.156, bf16[256,2048]{1,0:T(8,128)(2,1)S(1)} %copy-done.2, bf16[256,2048]{1,0:T(8,128)(2,1)S(1)} %copy-done.1, ...), kind=kLoop, calls=%fused_computation.1 | loop fusion | flops 37748736 | bytes 16811008 | tf_op jit(solution)/shard_map/convert_element_type | solution.py:1154
  834.2 19.0 %adam.3 = (f32[2,256,1536]{2,1,0:T(8,128)}, f32[2,256,1536]{2,1,0:T(8,128)}, f32[2,256,1536]{2,1,0:T(8,128)}, f32[2,256,1536]{2,1,0:T(8,128)}, f32[2,512,256]{2,...) custom-call(bf16[2,256,1536]{2,1,0:T(8,128)(2,1)} %refs_0_.9, ...), custom_call_target="tpu_custom_call", output_to_operand_aliasing={{0}: (16, {}), {1}: (17, {}), {2}: (18, {}), {3}: (19, {}),... | custom-call | flops 31457280 | bytes 47185920 | tf_op jit(solution)/shard_map/adam/pallas_call | solution.py:1002
  (106 shorter events, 6.1 us)
Async XLA Ops:
  7.2 569.9 %all-reduce.5.cloned.1.call-start = ((), (), s32[]{:S(2)}) async-start(), calls=%async_computation | async-start | bytes 2097152 | tf_op jit(solution)/shard_map/psum | solution.py:1131
  8.8 78.0 %copy-start.7 = (pred[1024]{0:T(1024)(128)(4,1)}, pred[1024]{0:T(1024)(128)(4,1)S(1)}, u32[]{:S(2)}) copy-start(pred[1024]{0:T(1024)(128)(4,1)S(1)} %fusion.20) | copy-start | bytes 3076
  352.3 293.2 %all-reduce.7.cloned.1.call-start = ((), (), s32[]{:S(2)}) async-start(), calls=%async_computation.1 | async-start | bytes 2097152 | tf_op jit(solution)/shard_map/psum | solution.py:1146
  405.0 149.7 %copy-start.5 = (f32[4,2048]{1,0:T(4,128)S(1)}, f32[4,2048]{1,0:T(4,128)}, u32[]{:S(2)}) copy-start(f32[4,2048]{1,0:T(4,128)} %get-tuple-element.200) | copy-start | bytes 98308
  621.8 23.0 %copy-start.17 = (f32[1,2048]{1,0:T(1,128)S(1)}, f32[1,2048]{1,0:T(1,128)}, u32[]{:S(2)}) copy-start(f32[1,2048]{1,0:T(1,128)} %get-tuple-element.205) | copy-start | bytes 24580
  645.5 160.7 %copy-start.9 = (bf16[2,12,16]{2,0,1:T(2,128)(2,1)S(1)}, bf16[2,12,16]{2,0,1:T(2,128)(2,1)}, u32[]{:S(2)}) copy-start(bf16[2,12,16]{2,0,1:T(2,128)(2,1)} %param.31) | copy-start | bytes 2308
  645.5 160.7 %copy-start.13 = (f32[2,12,16]{2,0,1:T(2,128)S(1)}, f32[2,12,16]{2,0,1:T(2,128)}, u32[]{:S(2)}) copy-start(f32[2,12,16]{2,0,1:T(2,128)} %param.45) | copy-start | bytes 4612
  645.5 160.7 %copy-start.14 = (f32[2,12,16]{2,0,1:T(2,128)S(1)}, f32[2,12,16]{2,0,1:T(2,128)}, u32[]{:S(2)}) copy-start(f32[2,12,16]{2,0,1:T(2,128)} %param.38) | copy-start | bytes 4612
  805.4 15.1 %copy-start.4 = (f32[2,6,256]{2,0,1:T(2,128)}, f32[2,6,256]{2,0,1:T(2,128)S(1)}, u32[]{:S(2)}) copy-start(f32[2,6,256]{2,0,1:T(2,128)S(1)} %constant_dynamic-update-slice_fusion) | copy-start | bytes 36868
  806.2 15.0 %copy-start.3 = (f32[2,16,16]{2,1,0:T(8,128)}, f32[2,16,16]{2,1,0:T(8,128)S(1)}, u32[]{:S(2)}) copy-start(f32[2,16,16]{2,1,0:T(8,128)S(1)} %reshape.271) | copy-start | bytes 6148
  808.1 12.5 %copy-start.10 = (bf16[2,6,256]{2,0,1:T(2,128)(2,1)S(1)}, bf16[2,6,256]{2,0,1:T(2,128)(2,1)}, u32[]{:S(2)}) copy-start(bf16[2,6,256]{2,0,1:T(2,128)(2,1)} %param.33) | copy-start | bytes 18436
  808.1 12.5 %copy-start.15 = (f32[2,6,256]{2,0,1:T(2,128)S(1)}, f32[2,6,256]{2,0,1:T(2,128)}, u32[]{:S(2)}) copy-start(f32[2,6,256]{2,0,1:T(2,128)} %param.47) | copy-start | bytes 36868
  808.1 12.5 %copy-start.16 = (f32[2,6,256]{2,0,1:T(2,128)S(1)}, f32[2,6,256]{2,0,1:T(2,128)}, u32[]{:S(2)}) copy-start(f32[2,6,256]{2,0,1:T(2,128)} %param.40) | copy-start | bytes 36868
  808.1 13.1 %copy-start.6 = (bf16[2,16,16]{2,1,0:T(8,128)(2,1)S(1)}, bf16[2,16,16]{2,1,0:T(8,128)(2,1)}, u32[]{:S(2)}) copy-start(bf16[2,16,16]{2,1,0:T(8,128)(2,1)} %param.32) | copy-start | bytes 3076
  808.1 13.1 %copy-start.11 = (f32[2,16,16]{2,1,0:T(8,128)S(1)}, f32[2,16,16]{2,1,0:T(8,128)}, u32[]{:S(2)}) copy-start(f32[2,16,16]{2,1,0:T(8,128)} %param.46) | copy-start | bytes 6148
  808.1 13.1 %copy-start.12 = (f32[2,16,16]{2,1,0:T(8,128)S(1)}, f32[2,16,16]{2,1,0:T(8,128)}, u32[]{:S(2)}) copy-start(f32[2,16,16]{2,1,0:T(8,128)} %param.39) | copy-start | bytes 6148
  808.1 13.8 %copy-start = (bf16[256,2048]{1,0:T(8,128)(2,1)S(1)}, bf16[256,2048]{1,0:T(8,128)(2,1)}, u32[]{:S(2)}) copy-start(bf16[256,2048]{1,0:T(8,128)(2,1)} %all-reduce.5.cloned.1.call-done) | copy-start | bytes 3145732
  808.2 13.8 %copy-start.1 = (bf16[256,2048]{1,0:T(8,128)(2,1)S(1)}, bf16[256,2048]{1,0:T(8,128)(2,1)}, u32[]{:S(2)}) copy-start(bf16[256,2048]{1,0:T(8,128)(2,1)} %get-tuple-element.143) | copy-start | bytes 3145732
  808.2 13.7 %copy-start.2 = (bf16[256,2048]{1,0:T(8,128)(2,1)S(1)}, bf16[256,2048]{1,0:T(8,128)(2,1)}, u32[]{:S(2)}) copy-start(bf16[256,2048]{1,0:T(8,128)(2,1)} %all-reduce.7.cloned.1.call-done) | copy-start | bytes 3145732
  808.2 13.7 %copy-start.8 = (pred[1024]{0:T(1024)(128)(4,1)S(1)}, pred[1024]{0:T(1024)(128)(4,1)}, u32[]{:S(2)}) copy-start(pred[1024]{0:T(1024)(128)(4,1)} %copy-done.7) | copy-start | bytes 3076
Sparse Core Ops, SparseCore 0:
  352.4 49.4 all-reduce.4
  577.2 49.3 all-reduce.6

commit v6 on v5

--- a/solution.py
+++ b/solution.py
@@ -159,8 +159,8 @@
                     a_r[rows, cols] = (f * phi).astype(BF)
                     gp_r[rows, cols] = (phi + f * (jnp.exp(-0.5 * f * f) * 0.3989422804014327)).astype(BF)
 
-        host(1, ("second", 0))
-        host(3, ("second", 1), ("third", 0))
+        host(2, ("second", 0))
+        host(4, ("second", 1), ("third", 0))
         host(5, ("third", 1), ("last", 0), ("last", 1), ("close",))
 
         @pl.when(j == nq + nu - 1)
@@ -368,45 +368,61 @@
                 flops=2 * n * M * N, nbytes=2 * (n * M + n * N + M * N), name="wgrad")(left, right)
 
 
-def norm_back(gout, e, base, extra, vec, stats, last):
+def norm_back(gout, e, base, extra, vec, stats):
     n, D = base.shape
     RB = 128
 
-    def kernel(*refs):
-        g_r, e_r, base_r = refs[:3]
-        refs = refs[3:]
-        if extra is not None:
-            extra_r, refs = refs[0], refs[1:]
-        vec_r, st_r, dx_r = refs[:3]
-        x = base_r[...].astype(F32)
-        if extra is not None:
-            x = x + extra_r[...].astype(F32) + vec_r[4:5, :] + vec_r[5:6, :]
-        xhat = (x - st_r[:, 0:1]) * st_r[:, 1:2]
-        ev = e_r[...].astype(F32)
-        me = jnp.mean(ev, axis=1, keepdims=True)
-        mx = jnp.mean(ev * xhat, axis=1, keepdims=True)
-        dx = g_r[...].astype(F32) + (ev - me - xhat * mx) * st_r[:, 1:2]
+    def kernel(g_r, e_r, base_r, extra_r, vec_r, st_r, dx_r, low_r, sum_r):
+        x = base_r[...].astype(F32) + extra_r[...].astype(F32) + vec_r[4:5, :] + vec_r[5:6, :]
+        dx = g_r[...].astype(F32) + norm_pullback(x, e_r, st_r)
         dx_r[...] = dx
-        if not last:
-            low_r, sum_r = refs[3:]
-            low_r[...] = dx.astype(BF)
-
-            @pl.when(pl.program_id(0) == 0)
-            def _():
-                sum_r[...] = jnp.zeros_like(sum_r)
-
-            sum_r[...] += jnp.sum(dx, axis=0, keepdims=True)
+        low_r[...] = dx.astype(BF)
+
+        @pl.when(pl.program_id(0) == 0)
+        def _():
+            sum_r[...] = jnp.zeros_like(sum_r)
+
+        sum_r[...] += jnp.sum(dx, axis=0, keepdims=True)
 
     row = lambda i: (i, 0)
     whole = lambda i: (0, 0)
     rows = spec((RB, D), row)
-    ins = [rows, rows, rows] + ([] if extra is None else [rows]) + [spec((6, D), whole), spec((RB, 128), row)]
-    args = [gout, e, base] + ([] if extra is None else [extra]) + [vec, stats]
-    outs, shapes = [rows], [jax.ShapeDtypeStruct((n, D), F32)]
-    if not last:
-        outs += [rows, spec((1, D), whole)]
-        shapes += [jax.ShapeDtypeStruct((n, D), BF), jax.ShapeDtypeStruct((1, D), F32)]
-    return call(kernel, (n // RB,), ins, outs, shapes, flops=10 * n * D, nbytes=16 * n * D, name="norm_back")(*args)
+    shapes = [jax.ShapeDtypeStruct((n, D), F32), jax.ShapeDtypeStruct((n, D), BF), jax.ShapeDtypeStruct((1, D), F32)]
+    return call(kernel, (n // RB,), [rows] * 4 + [spec((6, D), whole), spec((RB, 128), row)], [rows, rows, spec((1, D), whole)], shapes,
+                flops=10 * n * D, nbytes=16 * n * D, name="norm_back")(gout, e, base, extra, vec, stats)
+
+
+def norm_pullback(x, e_r, st_r):
+    xhat = (x - st_r[:, 0:1]) * st_r[:, 1:2]
+    ev = e_r[...].astype(F32)
+    me = jnp.mean(ev, axis=1, keepdims=True)
+    mx = jnp.mean(ev * xhat, axis=1, keepdims=True)
+    return (ev - me - xhat * mx) * st_r[:, 1:2]
+
+
+def finish(gout, e, base, extra, branches, held, live, stats):
+    n, D = base.shape
+    RB = 128
+    each = n // len(branches) // RB
+
+    def kernel(g_r, e_r, base_r, extra_r, *refs):
+        branch_rs, (held_r, live_r, st_r, dx_r, out_r) = refs[:len(branches)], refs[len(branches):]
+        i = pl.program_id(0)
+        x = base_r[...].astype(F32)
+        dx_r[...] = g_r[...] + norm_pullback(x, e_r, st_r)
+        for k, b_r in enumerate(branch_rs):
+            @pl.when(lax.div(i, each) == k)
+            def _(b_r=b_r):
+                last = base_r[...].astype(F32) + extra_r[...].astype(F32) + b_r[...].astype(F32) + held_r[...]
+                out_r[...] = jnp.where(live_r[...] > 0.0, last, 0.0).astype(BF)
+
+    row = lambda i: (i, 0)
+    whole = lambda i: (0, 0)
+    rows = spec((RB, D), row)
+    part = lambda k: spec((RB, D), lambda i: (jnp.clip(i - k * each, 0, each - 1), 0))
+    ins = [rows] * 4 + [part(k) for k in range(len(branches))] + [spec((1, D), whole), spec((RB, 1), row), spec((RB, 128), row)]
+    return call(kernel, (n // RB,), ins, [rows, rows], [jax.ShapeDtypeStruct((n, D), F32), jax.ShapeDtypeStruct((n, D), BF)],
+                flops=10 * n * D, nbytes=18 * n * D, name="finish")(gout, e, base, extra, *branches, held, live, stats)
 
 
 MESH = pl.DeviceIdType.MESH
@@ -514,6 +530,9 @@
             send_to("dp", peer, src, dst, self.send.at[k, n], self.recv.at[k, n]).wait_send()
 
 
+AHEAD, LAG, BACK = 3, 2, 7
+
+
 class LineSum:
     copies = 3
 
@@ -562,13 +581,13 @@
 
         @pl.when(self.spot.outer)
         def _():
-            if 0 <= t - 2 < n:
-                self.copy(t - 2, 0).wait_send()
+            if 0 <= t - AHEAD < n:
+                self.copy(t - AHEAD, 0).wait_send()
             if t < n:
                 self.copy(t, 0).start()
-            if 0 <= t - 4 < n:
-                self.copy(t - 4, 2).wait_recv()
-                self.keep(t - 4).start()
+            if 0 <= t - BACK < n:
+                self.copy(t - BACK, 2).wait_recv()
+                self.keep(t - BACK).start()
 
     def add_step(self, t):
         n = self.chunks
@@ -584,12 +603,30 @@
                 self.copy(t, 0).wait_recv()
                 self.add(t, self.land, self.stage.at[t % 2], self.land, 0)
                 self.copy(t, 1).start()
-            if 0 <= t - 1 < n:
-                self.copy(t - 1, 1).wait_recv()
-                self.copy(t - 1, 1).wait_send()
-                self.add(t - 1, self.swap, self.land, self.swap, (t - 1) * self.rows)
-                self.copy(t - 1, 2).start()
-                self.keep(t - 1).start()
+            if 0 <= t - LAG < n:
+                self.copy(t - LAG, 1).wait_recv()
+                self.copy(t - LAG, 1).wait_send()
+                self.add(t - LAG, self.swap, self.land, self.swap, (t - LAG) * self.rows)
+                self.copy(t - LAG, 2).start()
+                self.keep(t - LAG).start()
+
+    def begin(self):
+        self.sent_to, self.added_to = 0, 0
+        for _ in range(AHEAD):
+            self.send_step(self.sent_to)
+            self.sent_to += 1
+
+    def slot(self):
+        if self.added_to < self.chunks + LAG:
+            self.add_step(self.added_to)
+            self.added_to += 1
+        if self.sent_to < self.chunks + BACK:
+            self.send_step(self.sent_to)
+            self.sent_to += 1
+
+    def finish(self):
+        while self.added_to < self.chunks + LAG or self.sent_to < self.chunks + BACK:
+            self.slot()
 
     def close(self):
         for k in range(self.chunks):
@@ -608,12 +645,11 @@
         self.spot, self.items = spot, items
         self.own, self.sib, self.fx, self.fy, self.gx, self.gy = own, sib, fx, fy, gx, gy
         self.send, self.recv, self.local = send, recv, local
-        self.sent, self.loads = [], {}
+        self.sent = []
 
     def go(self, k, n, peer, src, dst):
-        copy = send_to("dp", peer, src, dst, self.send.at[k, n], self.recv.at[k, n])
-        copy.start()
-        self.sent.append(copy)
+        send_to("dp", peer(), src(), dst(), self.send.at[k, n], self.recv.at[k, n]).start()
+        self.sent.append((k, n, src))
 
     def arrived(self, k, n, dst):
         send_to("dp", self.spot.nc, dst, dst, self.send.at[k, n], self.recv.at[k, n]).wait_recv()
@@ -621,12 +657,14 @@
     def first(self, k):
         s, grad = self.spot, self.items[k][0]
         for m, slot in enumerate((s.me, s.nx, s.ny, s.diag)):
-            self.go(k, m, s.nc, grad.at[slot + s.dc], self.sib[k].at[m])
-        self.loads[k] = []
-        for m, slot in enumerate((s.me, s.nx, s.ny, s.diag)):
-            copy = pltpu.make_async_copy(grad.at[slot], self.own[k].at[m], self.local.at[k, m])
-            copy.start()
-            self.loads[k].append(copy)
+            self.go(k, m, lambda: s.nc, lambda slot=slot: grad.at[slot + s.dc], lambda m=m: self.sib[k].at[m])
+        for m in range(4):
+            self.load(k, m).start()
+
+    def load(self, k, m):
+        s = self.spot
+        slot = (s.me, s.nx, s.ny, s.diag)[m]
+        return pltpu.make_async_copy(self.items[k][0].at[slot], self.own[k].at[m], self.local.at[k, m])
 
     def over(self, r, c, body, start=0):
         step = 16
@@ -644,7 +682,7 @@
         h = r // 2
         low, high = pl.ds(0, h), pl.ds(h, h)
         for m in (3, 1, 2, 0):
-            self.loads[k][m].wait()
+            self.load(k, m).wait()
             self.arrived(k, m, sib.at[m])
 
             def add(rows, _, m=m):
@@ -652,12 +690,12 @@
 
             self.over(r, c, add)
             if m == 3:
-                self.go(k, 5, s.nx, own.at[3, low], self.fx[k].at[1])
-                self.go(k, 7, s.ny, own.at[3, high], self.fy[k].at[1])
+                self.go(k, 5, lambda: s.nx, lambda: own.at[3, low], lambda: self.fx[k].at[1])
+                self.go(k, 7, lambda: s.ny, lambda: own.at[3, high], lambda: self.fy[k].at[1])
             if m == 1:
-                self.go(k, 4, s.nx, own.at[1, low], self.fx[k].at[0])
+                self.go(k, 4, lambda: s.nx, lambda: own.at[1, low], lambda: self.fx[k].at[0])
             if m == 2:
-                self.go(k, 6, s.ny, own.at[2, high], self.fy[k].at[0])
+                self.go(k, 6, lambda: s.ny, lambda: own.at[2, high], lambda: self.fy[k].at[0])
 
     def third(self, k):
         s = self.spot
@@ -670,14 +708,14 @@
             fx[1, rows, :] = (own[2, rows, :].astype(F32) + fx[1, rows, :].astype(F32)).astype(BF)
 
         self.over(h, c, add_low)
-        self.go(k, 8, s.ny, fx.at[1], self.gy[k])
+        self.go(k, 8, lambda: s.ny, lambda: fx.at[1], lambda: self.gy[k])
         self.arrived(k, 7, fy.at[1])
 
         def add_high(rows, there):
             fy[1, rows, :] = (own[1, there, :].astype(F32) + fy[1, rows, :].astype(F32)).astype(BF)
 
         self.over(h, c, add_high, h)
-        self.go(k, 9, s.nx, fy.at[1], self.gx[k])
+        self.go(k, 9, lambda: s.nx, lambda: fy.at[1], lambda: self.gx[k])
 
     def last(self, k):
         own, out = self.own[k], self.items[k][1]
@@ -700,11 +738,11 @@
         self.over(h, c, high, h)
 
     def close(self):
-        for copy in self.sent:
-            copy.wait_send()
-
-
-def link_kernel(name, ident, shards, layers, part=None, chunks=8):
+        for k, n, src in self.sent:
+            send_to("dp", self.spot.nc, src(), src(), self.send.at[k, n], self.recv.at[k, n]).wait_send()
+
+
+def link_kernel(name, ident, shards, layers, part=None, chunks=16):
     ng = len(shards)
     HBM = pl.BlockSpec(memory_space=pl.ANY)
     DMA = pltpu.SemaphoreType.DMA
@@ -754,26 +792,26 @@
         return pltpu.make_async_copy(self.rights[i], self.rhs[slot], self.rsem.at[i])
 
     def left(self, k, m):
-        cols = pl.ds(pl.multiple_of(m * 256, 256), 256)
-        return pltpu.make_async_copy(self.lefts[k].at[:, cols], self.lbuf.at[lax.rem(m, 2)], self.lsem.at[lax.rem(m, 2)])
+        odd = m % 2 if isinstance(m, int) else lax.rem(m, 2)
+        cols = pl.ds(m * 256 if isinstance(m, int) else pl.multiple_of(m * 256, 256), 256)
+        return pltpu.make_async_copy(self.lefts[k].at[:, cols], self.lbuf.at[odd], self.lsem.at[odd])
 
     def stores(self, k, m):
-        grad, o = self.grads[k], self.obuf.at[lax.rem(m, 2)]
-        sem = self.osem.at[lax.rem(m, 2)]
+        odd = m % 2 if isinstance(m, int) else lax.rem(m, 2)
+        grad, o, sem = self.grads[k], self.obuf.at[odd], self.osem.at[odd]
         slots, r, c = grad.shape
         if r == 256 and self.lefts[k].shape[1] == slots * r:
             return [pltpu.make_async_copy(o.at[:, pl.ds(0, c)], grad.at[m], sem.at[0])]
-        rows = pl.ds(pl.multiple_of(m * 256, 256), 256)
+        rows = pl.ds(m * 256 if isinstance(m, int) else pl.multiple_of(m * 256, 256), 256)
         return [pltpu.make_async_copy(o.at[:, pl.ds(s * c, c)], grad.at[s, rows], sem.at[s]) for s in range(slots)]
 
-    def run(self, k, slot, start, stop):
+    def run(self, k, slot, hooks):
         count = self.lefts[k].shape[1] // 256
         right = self.rhs[slot]
         width = right.shape[1]
-        if start == 0:
-            self.left(k, 0).start()
-
-        @pl.loop(start, stop)
+        self.left(k, 0).start()
+
+        @pl.loop(0, count)
         def _(m):
             self.left(k, m).wait()
 
@@ -790,11 +828,12 @@
             self.obuf[lax.rem(m, 2), :, :width] = g.astype(BF)
             for copy in self.stores(k, m):
                 copy.start()
-
-        if stop == count:
-            for m in (count - 2, count - 1):
-                for copy in self.stores(k, jnp.int32(m)):
-                    copy.wait()
+            for at in sorted(hooks):
+                pl.when(m == at)(hooks[at])
+
+        for m in (count - 2, count - 1):
+            for copy in self.stores(k, m):
+                copy.wait()
 
     def sums(self, slot, out):
         right = self.rhs[slot]
@@ -808,20 +847,19 @@
 def plan_sum_gather(G, line):
     for k in range(4):
         G.first(k)
-    stages = {3: [("second", 0), ("second", 1)], 5: [("second", 2)], 7: [("second", 3)], 8: [("third", 0), ("third", 1)], 9: [("third", 2)],
-              10: [("third", 3)]}
-    line.send_step(0)
-    for at in range(1, 12):
-        line.send_step(at)
-        if at - 1 <= line.chunks:
-            line.add_step(at - 1)
+    stages = {5: [("second", 0), ("second", 1)], 9: [("second", 2)], 12: [("second", 3)], 14: [("third", 0), ("third", 1)], 15: [("third", 2)],
+              17: [("third", 3)]}
+    line.begin()
+    for at in range(18):
+        line.slot()
         for name, k in stages.get(at, ()):
             getattr(G, name)(k)
+    line.finish()
     for k in range(4):
         G.last(k)
 
 
-def sum_scatter(ident, e, more, first_row, more_rows, lefts, rights, step=128):
+def sum_scatter(ident, e, more, first_row, more_rows, lefts, rights, step=64):
     n, D = e.shape
     HBM = pl.BlockSpec(memory_space=pl.ANY)
     VM_ = pl.BlockSpec(memory_space=pltpu.VMEM)
@@ -830,9 +868,9 @@
     dims = [(lefts[0].shape[1], w), (lefts[1].shape[1], w), (w, C), (w, U)]
     DMA = pltpu.SemaphoreType.DMA
     chunks = (n + more_rows) // step
-    outs = [HBM] * 2 + [HBM] * 4 + [VM_] * 4 + [VM_] * 2
+    outs = [HBM] * 2 + [HBM] * 4 + [VM_] * 4 + [VM_] * 3
     shapes = [jax.ShapeDtypeStruct(e.shape, BF), jax.ShapeDtypeStruct((more_rows, D), BF)] + [jax.ShapeDtypeStruct((8,) + d, BF) for d in dims] + [jax.ShapeDtypeStruct(d, F32) for d in dims]
-    shapes += [jax.ShapeDtypeStruct((1, C), F32), jax.ShapeDtypeStruct((1, U), F32)]
+    shapes += [jax.ShapeDtypeStruct((1, C), F32), jax.ShapeDtypeStruct((1, U), F32), jax.ShapeDtypeStruct((1, D), F32)]
     scratch = [pltpu.VMEM((2, step, D), BF)] + [pltpu.VMEM((n + more_rows, D), BF)] * 2 + [DMA((chunks, 3)), DMA((chunks, 3)), DMA((chunks + 2,))]
     scratch += [DMA((4, 10)), DMA((4, 10)), DMA((4, 4))]
     for r, c in dims:
@@ -846,7 +884,7 @@
         refs = list(refs)
         take = lambda k: [refs.pop(0) for _ in range(k)]
         (e_r, more_r), left_rs, right_rs = take(2), take(4), take(3)
-        (total, more_total), grads, owned, sum_rs = take(2), take(4), take(4), take(2)
+        (total, more_total), grads, owned, sum_rs = take(2), take(4), take(4), take(3)
         stage, land, swap, send, recv, local = take(6)
         spot = Spot()
         spot.meet(True)
@@ -858,58 +896,48 @@
         W = Products(left_rs, right_rs, grads, (wide_r, narrow_r), lbuf, obuf, rsem, lsem, osem)
         W.right(0, 0).start()
         W.right(1, 1).start()
-        half = left_rs[1].shape[1] // 512
-        state = [2, 0]
-
-        def slot():
-            send_at, add_at = state
-            if add_at <= chunks:
-                line.add_step(add_at)
-            if send_at < chunks + 4:
-                line.send_step(send_at)
-            state[:] = send_at + 1, add_at + 1
-
-        line.send_step(0)
-        line.send_step(1)
+        def steps(*what):
+            def go():
+                for step, *args in what:
+                    step(*args)
+
+            return go
+
+        slot = (line.slot,)
+        line.begin()
         W.right(0, 0).wait()
-        W.run(0, 0, 0, left_rs[0].shape[1] // 256)
+        W.run(0, 0, {})
         S.first(0)
-        W.run(1, 0, 0, half)
-        slot()
-        S.second(0)
-        W.run(1, 0, half, 2 * half)
+        W.run(1, 0, {1: steps(slot), 3: steps(slot), 5: steps(slot, (S.second, 0)), 7: steps(slot)})
         S.first(1)
+        W.sums(0, sum_rs[2])
         W.right(2, 0).start()
         W.right(1, 1).wait()
-        W.run(2, 1, 0, 2)
-        slot()
-        W.run(2, 1, 2, 8)
+        W.run(2, 1, {2: steps(slot), 5: steps(slot, (S.second, 1))})
         S.first(2)
-        S.second(1)
-        slot()
+        line.slot()
         W.right(2, 0).wait()
-        W.run(3, 0, 0, 4)
-        S.third(0)
-        slot()
-        S.second(2)
-        W.run(3, 0, 4, 8)
+        W.run(3, 0, {1: steps(slot), 2: steps((S.third, 0)), 4: steps(slot, (S.second, 2)), 7: steps(slot)})
         S.first(3)
+        line.slot()
         W.sums(1, sum_rs[0])
-        slot()
         S.third(1)
+        line.slot()
         S.second(3)
-        slot()
+        line.slot()
         W.sums(0, sum_rs[1])
         S.last(0)
-        slot()
+        line.slot()
+        line.slot()
         S.third(2)
+        line.slot()
         S.last(1)
-        slot()
-        slot()
+        line.slot()
+        line.slot()
         S.third(3)
+        line.slot()
         S.last(2)
-        while state[0] < chunks + 4:
-            slot()
+        line.finish()
         S.last(3)
         line.close()
         S.close()
@@ -920,7 +948,7 @@
         compiler_params=pltpu.CompilerParams(vmem_limit_bytes=VM2, collective_id=ident, has_side_effects=True),
         cost_estimate=pl.CostEstimate(flops=flops, bytes_accessed=2 * n * D * 12, transcendentals=0), name="sum_scatter")(e, more, *lefts, *rights)
     gd, gn, gq, gu = got[6:10]
-    return got[0], got[1], (gq, gd, gu, gn), got[10], got[11]
+    return got[0], got[1], (gq, gd, gu, gn), got[10], got[11], got[12]
 
 
 def small_sum(pieces, shared):
@@ -1048,12 +1076,12 @@
         ctx, act, h1, h2 = lefts
         gr, dmix, df = rights
         w = gr.shape[1] // lax.axis_size("dp")
-        gd, _ = weight_grad(ctx, gr, w=w)
+        gd, low_sums = weight_grad(ctx, gr, w=w)
         gn, _ = weight_grad(act, gr, w=w)
         gq, qsum = weight_grad(h1, dmix)
         gu, usum = weight_grad(h2, df)
         more = self.share(more[first_row:first_row + more_rows])
-        return self.share(e), more, self.owned((gq, gd, gu, gn)), qsum, usum
+        return self.share(e), more, self.owned((gq, gd, gu, gn)), qsum, usum, low_sums
 
 
 class ChipLinks:
@@ -1124,7 +1152,7 @@
             full.append(made)
         else:
             gout = gr = jnp.where(live, cotangent, 0).astype(BF)
-            sums = jnp.sum(gout.astype(F32), axis=0, keepdims=True)
+            sums = None
             branch, gr = lax.optimization_barrier((branch, gr))
             branch_sum = [None] * 4
             quarter = rows // 4
@@ -1139,19 +1167,15 @@
         if layer == 0:
             branch_sum[2], e = lax.optimization_barrier((branch_sum[2], e))
         at = 1 if layer else 3
-        e, branch_sum[at], big[layer], qsum, usum = links.turn(e, branch, at * quarter, quarter, (ctx, act, h1, h2), (gr, dmix, df), 3 + layer)
-        little[layer] = (qsum, usum, norm_sums, sums)
+        e, branch_sum[at], big[layer], qsum, usum, low_sums = links.turn(e, branch, at * quarter, quarter, (ctx, act, h1, h2), (gr, dmix, df), 3 + layer)
+        little[layer] = (qsum, usum, norm_sums, low_sums if sums is None else sums)
         if layer:
             branch_sum[0], e, third = lax.optimization_barrier((branch_sum[0], e, branch[2 * quarter:3 * quarter]))
             branch_sum[2] = lax.psum(third, "mp")
-        made = norm_back(gout, e, tokens_in, extra, held[layer], stats, layer == 0)
         if layer:
-            gout, gr, sums = made
-        else:
-            input_grad = made[0]
-    branch = jnp.concatenate(branch_sum)
-    x_last = tokens_in.astype(F32) + kept[1][-1].astype(F32) + vecs[0, 4] + vecs[0, 5] + branch.astype(F32) + vecs[1, 4] + vecs[1, 5]
-    output = jnp.where(live, x_last, 0.0).astype(BF)
+            gout, gr, sums = norm_back(gout, e, tokens_in, extra, held[layer], stats)
+    every = (vecs[0, 4:5] + vecs[0, 5:6]) + (vecs[1, 4:5] + vecs[1, 5:6])
+    input_grad, output = finish(gout, e, tokens_in, kept[1][-1], branch_sum, every, live.astype(F32), stats)
 
     done = None
     for layer in reversed(range(LAYERS)):

time: 872 us -> 846 us (0.970)
  other arithmetic: 31 us -> 19.8 us
  Pallas kernels: 799 us -> 789 us
    convert_element_type x1, other arithmetic: 12.3 us -> 0.01 us  [body(): live.astype(F32)]
  transfers between devices with their start and end apart: 2 -> 2, of which waited for: 0 -> 0; matrix products, arithmetic and copies ran while one was open for 1% -> 1% of each run, Pallas kernels for 34% -> 32%
where the time goes in v6:
time: 846 us; the launch traced here: 840 us
  Pallas kernels  789 us (93%)
  other arithmetic  19.8 us (2%)
  local copies, waits for them, and re-layouts  15.8 us (2%)
  between operations  14.9 us (2%)
    pallas_call x2, Pallas kernels, sum_scatter(): pl.pallas_call(kernel, in_specs=[HBM] * 9, out_specs=outs, out_shape=shap...  289 us
    pallas_call x2, Pallas kernels, link_kernel(): pl.pallas_call(kernel, in_specs=[HBM] * (ng + len(parts)), out_specs=[HBM...  183 us
    pallas_call x2, Pallas kernels, project(): call(kernel, (nq + nu,), ins, outs, shapes, scratch, ident=5 if ng else N...  86.5 us
    pallas_call x2, Pallas kernels, back_out(): call(kernel, (D // NB,), [spec((n, C), whole, True), spec((n, U), whole,...  45.6 us
    pallas_call x2, Pallas kernels, adam_layer(): pl.pallas_call(kernel, grid=(steps,), in_specs=ins, out_specs=[at(b) for...  38.4 us
    pallas_call x2, Pallas kernels, back_in(): call(kernel, (nr + nu,), [spec((n, D), lambda j: (0, 0), True), spec((n,...  36.3 us
    pallas_call x2, Pallas kernels, branch_out(): call(kernel, (dp,), [spec((n, R), whole, True), spec((n, U), whole, True)...  32.2 us
    pallas_call x2, Pallas kernels, attend_backward(): call(kernel, (H,), [part(0), part(1), part(2), spec((n, HD), lambda h: (0...  23 us
  transfers between devices with their start and end apart: 2, of which 0 were waited for; matrix products, arithmetic and copies ran while one was open for 1% of the time, Pallas kernels for 32%

profile of v6, /device:TPU:0, one launch (start us, length us, event | category | flops | bytes accessed | tf_op | source)
XLA Modules:
  0.0 839.7 jit_solution(8496880060332269760)
XLA Ops:
  7.3 0.7 copy.132
  8.0 0.8 reshape.300
  8.8 0.7 copy.131
  9.6 0.6 fusion.18.refs_0_
  10.2 67.6 %gather.1 = (bf16[8,32,128]{2,1,0:T(8,128)(2,1)}, bf16[8,256,1536]{2,1,0:T(8,128)(2,1)}, bf16[8,256,2048]{2,1,0:T(8,128)(2,1)}) custom-call(bf16[32,128]{1,0:T(8,128)(2,1)} %fusion.18.refs_0_, bf16[2,256,1536]{2,1,0:T(8,128)(2,1)} %refs_0_.9, bf16[2,256,2048]{2,1,0:T(8,128)(2,1)} %refs_2_.7), custom_call_target="tpu_custom_call" | custom-call | bytes 14712832 | tf_op jit(solution)/shard_map/gather/pallas_call | solution.py:773
  77.8 0.9 copy.188
  79.3 0.7 squeeze.31.refs_3_
  80.3 0.7 squeeze.32.refs_7_
  81.3 4.6 broadcast_select_fusion.g_r.refs_6_
  85.8 1.0 add_select_fusion.sc_r
  87.5 0.7 pad_maximum_fusion.refs_1_.refs_5_
  88.1 1.9 fusion
  90.1 1.3 maximum_maximum_fusion
  91.4 53.8 %project.2 = (bf16[1024,2048]{1,0:T(8,128)(2,1)}, bf16[1024,2048]{1,0:T(8,128)(2,1)}, bf16[1024,1536]{1,0:T(8,128)(2,1)}, bf16[1024,2048]{1,0:T(8,128)(2,1)}, bf...) custom-call(bf16[1024,2048]{1,0:T(8,128)(2,1)} %base_r.3, ...), custom_call_target="tpu_custom_call" | custom-call | flops 15032385536 | bytes 38797312 | tf_op jit(solution)/shard_map/project/pallas_call | solution.py:186
  145.2 6.6 attend.2.c_r.refs_2_
  151.8 16.1 %branch.2.refs_4_ = bf16[1024,2048]{1,0:T(8,128)(2,1)} custom-call(bf16[1024,512]{1,0:T(8,128)(2,1)} %attend.2.c_r.refs_2_, bf16[1024,2048]{1,0:T(8,128)(2,1)} %get-tuple-element.125.a_r.refs_3_, bf16[8,512,256]{2,1,0:T(8,128)(2,1)} %get-tuple-element.126.wd_r, bf16[8,2048,256]{2,1,0:T(8,128)(2,1)} %get-tuple-element.127.wn_r), custom_call_target="tpu_custom_call" | custom-call | flops 10737418240 | bytes 19922944 | tf_op jit(solution)/shard_map/branch/pallas_call | solution.py:269
  167.9 115.2 %sum_gather.1 = (bf16[8,256,1536]{2,1,0:T(8,128)(2,1)}, bf16[8,512,256]{2,1,0:T(8,128)(2,1)}, bf16[8,256,2048]{2,1,0:T(8,128)(2,1)}, bf16[8,2048,256]{2,1,0:T(8,128)(2,1)}, bf16[1024,2048]{1,0:T(8,128)(2,1)}) custom-call(bf16[2,256,1536]{2,1,0:T(8,128)(2,1)} %refs_0_.9, bf16[2,512,256]{2,1,0:T(8,128)(2,1)} %refs_1_.7, bf16[2,256,2048]{2,1,0:T(8,128)(2,1)} %refs_2_.7, ...), custom_call_target="tpu_custom_call" | custom-call | bytes 29360128 | tf_op jit(solution)/shard_map/sum_gather/pallas_call | solution.py:773
  283.2 0.7 squeeze.35.refs_4_
  283.9 0.7 squeeze.36.refs_8_
  284.6 0.7 pad_maximum_fusion.1.refs_2_.refs_6_.vec_r
  285.2 32.6 %project.3 = (bf16[1024,2048]{1,0:T(8,128)(2,1)}, bf16[1024,2048]{1,0:T(8,128)(2,1)}, bf16[1024,1536]{1,0:T(8,128)(2,1)}, bf16[1024,2048]{1,0:T(8,128)(2,1)}, bf...) custom-call(bf16[1024,2048]{1,0:T(8,128)(2,1)} %base_r.3, bf16[1024,2048]{1,0:T(8,128)(2,1)} %get-tuple-element.128.refs_1_.refs_5_.extra_r, ...), custom_call_target="tpu_custom_call" | custom-call | flops 15032385536 | bytes 38797312 | tf_op jit(solution)/shard_map/project/pallas_call | solution.py:186
  317.8 6.7 attend.3.c_r.refs_2_
  324.6 16.1 %branch.3.refs_1_ = bf16[1024,2048]{1,0:T(8,128)(2,1)} custom-call(bf16[1024,512]{1,0:T(8,128)(2,1)} %attend.3.c_r.refs_2_, bf16[1024,2048]{1,0:T(8,128)(2,1)} %get-tuple-element.132.a_r.refs_3_, bf16[8,512,256]{2,1,0:T(8,128)(2,1)} %get-tuple-element.133.wd_r, bf16[8,2048,256]{2,1,0:T(8,128)(2,1)} %get-tuple-element.134.wn_r), custom_call_target="tpu_custom_call" | custom-call | flops 10737418240 | bytes 19922944 | tf_op jit(solution)/shard_map/branch/pallas_call | solution.py:269
  340.7 3.1 fusion.27
  343.9 18.2 %back_in.2 = (bf16[1024,512]{1,0:T(8,128)(2,1)}, bf16[1024,2048]{1,0:T(8,128)(2,1)}) custom-call(bf16[1024,2048]{1,0:T(8,128)(2,1)} %broadcast_select_fusion.g_r.refs_6_, bf16[1024,2048]{1,0:T(8,128)(2,1)} %get-tuple-element.137.gp_r, bf16[8,512,256]{2,1,0:T(8,128)(2,1)} %get-tuple-element.133.wd_r, bf16[8,2048,256]{2,1,0:T(8,128)(2,1)} %get-tuple-element.134.wn_r), custom_call_target="tpu_custom_call" | custom-call | flops 10737418240 | bytes 24117248 | tf_op jit(solution)/shard_map/back_in/pallas_call | solution.py:301
  362.0 11.4 %attend_back.2.refs_0_.refs_7_ = bf16[1024,1536]{1,0:T(8,128)(2,1)} custom-call(bf16[1024,1536]{1,0:T(8,128)(2,1)} %get-tuple-element.131.q_r.k_r.v_r, bf16[1024,1536]{1,0:T(8,128)(2,1)} %get-tuple-element.131.q_r.k_r.v_r, bf16[1024,1536]{1,0:T(8,128)(2,1)} %get-tuple-element.131.q_r.k_r.v_r, bf16[1024,512]{1,0:T(8,128)(2,1)} %get-tuple-element.138.do_r, ...), custom_call_target="tpu_custom_call" | custom-call | flops 3355443200 | bytes 6291456 | tf_op jit(solution)/shard_map/attend_back/pallas_call | solution.py:252
  373.5 23.1 %back_out.2 = (bf16[1024,2048]{1,0:T(8,128)(2,1)}, f32[4,2048]{1,0:T(4,128)}) custom-call(bf16[1024,1536]{1,0:T(8,128)(2,1)} %attend_back.2.refs_0_.refs_7_, bf16[1024,2048]{1,0:T(8,128)(2,1)} %get-tuple-element.139.refs_1_.refs_8_, bf16[2048,1536]{1,0:T(8,128)(2,1)} %bitcast.99, bf16[2048,2048]{1,0:T(8,128)(2,1)} %bitcast.95, bf16[1024,2048]{1,0:T(8,128)(2,1)} %base_r.3, ...), custom_call_target="tpu_custom_call" | custom-call | flops 15032385536 | bytes 34603008 | tf_op jit(solution)/shard_map/back_out/pallas_call | solution.py:337
  396.6 144.0 %sum_scatter.2 = (bf16[1024,2048]{1,0:T(8,128)(2,1)}, bf16[256,2048]{1,0:T(8,128)(2,1)}, bf16[8,512,256]{2,1,0:T(8,128)(2,1)}, bf16[8,2048,256]{2,1,0:T(8,128)(2...) custom-call(bf16[1024,2048]{1,0:T(8,128)(2,1)} %get-tuple-element.14, ...), custom_call_target="tpu_custom_call" | custom-call | flops 25769803776 | bytes 50331648 | tf_op jit(solution)/shard_map/sum_scatter/pallas_call | solution.py:946
  540.7 1.0 copy.145.refs_5_
  541.7 0.7 reduce.1
  543.1 1.4 reduce.15
  544.7 1.4 reduce.17
  546.1 19.4 %adam.2 = (f32[2,256,1536]{2,1,0:T(8,128)}, f32[2,256,1536]{2,1,0:T(8,128)}, f32[2,256,1536]{2,1,0:T(8,128)}, f32[2,256,1536]{2,1,0:T(8,128)}, f32[2,512,256]{2,...) custom-call(bf16[2,256,1536]{2,1,0:T(8,128)(2,1)} %refs_0_.9, ...), custom_call_target="tpu_custom_call" | custom-call | flops 31457280 | bytes 47185920 | tf_op jit(solution)/shard_map/adam/pallas_call | solution.py:1030
  565.4 0.6 fusion.20.refs_4_
  566.1 14.8 %norm_back.1 = (f32[1024,2048]{1,0:T(8,128)}, bf16[1024,2048]{1,0:T(8,128)(2,1)}, f32[1,2048]{1,0:T(1,128)}) custom-call(bf16[1024,2048]{1,0:T(8,128)(2,1)} %broadcast_select_fusion.g_r.refs_6_, bf16[1024,2048]{1,0:T(8,128)(2,1)} %get-tuple-element.145.e_r, bf16[1024,2048]{1,0:T(8,128)(2,1)} %base_r.3, ...), custom_call_target="tpu_custom_call" | custom-call | flops 20971520 | bytes 33554432 | tf_op jit(solution)/shard_map/norm_back/pallas_call | solution.py:391
  580.9 18.2 %back_in.3 = (bf16[1024,512]{1,0:T(8,128)(2,1)}, bf16[1024,2048]{1,0:T(8,128)(2,1)}) custom-call(bf16[1024,2048]{1,0:T(8,128)(2,1)} %get-tuple-element.148.g_r.refs_6_, bf16[1024,2048]{1,0:T(8,128)(2,1)} %get-tuple-element.149.gp_r, bf16[8,512,256]{2,1,0:T(8,128)(2,1)} %get-tuple-element.126.wd_r, bf16[8,2048,256]{2,1,0:T(8,128)(2,1)} %get-tuple-element.127.wn_r), custom_call_target="tpu_custom_call" | custom-call | flops 10737418240 | bytes 24117248 | tf_op jit(solution)/shard_map/back_in/pallas_call | solution.py:301
  599.1 11.5 %attend_back.3.refs_0_.refs_7_ = bf16[1024,1536]{1,0:T(8,128)(2,1)} custom-call(bf16[1024,1536]{1,0:T(8,128)(2,1)} %get-tuple-element.124.q_r.k_r.v_r, bf16[1024,1536]{1,0:T(8,128)(2,1)} %get-tuple-element.124.q_r.k_r.v_r, bf16[1024,1536]{1,0:T(8,128)(2,1)} %get-tuple-element.124.q_r.k_r.v_r, bf16[1024,512]{1,0:T(8,128)(2,1)} %get-tuple-element.150.do_r, ...), custom_call_target="tpu_custom_call" | custom-call | flops 3355443200 | bytes 6291456 | tf_op jit(solution)/shard_map/attend_back/pallas_call | solution.py:252
  610.6 0.7 reduce.16
  611.3 22.5 %back_out.3 = (bf16[1024,2048]{1,0:T(8,128)(2,1)}, f32[4,2048]{1,0:T(4,128)}) custom-call(bf16[1024,1536]{1,0:T(8,128)(2,1)} %attend_back.3.refs_0_.refs_7_, bf16[1024,2048]{1,0:T(8,128)(2,1)} %get-tuple-element.151.refs_1_.refs_8_, bf16[2048,1536]{1,0:T(8,128)(2,1)} %bitcast.97, bf16[2048,2048]{1,0:T(8,128)(2,1)} %bitcast.93, bf16[1024,2048]{1,0:T(8,128)(2,1)} %base_r.3, ...), custom_call_target="tpu_custom_call" | custom-call | flops 15032385536 | bytes 34603008 | tf_op jit(solution)/shard_map/back_out/pallas_call | solution.py:337
  633.8 0.8 copy.192
  634.7 145.4 %sum_scatter.3 = (bf16[1024,2048]{1,0:T(8,128)(2,1)}, bf16[256,2048]{1,0:T(8,128)(2,1)}, bf16[8,512,256]{2,1,0:T(8,128)(2,1)}, bf16[8,2048,256]{2,1,0:T(8,128)(2...) custom-call(bf16[1024,2048]{1,0:T(8,128)(2,1)} %get-tuple-element.15, ...), custom_call_target="tpu_custom_call" | custom-call | flops 25769803776 | bytes 50331648 | tf_op jit(solution)/shard_map/sum_scatter/pallas_call | solution.py:946
  780.1 0.7 reduce
  781.0 1.4 reduce.14
  782.7 9.5 %small_sum.1 = f32[32,128]{1,0:T(8,128)S(1)} custom-call(f32[8,32,128]{2,1,0:T(8,128)S(1)} %bitcast.74), custom_call_target="tpu_custom_call" | custom-call | tf_op jit(solution)/shard_map/small_sum/pallas_call | solution.py:993
  795.0 0.6 subtract_subtract_fusion
  795.6 0.7 subtract_subtract_fusion.2
  796.3 17.3 %finish.1 = (f32[1024,2048]{1,0:T(8,128)}, bf16[1024,2048]{1,0:T(8,128)(2,1)}) custom-call(f32[1024,2048]{1,0:T(8,128)} %get-tuple-element.146.g_r, bf16[1024,2048]{1,0:T(8,128)(2,1)} %get-tuple-element.157.e_r, bf16[1024,2048]{1,0:T(8,128)(2,1)} %base_r.3, bf16[1024,2048]{1,0:T(8,128)(2,1)} %get-tuple-element.128.refs_1_.refs_5_.extra_r, ...), custom_call_target="tpu_custom_call" | custom-call | flops 20971520 | bytes 37748736 | tf_op jit(solution)/shard_map/finish/pallas_call | solution.py:424
  813.6 19.1 %adam.3 = (f32[2,256,1536]{2,1,0:T(8,128)}, f32[2,256,1536]{2,1,0:T(8,128)}, f32[2,256,1536]{2,1,0:T(8,128)}, f32[2,256,1536]{2,1,0:T(8,128)}, f32[2,512,256]{2,...) custom-call(bf16[2,256,1536]{2,1,0:T(8,128)(2,1)} %refs_0_.9, ...), custom_call_target="tpu_custom_call", output_to_operand_aliasing={{0}: (16, {}), {1}: (17, {}), {2}: (18, {}), {3}: (19, {}),... | custom-call | flops 31457280 | bytes 47185920 | tf_op jit(solution)/shard_map/adam/pallas_call | solution.py:1030
  (100 shorter events, 6.1 us)
Async XLA Ops:
  7.2 71.7 %copy-start.13 = (s32[1,4]{1,0:T(1,128)S(1)}, s32[1,4]{1,0:T(1,128)}, u32[]{:S(2)}) copy-start(s32[1,4]{1,0:T(1,128)} %param.26) | copy-start | bytes 52
  7.2 558.8 %all-reduce.5.cloned.1.call-start = ((), (), s32[]{:S(2)}) async-start(), calls=%async_computation | async-start | bytes 2097152 | tf_op jit(solution)/shard_map/psum | solution.py:1159
  343.8 290.8 %all-reduce.7.cloned.1.call-start = ((), (), s32[]{:S(2)}) async-start(), calls=%async_computation.1 | async-start | bytes 2097152 | tf_op jit(solution)/shard_map/psum | solution.py:1174
  396.6 149.5 %copy-start.2 = (f32[4,2048]{1,0:T(4,128)S(1)}, f32[4,2048]{1,0:T(4,128)}, u32[]{:S(2)}) copy-start(f32[4,2048]{1,0:T(4,128)} %get-tuple-element.205) | copy-start | bytes 98308
  599.1 11.6 %copy-start.12 = (f32[1,2048]{1,0:T(1,128)S(1)}, f32[1,2048]{1,0:T(1,128)}, u32[]{:S(2)}) copy-start(f32[1,2048]{1,0:T(1,128)} %get-tuple-element.210) | copy-start | bytes 24580
  634.6 158.3 %copy-start.4 = (bf16[2,12,16]{2,0,1:T(2,128)(2,1)S(1)}, bf16[2,12,16]{2,0,1:T(2,128)(2,1)}, u32[]{:S(2)}) copy-start(bf16[2,12,16]{2,0,1:T(2,128)(2,1)} %param.31) | copy-start | bytes 2308
  634.6 158.3 %copy-start.8 = (f32[2,12,16]{2,0,1:T(2,128)S(1)}, f32[2,12,16]{2,0,1:T(2,128)}, u32[]{:S(2)}) copy-start(f32[2,12,16]{2,0,1:T(2,128)} %param.45) | copy-start | bytes 4612
  634.6 158.3 %copy-start.9 = (f32[2,12,16]{2,0,1:T(2,128)S(1)}, f32[2,12,16]{2,0,1:T(2,128)}, u32[]{:S(2)}) copy-start(f32[2,12,16]{2,0,1:T(2,128)} %param.38) | copy-start | bytes 4612
  634.6 160.3 %copy-start.3 = (bf16[2,16,16]{2,1,0:T(8,128)(2,1)S(1)}, bf16[2,16,16]{2,1,0:T(8,128)(2,1)}, u32[]{:S(2)}) copy-start(bf16[2,16,16]{2,1,0:T(8,128)(2,1)} %param.32) | copy-start | bytes 3076
  634.7 160.3 %copy-start.6 = (f32[2,16,16]{2,1,0:T(8,128)S(1)}, f32[2,16,16]{2,1,0:T(8,128)}, u32[]{:S(2)}) copy-start(f32[2,16,16]{2,1,0:T(8,128)} %param.46) | copy-start | bytes 6148
  634.7 160.3 %copy-start.7 = (f32[2,16,16]{2,1,0:T(8,128)S(1)}, f32[2,16,16]{2,1,0:T(8,128)}, u32[]{:S(2)}) copy-start(f32[2,16,16]{2,1,0:T(8,128)} %param.39) | copy-start | bytes 6148
  634.7 160.9 %copy-start.5 = (bf16[2,6,256]{2,0,1:T(2,128)(2,1)S(1)}, bf16[2,6,256]{2,0,1:T(2,128)(2,1)}, u32[]{:S(2)}) copy-start(bf16[2,6,256]{2,0,1:T(2,128)(2,1)} %param.33) | copy-start | bytes 18436
  634.7 160.9 %copy-start.10 = (f32[2,6,256]{2,0,1:T(2,128)S(1)}, f32[2,6,256]{2,0,1:T(2,128)}, u32[]{:S(2)}) copy-start(f32[2,6,256]{2,0,1:T(2,128)} %param.47) | copy-start | bytes 36868
  634.7 160.9 %copy-start.11 = (f32[2,6,256]{2,0,1:T(2,128)S(1)}, f32[2,6,256]{2,0,1:T(2,128)}, u32[]{:S(2)}) copy-start(f32[2,6,256]{2,0,1:T(2,128)} %param.40) | copy-start | bytes 36868
  794.9 18.7 %copy-start = (f32[2,16,16]{2,1,0:T(8,128)}, f32[2,16,16]{2,1,0:T(8,128)S(1)}, u32[]{:S(2)}) copy-start(f32[2,16,16]{2,1,0:T(8,128)S(1)} %reshape.322) | copy-start | bytes 6148
  795.0 18.6 %copy-start.1 = (f32[2,6,256]{2,0,1:T(2,128)}, f32[2,6,256]{2,0,1:T(2,128)S(1)}, u32[]{:S(2)}) copy-start(f32[2,6,256]{2,0,1:T(2,128)S(1)} %constant_dynamic-update-slice_fusion) | copy-start | bytes 36868
Sparse Core Ops, SparseCore 0:
  343.9 51.3 all-reduce.4
  581.0 51.2 all-reduce.6

commit v7 on v6

--- a/solution.py
+++ b/solution.py
@@ -402,8 +402,9 @@
 
 def finish(gout, e, base, extra, branches, held, live, stats):
     n, D = base.shape
-    RB = 128
-    each = n // len(branches) // RB
+    RB = 64
+    counts = [b.shape[0] // RB for b in branches]
+    starts = [sum(counts[:k]) for k in range(len(counts))]
 
     def kernel(g_r, e_r, base_r, extra_r, *refs):
         branch_rs, (held_r, live_r, st_r, dx_r, out_r) = refs[:len(branches)], refs[len(branches):]
@@ -411,7 +412,7 @@
         x = base_r[...].astype(F32)
         dx_r[...] = g_r[...] + norm_pullback(x, e_r, st_r)
         for k, b_r in enumerate(branch_rs):
-            @pl.when(lax.div(i, each) == k)
+            @pl.when((i >= starts[k]) & (i < starts[k] + counts[k]))
             def _(b_r=b_r):
                 last = base_r[...].astype(F32) + extra_r[...].astype(F32) + b_r[...].astype(F32) + held_r[...]
                 out_r[...] = jnp.where(live_r[...] > 0.0, last, 0.0).astype(BF)
@@ -419,7 +420,7 @@
     row = lambda i: (i, 0)
     whole = lambda i: (0, 0)
     rows = spec((RB, D), row)
-    part = lambda k: spec((RB, D), lambda i: (jnp.clip(i - k * each, 0, each - 1), 0))
+    part = lambda k: spec((RB, D), lambda i: (jnp.clip(i - starts[k], 0, counts[k] - 1), 0))
     ins = [rows] * 4 + [part(k) for k in range(len(branches))] + [spec((1, D), whole), spec((RB, 1), row), spec((RB, 128), row)]
     return call(kernel, (n // RB,), ins, [rows, rows], [jax.ShapeDtypeStruct((n, D), F32), jax.ShapeDtypeStruct((n, D), BF)],
                 flops=10 * n * D, nbytes=18 * n * D, name="finish")(gout, e, base, extra, *branches, held, live, stats)
@@ -432,7 +433,7 @@
     def __init__(self):
         i = lax.axis_index("dp")
         c, x, y = lax.rem(i, 2), lax.rem(lax.div(i, 2), 2), lax.div(i, 4)
-        self.me = i
+        self.me, self.core = i, c
         self.dx, self.dy, self.dc = 2 - 4 * x, 4 - 8 * y, 1 - 2 * c
         self.nx, self.ny, self.nc = i + self.dx, i + self.dy, i + self.dc
         self.diag = i + self.dx + self.dy
@@ -530,7 +531,7 @@
             send_to("dp", peer, src, dst, self.send.at[k, n], self.recv.at[k, n]).wait_send()
 
 
-AHEAD, LAG, BACK = 3, 2, 7
+AHEAD, LAG, BACK = 3, 1, 5
 
 
 class LineSum:
@@ -654,12 +655,18 @@
     def arrived(self, k, n, dst):
         send_to("dp", self.spot.nc, dst, dst, self.send.at[k, n], self.recv.at[k, n]).wait_recv()
 
-    def first(self, k):
+    def hand(self, k):
         s, grad = self.spot, self.items[k][0]
         for m, slot in enumerate((s.me, s.nx, s.ny, s.diag)):
             self.go(k, m, lambda: s.nc, lambda slot=slot: grad.at[slot + s.dc], lambda m=m: self.sib[k].at[m])
+
+    def hold(self, k):
         for m in range(4):
             self.load(k, m).start()
+
+    def first(self, k):
+        self.hand(k)
+        self.hold(k)
 
     def load(self, k, m):
         s = self.spot
@@ -784,42 +791,54 @@
 
 
 class Products:
-    def __init__(self, lefts, rights, grads, rhs, lbuf, obuf, rsem, lsem, osem):
+    def __init__(self, core, lefts, rights, grads, rhs, lbuf, obuf, rsem, lsem, osem):
+        self.core = core
         self.lefts, self.rights, self.grads = lefts, rights, grads
         self.rhs, self.lbuf, self.obuf, self.rsem, self.lsem, self.osem = rhs, lbuf, obuf, rsem, lsem, osem
 
     def right(self, i, slot):
         return pltpu.make_async_copy(self.rights[i], self.rhs[slot], self.rsem.at[i])
 
+    def split(self, k):
+        slots, r, _ = self.grads[k].shape
+        return r == 256 and self.lefts[k].shape[1] == slots * r
+
+    def block(self, k, m):
+        if self.split(k):
+            late = m // 4 if isinstance(m, int) else lax.div(m, 4)
+            return 2 * (m - 4 * late) + 1 - self.core - late + 2 * late * self.core
+        return m
+
+    def columns(self, block):
+        return pl.ds(block * 256 if isinstance(block, int) else pl.multiple_of(block * 256, 256), 256)
+
     def left(self, k, m):
         odd = m % 2 if isinstance(m, int) else lax.rem(m, 2)
-        cols = pl.ds(m * 256 if isinstance(m, int) else pl.multiple_of(m * 256, 256), 256)
-        return pltpu.make_async_copy(self.lefts[k].at[:, cols], self.lbuf.at[odd], self.lsem.at[odd])
+        return pltpu.make_async_copy(self.lefts[k].at[:, self.columns(self.block(k, m))], self.lbuf.at[odd], self.lsem.at[odd])
 
     def stores(self, k, m):
         odd = m % 2 if isinstance(m, int) else lax.rem(m, 2)
         grad, o, sem = self.grads[k], self.obuf.at[odd], self.osem.at[odd]
-        slots, r, c = grad.shape
-        if r == 256 and self.lefts[k].shape[1] == slots * r:
-            return [pltpu.make_async_copy(o.at[:, pl.ds(0, c)], grad.at[m], sem.at[0])]
-        rows = pl.ds(m * 256 if isinstance(m, int) else pl.multiple_of(m * 256, 256), 256)
-        return [pltpu.make_async_copy(o.at[:, pl.ds(s * c, c)], grad.at[s, rows], sem.at[s]) for s in range(slots)]
-
-    def run(self, k, slot, hooks):
-        count = self.lefts[k].shape[1] // 256
+        slots, _, c = grad.shape
+        block = self.block(k, m)
+        if self.split(k):
+            return [pltpu.make_async_copy(o.at[:, pl.ds(0, c)], grad.at[block], sem.at[0])]
+        return [pltpu.make_async_copy(o.at[:, pl.ds(s * c, c)], grad.at[s, self.columns(block)], sem.at[s]) for s in range(slots)]
+
+    def run(self, k, slot, start, stop, hooks):
         right = self.rhs[slot]
         width = right.shape[1]
-        self.left(k, 0).start()
-
-        @pl.loop(0, count)
+        self.left(k, start).start()
+
+        @pl.loop(start, stop)
         def _(m):
             self.left(k, m).wait()
 
-            @pl.when(m + 1 < count)
+            @pl.when(m + 1 < stop)
             def _():
                 self.left(k, m + 1).start()
 
-            @pl.when(m >= 2)
+            @pl.when(m >= start + 2)
             def _():
                 for copy in self.stores(k, m - 2):
                     copy.wait()
@@ -831,7 +850,7 @@
             for at in sorted(hooks):
                 pl.when(m == at)(hooks[at])
 
-        for m in (count - 2, count - 1):
+        for m in (stop - 2, stop - 1):
             for copy in self.stores(k, m):
                 copy.wait()
 
@@ -872,8 +891,9 @@
     shapes = [jax.ShapeDtypeStruct(e.shape, BF), jax.ShapeDtypeStruct((more_rows, D), BF)] + [jax.ShapeDtypeStruct((8,) + d, BF) for d in dims] + [jax.ShapeDtypeStruct(d, F32) for d in dims]
     shapes += [jax.ShapeDtypeStruct((1, C), F32), jax.ShapeDtypeStruct((1, U), F32), jax.ShapeDtypeStruct((1, D), F32)]
     scratch = [pltpu.VMEM((2, step, D), BF)] + [pltpu.VMEM((n + more_rows, D), BF)] * 2 + [DMA((chunks, 3)), DMA((chunks, 3)), DMA((chunks + 2,))]
-    scratch += [DMA((4, 10)), DMA((4, 10)), DMA((4, 4))]
-    for r, c in dims:
+    cut = [dims[0], (dims[1][0] // 2, w), (dims[1][0] // 2, w), dims[2], dims[3]]
+    scratch += [DMA((5, 10)), DMA((5, 10)), DMA((5, 4))]
+    for r, c in cut:
         scratch += [pltpu.VMEM((4, r, c), BF), pltpu.VMEM((4, r, c), BF), pltpu.VMEM((2, r // 2, c), BF), pltpu.VMEM((2, r // 2, c), BF),
                     pltpu.VMEM((r // 2, c), BF), pltpu.VMEM((r // 2, c), BF)]
     wide = max(D, U)
@@ -890,10 +910,14 @@
         spot.meet(True)
         line = LineSum(spot, [(e_r, 0, total, n), (more_r, first_row, more_total, more_rows)], stage, land, swap, send, recv, local)
         send, recv, local = take(3)
-        bufs = [take(6) for _ in range(4)]
-        S = Scatter(spot, list(zip(grads, owned)), *[[b[i] for b in bufs] for i in range(6)], send, recv, local)
+        bufs = [take(6) for _ in range(5)]
+        half = cut[1][0]
+        low, high = pl.ds(0, half), pl.ds(half, half)
+        items = [(grads[0], owned[0]), (grads[1].at[:, low], owned[1].at[low]), (grads[1].at[:, high], owned[1].at[high])]
+        items += [(grads[2], owned[2]), (grads[3], owned[3])]
+        S = Scatter(spot, items, *[[b[i] for b in bufs] for i in range(6)], send, recv, local)
         wide_r, narrow_r, lbuf, obuf, rsem, lsem, osem = take(7)
-        W = Products(left_rs, right_rs, grads, (wide_r, narrow_r), lbuf, obuf, rsem, lsem, osem)
+        W = Products(spot.core, left_rs, right_rs, grads, (wide_r, narrow_r), lbuf, obuf, rsem, lsem, osem)
         W.right(0, 0).start()
         W.right(1, 1).start()
         def steps(*what):
@@ -906,39 +930,47 @@
         slot = (line.slot,)
         line.begin()
         W.right(0, 0).wait()
-        W.run(0, 0, {})
+        W.run(1, 0, 0, 4, {1: steps(slot)})
+        S.first(1)
+        line.slot()
+        W.run(0, 0, 0, left_rs[0].shape[1] // 256, {})
         S.first(0)
-        W.run(1, 0, {1: steps(slot), 3: steps(slot), 5: steps(slot, (S.second, 0)), 7: steps(slot)})
-        S.first(1)
+        S.second(1)
+        line.slot()
+        W.run(1, 0, 4, 8, {5: steps(slot)})
+        S.first(2)
         W.sums(0, sum_rs[2])
         W.right(2, 0).start()
+        S.second(0)
+        line.slot()
         W.right(1, 1).wait()
-        W.run(2, 1, {2: steps(slot), 5: steps(slot, (S.second, 1))})
-        S.first(2)
+        W.run(2, 1, 0, 8, {0: steps((S.second, 2), (S.third, 1)), 2: steps(slot), 5: steps((S.hand, 3), slot)})
+        S.hold(3)
         line.slot()
+        S.third(0)
+        S.second(3)
         W.right(2, 0).wait()
-        W.run(3, 0, {1: steps(slot), 2: steps((S.third, 0)), 4: steps(slot, (S.second, 2)), 7: steps(slot)})
-        S.first(3)
+        W.run(3, 0, 0, 8, {1: steps(slot), 3: steps((S.third, 2)), 4: steps(slot), 5: steps((S.hand, 4)), 6: steps(slot)})
+        S.hold(4)
         line.slot()
+        S.second(4)
         W.sums(1, sum_rs[0])
-        S.third(1)
-        line.slot()
-        S.second(3)
-        line.slot()
-        W.sums(0, sum_rs[1])
-        S.last(0)
-        line.slot()
-        line.slot()
-        S.third(2)
-        line.slot()
-        S.last(1)
-        line.slot()
         line.slot()
         S.third(3)
         line.slot()
+        W.sums(0, sum_rs[1])
+        line.slot()
+        S.last(0)
+        S.last(1)
+        line.slot()
         S.last(2)
+        line.slot()
+        line.slot()
+        S.third(4)
+        line.slot()
+        S.last(3)
         line.finish()
-        S.last(3)
+        S.last(4)
         line.close()
         S.close()
 
@@ -1155,8 +1187,8 @@
             sums = None
             branch, gr = lax.optimization_barrier((branch, gr))
             branch_sum = [None] * 4
-            quarter = rows // 4
-            branch_sum[0] = lax.psum(branch[:quarter], "mp")
+            cuts = [0, rows // 4, rows * 7 // 16, rows * 13 // 16, rows]
+            branch_sum[0] = lax.psum(branch[:cuts[1]], "mp")
     big, little = [None] * LAYERS, [None] * LAYERS
     for layer in reversed(range(LAYERS)):
         wq, wd, wu, wn = full[layer]
@@ -1164,13 +1196,13 @@
         dctx, df = back_in(gr, gp, wd, wn)
         dmix = attend_backward(mixed, dctx, seg_col, seg_row, cos, sin)
         e, norm_sums = back_out(dmix, df, wq, wu, tokens_in, extra, held[layer], stats)
-        if layer == 0:
-            branch_sum[2], e = lax.optimization_barrier((branch_sum[2], e))
+        before = 0 if layer else 2
+        branch_sum[before], e = lax.optimization_barrier((branch_sum[before], e))
         at = 1 if layer else 3
-        e, branch_sum[at], big[layer], qsum, usum, low_sums = links.turn(e, branch, at * quarter, quarter, (ctx, act, h1, h2), (gr, dmix, df), 3 + layer)
+        e, branch_sum[at], big[layer], qsum, usum, low_sums = links.turn(e, branch, cuts[at], cuts[at + 1] - cuts[at], (ctx, act, h1, h2), (gr, dmix, df), 3 + layer)
         little[layer] = (qsum, usum, norm_sums, low_sums if sums is None else sums)
         if layer:
-            branch_sum[0], e, third = lax.optimization_barrier((branch_sum[0], e, branch[2 * quarter:3 * quarter]))
+            e, third = lax.optimization_barrier((e, branch[cuts[2]:cuts[3]]))
             branch_sum[2] = lax.psum(third, "mp")
         if layer:
             gout, gr, sums = norm_back(gout, e, tokens_in, extra, held[layer], stats)

time: 846 us -> 825 us (0.975)
  Pallas kernels: 789 us -> 766 us
    pallas_call x2, Pallas kernels: 289 us -> 267 us  [sum_scatter(): pl.pallas_call(kernel, in_specs=[HBM] * 9, out_specs=outs, out_shape=shap...]
  transfers between devices with their start and end apart: 2 -> 2, of which waited for: 0 -> 0; matrix products, arithmetic and copies ran while one was open for 1% -> 1% of each run, Pallas kernels for 32% -> 15%
where the time goes in v7:
time: 825 us; the launch traced here: 818 us
  Pallas kernels  766 us (93%)
  local copies, waits for them, and re-layouts  18.4 us (2%)
  other arithmetic  18.4 us (2%)
  between operations  14.9 us (2%)
    pallas_call x2, Pallas kernels, sum_scatter(): pl.pallas_call(kernel, in_specs=[HBM] * 9, out_specs=outs, out_shape=shap...  267 us
    pallas_call x2, Pallas kernels, link_kernel(): pl.pallas_call(kernel, in_specs=[HBM] * (ng + len(parts)), out_specs=[HBM...  181 us
    pallas_call x2, Pallas kernels, project(): call(kernel, (nq + nu,), ins, outs, shapes, scratch, ident=5 if ng else N...  86.5 us
    pallas_call x2, Pallas kernels, back_out(): call(kernel, (D // NB,), [spec((n, C), whole, True), spec((n, U), whole,...  45.3 us
    pallas_call x2, Pallas kernels, adam_layer(): pl.pallas_call(kernel, grid=(steps,), in_specs=ins, out_specs=[at(b) for...  38.4 us
    pallas_call x2, Pallas kernels, back_in(): call(kernel, (nr + nu,), [spec((n, D), lambda j: (0, 0), True), spec((n,...  36.5 us
    pallas_call x2, Pallas kernels, branch_out(): call(kernel, (dp,), [spec((n, R), whole, True), spec((n, U), whole, True)...  32.2 us
    pallas_call x2, Pallas kernels, attend_backward(): call(kernel, (H,), [part(0), part(1), part(2), spec((n, HD), lambda h: (0...  23 us
  transfers between devices with their start and end apart: 2, of which 0 were waited for; matrix products, arithmetic and copies ran while one was open for 1% of the time, Pallas kernels for 15%

profile of v7, /device:TPU:0, one launch (start us, length us, event | category | flops | bytes accessed | tf_op | source)
XLA Modules:
  0.0 818.3 jit_solution(1255148400468730132)
XLA Ops:
  7.3 0.7 copy.132
  8.0 0.8 reshape.300
  8.8 0.7 copy.131
  9.6 0.6 fusion.18.refs_0_
  10.2 67.6 %gather.1 = (bf16[8,32,128]{2,1,0:T(8,128)(2,1)}, bf16[8,256,1536]{2,1,0:T(8,128)(2,1)}, bf16[8,256,2048]{2,1,0:T(8,128)(2,1)}) custom-call(bf16[32,128]{1,0:T(8,128)(2,1)} %fusion.18.refs_0_, bf16[2,256,1536]{2,1,0:T(8,128)(2,1)} %refs_0_.9, bf16[2,256,2048]{2,1,0:T(8,128)(2,1)} %refs_2_.7), custom_call_target="tpu_custom_call" | custom-call | bytes 14712832 | tf_op jit(solution)/shard_map/gather/pallas_call | solution.py:780
  77.8 0.9 copy.188
  79.3 0.7 squeeze.31.refs_3_
  80.3 0.7 squeeze.32.refs_7_
  81.3 4.6 broadcast_select_fusion.g_r.refs_6_
  85.8 1.0 add_select_fusion.sc_r
  87.5 0.6 pad_maximum_fusion.refs_1_.refs_5_
  88.1 1.9 fusion
  90.0 1.3 maximum_maximum_fusion
  91.3 53.9 %project.2 = (bf16[1024,2048]{1,0:T(8,128)(2,1)}, bf16[1024,2048]{1,0:T(8,128)(2,1)}, bf16[1024,1536]{1,0:T(8,128)(2,1)}, bf16[1024,2048]{1,0:T(8,128)(2,1)}, bf...) custom-call(bf16[1024,2048]{1,0:T(8,128)(2,1)} %base_r.3, ...), custom_call_target="tpu_custom_call" | custom-call | flops 15032385536 | bytes 38797312 | tf_op jit(solution)/shard_map/project/pallas_call | solution.py:186
  145.2 6.6 attend.2.c_r.refs_2_
  151.8 16.1 %branch.2.refs_4_ = bf16[1024,2048]{1,0:T(8,128)(2,1)} custom-call(bf16[1024,512]{1,0:T(8,128)(2,1)} %attend.2.c_r.refs_2_, bf16[1024,2048]{1,0:T(8,128)(2,1)} %get-tuple-element.126.a_r.refs_3_, bf16[8,512,256]{2,1,0:T(8,128)(2,1)} %get-tuple-element.127.wd_r, bf16[8,2048,256]{2,1,0:T(8,128)(2,1)} %get-tuple-element.128.wn_r), custom_call_target="tpu_custom_call" | custom-call | flops 10737418240 | bytes 19922944 | tf_op jit(solution)/shard_map/branch/pallas_call | solution.py:269
  167.9 113.7 %sum_gather.1 = (bf16[8,256,1536]{2,1,0:T(8,128)(2,1)}, bf16[8,512,256]{2,1,0:T(8,128)(2,1)}, bf16[8,256,2048]{2,1,0:T(8,128)(2,1)}, bf16[8,2048,256]{2,1,0:T(8,128)(2,1)}, bf16[1024,2048]{1,0:T(8,128)(2,1)}) custom-call(bf16[2,256,1536]{2,1,0:T(8,128)(2,1)} %refs_0_.9, bf16[2,512,256]{2,1,0:T(8,128)(2,1)} %refs_1_.7, bf16[2,256,2048]{2,1,0:T(8,128)(2,1)} %refs_2_.7, ...), custom_call_target="tpu_custom_call" | custom-call | bytes 29360128 | tf_op jit(solution)/shard_map/sum_gather/pallas_call | solution.py:780
  281.6 0.7 squeeze.35.refs_4_
  282.3 0.7 squeeze.36.refs_8_
  283.0 0.6 pad_maximum_fusion.1.refs_2_.refs_6_.vec_r
  283.7 32.6 %project.3 = (bf16[1024,2048]{1,0:T(8,128)(2,1)}, bf16[1024,2048]{1,0:T(8,128)(2,1)}, bf16[1024,1536]{1,0:T(8,128)(2,1)}, bf16[1024,2048]{1,0:T(8,128)(2,1)}, bf...) custom-call(bf16[1024,2048]{1,0:T(8,128)(2,1)} %base_r.3, bf16[1024,2048]{1,0:T(8,128)(2,1)} %get-tuple-element.129.refs_1_.refs_5_.extra_r, ...), custom_call_target="tpu_custom_call" | custom-call | flops 15032385536 | bytes 38797312 | tf_op jit(solution)/shard_map/project/pallas_call | solution.py:186
  316.2 6.7 attend.3.c_r.refs_2_
  323.0 16.1 %branch.3.refs_1_ = bf16[1024,2048]{1,0:T(8,128)(2,1)} custom-call(bf16[1024,512]{1,0:T(8,128)(2,1)} %attend.3.c_r.refs_2_, bf16[1024,2048]{1,0:T(8,128)(2,1)} %get-tuple-element.133.a_r.refs_3_, bf16[8,512,256]{2,1,0:T(8,128)(2,1)} %get-tuple-element.134.wd_r, bf16[8,2048,256]{2,1,0:T(8,128)(2,1)} %get-tuple-element.135.wn_r), custom_call_target="tpu_custom_call" | custom-call | flops 10737418240 | bytes 19922944 | tf_op jit(solution)/shard_map/branch/pallas_call | solution.py:269
  339.0 2.3 slice.85
  341.4 18.2 %back_in.2 = (bf16[1024,512]{1,0:T(8,128)(2,1)}, bf16[1024,2048]{1,0:T(8,128)(2,1)}) custom-call(bf16[1024,2048]{1,0:T(8,128)(2,1)} %broadcast_select_fusion.g_r.refs_6_, bf16[1024,2048]{1,0:T(8,128)(2,1)} %get-tuple-element.138.gp_r, bf16[8,512,256]{2,1,0:T(8,128)(2,1)} %get-tuple-element.134.wd_r, bf16[8,2048,256]{2,1,0:T(8,128)(2,1)} %get-tuple-element.135.wn_r), custom_call_target="tpu_custom_call" | custom-call | flops 10737418240 | bytes 24117248 | tf_op jit(solution)/shard_map/back_in/pallas_call | solution.py:301
  359.6 11.5 %attend_back.2.refs_0_.refs_7_ = bf16[1024,1536]{1,0:T(8,128)(2,1)} custom-call(bf16[1024,1536]{1,0:T(8,128)(2,1)} %get-tuple-element.132.q_r.k_r.v_r, bf16[1024,1536]{1,0:T(8,128)(2,1)} %get-tuple-element.132.q_r.k_r.v_r, bf16[1024,1536]{1,0:T(8,128)(2,1)} %get-tuple-element.132.q_r.k_r.v_r, bf16[1024,512]{1,0:T(8,128)(2,1)} %get-tuple-element.139.do_r, ...), custom_call_target="tpu_custom_call" | custom-call | flops 3355443200 | bytes 6291456 | tf_op jit(solution)/shard_map/attend_back/pallas_call | solution.py:252
  371.1 23.0 %back_out.2 = (bf16[1024,2048]{1,0:T(8,128)(2,1)}, f32[4,2048]{1,0:T(4,128)}) custom-call(bf16[1024,1536]{1,0:T(8,128)(2,1)} %attend_back.2.refs_0_.refs_7_, bf16[1024,2048]{1,0:T(8,128)(2,1)} %get-tuple-element.140.refs_1_.refs_8_, bf16[2048,1536]{1,0:T(8,128)(2,1)} %bitcast.99, bf16[2048,2048]{1,0:T(8,128)(2,1)} %bitcast.95, bf16[1024,2048]{1,0:T(8,128)(2,1)} %base_r.3, ...), custom_call_target="tpu_custom_call" | custom-call | flops 15032385536 | bytes 34603008 | tf_op jit(solution)/shard_map/back_out/pallas_call | solution.py:337
  394.1 2.8 slice.86
  396.8 1.0 copy.145.refs_5_
  397.9 0.8 copy.191
  399.3 134.3 %sum_scatter.2 = (bf16[1024,2048]{1,0:T(8,128)(2,1)}, bf16[192,2048]{1,0:T(8,128)(2,1)}, bf16[8,512,256]{2,1,0:T(8,128)(2,1)}, bf16[8,2048,256]{2,1,0:T(8,128)(2...) custom-call(bf16[1024,2048]{1,0:T(8,128)(2,1)} %get-tuple-element.14, ...), custom_call_target="tpu_custom_call" | custom-call | flops 25769803776 | bytes 50331648 | tf_op jit(solution)/shard_map/sum_scatter/pallas_call | solution.py:978
  533.6 14.8 %norm_back.1 = (f32[1024,2048]{1,0:T(8,128)}, bf16[1024,2048]{1,0:T(8,128)(2,1)}, f32[1,2048]{1,0:T(1,128)}) custom-call(bf16[1024,2048]{1,0:T(8,128)(2,1)} %broadcast_select_fusion.g_r.refs_6_, bf16[1024,2048]{1,0:T(8,128)(2,1)} %get-tuple-element.147.e_r, bf16[1024,2048]{1,0:T(8,128)(2,1)} %base_r.3, ...), custom_call_target="tpu_custom_call" | custom-call | flops 20971520 | bytes 33554432 | tf_op jit(solution)/shard_map/norm_back/pallas_call | solution.py:391
  549.2 0.7 reduce.15
  550.0 1.4 reduce.16
  551.4 0.7 reduce.17
  552.1 18.3 %back_in.3 = (bf16[1024,512]{1,0:T(8,128)(2,1)}, bf16[1024,2048]{1,0:T(8,128)(2,1)}) custom-call(bf16[1024,2048]{1,0:T(8,128)(2,1)} %get-tuple-element.150.g_r.refs_6_, bf16[1024,2048]{1,0:T(8,128)(2,1)} %get-tuple-element.151.gp_r, bf16[8,512,256]{2,1,0:T(8,128)(2,1)} %get-tuple-element.127.wd_r, bf16[8,2048,256]{2,1,0:T(8,128)(2,1)} %get-tuple-element.128.wn_r), custom_call_target="tpu_custom_call" | custom-call | flops 10737418240 | bytes 24117248 | tf_op jit(solution)/shard_map/back_in/pallas_call | solution.py:301
  570.4 11.6 %attend_back.3.refs_0_.refs_7_ = bf16[1024,1536]{1,0:T(8,128)(2,1)} custom-call(bf16[1024,1536]{1,0:T(8,128)(2,1)} %get-tuple-element.125.q_r.k_r.v_r, bf16[1024,1536]{1,0:T(8,128)(2,1)} %get-tuple-element.125.q_r.k_r.v_r, bf16[1024,1536]{1,0:T(8,128)(2,1)} %get-tuple-element.125.q_r.k_r.v_r, bf16[1024,512]{1,0:T(8,128)(2,1)} %get-tuple-element.152.do_r, ...), custom_call_target="tpu_custom_call" | custom-call | flops 3355443200 | bytes 6291456 | tf_op jit(solution)/shard_map/attend_back/pallas_call | solution.py:252
  582.0 22.3 %back_out.3 = (bf16[1024,2048]{1,0:T(8,128)(2,1)}, f32[4,2048]{1,0:T(4,128)}) custom-call(bf16[1024,1536]{1,0:T(8,128)(2,1)} %attend_back.3.refs_0_.refs_7_, bf16[1024,2048]{1,0:T(8,128)(2,1)} %get-tuple-element.153.refs_1_.refs_8_, bf16[2048,1536]{1,0:T(8,128)(2,1)} %bitcast.97, bf16[2048,2048]{1,0:T(8,128)(2,1)} %bitcast.93, bf16[1024,2048]{1,0:T(8,128)(2,1)} %base_r.3, ...), custom_call_target="tpu_custom_call" | custom-call | flops 15032385536 | bytes 34603008 | tf_op jit(solution)/shard_map/back_out/pallas_call | solution.py:337
  604.3 0.8 copy.192
  605.1 19.3 %adam.2 = (f32[2,256,1536]{2,1,0:T(8,128)}, f32[2,256,1536]{2,1,0:T(8,128)}, f32[2,256,1536]{2,1,0:T(8,128)}, f32[2,256,1536]{2,1,0:T(8,128)}, f32[2,512,256]{2,...) custom-call(bf16[2,256,1536]{2,1,0:T(8,128)(2,1)} %refs_0_.9, ...), custom_call_target="tpu_custom_call" | custom-call | flops 31457280 | bytes 47185920 | tf_op jit(solution)/shard_map/adam/pallas_call | solution.py:1062
  624.5 132.7 %sum_scatter.3 = (bf16[1024,2048]{1,0:T(8,128)(2,1)}, bf16[192,2048]{1,0:T(8,128)(2,1)}, bf16[8,512,256]{2,1,0:T(8,128)(2,1)}, bf16[8,2048,256]{2,1,0:T(8,128)(2...) custom-call(bf16[1024,2048]{1,0:T(8,128)(2,1)} %get-tuple-element.15, ...), custom_call_target="tpu_custom_call" | custom-call | flops 25769803776 | bytes 50331648 | tf_op jit(solution)/shard_map/sum_scatter/pallas_call | solution.py:978
  757.1 0.7 reduce
  758.0 1.4 reduce.14
  759.7 8.6 %small_sum.1 = f32[32,128]{1,0:T(8,128)S(1)} custom-call(f32[8,32,128]{2,1,0:T(8,128)S(1)} %bitcast.74), custom_call_target="tpu_custom_call" | custom-call | tf_op jit(solution)/shard_map/small_sum/pallas_call | solution.py:1025
  771.1 0.6 subtract_subtract_fusion
  771.7 0.7 subtract_subtract_fusion.2
  772.4 19.7 %finish.1 = (f32[1024,2048]{1,0:T(8,128)}, bf16[1024,2048]{1,0:T(8,128)(2,1)}) custom-call(f32[1024,2048]{1,0:T(8,128)} %get-tuple-element.148.g_r, bf16[1024,2048]{1,0:T(8,128)(2,1)} %get-tuple-element.159.e_r, bf16[1024,2048]{1,0:T(8,128)(2,1)} %base_r.3, bf16[1024,2048]{1,0:T(8,128)(2,1)} %get-tuple-element.129.refs_1_.refs_5_.extra_r, ...), custom_call_target="tpu_custom_call" | custom-call | flops 20971520 | bytes 37748736 | tf_op jit(solution)/shard_map/finish/pallas_call | solution.py:425
  792.1 19.1 %adam.3 = (f32[2,256,1536]{2,1,0:T(8,128)}, f32[2,256,1536]{2,1,0:T(8,128)}, f32[2,256,1536]{2,1,0:T(8,128)}, f32[2,256,1536]{2,1,0:T(8,128)}, f32[2,512,256]{2,...) custom-call(bf16[2,256,1536]{2,1,0:T(8,128)(2,1)} %refs_0_.9, ...), custom_call_target="tpu_custom_call", output_to_operand_aliasing={{0}: (16, {}), {1}: (17, {}), {2}: (18, {}), {3}: (19, {}),... | custom-call | flops 31457280 | bytes 47185920 | tf_op jit(solution)/shard_map/adam/pallas_call | solution.py:1062
  (103 shorter events, 6.8 us)
Async XLA Ops:
  7.2 71.7 %copy-start.14 = (s32[1,4]{1,0:T(1,128)S(1)}, s32[1,4]{1,0:T(1,128)}, u32[]{:S(2)}) copy-start(s32[1,4]{1,0:T(1,128)} %param.26) | copy-start | bytes 52
  7.2 392.0 %all-reduce.5.cloned.1.call-start = ((), (), s32[]{:S(2)}) async-start(), calls=%async_computation | async-start | bytes 2097152 | tf_op jit(solution)/shard_map/psum | solution.py:1191
  341.4 283.0 %all-reduce.7.cloned.1.call-start = ((), (), s32[]{:S(2)}) async-start(), calls=%async_computation.1 | async-start | bytes 3145728 | tf_op jit(solution)/shard_map/psum | solution.py:1206
  533.6 14.8 %copy-start.13 = (f32[1,1536]{1,0:T(1,128)S(1)}, f32[1,1536]{1,0:T(1,128)}, u32[]{:S(2)}) copy-start(f32[1,1536]{1,0:T(1,128)} %get-tuple-element.209) | copy-start | bytes 18436
  533.6 15.6 %copy-start.12 = (f32[1,2048]{1,0:T(1,128)S(1)}, f32[1,2048]{1,0:T(1,128)}, u32[]{:S(2)}) copy-start(f32[1,2048]{1,0:T(1,128)} %get-tuple-element.211) | copy-start | bytes 24580
  533.6 17.8 %copy-start.11 = (f32[1,2048]{1,0:T(1,128)S(1)}, f32[1,2048]{1,0:T(1,128)}, u32[]{:S(2)}) copy-start(f32[1,2048]{1,0:T(1,128)} %get-tuple-element.213) | copy-start | bytes 24580
  624.4 144.7 %copy-start.3 = (bf16[2,12,16]{2,0,1:T(2,128)(2,1)S(1)}, bf16[2,12,16]{2,0,1:T(2,128)(2,1)}, u32[]{:S(2)}) copy-start(bf16[2,12,16]{2,0,1:T(2,128)(2,1)} %param.31) | copy-start | bytes 2308
  624.4 144.7 %copy-start.7 = (f32[2,12,16]{2,0,1:T(2,128)S(1)}, f32[2,12,16]{2,0,1:T(2,128)}, u32[]{:S(2)}) copy-start(f32[2,12,16]{2,0,1:T(2,128)} %param.45) | copy-start | bytes 4612
  624.4 144.7 %copy-start.8 = (f32[2,12,16]{2,0,1:T(2,128)S(1)}, f32[2,12,16]{2,0,1:T(2,128)}, u32[]{:S(2)}) copy-start(f32[2,12,16]{2,0,1:T(2,128)} %param.38) | copy-start | bytes 4612
  624.4 146.7 %copy-start.2 = (bf16[2,16,16]{2,1,0:T(8,128)(2,1)S(1)}, bf16[2,16,16]{2,1,0:T(8,128)(2,1)}, u32[]{:S(2)}) copy-start(bf16[2,16,16]{2,1,0:T(8,128)(2,1)} %param.32) | copy-start | bytes 3076
  624.4 146.7 %copy-start.5 = (f32[2,16,16]{2,1,0:T(8,128)S(1)}, f32[2,16,16]{2,1,0:T(8,128)}, u32[]{:S(2)}) copy-start(f32[2,16,16]{2,1,0:T(8,128)} %param.46) | copy-start | bytes 6148
  624.4 146.7 %copy-start.6 = (f32[2,16,16]{2,1,0:T(8,128)S(1)}, f32[2,16,16]{2,1,0:T(8,128)}, u32[]{:S(2)}) copy-start(f32[2,16,16]{2,1,0:T(8,128)} %param.39) | copy-start | bytes 6148
  624.4 147.3 %copy-start.4 = (bf16[2,6,256]{2,0,1:T(2,128)(2,1)S(1)}, bf16[2,6,256]{2,0,1:T(2,128)(2,1)}, u32[]{:S(2)}) copy-start(bf16[2,6,256]{2,0,1:T(2,128)(2,1)} %param.33) | copy-start | bytes 18436
  624.4 147.3 %copy-start.9 = (f32[2,6,256]{2,0,1:T(2,128)S(1)}, f32[2,6,256]{2,0,1:T(2,128)}, u32[]{:S(2)}) copy-start(f32[2,6,256]{2,0,1:T(2,128)} %param.47) | copy-start | bytes 36868
  624.4 147.3 %copy-start.10 = (f32[2,6,256]{2,0,1:T(2,128)S(1)}, f32[2,6,256]{2,0,1:T(2,128)}, u32[]{:S(2)}) copy-start(f32[2,6,256]{2,0,1:T(2,128)} %param.40) | copy-start | bytes 36868
  771.0 21.1 %copy-start = (f32[2,16,16]{2,1,0:T(8,128)}, f32[2,16,16]{2,1,0:T(8,128)S(1)}, u32[]{:S(2)}) copy-start(f32[2,16,16]{2,1,0:T(8,128)S(1)} %reshape.322) | copy-start | bytes 6148
  771.1 21.0 %copy-start.1 = (f32[2,6,256]{2,0,1:T(2,128)}, f32[2,6,256]{2,0,1:T(2,128)S(1)}, u32[]{:S(2)}) copy-start(f32[2,6,256]{2,0,1:T(2,128)S(1)} %constant_dynamic-update-slice_fusion) | copy-start | bytes 36868
Sparse Core Ops, SparseCore 0:
  341.5 49.4 all-reduce.4
  548.6 67.1 all-reduce.6

commit v8 on v7

--- a/solution.py
+++ b/solution.py
@@ -256,18 +256,22 @@
                 flops=H * n * 640 * HD * 10, nbytes=4 * n * C, name="attend_back")(mixed, mixed, mixed, dctx, seg_col, seg_row, cos, sin)
 
 
-def branch_out(ctx, act, wd, wn):
+def branch_out(ctx, act, wd, wn, cuts=None):
     n, R = ctx.shape
     U = act.shape[1]
     dp, _, w = wd.shape
-
-    def kernel(c_r, a_r, wd_r, wn_r, o_r):
-        o_r[...] = (jnp.dot(c_r[...], wd_r[...], preferred_element_type=F32) + jnp.dot(a_r[...], wn_r[...], preferred_element_type=F32)).astype(BF)
+    cuts = cuts or [0, n]
+    parts = list(zip(cuts, cuts[1:]))
+
+    def kernel(c_r, a_r, wd_r, wn_r, *o_rs):
+        out = (jnp.dot(c_r[...], wd_r[...], preferred_element_type=F32) + jnp.dot(a_r[...], wn_r[...], preferred_element_type=F32)).astype(BF)
+        for (low, high), o_r in zip(parts, o_rs):
+            o_r[...] = out[low:high]
 
     whole = lambda s: (0, 0)
     pick = lambda s: (s, 0, 0)
     return call(kernel, (dp,), [spec((n, R), whole, True), spec((n, U), whole, True), spec((None, R, w), pick), spec((None, U, w), pick)],
-                spec((n, w), lambda s: (0, s)), jax.ShapeDtypeStruct((n, dp * w), BF),
+                [spec((high - low, w), lambda s: (0, s)) for low, high in parts], [jax.ShapeDtypeStruct((high - low, dp * w), BF) for low, high in parts],
                 flops=2 * n * dp * w * (R + U), nbytes=2 * (n * (R + U) + dp * w * (R + U + n)), name="branch")(ctx, act, wd, wn)
 
 
@@ -370,7 +374,7 @@
 
 def norm_back(gout, e, base, extra, vec, stats):
     n, D = base.shape
-    RB = 128
+    RB = 256
 
     def kernel(g_r, e_r, base_r, extra_r, vec_r, st_r, dx_r, low_r, sum_r):
         x = base_r[...].astype(F32) + extra_r[...].astype(F32) + vec_r[4:5, :] + vec_r[5:6, :]
@@ -402,7 +406,7 @@
 
 def finish(gout, e, base, extra, branches, held, live, stats):
     n, D = base.shape
-    RB = 64
+    RB = 128
     counts = [b.shape[0] // RB for b in branches]
     starts = [sum(counts[:k]) for k in range(len(counts))]
 
@@ -878,7 +882,7 @@
         G.last(k)
 
 
-def sum_scatter(ident, e, more, first_row, more_rows, lefts, rights, step=64):
+def sum_scatter(ident, e, more, lefts, rights, step=64):
     n, D = e.shape
     HBM = pl.BlockSpec(memory_space=pl.ANY)
     VM_ = pl.BlockSpec(memory_space=pltpu.VMEM)
@@ -886,6 +890,7 @@
     w = D // 8
     dims = [(lefts[0].shape[1], w), (lefts[1].shape[1], w), (w, C), (w, U)]
     DMA = pltpu.SemaphoreType.DMA
+    more_rows = more.shape[0]
     chunks = (n + more_rows) // step
     outs = [HBM] * 2 + [HBM] * 4 + [VM_] * 4 + [VM_] * 3
     shapes = [jax.ShapeDtypeStruct(e.shape, BF), jax.ShapeDtypeStruct((more_rows, D), BF)] + [jax.ShapeDtypeStruct((8,) + d, BF) for d in dims] + [jax.ShapeDtypeStruct(d, F32) for d in dims]
@@ -908,7 +913,7 @@
         stage, land, swap, send, recv, local = take(6)
         spot = Spot()
         spot.meet(True)
-        line = LineSum(spot, [(e_r, 0, total, n), (more_r, first_row, more_total, more_rows)], stage, land, swap, send, recv, local)
+        line = LineSum(spot, [(e_r, 0, total, n), (more_r, 0, more_total, more_rows)], stage, land, swap, send, recv, local)
         send, recv, local = take(3)
         bufs = [take(6) for _ in range(5)]
         half = cut[1][0]
@@ -1038,7 +1043,7 @@
 
 
 def adam_layer(layer, weights, grads, firsts, seconds, before):
-    steps = 8
+    steps = 4
     blocks = [(w.shape[1] // steps, w.shape[2]) for w in weights]
 
     def kernel(*refs):
@@ -1104,7 +1109,7 @@
     def middle(self, branch, shards):
         return self.share(branch), self.weights(shards, 1)
 
-    def turn(self, e, more, first_row, more_rows, lefts, rights, ident):
+    def turn(self, e, more, lefts, rights, ident):
         ctx, act, h1, h2 = lefts
         gr, dmix, df = rights
         w = gr.shape[1] // lax.axis_size("dp")
@@ -1112,8 +1117,7 @@
         gn, _ = weight_grad(act, gr, w=w)
         gq, qsum = weight_grad(h1, dmix)
         gu, usum = weight_grad(h2, df)
-        more = self.share(more[first_row:first_row + more_rows])
-        return self.share(e), more, self.owned((gq, gd, gu, gn)), qsum, usum, low_sums
+        return self.share(e), self.share(more), self.owned((gq, gd, gu, gn)), qsum, usum, low_sums
 
 
 class ChipLinks:
@@ -1130,8 +1134,8 @@
         got = link_kernel("sum_gather", 2, shards, [1] * 4, branch)
         return got[4], self.full(got[:4])
 
-    def turn(self, e, more, first_row, more_rows, lefts, rights, ident):
-        return sum_scatter(ident, e, more, first_row, more_rows, lefts, rights)
+    def turn(self, e, more, lefts, rights, ident):
+        return sum_scatter(ident, e, more, lefts, rights)
 
     def small(self, pieces, shared):
         return small_sum(pieces, shared)
@@ -1177,18 +1181,16 @@
             wd, wn = more
             full[0] = wq, wd, wu, wn
         ctx = attend_forward(mixed, seg_col, seg_row)
-        branch = branch_out(ctx, act, wd, wn)
+        branch = branch_out(ctx, act, wd, wn, [0, rows // 4, rows * 3 // 8, rows * 3 // 4, rows] if layer else None)
         kept.append((h1, h2, mixed, act, gp, stats, ctx, extra))
         if layer == 0:
-            extra, made = links.middle(branch, weights)
+            extra, made = links.middle(branch[0], weights)
             full.append(made)
         else:
             gout = gr = jnp.where(live, cotangent, 0).astype(BF)
             sums = None
             branch, gr = lax.optimization_barrier((branch, gr))
-            branch_sum = [None] * 4
-            cuts = [0, rows // 4, rows * 7 // 16, rows * 13 // 16, rows]
-            branch_sum[0] = lax.psum(branch[:cuts[1]], "mp")
+            branch_sum = [lax.psum(branch[0], "mp"), None, None, None]
     big, little = [None] * LAYERS, [None] * LAYERS
     for layer in reversed(range(LAYERS)):
         wq, wd, wu, wn = full[layer]
@@ -1199,10 +1201,10 @@
         before = 0 if layer else 2
         branch_sum[before], e = lax.optimization_barrier((branch_sum[before], e))
         at = 1 if layer else 3
-        e, branch_sum[at], big[layer], qsum, usum, low_sums = links.turn(e, branch, cuts[at], cuts[at + 1] - cuts[at], (ctx, act, h1, h2), (gr, dmix, df), 3 + layer)
+        e, branch_sum[at], big[layer], qsum, usum, low_sums = links.turn(e, branch[at], (ctx, act, h1, h2), (gr, dmix, df), 3 + layer)
         little[layer] = (qsum, usum, norm_sums, low_sums if sums is None else sums)
         if layer:
-            e, third = lax.optimization_barrier((e, branch[cuts[2]:cuts[3]]))
+            e, third = lax.optimization_barrier((e, branch[2]))
             branch_sum[2] = lax.psum(third, "mp")
         if layer:
             gout, gr, sums = norm_back(gout, e, tokens_in, extra, held[layer], stats)

time: 825 us -> 815 us (0.988)
  no operation moved by 1% of the time
where the time goes in v8:
time: 815 us; the launch traced here: 809 us
  Pallas kernels  762 us (93%)
  other arithmetic  18.4 us (2%)
  between operations  14.9 us (2%)
  local copies, waits for them, and re-layouts  13.4 us (2%)
    pallas_call x2, Pallas kernels, sum_scatter(): pl.pallas_call(kernel, in_specs=[HBM] * 9, out_specs=outs, out_shape=shap...  270 us
    pallas_call x2, Pallas kernels, link_kernel(): pl.pallas_call(kernel, in_specs=[HBM] * (ng + len(parts)), out_specs=[HBM...  181 us
    pallas_call x2, Pallas kernels, project(): call(kernel, (nq + nu,), ins, outs, shapes, scratch, ident=5 if ng else N...  86.5 us
    pallas_call x2, Pallas kernels, back_out(): call(kernel, (D // NB,), [spec((n, C), whole, True), spec((n, U), whole,...  45.2 us
    pallas_call x2, Pallas kernels, back_in(): call(kernel, (nr + nu,), [spec((n, D), lambda j: (0, 0), True), spec((n,...  36.5 us
    pallas_call x2, Pallas kernels, adam_layer(): pl.pallas_call(kernel, grid=(steps,), in_specs=ins, out_specs=[at(b) for...  34.1 us
    pallas_call x2, Pallas kernels, branch_out(): call(kernel, (dp,), [spec((n, R), whole, True), spec((n, U), whole, True)...  32.1 us
    pallas_call x2, Pallas kernels, attend_backward(): call(kernel, (H,), [part(0), part(1), part(2), spec((n, HD), lambda h: (0...  23 us
  transfers between devices with their start and end apart: 2, of which 0 were waited for; matrix products, arithmetic and copies ran while one was open for 1% of the time, Pallas kernels for 15%

profile of v8, /device:TPU:0, one launch (start us, length us, event | category | flops | bytes accessed | tf_op | source)
XLA Modules:
  0.0 808.8 jit_solution(4243094451713379769)
XLA Ops:
  7.3 0.7 copy.132
  8.0 0.8 reshape.300
  8.8 0.7 copy.131
  9.6 0.6 fusion.18.refs_0_
  10.2 67.6 %gather.1 = (bf16[8,32,128]{2,1,0:T(8,128)(2,1)}, bf16[8,256,1536]{2,1,0:T(8,128)(2,1)}, bf16[8,256,2048]{2,1,0:T(8,128)(2,1)}) custom-call(bf16[32,128]{1,0:T(8,128)(2,1)} %fusion.18.refs_0_, bf16[2,256,1536]{2,1,0:T(8,128)(2,1)} %refs_0_.9, bf16[2,256,2048]{2,1,0:T(8,128)(2,1)} %refs_2_.7), custom_call_target="tpu_custom_call" | custom-call | bytes 14712832 | tf_op jit(solution)/shard_map/gather/pallas_call | solution.py:784
  77.8 0.9 copy.188
  79.3 0.7 squeeze.31.refs_3_
  80.3 0.7 squeeze.32.refs_7_
  81.3 4.6 broadcast_select_fusion.g_r.refs_6_
  85.8 1.0 add_select_fusion.sc_r
  87.5 0.6 pad_maximum_fusion.refs_1_.refs_5_
  88.1 1.9 fusion
  90.0 1.3 maximum_maximum_fusion
  91.3 53.9 %project.2 = (bf16[1024,2048]{1,0:T(8,128)(2,1)}, bf16[1024,2048]{1,0:T(8,128)(2,1)}, bf16[1024,1536]{1,0:T(8,128)(2,1)}, bf16[1024,2048]{1,0:T(8,128)(2,1)}, bf...) custom-call(bf16[1024,2048]{1,0:T(8,128)(2,1)} %base_r.3, ...), custom_call_target="tpu_custom_call" | custom-call | flops 15032385536 | bytes 38797312 | tf_op jit(solution)/shard_map/project/pallas_call | solution.py:186
  145.2 6.6 attend.2.c_r.refs_2_
  151.8 16.1 %branch.2.refs_4_ = bf16[1024,2048]{1,0:T(8,128)(2,1)} custom-call(bf16[1024,512]{1,0:T(8,128)(2,1)} %attend.2.c_r.refs_2_, bf16[1024,2048]{1,0:T(8,128)(2,1)} %get-tuple-element.133.a_r.refs_3_, bf16[8,512,256]{2,1,0:T(8,128)(2,1)} %get-tuple-element.134.wd_r, bf16[8,2048,256]{2,1,0:T(8,128)(2,1)} %get-tuple-element.135.wn_r), custom_call_target="tpu_custom_call" | custom-call | flops 10737418240 | bytes 19922944 | tf_op jit(solution)/shard_map/branch/pallas_call | solution.py:273
  167.9 113.7 %sum_gather.1 = (bf16[8,256,1536]{2,1,0:T(8,128)(2,1)}, bf16[8,512,256]{2,1,0:T(8,128)(2,1)}, bf16[8,256,2048]{2,1,0:T(8,128)(2,1)}, bf16[8,2048,256]{2,1,0:T(8,128)(2,1)}, bf16[1024,2048]{1,0:T(8,128)(2,1)}) custom-call(bf16[2,256,1536]{2,1,0:T(8,128)(2,1)} %refs_0_.9, bf16[2,512,256]{2,1,0:T(8,128)(2,1)} %refs_1_.7, bf16[2,256,2048]{2,1,0:T(8,128)(2,1)} %refs_2_.7, ...), custom_call_target="tpu_custom_call" | custom-call | bytes 29360128 | tf_op jit(solution)/shard_map/sum_gather/pallas_call | solution.py:784
  281.7 0.7 squeeze.35.refs_4_
  282.4 0.7 squeeze.36.refs_8_
  283.1 0.6 pad_maximum_fusion.1.refs_2_.refs_6_.vec_r
  283.7 32.6 %project.3 = (bf16[1024,2048]{1,0:T(8,128)(2,1)}, bf16[1024,2048]{1,0:T(8,128)(2,1)}, bf16[1024,1536]{1,0:T(8,128)(2,1)}, bf16[1024,2048]{1,0:T(8,128)(2,1)}, bf...) custom-call(bf16[1024,2048]{1,0:T(8,128)(2,1)} %base_r.3, bf16[1024,2048]{1,0:T(8,128)(2,1)} %get-tuple-element.136.refs_1_.refs_5_.extra_r, ...), custom_call_target="tpu_custom_call" | custom-call | flops 15032385536 | bytes 38797312 | tf_op jit(solution)/shard_map/project/pallas_call | solution.py:186
  316.3 6.7 attend.3.c_r.refs_2_
  323.0 16.0 %branch.3 = (bf16[256,2048]{1,0:T(8,128)(2,1)}, bf16[128,2048]{1,0:T(8,128)(2,1)}, bf16[384,2048]{1,0:T(8,128)(2,1)}, bf16[256,2048]{1,0:T(8,128)(2,1)}) custom-call(bf16[1024,512]{1,0:T(8,128)(2,1)} %attend.3.c_r.refs_2_, bf16[1024,2048]{1,0:T(8,128)(2,1)} %get-tuple-element.140.a_r.refs_3_, bf16[8,512,256]{2,1,0:T(8,128)(2,1)} %get-tuple-element.141.wd_r, ...), custom_call_target="tpu_custom_call" | custom-call | flops 10737418240 | bytes 19922944 | tf_op jit(solution)/shard_map/branch/pallas_call | solution.py:273
  339.1 18.2 %back_in.2 = (bf16[1024,512]{1,0:T(8,128)(2,1)}, bf16[1024,2048]{1,0:T(8,128)(2,1)}) custom-call(bf16[1024,2048]{1,0:T(8,128)(2,1)} %broadcast_select_fusion.g_r.refs_6_, bf16[1024,2048]{1,0:T(8,128)(2,1)} %get-tuple-element.149.gp_r, bf16[8,512,256]{2,1,0:T(8,128)(2,1)} %get-tuple-element.141.wd_r, bf16[8,2048,256]{2,1,0:T(8,128)(2,1)} %get-tuple-element.142.wn_r), custom_call_target="tpu_custom_call" | custom-call | flops 10737418240 | bytes 24117248 | tf_op jit(solution)/shard_map/back_in/pallas_call | solution.py:305
  357.3 11.5 %attend_back.2.refs_0_.refs_7_ = bf16[1024,1536]{1,0:T(8,128)(2,1)} custom-call(bf16[1024,1536]{1,0:T(8,128)(2,1)} %get-tuple-element.139.q_r.k_r.v_r, bf16[1024,1536]{1,0:T(8,128)(2,1)} %get-tuple-element.139.q_r.k_r.v_r, bf16[1024,1536]{1,0:T(8,128)(2,1)} %get-tuple-element.139.q_r.k_r.v_r, bf16[1024,512]{1,0:T(8,128)(2,1)} %get-tuple-element.150.do_r, ...), custom_call_target="tpu_custom_call" | custom-call | flops 3355443200 | bytes 6291456 | tf_op jit(solution)/shard_map/attend_back/pallas_call | solution.py:252
  368.8 23.0 %back_out.2 = (bf16[1024,2048]{1,0:T(8,128)(2,1)}, f32[4,2048]{1,0:T(4,128)}) custom-call(bf16[1024,1536]{1,0:T(8,128)(2,1)} %attend_back.2.refs_0_.refs_7_, bf16[1024,2048]{1,0:T(8,128)(2,1)} %get-tuple-element.151.refs_1_.refs_8_, bf16[2048,1536]{1,0:T(8,128)(2,1)} %bitcast.99, bf16[2048,2048]{1,0:T(8,128)(2,1)} %bitcast.95, bf16[1024,2048]{1,0:T(8,128)(2,1)} %base_r.3, ...), custom_call_target="tpu_custom_call" | custom-call | flops 15032385536 | bytes 34603008 | tf_op jit(solution)/shard_map/back_out/pallas_call | solution.py:341
  391.8 1.0 copy.145.refs_5_
  392.8 0.8 copy.191
  393.6 0.6 fusion.20.refs_4_
  394.2 128.4 %sum_scatter.2 = (bf16[1024,2048]{1,0:T(8,128)(2,1)}, bf16[128,2048]{1,0:T(8,128)(2,1)}, bf16[8,512,256]{2,1,0:T(8,128)(2,1)}, bf16[8,2048,256]{2,1,0:T(8,128)(2...) custom-call(bf16[1024,2048]{1,0:T(8,128)(2,1)} %get-tuple-element.15, ...), custom_call_target="tpu_custom_call" | custom-call | flops 25769803776 | bytes 50331648 | tf_op jit(solution)/shard_map/sum_scatter/pallas_call | solution.py:983
  522.6 13.4 %norm_back.1 = (f32[1024,2048]{1,0:T(8,128)}, bf16[1024,2048]{1,0:T(8,128)(2,1)}, f32[1,2048]{1,0:T(1,128)}) custom-call(bf16[1024,2048]{1,0:T(8,128)(2,1)} %broadcast_select_fusion.g_r.refs_6_, bf16[1024,2048]{1,0:T(8,128)(2,1)} %get-tuple-element.160.e_r, bf16[1024,2048]{1,0:T(8,128)(2,1)} %base_r.3, ...), custom_call_target="tpu_custom_call" | custom-call | flops 20971520 | bytes 33554432 | tf_op jit(solution)/shard_map/norm_back/pallas_call | solution.py:395
  536.8 0.7 reduce.15
  537.6 1.4 reduce.16
  539.0 0.7 reduce.17
  539.7 18.3 %back_in.3 = (bf16[1024,512]{1,0:T(8,128)(2,1)}, bf16[1024,2048]{1,0:T(8,128)(2,1)}) custom-call(bf16[1024,2048]{1,0:T(8,128)(2,1)} %get-tuple-element.163.g_r.refs_6_, bf16[1024,2048]{1,0:T(8,128)(2,1)} %get-tuple-element.164.gp_r, bf16[8,512,256]{2,1,0:T(8,128)(2,1)} %get-tuple-element.134.wd_r, bf16[8,2048,256]{2,1,0:T(8,128)(2,1)} %get-tuple-element.135.wn_r), custom_call_target="tpu_custom_call" | custom-call | flops 10737418240 | bytes 24117248 | tf_op jit(solution)/shard_map/back_in/pallas_call | solution.py:305
  558.1 11.5 %attend_back.3.refs_0_.refs_7_ = bf16[1024,1536]{1,0:T(8,128)(2,1)} custom-call(bf16[1024,1536]{1,0:T(8,128)(2,1)} %get-tuple-element.132.q_r.k_r.v_r, bf16[1024,1536]{1,0:T(8,128)(2,1)} %get-tuple-element.132.q_r.k_r.v_r, bf16[1024,1536]{1,0:T(8,128)(2,1)} %get-tuple-element.132.q_r.k_r.v_r, bf16[1024,512]{1,0:T(8,128)(2,1)} %get-tuple-element.165.do_r, ...), custom_call_target="tpu_custom_call" | custom-call | flops 3355443200 | bytes 6291456 | tf_op jit(solution)/shard_map/attend_back/pallas_call | solution.py:252
  569.6 22.3 %back_out.3 = (bf16[1024,2048]{1,0:T(8,128)(2,1)}, f32[4,2048]{1,0:T(4,128)}) custom-call(bf16[1024,1536]{1,0:T(8,128)(2,1)} %attend_back.3.refs_0_.refs_7_, bf16[1024,2048]{1,0:T(8,128)(2,1)} %get-tuple-element.166.refs_1_.refs_8_, bf16[2048,1536]{1,0:T(8,128)(2,1)} %bitcast.97, bf16[2048,2048]{1,0:T(8,128)(2,1)} %bitcast.93, bf16[1024,2048]{1,0:T(8,128)(2,1)} %base_r.3, ...), custom_call_target="tpu_custom_call" | custom-call | flops 15032385536 | bytes 34603008 | tf_op jit(solution)/shard_map/back_out/pallas_call | solution.py:341
  591.8 0.8 copy.192
  592.6 17.2 %adam.2 = (f32[2,256,1536]{2,1,0:T(8,128)}, f32[2,256,1536]{2,1,0:T(8,128)}, f32[2,256,1536]{2,1,0:T(8,128)}, f32[2,256,1536]{2,1,0:T(8,128)}, f32[2,512,256]{2,...) custom-call(bf16[2,256,1536]{2,1,0:T(8,128)(2,1)} %refs_0_.9, ...), custom_call_target="tpu_custom_call" | custom-call | flops 31457280 | bytes 47185920 | tf_op jit(solution)/shard_map/adam/pallas_call | solution.py:1067
  610.0 141.6 %sum_scatter.3 = (bf16[1024,2048]{1,0:T(8,128)(2,1)}, bf16[256,2048]{1,0:T(8,128)(2,1)}, bf16[8,512,256]{2,1,0:T(8,128)(2,1)}, bf16[8,2048,256]{2,1,0:T(8,128)(2...) custom-call(bf16[1024,2048]{1,0:T(8,128)(2,1)} %get-tuple-element.16, ...), custom_call_target="tpu_custom_call" | custom-call | flops 25769803776 | bytes 50331648 | tf_op jit(solution)/shard_map/sum_scatter/pallas_call | solution.py:983
  751.6 0.7 reduce
  752.5 1.4 reduce.14
  754.2 9.0 %small_sum.1 = f32[32,128]{1,0:T(8,128)S(1)} custom-call(f32[8,32,128]{2,1,0:T(8,128)S(1)} %bitcast.74), custom_call_target="tpu_custom_call" | custom-call | tf_op jit(solution)/shard_map/small_sum/pallas_call | solution.py:1030
  763.4 0.6 copy.154
  766.0 0.6 subtract_subtract_fusion
  766.7 0.7 subtract_subtract_fusion.2
  767.3 17.5 %finish.1 = (f32[1024,2048]{1,0:T(8,128)}, bf16[1024,2048]{1,0:T(8,128)(2,1)}) custom-call(f32[1024,2048]{1,0:T(8,128)} %get-tuple-element.161.g_r, bf16[1024,2048]{1,0:T(8,128)(2,1)} %get-tuple-element.173.e_r, bf16[1024,2048]{1,0:T(8,128)(2,1)} %base_r.3, bf16[1024,2048]{1,0:T(8,128)(2,1)} %get-tuple-element.136.refs_1_.refs_5_.extra_r, ...), custom_call_target="tpu_custom_call" | custom-call | flops 20971520 | bytes 37748736 | tf_op jit(solution)/shard_map/finish/pallas_call | solution.py:429
  784.8 16.9 %adam.3 = (f32[2,256,1536]{2,1,0:T(8,128)}, f32[2,256,1536]{2,1,0:T(8,128)}, f32[2,256,1536]{2,1,0:T(8,128)}, f32[2,256,1536]{2,1,0:T(8,128)}, f32[2,512,256]{2,...) custom-call(bf16[2,256,1536]{2,1,0:T(8,128)(2,1)} %refs_0_.9, ...), custom_call_target="tpu_custom_call", output_to_operand_aliasing={{0}: (16, {}), {1}: (17, {}), {2}: (18, {}), {3}: (19, {}),... | custom-call | flops 31457280 | bytes 47185920 | tf_op jit(solution)/shard_map/adam/pallas_call | solution.py:1067
  (101 shorter events, 5.5 us)
Async XLA Ops:
  7.2 71.7 %copy-start.14 = (s32[1,4]{1,0:T(1,128)S(1)}, s32[1,4]{1,0:T(1,128)}, u32[]{:S(2)}) copy-start(s32[1,4]{1,0:T(1,128)} %param.26) | copy-start | bytes 52
  7.2 386.9 %all-reduce.5.cloned.1.call-start = ((), (), s32[]{:S(2)}) async-start(), calls=%async_computation | async-start | bytes 2097152 | tf_op jit(solution)/shard_map/psum | solution.py:1193
  339.0 270.8 %all-reduce.7.cloned.1.call-start = ((), (), s32[]{:S(2)}) async-start(), calls=%async_computation.1 | async-start | bytes 3145728 | tf_op jit(solution)/shard_map/psum | solution.py:1208
  522.5 13.5 %copy-start.13 = (f32[1,1536]{1,0:T(1,128)S(1)}, f32[1,1536]{1,0:T(1,128)}, u32[]{:S(2)}) copy-start(f32[1,1536]{1,0:T(1,128)} %get-tuple-element.223) | copy-start | bytes 18436
  522.6 14.2 %copy-start.12 = (f32[1,2048]{1,0:T(1,128)S(1)}, f32[1,2048]{1,0:T(1,128)}, u32[]{:S(2)}) copy-start(f32[1,2048]{1,0:T(1,128)} %get-tuple-element.225) | copy-start | bytes 24580
  522.6 16.5 %copy-start.11 = (f32[1,2048]{1,0:T(1,128)S(1)}, f32[1,2048]{1,0:T(1,128)}, u32[]{:S(2)}) copy-start(f32[1,2048]{1,0:T(1,128)} %get-tuple-element.227) | copy-start | bytes 24580
  609.9 154.1 %copy-start.3 = (bf16[2,12,16]{2,0,1:T(2,128)(2,1)S(1)}, bf16[2,12,16]{2,0,1:T(2,128)(2,1)}, u32[]{:S(2)}) copy-start(bf16[2,12,16]{2,0,1:T(2,128)(2,1)} %param.31) | copy-start | bytes 2308
  609.9 154.1 %copy-start.7 = (f32[2,12,16]{2,0,1:T(2,128)S(1)}, f32[2,12,16]{2,0,1:T(2,128)}, u32[]{:S(2)}) copy-start(f32[2,12,16]{2,0,1:T(2,128)} %param.45) | copy-start | bytes 4612
  609.9 154.1 %copy-start.8 = (f32[2,12,16]{2,0,1:T(2,128)S(1)}, f32[2,12,16]{2,0,1:T(2,128)}, u32[]{:S(2)}) copy-start(f32[2,12,16]{2,0,1:T(2,128)} %param.38) | copy-start | bytes 4612
  609.9 156.1 %copy-start.2 = (bf16[2,16,16]{2,1,0:T(8,128)(2,1)S(1)}, bf16[2,16,16]{2,1,0:T(8,128)(2,1)}, u32[]{:S(2)}) copy-start(bf16[2,16,16]{2,1,0:T(8,128)(2,1)} %param.32) | copy-start | bytes 3076
  609.9 156.1 %copy-start.5 = (f32[2,16,16]{2,1,0:T(8,128)S(1)}, f32[2,16,16]{2,1,0:T(8,128)}, u32[]{:S(2)}) copy-start(f32[2,16,16]{2,1,0:T(8,128)} %param.46) | copy-start | bytes 6148
  609.9 156.1 %copy-start.6 = (f32[2,16,16]{2,1,0:T(8,128)S(1)}, f32[2,16,16]{2,1,0:T(8,128)}, u32[]{:S(2)}) copy-start(f32[2,16,16]{2,1,0:T(8,128)} %param.39) | copy-start | bytes 6148
  610.0 156.7 %copy-start.4 = (bf16[2,6,256]{2,0,1:T(2,128)(2,1)S(1)}, bf16[2,6,256]{2,0,1:T(2,128)(2,1)}, u32[]{:S(2)}) copy-start(bf16[2,6,256]{2,0,1:T(2,128)(2,1)} %param.33) | copy-start | bytes 18436
  610.0 156.7 %copy-start.9 = (f32[2,6,256]{2,0,1:T(2,128)S(1)}, f32[2,6,256]{2,0,1:T(2,128)}, u32[]{:S(2)}) copy-start(f32[2,6,256]{2,0,1:T(2,128)} %param.47) | copy-start | bytes 36868
  610.0 156.7 %copy-start.10 = (f32[2,6,256]{2,0,1:T(2,128)S(1)}, f32[2,6,256]{2,0,1:T(2,128)}, u32[]{:S(2)}) copy-start(f32[2,6,256]{2,0,1:T(2,128)} %param.40) | copy-start | bytes 36868
  765.9 18.9 %copy-start = (f32[2,16,16]{2,1,0:T(8,128)}, f32[2,16,16]{2,1,0:T(8,128)S(1)}, u32[]{:S(2)}) copy-start(f32[2,16,16]{2,1,0:T(8,128)S(1)} %reshape.322) | copy-start | bytes 6148
  766.0 18.8 %copy-start.1 = (f32[2,6,256]{2,0,1:T(2,128)}, f32[2,6,256]{2,0,1:T(2,128)S(1)}, u32[]{:S(2)}) copy-start(f32[2,6,256]{2,0,1:T(2,128)S(1)} %constant_dynamic-update-slice_fusion) | copy-start | bytes 36868
Sparse Core Ops, SparseCore 0:
  339.1 49.4 all-reduce.4
  536.2 67.8 all-reduce.6

commit v9 on v8

--- a/solution.py
+++ b/solution.py
@@ -99,7 +99,9 @@
         side = None
         if ng:
             spot = Spot()
-            side = Gather(spot, [(a.at[0], b) for a, b in zip(shard_rs, full_rs)], *take(3))
+            half = full_rs[0].shape[1] // 2
+            pieces = [pl.ds(0, half), pl.ds(half, half)]
+            side = Gather(spot, [(shard_rs[0].at[0, p], full_rs[0].at[:, p]) for p in pieces], *take(3))
 
             @pl.when(j == 0)
             def _():
@@ -181,7 +183,7 @@
     DMA = pltpu.SemaphoreType.DMA
     scratch = [pltpu.VMEM((n, D), BF)] * (2 + len(xs)) + [DMA((len(xs), nr)), DMA((2, nr))]
     if ng:
-        scratch += [DMA((ng, 9)), DMA((ng, 9)), DMA((ng,))]
+        scratch += [DMA((2, 9)), DMA((2, 9)), DMA((2,))]
         shapes += [jax.ShapeDtypeStruct((8,) + v.shape[1:], v.dtype) for v in shards]
     return call(kernel, (nq + nu,), ins, outs, shapes, scratch, ident=5 if ng else None, flops=2 * n * D * (C + U), nbytes=2 * (n * D * 3 + D * (C + U) + n * (C + 2 * U)), name="project")(*xs, vec, wq, bq, cos, sin, wu, bu, *(shards or ()))
 
@@ -1127,8 +1129,8 @@
 
     def begin(self, shards, flat):
         wq, wd, wu, wn = shards
-        flat, wq, wu = link_kernel("gather", 1, [flat, wq, wu], [None, 0, 0])
-        return (wq.reshape(-1, wq.shape[2]), None, wu.reshape(-1, wu.shape[2]), None), flat, (wd, wn)
+        flat, wq, wu, wd = link_kernel("gather", 1, [flat, wq, wu, wd], [None, 0, 0, 0])
+        return (wq.reshape(-1, wq.shape[2]), wd, wu.reshape(-1, wu.shape[2]), None), flat, (wn,)
 
     def middle(self, branch, shards):
         got = link_kernel("sum_gather", 2, shards, [1] * 4, branch)
@@ -1178,7 +1180,7 @@
         wq, wd, wu, wn = full[layer]
         h1, h2, mixed, act, gp, stats, *more = project(tokens_in, extra, held[layer], wq, qb[layer], cos, sin, wu, ub[layer], later if layer == 0 else None)
         if more:
-            wd, wn = more
+            wn = more[0]
             full[0] = wq, wd, wu, wn
         ctx = attend_forward(mixed, seg_col, seg_row)
         branch = branch_out(ctx, act, wd, wn, [0, rows // 4, rows * 3 // 8, rows * 3 // 4, rows] if layer else None)

time: 815 us -> 813 us (level)
    pallas_call x2, Pallas kernels: 86.5 us -> 77.3 us  [project(): call(kernel, (nq + nu,), ins, outs, shapes, scratch, ident=5 if ng else N...]
where the time goes in v9:
time: 813 us; the launch traced here: 807 us
  Pallas kernels  760 us (93%)
  other arithmetic  18.4 us (2%)
  between operations  14.9 us (2%)
  local copies, waits for them, and re-layouts  13.4 us (2%)
    pallas_call x2, Pallas kernels, sum_scatter(): pl.pallas_call(kernel, in_specs=[HBM] * 9, out_specs=outs, out_shape=shap...  270 us
    pallas_call x2, Pallas kernels, link_kernel(): pl.pallas_call(kernel, in_specs=[HBM] * (ng + len(parts)), out_specs=[HBM...  189 us
    pallas_call x2, Pallas kernels, project(): call(kernel, (nq + nu,), ins, outs, shapes, scratch, ident=5 if ng else N...  77.3 us
    pallas_call x2, Pallas kernels, back_out(): call(kernel, (D // NB,), [spec((n, C), whole, True), spec((n, U), whole,...  45.2 us
    pallas_call x2, Pallas kernels, back_in(): call(kernel, (nr + nu,), [spec((n, D), lambda j: (0, 0), True), spec((n,...  36.6 us
    pallas_call x2, Pallas kernels, adam_layer(): pl.pallas_call(kernel, grid=(steps,), in_specs=ins, out_specs=[at(b) for...  34.1 us
    pallas_call x2, Pallas kernels, branch_out(): call(kernel, (dp,), [spec((n, R), whole, True), spec((n, U), whole, True)...  32.1 us
    pallas_call x2, Pallas kernels, attend_backward(): call(kernel, (H,), [part(0), part(1), part(2), spec((n, HD), lambda h: (0...  23 us
  transfers between devices with their start and end apart: 2, of which 0 were waited for; matrix products, arithmetic and copies ran while one was open for 1% of the time, Pallas kernels for 15%

profile of v9, /device:TPU:0, one launch (start us, length us, event | category | flops | bytes accessed | tf_op | source)
XLA Modules:
  0.0 807.2 jit_solution(16182562234492436370)
XLA Ops:
  7.3 0.7 copy.132
  8.0 0.8 reshape.300
  8.8 0.7 copy.131
  9.6 0.6 fusion.18.refs_0_
  10.2 75.1 %gather.1 = (bf16[8,32,128]{2,1,0:T(8,128)(2,1)}, bf16[8,256,1536]{2,1,0:T(8,128)(2,1)}, bf16[8,256,2048]{2,1,0:T(8,128)(2,1)}, bf16[8,512,256]{2,1,0:T(8,128)(2,1)}) custom-call(bf16[32,128]{1,0:T(8,128)(2,1)} %fusion.18.refs_0_, bf16[2,256,1536]{2,1,0:T(8,128)(2,1)} %refs_0_.9, bf16[2,256,2048]{2,1,0:T(8,128)(2,1)} %refs_2_.7, bf16[2,512,256]{2,1,0:T(8,128)(2,1)} %refs_1_.7), custom_call_target="tpu_custom_call" | custom-call | bytes 16809984 | tf_op jit(solution)/shard_map/gather/pallas_call | solution.py:786
  85.2 0.9 copy.188
  86.8 0.7 squeeze.31.refs_3_
  87.8 0.7 squeeze.32.refs_7_
  88.7 4.6 broadcast_select_fusion.g_r.refs_6_
  93.3 1.0 add_select_fusion.sc_r
  95.0 0.6 pad_maximum_fusion.refs_1_.refs_5_
  95.6 1.9 fusion
  97.5 1.3 maximum_maximum_fusion
  98.8 44.7 %project.2 = (bf16[1024,2048]{1,0:T(8,128)(2,1)}, bf16[1024,2048]{1,0:T(8,128)(2,1)}, bf16[1024,1536]{1,0:T(8,128)(2,1)}, bf16[1024,2048]{1,0:T(8,128)(2,1)}, bf...) custom-call(bf16[1024,2048]{1,0:T(8,128)(2,1)} %base_r.3, ...), custom_call_target="tpu_custom_call" | custom-call | flops 15032385536 | bytes 38797312 | tf_op jit(solution)/shard_map/project/pallas_call | solution.py:188
  143.5 6.6 attend.2.c_r.refs_2_
  150.1 16.1 %branch.2.refs_4_ = bf16[1024,2048]{1,0:T(8,128)(2,1)} custom-call(bf16[1024,512]{1,0:T(8,128)(2,1)} %attend.2.c_r.refs_2_, bf16[1024,2048]{1,0:T(8,128)(2,1)} %get-tuple-element.133.a_r.refs_3_, bf16[8,512,256]{2,1,0:T(8,128)(2,1)} %get-tuple-element.134.wd_r, bf16[8,2048,256]{2,1,0:T(8,128)(2,1)} %get-tuple-element.135.wn_r), custom_call_target="tpu_custom_call" | custom-call | flops 10737418240 | bytes 19922944 | tf_op jit(solution)/shard_map/branch/pallas_call | solution.py:275
  166.2 113.8 %sum_gather.1 = (bf16[8,256,1536]{2,1,0:T(8,128)(2,1)}, bf16[8,512,256]{2,1,0:T(8,128)(2,1)}, bf16[8,256,2048]{2,1,0:T(8,128)(2,1)}, bf16[8,2048,256]{2,1,0:T(8,128)(2,1)}, bf16[1024,2048]{1,0:T(8,128)(2,1)}) custom-call(bf16[2,256,1536]{2,1,0:T(8,128)(2,1)} %refs_0_.9, bf16[2,512,256]{2,1,0:T(8,128)(2,1)} %refs_1_.7, bf16[2,256,2048]{2,1,0:T(8,128)(2,1)} %refs_2_.7, ...), custom_call_target="tpu_custom_call" | custom-call | bytes 29360128 | tf_op jit(solution)/shard_map/sum_gather/pallas_call | solution.py:786
  280.0 0.7 squeeze.35.refs_4_
  280.7 0.7 squeeze.36.refs_8_
  281.4 0.6 pad_maximum_fusion.1.refs_2_.refs_6_.vec_r
  282.0 32.6 %project.3 = (bf16[1024,2048]{1,0:T(8,128)(2,1)}, bf16[1024,2048]{1,0:T(8,128)(2,1)}, bf16[1024,1536]{1,0:T(8,128)(2,1)}, bf16[1024,2048]{1,0:T(8,128)(2,1)}, bf...) custom-call(bf16[1024,2048]{1,0:T(8,128)(2,1)} %base_r.3, bf16[1024,2048]{1,0:T(8,128)(2,1)} %get-tuple-element.136.refs_1_.refs_5_.extra_r, ...), custom_call_target="tpu_custom_call" | custom-call | flops 15032385536 | bytes 38797312 | tf_op jit(solution)/shard_map/project/pallas_call | solution.py:188
  314.6 6.7 attend.3.c_r.refs_2_
  321.3 16.0 %branch.3 = (bf16[256,2048]{1,0:T(8,128)(2,1)}, bf16[128,2048]{1,0:T(8,128)(2,1)}, bf16[384,2048]{1,0:T(8,128)(2,1)}, bf16[256,2048]{1,0:T(8,128)(2,1)}) custom-call(bf16[1024,512]{1,0:T(8,128)(2,1)} %attend.3.c_r.refs_2_, bf16[1024,2048]{1,0:T(8,128)(2,1)} %get-tuple-element.140.a_r.refs_3_, bf16[8,512,256]{2,1,0:T(8,128)(2,1)} %get-tuple-element.141.wd_r, ...), custom_call_target="tpu_custom_call" | custom-call | flops 10737418240 | bytes 19922944 | tf_op jit(solution)/shard_map/branch/pallas_call | solution.py:275
  337.4 18.2 %back_in.2 = (bf16[1024,512]{1,0:T(8,128)(2,1)}, bf16[1024,2048]{1,0:T(8,128)(2,1)}) custom-call(bf16[1024,2048]{1,0:T(8,128)(2,1)} %broadcast_select_fusion.g_r.refs_6_, bf16[1024,2048]{1,0:T(8,128)(2,1)} %get-tuple-element.149.gp_r, bf16[8,512,256]{2,1,0:T(8,128)(2,1)} %get-tuple-element.141.wd_r, bf16[8,2048,256]{2,1,0:T(8,128)(2,1)} %get-tuple-element.142.wn_r), custom_call_target="tpu_custom_call" | custom-call | flops 10737418240 | bytes 24117248 | tf_op jit(solution)/shard_map/back_in/pallas_call | solution.py:307
  355.6 11.5 %attend_back.2.refs_0_.refs_7_ = bf16[1024,1536]{1,0:T(8,128)(2,1)} custom-call(bf16[1024,1536]{1,0:T(8,128)(2,1)} %get-tuple-element.139.q_r.k_r.v_r, bf16[1024,1536]{1,0:T(8,128)(2,1)} %get-tuple-element.139.q_r.k_r.v_r, bf16[1024,1536]{1,0:T(8,128)(2,1)} %get-tuple-element.139.q_r.k_r.v_r, bf16[1024,512]{1,0:T(8,128)(2,1)} %get-tuple-element.150.do_r, ...), custom_call_target="tpu_custom_call" | custom-call | flops 3355443200 | bytes 6291456 | tf_op jit(solution)/shard_map/attend_back/pallas_call | solution.py:254
  367.1 23.0 %back_out.2 = (bf16[1024,2048]{1,0:T(8,128)(2,1)}, f32[4,2048]{1,0:T(4,128)}) custom-call(bf16[1024,1536]{1,0:T(8,128)(2,1)} %attend_back.2.refs_0_.refs_7_, bf16[1024,2048]{1,0:T(8,128)(2,1)} %get-tuple-element.151.refs_1_.refs_8_, bf16[2048,1536]{1,0:T(8,128)(2,1)} %bitcast.99, bf16[2048,2048]{1,0:T(8,128)(2,1)} %bitcast.95, bf16[1024,2048]{1,0:T(8,128)(2,1)} %base_r.3, ...), custom_call_target="tpu_custom_call" | custom-call | flops 15032385536 | bytes 34603008 | tf_op jit(solution)/shard_map/back_out/pallas_call | solution.py:343
  390.0 1.0 copy.145.refs_5_
  391.1 0.8 copy.191
  391.8 0.6 fusion.20.refs_4_
  392.5 128.4 %sum_scatter.2 = (bf16[1024,2048]{1,0:T(8,128)(2,1)}, bf16[128,2048]{1,0:T(8,128)(2,1)}, bf16[8,512,256]{2,1,0:T(8,128)(2,1)}, bf16[8,2048,256]{2,1,0:T(8,128)(2...) custom-call(bf16[1024,2048]{1,0:T(8,128)(2,1)} %get-tuple-element.15, ...), custom_call_target="tpu_custom_call" | custom-call | flops 25769803776 | bytes 50331648 | tf_op jit(solution)/shard_map/sum_scatter/pallas_call | solution.py:985
  520.9 13.4 %norm_back.1 = (f32[1024,2048]{1,0:T(8,128)}, bf16[1024,2048]{1,0:T(8,128)(2,1)}, f32[1,2048]{1,0:T(1,128)}) custom-call(bf16[1024,2048]{1,0:T(8,128)(2,1)} %broadcast_select_fusion.g_r.refs_6_, bf16[1024,2048]{1,0:T(8,128)(2,1)} %get-tuple-element.160.e_r, bf16[1024,2048]{1,0:T(8,128)(2,1)} %base_r.3, ...), custom_call_target="tpu_custom_call" | custom-call | flops 20971520 | bytes 33554432 | tf_op jit(solution)/shard_map/norm_back/pallas_call | solution.py:397
  535.1 0.7 reduce.15
  536.0 1.4 reduce.16
  537.4 0.7 reduce.17
  538.0 18.4 %back_in.3 = (bf16[1024,512]{1,0:T(8,128)(2,1)}, bf16[1024,2048]{1,0:T(8,128)(2,1)}) custom-call(bf16[1024,2048]{1,0:T(8,128)(2,1)} %get-tuple-element.163.g_r.refs_6_, bf16[1024,2048]{1,0:T(8,128)(2,1)} %get-tuple-element.164.gp_r, bf16[8,512,256]{2,1,0:T(8,128)(2,1)} %get-tuple-element.134.wd_r, bf16[8,2048,256]{2,1,0:T(8,128)(2,1)} %get-tuple-element.135.wn_r), custom_call_target="tpu_custom_call" | custom-call | flops 10737418240 | bytes 24117248 | tf_op jit(solution)/shard_map/back_in/pallas_call | solution.py:307
  556.4 11.5 %attend_back.3.refs_0_.refs_7_ = bf16[1024,1536]{1,0:T(8,128)(2,1)} custom-call(bf16[1024,1536]{1,0:T(8,128)(2,1)} %get-tuple-element.132.q_r.k_r.v_r, bf16[1024,1536]{1,0:T(8,128)(2,1)} %get-tuple-element.132.q_r.k_r.v_r, bf16[1024,1536]{1,0:T(8,128)(2,1)} %get-tuple-element.132.q_r.k_r.v_r, bf16[1024,512]{1,0:T(8,128)(2,1)} %get-tuple-element.165.do_r, ...), custom_call_target="tpu_custom_call" | custom-call | flops 3355443200 | bytes 6291456 | tf_op jit(solution)/shard_map/attend_back/pallas_call | solution.py:254
  567.9 22.2 %back_out.3 = (bf16[1024,2048]{1,0:T(8,128)(2,1)}, f32[4,2048]{1,0:T(4,128)}) custom-call(bf16[1024,1536]{1,0:T(8,128)(2,1)} %attend_back.3.refs_0_.refs_7_, bf16[1024,2048]{1,0:T(8,128)(2,1)} %get-tuple-element.166.refs_1_.refs_8_, bf16[2048,1536]{1,0:T(8,128)(2,1)} %bitcast.97, bf16[2048,2048]{1,0:T(8,128)(2,1)} %bitcast.93, bf16[1024,2048]{1,0:T(8,128)(2,1)} %base_r.3, ...), custom_call_target="tpu_custom_call" | custom-call | flops 15032385536 | bytes 34603008 | tf_op jit(solution)/shard_map/back_out/pallas_call | solution.py:343
  590.2 0.8 copy.192
  591.0 17.2 %adam.2 = (f32[2,256,1536]{2,1,0:T(8,128)}, f32[2,256,1536]{2,1,0:T(8,128)}, f32[2,256,1536]{2,1,0:T(8,128)}, f32[2,256,1536]{2,1,0:T(8,128)}, f32[2,512,256]{2,...) custom-call(bf16[2,256,1536]{2,1,0:T(8,128)(2,1)} %refs_0_.9, ...), custom_call_target="tpu_custom_call" | custom-call | flops 31457280 | bytes 47185920 | tf_op jit(solution)/shard_map/adam/pallas_call | solution.py:1069
  608.3 141.7 %sum_scatter.3 = (bf16[1024,2048]{1,0:T(8,128)(2,1)}, bf16[256,2048]{1,0:T(8,128)(2,1)}, bf16[8,512,256]{2,1,0:T(8,128)(2,1)}, bf16[8,2048,256]{2,1,0:T(8,128)(2...) custom-call(bf16[1024,2048]{1,0:T(8,128)(2,1)} %get-tuple-element.16, ...), custom_call_target="tpu_custom_call" | custom-call | flops 25769803776 | bytes 50331648 | tf_op jit(solution)/shard_map/sum_scatter/pallas_call | solution.py:985
  750.0 0.7 reduce
  750.9 1.4 reduce.14
  752.6 9.0 %small_sum.1 = f32[32,128]{1,0:T(8,128)S(1)} custom-call(f32[8,32,128]{2,1,0:T(8,128)S(1)} %bitcast.74), custom_call_target="tpu_custom_call" | custom-call | tf_op jit(solution)/shard_map/small_sum/pallas_call | solution.py:1032
  761.8 0.6 copy.154
  764.4 0.6 subtract_subtract_fusion
  765.1 0.7 subtract_subtract_fusion.2
  765.7 17.5 %finish.1 = (f32[1024,2048]{1,0:T(8,128)}, bf16[1024,2048]{1,0:T(8,128)(2,1)}) custom-call(f32[1024,2048]{1,0:T(8,128)} %get-tuple-element.161.g_r, bf16[1024,2048]{1,0:T(8,128)(2,1)} %get-tuple-element.173.e_r, bf16[1024,2048]{1,0:T(8,128)(2,1)} %base_r.3, bf16[1024,2048]{1,0:T(8,128)(2,1)} %get-tuple-element.136.refs_1_.refs_5_.extra_r, ...), custom_call_target="tpu_custom_call" | custom-call | flops 20971520 | bytes 37748736 | tf_op jit(solution)/shard_map/finish/pallas_call | solution.py:431
  783.2 16.9 %adam.3 = (f32[2,256,1536]{2,1,0:T(8,128)}, f32[2,256,1536]{2,1,0:T(8,128)}, f32[2,256,1536]{2,1,0:T(8,128)}, f32[2,256,1536]{2,1,0:T(8,128)}, f32[2,512,256]{2,...) custom-call(bf16[2,256,1536]{2,1,0:T(8,128)(2,1)} %refs_0_.9, ...), custom_call_target="tpu_custom_call", output_to_operand_aliasing={{0}: (16, {}), {1}: (17, {}), {2}: (18, {}), {3}: (19, {}),... | custom-call | flops 31457280 | bytes 47185920 | tf_op jit(solution)/shard_map/adam/pallas_call | solution.py:1069
  (101 shorter events, 5.5 us)
Async XLA Ops:
  7.2 79.1 %copy-start.14 = (s32[1,4]{1,0:T(1,128)S(1)}, s32[1,4]{1,0:T(1,128)}, u32[]{:S(2)}) copy-start(s32[1,4]{1,0:T(1,128)} %param.26) | copy-start | bytes 52
  7.2 385.2 %all-reduce.5.cloned.1.call-start = ((), (), s32[]{:S(2)}) async-start(), calls=%async_computation | async-start | bytes 2097152 | tf_op jit(solution)/shard_map/psum | solution.py:1195
  337.3 270.9 %all-reduce.7.cloned.1.call-start = ((), (), s32[]{:S(2)}) async-start(), calls=%async_computation.1 | async-start | bytes 3145728 | tf_op jit(solution)/shard_map/psum | solution.py:1210
  520.9 13.5 %copy-start.13 = (f32[1,1536]{1,0:T(1,128)S(1)}, f32[1,1536]{1,0:T(1,128)}, u32[]{:S(2)}) copy-start(f32[1,1536]{1,0:T(1,128)} %get-tuple-element.223) | copy-start | bytes 18436
  520.9 14.2 %copy-start.12 = (f32[1,2048]{1,0:T(1,128)S(1)}, f32[1,2048]{1,0:T(1,128)}, u32[]{:S(2)}) copy-start(f32[1,2048]{1,0:T(1,128)} %get-tuple-element.225) | copy-start | bytes 24580
  520.9 16.5 %copy-start.11 = (f32[1,2048]{1,0:T(1,128)S(1)}, f32[1,2048]{1,0:T(1,128)}, u32[]{:S(2)}) copy-start(f32[1,2048]{1,0:T(1,128)} %get-tuple-element.227) | copy-start | bytes 24580
  608.2 154.2 %copy-start.3 = (bf16[2,12,16]{2,0,1:T(2,128)(2,1)S(1)}, bf16[2,12,16]{2,0,1:T(2,128)(2,1)}, u32[]{:S(2)}) copy-start(bf16[2,12,16]{2,0,1:T(2,128)(2,1)} %param.31) | copy-start | bytes 2308
  608.2 154.2 %copy-start.7 = (f32[2,12,16]{2,0,1:T(2,128)S(1)}, f32[2,12,16]{2,0,1:T(2,128)}, u32[]{:S(2)}) copy-start(f32[2,12,16]{2,0,1:T(2,128)} %param.45) | copy-start | bytes 4612
  608.3 154.1 %copy-start.8 = (f32[2,12,16]{2,0,1:T(2,128)S(1)}, f32[2,12,16]{2,0,1:T(2,128)}, u32[]{:S(2)}) copy-start(f32[2,12,16]{2,0,1:T(2,128)} %param.38) | copy-start | bytes 4612
  608.3 156.1 %copy-start.2 = (bf16[2,16,16]{2,1,0:T(8,128)(2,1)S(1)}, bf16[2,16,16]{2,1,0:T(8,128)(2,1)}, u32[]{:S(2)}) copy-start(bf16[2,16,16]{2,1,0:T(8,128)(2,1)} %param.32) | copy-start | bytes 3076
  608.3 156.1 %copy-start.5 = (f32[2,16,16]{2,1,0:T(8,128)S(1)}, f32[2,16,16]{2,1,0:T(8,128)}, u32[]{:S(2)}) copy-start(f32[2,16,16]{2,1,0:T(8,128)} %param.46) | copy-start | bytes 6148
  608.3 156.1 %copy-start.6 = (f32[2,16,16]{2,1,0:T(8,128)S(1)}, f32[2,16,16]{2,1,0:T(8,128)}, u32[]{:S(2)}) copy-start(f32[2,16,16]{2,1,0:T(8,128)} %param.39) | copy-start | bytes 6148
  608.3 156.8 %copy-start.4 = (bf16[2,6,256]{2,0,1:T(2,128)(2,1)S(1)}, bf16[2,6,256]{2,0,1:T(2,128)(2,1)}, u32[]{:S(2)}) copy-start(bf16[2,6,256]{2,0,1:T(2,128)(2,1)} %param.33) | copy-start | bytes 18436
  608.3 156.8 %copy-start.9 = (f32[2,6,256]{2,0,1:T(2,128)S(1)}, f32[2,6,256]{2,0,1:T(2,128)}, u32[]{:S(2)}) copy-start(f32[2,6,256]{2,0,1:T(2,128)} %param.47) | copy-start | bytes 36868
  608.3 156.8 %copy-start.10 = (f32[2,6,256]{2,0,1:T(2,128)S(1)}, f32[2,6,256]{2,0,1:T(2,128)}, u32[]{:S(2)}) copy-start(f32[2,6,256]{2,0,1:T(2,128)} %param.40) | copy-start | bytes 36868
  764.3 18.9 %copy-start = (f32[2,16,16]{2,1,0:T(8,128)}, f32[2,16,16]{2,1,0:T(8,128)S(1)}, u32[]{:S(2)}) copy-start(f32[2,16,16]{2,1,0:T(8,128)S(1)} %reshape.322) | copy-start | bytes 6148
  764.4 18.8 %copy-start.1 = (f32[2,6,256]{2,0,1:T(2,128)}, f32[2,6,256]{2,0,1:T(2,128)S(1)}, u32[]{:S(2)}) copy-start(f32[2,6,256]{2,0,1:T(2,128)S(1)} %constant_dynamic-update-slice_fusion) | copy-start | bytes 36868
Sparse Core Ops, SparseCore 0:
  337.5 49.3 all-reduce.4
  534.5 67.9 all-reduce.6
